TPU v7x, 32 devices: a whole 2x2x4 slice. The times are simulated.
32 devices in a mesh: row: 8 (over y, x, core), col: 4 (over z).
Axes of the slice: x: 2, y: 2, z: 4, core: 2. Of those that a mesh axis runs over, the one named last changes fastest.
Arguments:
- screened: bfloat16 [16384, 16384], P('row', 'col'), may hold values from -0.046875 to 0.046875
- val_orbitals: bfloat16 [45, 16384], P(None, 'col'), may hold values from -6 to 6
- con_orbitals: bfloat16 [64, 16384], replicated, may hold values from -6 to 6
- val_pairs: int32 [1024, 2], replicated, may hold values from 0 to 44, as said below
- con_pairs: int32 [4096, 2], replicated, may hold values from 0 to 63
Outputs:
- kernel: float32 [4096, 1024], P('row', 'col')
Inputs may be any that keep to these rules, and one draw needn't show every extreme that they name: `val_pairs`: each row holds v <= v'.
All inputs are finite; a program needn't handle non-finite values.
Results may differ from a plain program's by a relative error of at most 0.0049.
Values may be sent and summed in bfloat16 or wider, within the bound.
No kernel may reach another device: no remote copies, remote signals or barrier semaphores. Data moves between devices by JAX's collectives and lax.ppermute only.
A program may use at most 128 MiB of HBM per device.

v0:
```python
import jax
import jax.numpy as jnp
from jax import lax
from jax.sharding import PartitionSpec as P

NG = 16384


def densities(orbitals, pairs):
    numbers = lax.broadcasted_iota(jnp.int32, (1, orbitals.shape[0]), 1)
    first_hot = (pairs[:, 0:1] == numbers).astype(jnp.bfloat16)
    second_hot = (pairs[:, 1:2] == numbers).astype(jnp.bfloat16)
    first = jnp.dot(first_hot, orbitals, preferred_element_type=jnp.float32)
    second = jnp.dot(second_hot, orbitals, preferred_element_type=jnp.float32)
    return (first * second).astype(jnp.bfloat16)


def per_device(screened, val_orbitals, con_orbitals, val_pairs, con_pairs):
    val_density = densities(val_orbitals, val_pairs)
    partial_sums = lax.dot_general(
        screened, val_density, (((1,), (1,)), ((), ())), preferred_element_type=jnp.float32
    )
    screened_val = lax.psum_scatter(partial_sums, "col", scatter_dimension=1, tiled=True).astype(
        jnp.bfloat16
    )
    own_rows = screened.shape[0]
    row_start = lax.axis_index("row") * own_rows
    con_columns = lax.dynamic_slice_in_dim(con_orbitals, row_start, own_rows, 1)
    con_density = densities(con_columns, con_pairs)
    kernel = lax.psum_scatter(
        jnp.dot(con_density, screened_val, preferred_element_type=jnp.float32),
        "row",
        scatter_dimension=0,
        tiled=True,
    )
    return kernel * jnp.float32(NG ** (-0.5))


def solution(mesh):
    in_specs = (P("row", "col"), P(None, "col"), P(), P(), P())
    out_specs = P("row", "col")
    return jax.shard_map(
        per_device, mesh=mesh, in_specs=in_specs, out_specs=out_specs, check_vma=False
    )
```

profile of v0, /device:TPU:0, one launch (start us, length us, event | category | flops | bytes accessed | tf_op | source)
XLA Modules:
  0.0 274.4 jit_solution(15686640867147554996)
XLA Ops:
  6.5 0.0 copy-start
  6.5 0.0 reduce-scatter.3.cloned.1.call-start
  6.5 0.9 fusion.19
  7.4 0.0 copy-start.1
  7.4 9.2 %fusion.8 = f32[1024,4096]{1,0:T(8,128)} fusion(bf16[45,4096]{1,0:T(8,128)(2,1)} %param.6, s32[1024]{0:T(1024)S(1)} %bitcast.11), kind=kOutput, calls=%fused_computation.13 | convolution fusion | flops 377533440 | bytes 17149952 | tf_op jit(solution)/shard_map/dot_general | solution.py:13
  16.6 0.0 copy-done.1
  16.6 31.7 %convolution_bitcast_fusion = f32[2048,1024]{0,1:T(8,128)} fusion(bf16[2048,4096]{1,0:T(8,128)(2,1)} %param.5, f32[1024,4096]{1,0:T(8,128)} %fusion.8, bf16[45,4096]{1,0:T(8,128)(2,1)S(1)} %copy-done.1, s32[1024]{0:T(1024)S(1)} %bitcast.12), kind=kOutput, calls=%fused_computation.4 | convolution fusion | flops 17565790208 | bytes 42315776 | tf_op jit(solution)/shard_map/dot_general | solution.py:20
  48.3 0.0 copy-start.2
  48.3 0.0 reduce-scatter.3.cloned.1.call-update
  48.3 0.0 reduce-scatter.5.cloned.1.call-start
  48.3 0.7 copy-done.2
  49.0 0.0 copy-done
  49.1 13.8 %fusion.3 = f32[4096,2048]{1,0:T(8,128)} fusion(s32[4096]{0:T(1024)S(1)} %bitcast.9, bf16[64,16384]{1,0:T(8,128)(2,1)S(1)} %copy-done, s32[]{:T(128)S(6)} %select_n.3), kind=kOutput, calls=%fused_computation.7 | convolution fusion | flops 1074003968 | bytes 33832964 | tf_op jit(solution)/shard_map/dot_general | solution.py:13
  62.8 132.9 %reduce-scatter.3.cloned.1.call-done = f32[2048,256]{0,1:T(8,128)} async-done(((f32[2048,1024]{0,1:T(8,128)}), f32[2048,256]{0,1:T(8,128)}) %reduce-scatter.3.cloned.1.call-update) | async-done | bytes 2097168 | tf_op jit(solution)/shard_map/reduce_scatter | solution.py:23
  195.8 18.0 %fusion = f32[4096,256]{1,0:T(8,128)} fusion(f32[4096,2048]{1,0:T(8,128)} %fusion.3, f32[2048,256]{0,1:T(8,128)} %reduce-scatter.3.cloned.1.call-done, s32[4096]{0:T(1024)S(1)} %bitcast.10, bf16[64,16384]{1,0:T(8,128)(2,1)S(1)} %copy-done, s32[]{:T(128)S(6)} %select_n.3), kind=kOutput, calls=%fused_computation.1 | convolution fusion | flops 5386272768 | bytes 40124420 | tf_op jit(solution)/shard_map/dot_general | solution.py:31
  213.7 0.0 reduce-scatter.5.cloned.1.call-update
  213.8 51.9 %reduce-scatter.5.cloned.1.call-done = f32[512,256]{1,0:T(8,128)} async-done(((f32[4096,256]{1,0:T(8,128)}), f32[512,256]{1,0:T(8,128)}) %reduce-scatter.5.cloned.1.call-update) | async-done | bytes 524304 | tf_op jit(solution)/shard_map/reduce_scatter | solution.py:30
  265.7 1.9 broadcast_multiply_fusion
  (1 shorter events, 0.0 us)
Async XLA Ops:
  6.5 42.5 %copy-start = (bf16[64,16384]{1,0:T(8,128)(2,1)S(1)}, bf16[64,16384]{1,0:T(8,128)(2,1)}, u32[]{:S(2)}) copy-start(bf16[64,16384]{1,0:T(8,128)(2,1)} %param.7) | copy-start | bytes 6291460
  6.5 189.2 %reduce-scatter.3.cloned.1.call-start = ((), (), s32[]{:S(2)}) async-start(), calls=%async_computation.2 | async-start | bytes 10485760 | tf_op jit(solution)/shard_map/reduce_scatter | solution.py:23
  7.4 9.2 %copy-start.1 = (bf16[45,4096]{1,0:T(8,128)(2,1)S(1)}, bf16[45,4096]{1,0:T(8,128)(2,1)}, u32[]{:S(2)}) copy-start(bf16[45,4096]{1,0:T(8,128)(2,1)} %param.6) | copy-start | bytes 1105924
  48.3 0.8 copy-start.2
  48.3 217.4 %reduce-scatter.5.cloned.1.call-start = ((), (), s32[]{:S(2)}) async-start(), calls=%async_computation.3 | async-start | bytes 4718592 | tf_op jit(solution)/shard_map/reduce_scatter | solution.py:30
Sparse Core Ops, SparseCore 0:
  48.4 147.3 reduce-scatter.2
  213.9 51.7 reduce-scatter.4
where the time goes:
time: 275 us; the launch traced here: 274 us
  waiting for transfers between devices  185 us (67%)
  matrix products  72.6 us (26%)
  between operations  13.4 us (5%)
    reduce_scatter x1, waiting for transfers between devices, per_device(): lax.psum_scatter(partial_sums, 'col', scatter_dimension=1, tiled=True)  133 us
    reduce_scatter x1, waiting for transfers between devices, per_device(): lax.psum_scatter(jnp.dot(con_density, screened_val, preferred_element_typ...  51.9 us
    dot_general x1, matrix products, per_device(): lax.dot_general(screened, val_density, (((1,), (1,)), ((), ())), preferre...  31.7 us
    dot_general x2, matrix products, densities(): first = jnp.dot(first_hot, orbitals, preferred_element_type=jnp.float32)  22.9 us
    dot_general x1, matrix products, per_device(): jnp.dot(con_density, screened_val, preferred_element_type=jnp.float32)  18 us
  transfers between devices with their start and end apart: 2, of which 2 were waited for; matrix products, arithmetic and copies ran while one was open for 5% of the time, Pallas kernels for 0%

commit v1 on v0

v1 whole, which is shorter than its diff:
```python
import jax
import jax.numpy as jnp
from jax import lax
from jax.sharding import PartitionSpec as P

CHUNKS = 4


def one_hot_rows(index, count):
    numbers = lax.broadcasted_iota(jnp.int32, (1, count), 1)
    return (index[:, None] == numbers).astype(jnp.bfloat16)


def densities(orbitals, first, second):
    count = orbitals.shape[0]
    a = jnp.dot(one_hot_rows(first, count), orbitals, preferred_element_type=jnp.float32)
    b = jnp.dot(one_hot_rows(second, count), orbitals, preferred_element_type=jnp.float32)
    return (a * b).astype(jnp.bfloat16)


def unordered_pairs(count):
    row = jnp.arange((count // 2 + 1) * count, dtype=jnp.int32)
    first = row % count
    return first, (first + row // count) % count


def unordered_row(pairs, count):
    c, other = pairs[:, 0], pairs[:, 1]
    apart = jnp.where(other >= c, other - c, other - c + count)
    return jnp.where(apart <= count // 2, apart * count + c, (count - apart) * count + other)


def halve(part, axis, bit, size):
    rows = part.shape[0] // 2
    mine = (lax.axis_index(axis) >> bit) & 1
    sent = lax.dynamic_slice_in_dim(part, (1 - mine) * rows, rows, 0).astype(jnp.bfloat16)
    kept = lax.dynamic_slice_in_dim(part, mine * rows, rows, 0)
    got = lax.ppermute(sent, axis, [(i, i ^ (1 << bit)) for i in range(size)])
    return kept + got.astype(jnp.float32)


def double(part, axis, bit, size):
    mine = (lax.axis_index(axis) >> bit) & 1
    got = lax.ppermute(part, axis, [(i, i ^ (1 << bit)) for i in range(size)])
    return jnp.where(mine == 0, jnp.concatenate([part, got]), jnp.concatenate([got, part]))


def solution(mesh):
    n_row, n_col = mesh.shape["row"], mesh.shape["col"]
    row_bits, col_bits = n_row.bit_length() - 1, n_col.bit_length() - 1

    def per_device(screened, val_orbitals, con_orbitals, val_pairs, con_pairs):
        own_rows, grid = screened.shape[0], con_orbitals.shape[1]
        count = con_orbitals.shape[0]
        n_pairs = val_pairs.shape[0]
        chunks = max(1, min(CHUNKS, n_pairs // (n_row * n_col)))
        width = n_pairs // n_col // chunks
        me = lax.axis_index("row")
        con_columns = lax.dynamic_slice_in_dim(con_orbitals, me * own_rows, own_rows, 1)
        con_density = densities(con_columns, *unordered_pairs(count))
        own = con_pairs.shape[0] // n_row
        asked = lax.dynamic_slice_in_dim(con_pairs, me * own, own, 0)
        pick = one_hot_rows(unordered_row(asked, count), con_density.shape[0])

        by_chunk = val_pairs.reshape(n_col, chunks, width, 2)
        results = []
        for k in range(chunks):
            order = [0] + (list(range(1, row_bits)) if k % 2 == 0 else list(range(row_bits - 1, 0, -1)))
            pairs = by_chunk[:, k].reshape(n_col, n_row, width // n_row, 2).transpose(1, 0, 2, 3)
            pairs = pairs.reshape(n_col * width, 2)
            val_density = densities(val_orbitals, pairs[:, 0], pairs[:, 1])
            screened_val = lax.dot_general(
                screened, val_density, (((1,), (1,)), ((), ())), preferred_element_type=jnp.float32
            ).astype(jnp.bfloat16)
            part = lax.dot_general(
                screened_val, con_density, (((0,), (1,)), ((), ())), preferred_element_type=jnp.float32
            )
            for bit in order:
                part = halve(part, "row", bit, n_row)
            for bit in reversed(range(col_bits)):
                part = halve(part, "col", bit, n_col)
            part = part.astype(jnp.bfloat16)
            for bit in reversed(order):
                part = double(part, "row", bit, n_row)
            results.append(part)
        whole = jnp.concatenate(results)
        kernel = lax.dot_general(
            pick, whole, (((1,), (1,)), ((), ())), preferred_element_type=jnp.float32
        )
        return kernel * jnp.float32(grid ** (-0.5))

    in_specs = (P("row", "col"), P(None, "col"), P(), P(), P())
    return jax.shard_map(
        per_device, mesh=mesh, in_specs=in_specs, out_specs=P("row", "col"), check_vma=False
    )
```

time: 275 us -> 172 us (0.63)
  waiting for transfers between devices: 185 us -> 15.1 us
  starting transfers between devices: 0.04 us -> 30.8 us
  local copies, waits for them, and re-layouts: 1.59 us -> 31.8 us
  matrix products: 72.6 us -> 87.6 us
  between operations: 13.4 us -> 0.66 us
  other arithmetic: 1.87 us -> 5.49 us
    reduce_scatter x2 -> x0, waiting for transfers between devices: 185 us -> none  [the longest x1 133 us: per_device(): lax.psum_scatter(partial_sums, 'col', scatter_dimension=1, tiled=True)]
    ppermute x0 -> x32, starting transfers between devices: none -> 30.8 us  [the longest x20 20.8 us: halve(): got = lax.ppermute(sent, axis, [(i, i ^ 1 << bit) for i in range(size)])]
    ppermute x0 -> x32, waiting for transfers between devices: none -> 15.1 us  [the longest x20 10.8 us: halve(): got = lax.ppermute(sent, axis, [(i, i ^ 1 << bit) for i in range(size)])]
    unnamed x6 -> x36, local copies, waits for them, and re-layouts: 0.69 us -> 12.1 us
    dot_general x1 -> x4, matrix products: 31.7 us -> 42 us  [per_device(): lax.dot_general(screened, val_density, (((1,), (1,)), ((), ())), preferre...]
    convert_element_type x0 -> x20, local copies, waits for them, and re-layouts: none -> 6.41 us  [halve(): lax.dynamic_slice_in_dim(part, (1 - mine) * rows, rows, 0)]
    dynamic_slice x0 -> x4, local copies, waits for them, and re-layouts: none -> 6.2 us  [halve(): kept = lax.dynamic_slice_in_dim(part, mine * rows, rows, 0)]
    ppermute x0 -> x4, local copies, waits for them, and re-layouts: none -> 5.34 us  [halve(): got = lax.ppermute(sent, axis, [(i, i ^ 1 << bit) for i in range(size)])]
  transfers between devices with their start and end apart: 2 -> 32, of which waited for: 2 -> 10; matrix products, arithmetic and copies ran while one was open for 5% -> 50% of each run, Pallas kernels for 0% -> 0%
where the time goes in v1:
time: 172 us; the launch traced here: 171 us
  matrix products  87.6 us (51%)
  local copies, waits for them, and re-layouts  31.8 us (18%)
  starting transfers between devices  30.8 us (18%)
  waiting for transfers between devices  15.1 us (9%)
  other arithmetic  5.49 us (3%)
    dot_general x4, matrix products, per_device(): lax.dot_general(screened, val_density, (((1,), (1,)), ((), ())), preferre...  42 us
    dot_general x4, matrix products, per_device(): lax.dot_general(screened_val, con_density, (((0,), (1,)), ((), ())), pref...  25 us
    ppermute x20, starting transfers between devices, halve(): got = lax.ppermute(sent, axis, [(i, i ^ 1 << bit) for i in range(size)])  20.8 us
    dot_general x5, matrix products, densities(): jnp.dot(one_hot_rows(first, count), orbitals, preferred_element_type=jnp....  13.7 us
    unnamed x36, local copies, waits for them, and re-layouts  12.1 us
    ppermute x20, waiting for transfers between devices, halve(): got = lax.ppermute(sent, axis, [(i, i ^ 1 << bit) for i in range(size)])  10.8 us
    ppermute x12, starting transfers between devices, double(): got = lax.ppermute(part, axis, [(i, i ^ 1 << bit) for i in range(size)])  9.95 us
    convert_element_type x20, local copies, waits for them, and re-layouts, halve(): lax.dynamic_slice_in_dim(part, (1 - mine) * rows, rows, 0)  6.41 us
  transfers between devices with their start and end apart: 32, of which 10 were waited for; matrix products, arithmetic and copies ran while one was open for 50% of the time, Pallas kernels for 0%

profile of v1, /device:TPU:0, one launch (start us, length us, event | category | flops | bytes accessed | tf_op | source)
XLA Modules:
  0.0 171.5 jit_solution(8588378974958162297)
XLA Ops:
  0.0 0.9 reshape.50
  1.6 2.4 %fusion.14 = f32[2112,2048]{1,0:T(8,128)S(1)} fusion(s32[2112]{0:T(1024)S(1)} %get-tuple-element.18, bf16[64,16384]{1,0:T(8,128)(2,1)S(1)} %copy-done, s32[]{:T(128)S(6)} %select_n.187), kind=kOutput, calls=%fused_computation.34 | convolution fusion | flops 553783296 | bytes 17575940 | tf_op jit(solution)/shard_map/dot_general | solution.py:16
  4.1 5.2 %multiply_convert_fusion = bf16[2112,2048]{1,0:T(8,128)(2,1)} fusion(f32[2112,2048]{1,0:T(8,128)S(1)} %fusion.14, s32[2112]{0:T(1024)S(1)} %get-tuple-element.17, bf16[64,16384]{1,0:T(8,128)(2,1)S(1)} %copy-done, s32[]{:T(128)S(6)} %select_n.187), kind=kOutput, calls=%fused_computation | convolution fusion | flops 562434048 | bytes 26226692 | tf_op jit(solution)/shard_map/dot_general | solution.py:17
  9.2 2.8 %fusion.19 = f32[256,4096]{1,0:T(8,128)} fusion(bf16[45,4096]{1,0:T(8,128)(2,1)S(1)} %copy-done.2, s32[256]{0:T(256)S(1)} %bitcast.55), kind=kOutput, calls=%fused_computation.79 | convolution fusion | flops 94383360 | bytes 4563968 | tf_op jit(solution)/shard_map/dot_general | solution.py:16
  12.1 10.4 %convolution_convert_fusion.3 = bf16[256,2048]{1,0:T(8,128)(2,1)S(1)} fusion(bf16[2048,4096]{1,0:T(8,128)(2,1)} %param.5, f32[256,4096]{1,0:T(8,128)} %fusion.19, bf16[45,4096]{1,0:T(8,128)(2,1)S(1)} %copy-done.2, s32[256]{0:T(256)S(1)} %bitcast.60), kind=kOutput, calls=%fused_computation.14 | convolution fusion | flops 4391971840 | bytes 22389760 | tf_op jit(solution)/shard_map/dot_general | solution.py:72
  22.5 7.2 %fusion.50 = f32[256,2112]{0,1:T(8,128)} fusion(bf16[256,2048]{1,0:T(8,128)(2,1)S(1)} %convolution_convert_fusion.3, bf16[2112,2048]{1,0:T(8,128)(2,1)} %multiply_convert_fusion), kind=kOutput, calls=%fused_computation.133 | convolution fusion | flops 2214592512 | bytes 11862016 | tf_op jit(solution)/shard_map/dot_general | solution.py:75
  29.7 1.3 dynamic-slice_convert_fusion.3
  31.8 2.8 %fusion.20 = f32[256,4096]{1,0:T(8,128)} fusion(bf16[45,4096]{1,0:T(8,128)(2,1)S(1)} %copy-done.2, s32[256]{0:T(256)S(1)} %bitcast.56), kind=kOutput, calls=%fused_computation.80 | convolution fusion | flops 94383360 | bytes 4563968 | tf_op jit(solution)/shard_map/dot_general | solution.py:16
  34.6 10.6 %convolution_convert_fusion.2 = bf16[256,2048]{1,0:T(8,128)(2,1)S(1)} fusion(bf16[2048,4096]{1,0:T(8,128)(2,1)} %param.5, f32[256,4096]{1,0:T(8,128)} %fusion.20, bf16[45,4096]{1,0:T(8,128)(2,1)S(1)} %copy-done.2, s32[256]{0:T(256)S(1)} %bitcast.61), kind=kOutput, calls=%fused_computation.13 | convolution fusion | flops 4391971840 | bytes 22389760 | tf_op jit(solution)/shard_map/dot_general | solution.py:72
  45.2 5.9 %fusion.51 = f32[256,2112]{0,1:T(8,128)S(1)} fusion(bf16[256,2048]{1,0:T(8,128)(2,1)S(1)} %convolution_convert_fusion.2, bf16[2112,2048]{1,0:T(8,128)(2,1)} %multiply_convert_fusion), kind=kOutput, calls=%fused_computation.134 | convolution fusion | flops 2214592512 | bytes 11862016 | tf_op jit(solution)/shard_map/dot_general | solution.py:75
  51.1 1.3 copy-done.11
  52.4 0.9 dynamic-slice_convert_fusion.2
  53.6 2.8 %fusion.21 = f32[256,4096]{1,0:T(8,128)} fusion(bf16[45,4096]{1,0:T(8,128)(2,1)S(1)} %copy-done.2, s32[256]{0:T(256)S(1)} %bitcast.57), kind=kOutput, calls=%fused_computation.81 | convolution fusion | flops 94383360 | bytes 4563968 | tf_op jit(solution)/shard_map/dot_general | solution.py:16
  56.4 10.4 %convolution_convert_fusion.1 = bf16[256,2048]{1,0:T(8,128)(2,1)S(1)} fusion(bf16[2048,4096]{1,0:T(8,128)(2,1)} %param.5, f32[256,4096]{1,0:T(8,128)} %fusion.21, bf16[45,4096]{1,0:T(8,128)(2,1)S(1)} %copy-done.2, s32[256]{0:T(256)S(1)} %bitcast.62), kind=kOutput, calls=%fused_computation.12 | convolution fusion | flops 4391971840 | bytes 22389760 | tf_op jit(solution)/shard_map/dot_general | solution.py:72
  66.8 5.9 %fusion.52 = f32[256,2112]{0,1:T(8,128)S(1)} fusion(bf16[256,2048]{1,0:T(8,128)(2,1)S(1)} %convolution_convert_fusion.1, bf16[2112,2048]{1,0:T(8,128)(2,1)} %multiply_convert_fusion), kind=kOutput, calls=%fused_computation.135 | convolution fusion | flops 2214592512 | bytes 11862016 | tf_op jit(solution)/shard_map/dot_general | solution.py:75
  72.7 1.3 copy-done.12
  74.0 0.9 dynamic-slice_convert_fusion.1
  75.6 2.8 %fusion.22 = f32[256,4096]{1,0:T(8,128)} fusion(bf16[45,4096]{1,0:T(8,128)(2,1)S(1)} %copy-done.2, s32[256]{0:T(256)S(1)} %bitcast.58), kind=kOutput, calls=%fused_computation.82 | convolution fusion | flops 94383360 | bytes 4563968 | tf_op jit(solution)/shard_map/dot_general | solution.py:16
  78.4 10.6 %convolution_convert_fusion = bf16[256,2048]{1,0:T(8,128)(2,1)S(1)} fusion(bf16[2048,4096]{1,0:T(8,128)(2,1)} %param.5, f32[256,4096]{1,0:T(8,128)} %fusion.22, bf16[45,4096]{1,0:T(8,128)(2,1)S(1)} %copy-done.2, s32[256]{0:T(256)S(1)} %bitcast.63), kind=kOutput, calls=%fused_computation.11 | convolution fusion | flops 4391971840 | bytes 22389760 | tf_op jit(solution)/shard_map/dot_general | solution.py:72
  89.1 5.9 %fusion.53 = f32[256,2112]{0,1:T(8,128)S(1)} fusion(bf16[256,2048]{1,0:T(8,128)(2,1)S(1)} %convolution_convert_fusion, bf16[2112,2048]{1,0:T(8,128)(2,1)} %multiply_convert_fusion), kind=kOutput, calls=%fused_computation.136 | convolution fusion | flops 2214592512 | bytes 11862016 | tf_op jit(solution)/shard_map/dot_general | solution.py:75
  95.0 1.3 copy-done.10
  96.4 0.9 dynamic-slice_convert_fusion
  97.3 1.5 constant_dynamic-slice_fusion.3
  98.7 1.3 constant_dynamic-slice_fusion.2
  100.1 1.1 constant_dynamic-slice_fusion.1
  101.1 1.4 copy.99
  102.5 1.4 copy.101
  104.2 2.3 %constant_dynamic-slice_fusion = f32[128,2112]{0,1:T(8,128)} fusion(f32[256,2112]{0,1:T(8,128)} %copy-done.10, s32[]{:T(128)S(6)} %select_n.190), kind=kLoop, calls=%fused_computation.119 | loop fusion | bytes 2162692 | tf_op jit(solution)/shard_map/dynamic_slice | solution.py:37
  106.6 1.6 copy.105
  108.2 0.8 compare_select_fusion
  109.0 1.3 copy.85
  110.4 1.3 convert_add_fusion.3
  111.7 1.0 copy-done.4
  113.5 3.0 %collective-permute-start.1 = (bf16[64,2112]{1,0:T(8,128)(2,1)}, bf16[64,2112]{1,0:T(8,128)(2,1)S(1)}, u32[]{:S(2)}, u32[]{:S(2)}) collective-permute-start(bf16[64,2112]{1,0:T(8,128)(2,1)} %dynamic-slice_convert_fusion.7), channel_id=1, source_target_pairs={{0,8},{4,12},{8,0},{12,4},{16,24},{20,28},{24,16},{28,20},{1,9},{5... | collective-permute-start | bytes 811016 | tf_op jit(solution)/shard_map/ppermute | solution.py:38
  116.5 1.3 copy.89
  117.8 1.3 convert_add_fusion.2
  119.1 1.0 copy-done.6
  120.9 1.5 collective-permute-start.9
  122.4 1.3 copy.93
  123.9 1.0 copy-done.8
  126.1 1.3 copy.97
  127.9 2.0 %collective-permute-start.2 = (bf16[32,2112]{1,0:T(8,128)(2,1)S(1)}, bf16[32,2112]{1,0:T(8,128)(2,1)S(1)}, u32[]{:S(2)}, u32[]{:S(2)}) collective-permute-start(bf16[32,2112]{1,0:T(8,128)(2,1)S(1)} %dynamic-slice_convert_fusion.11), channel_id=1, source_target_pairs={{0,16},{4,20},{8,24},{12,28},{16,0},{20,4},{24,8},{28,12},{1,17},{... | collective-permute-start | bytes 405512 | tf_op jit(solution)/shard_map/ppermute | solution.py:38
  130.0 1.6 collective-permute-start.10
  131.6 3.9 %collective-permute-done.17 = bf16[64,2112]{1,0:T(8,128)(2,1)} collective-permute-done((bf16[64,2112]{1,0:T(8,128)(2,1)}, bf16[64,2112]{1,0:T(8,128)(2,1)}, u32[]{:S(2)}, u32[]{:S(2)}) %collective-permute-start.17) | collective-permute-done | bytes 270368 | tf_op jit(solution)/shard_map/ppermute | solution.py:38
  135.4 1.0 convert_add_fusion.5
  137.3 1.6 collective-permute-start.26
  138.9 1.1 collective-permute-done.2
  140.1 2.7 %collective-permute-start.3 = (bf16[16,2112]{1,0:T(8,128)(2,1)S(1)}, bf16[16,2112]{1,0:T(8,128)(2,1)S(1)}, u32[]{:S(2)}, u32[]{:S(2)}) collective-permute-start(bf16[16,2112]{1,0:T(8,128)(2,1)S(1)} %dynamic-slice_convert_fusion.15), channel_id=1, source_target_pairs={{0,2},{1,3},{2,0},{3,1},{4,6},{5,7},{6,4},{7,5},{8,10},{9,11},{10,... | collective-permute-start | bytes 202760 | tf_op jit(solution)/shard_map/ppermute | solution.py:38
  143.2 2.7 %collective-permute-start.19 = (bf16[16,2112]{1,0:T(8,128)(2,1)S(1)}, bf16[16,2112]{1,0:T(8,128)(2,1)S(1)}, u32[]{:S(2)}, u32[]{:S(2)}) collective-permute-start(bf16[16,2112]{1,0:T(8,128)(2,1)S(1)} %dynamic-slice_convert_fusion.13), channel_id=1, source_target_pairs={{0,2},{1,3},{2,0},{3,1},{4,6},{5,7},{6,4},{7,5},{8,10},{9,11},{10,... | collective-permute-start | bytes 202760 | tf_op jit(solution)/shard_map/ppermute | solution.py:38
  146.3 2.7 %collective-permute-done.3 = bf16[16,2112]{1,0:T(8,128)(2,1)S(1)} collective-permute-done((bf16[16,2112]{1,0:T(8,128)(2,1)S(1)}, bf16[16,2112]{1,0:T(8,128)(2,1)S(1)}, u32[]{:S(2)}, u32[]{:S(2)}) %collective-permute-start.3) | collective-permute-done | bytes 67616 | tf_op jit(solution)/shard_map/ppermute | solution.py:38
  149.2 2.0 %collective-permute-done.11 = bf16[16,2112]{1,0:T(8,128)(2,1)S(1)} collective-permute-done((bf16[16,2112]{1,0:T(8,128)(2,1)S(1)}, bf16[16,2112]{1,0:T(8,128)(2,1)S(1)}, u32[]{:S(2)}, u32[]{:S(2)}) %collective-permute-start.11) | collective-permute-done | bytes 67616 | tf_op jit(solution)/shard_map/ppermute | solution.py:38
  151.7 0.9 collective-permute-done.19
  153.5 1.4 collective-permute-start.28
  154.9 2.3 %collective-permute-start.5 = (bf16[8,2112]{1,0:T(8,128)(2,1)S(1)}, bf16[8,2112]{1,0:T(8,128)(2,1)S(1)}, u32[]{:S(2)}, u32[]{:S(2)}) collective-permute-start(bf16[8,2112]{1,0:T(8,128)(2,1)S(1)} %add_convert_fusion.3), channel_id=1, source_target_pairs={{0,16},{4,20},{8,24},{12,28},{16,0},{20,4},{24,8},{28,12},{1,17},{... | collective-permute-start | bytes 101384 | tf_op jit(solution)/shard_map/ppermute | solution.py:44
  157.4 1.7 collective-permute-start.21
  159.0 1.3 collective-permute-start.29
  160.4 0.8 collective-permute-start.6
  161.3 1.1 collective-permute-start.14
  162.4 1.4 collective-permute-start.22
  163.8 0.9 collective-permute-start.30
  165.7 1.1 collective-permute-done.22
  166.9 1.3 collective-permute-done.30
  168.5 1.1 collective-permute-done.31
  169.7 1.7 %fusion.6 = f32[512,256]{1,0:T(8,128)} fusion(s32[512]{0:T(512)S(1)} %bitcast.59, bf16[64,2112]{1,0:T(8,128)(2,1)S(1)} %maximum_select_fusion.3, bf16[64,2112]{1,0:T(8,128)(2,1)S(1)} %maximum_select_fusion.2, bf16[64,2112]{1,0:T(8,128)(2,1)S(1)} %maximum_select_fusion.1, bf16[64,2112]{1,0:T(8,128)(2,1)S(1)} %maximum_select_fusion), kind=kOutput, calls=%fused_computation.16 | convolution fusion | flops 559185920 | bytes 1607680 | tf_op jit(solution)/shard_map/dot_general | solution.py:87
  (131 shorter events, 10.9 us)
Async XLA Ops:
  0.0 1.6 copy-start
  4.1 5.2 %copy-start.2 = (bf16[45,4096]{1,0:T(8,128)(2,1)S(1)}, bf16[45,4096]{1,0:T(8,128)(2,1)}, u32[]{:S(2)}) copy-start(bf16[45,4096]{1,0:T(8,128)(2,1)} %param.6) | copy-start | bytes 1105924
  31.0 78.0 %collective-permute-start = (bf16[128,2112]{0,1:T(8,128)(2,1)S(1)}, bf16[128,2112]{0,1:T(8,128)(2,1)}, u32[]{:S(2)}, u32[]{:S(2)}) collective-permute-start(bf16[128,2112]{0,1:T(8,128)(2,1)S(1)} %dynamic-slice_convert_fusion.3), channel_id=1, source_target_pairs={{0,4},{4,0},{8,12},{12,8},{16,20},{20,16},{24,28},{28,24},{1,5},{5... | collective-permute-start | bytes 1622024 | tf_op jit(solution)/shard_map/ppermute | solution.py:38
  51.1 1.3 copy-start.11
  53.3 63.1 %collective-permute-start.8 = (bf16[128,2112]{0,1:T(8,128)(2,1)}, bf16[128,2112]{0,1:T(8,128)(2,1)}, u32[]{:S(2)}, u32[]{:S(2)}) collective-permute-start(bf16[128,2112]{0,1:T(8,128)(2,1)} %dynamic-slice_convert_fusion.2), channel_id=1, source_target_pairs={{0,4},{4,0},{8,12},{12,8},{16,20},{20,16},{24,28},{28,24},{1,5},{5... | collective-permute-start | bytes 1622024 | tf_op jit(solution)/shard_map/ppermute | solution.py:38
  72.7 1.3 copy-start.12
  74.9 47.5 %collective-permute-start.16 = (bf16[128,2112]{0,1:T(8,128)(2,1)}, bf16[128,2112]{0,1:T(8,128)(2,1)}, u32[]{:S(2)}, u32[]{:S(2)}) collective-permute-start(bf16[128,2112]{0,1:T(8,128)(2,1)} %dynamic-slice_convert_fusion.1), channel_id=1, source_target_pairs={{0,4},{4,0},{8,12},{12,8},{16,20},{20,16},{24,28},{28,24},{1,5},{5... | collective-permute-start | bytes 1622024 | tf_op jit(solution)/shard_map/ppermute | solution.py:38
  95.0 1.4 copy-start.10
  97.2 28.9 %collective-permute-start.24 = (bf16[128,2112]{0,1:T(8,128)(2,1)}, bf16[128,2112]{0,1:T(8,128)(2,1)}, u32[]{:S(2)}, u32[]{:S(2)}) collective-permute-start(bf16[128,2112]{0,1:T(8,128)(2,1)} %dynamic-slice_convert_fusion), channel_id=1, source_target_pairs={{0,4},{4,0},{8,12},{12,8},{16,20},{20,16},{24,28},{28,24},{1,5},{5... | collective-permute-start | bytes 1622024 | tf_op jit(solution)/shard_map/ppermute | solution.py:38
  97.3 2.8 %copy-start.13 = (f32[256,2112]{0,1:T(8,128)S(1)}, f32[256,2112]{0,1:T(8,128)}, u32[]{:S(2)}) copy-start(f32[256,2112]{0,1:T(8,128)} %copy-done.12) | copy-start | bytes 6488068
  102.5 1.4 copy-start.3
  111.7 1.0 copy-start.4
  113.5 14.3 %collective-permute-start.1 = (bf16[64,2112]{1,0:T(8,128)(2,1)}, bf16[64,2112]{1,0:T(8,128)(2,1)S(1)}, u32[]{:S(2)}, u32[]{:S(2)}) collective-permute-start(bf16[64,2112]{1,0:T(8,128)(2,1)} %dynamic-slice_convert_fusion.7), channel_id=1, source_target_pairs={{0,8},{4,12},{8,0},{12,4},{16,24},{20,28},{24,16},{28,20},{1,9},{5... | collective-permute-start | bytes 811016 | tf_op jit(solution)/shard_map/ppermute | solution.py:38
  119.1 1.0 copy-start.6
  120.9 9.0 %collective-permute-start.9 = (bf16[64,2112]{1,0:T(8,128)(2,1)}, bf16[64,2112]{1,0:T(8,128)(2,1)S(1)}, u32[]{:S(2)}, u32[]{:S(2)}) collective-permute-start(bf16[64,2112]{1,0:T(8,128)(2,1)} %dynamic-slice_convert_fusion.6), channel_id=1, source_target_pairs={{0,16},{4,20},{8,24},{12,28},{16,0},{20,4},{24,8},{28,12},{1,17},{... | collective-permute-start | bytes 811016 | tf_op jit(solution)/shard_map/ppermute | solution.py:38
  123.9 1.0 copy-start.8
  125.6 2.2 %copy-start.5 = (f32[128,2112]{1,0:T(8,128)S(1)}, f32[128,2112]{1,0:T(8,128)}, u32[]{:S(2)}) copy-start(f32[128,2112]{1,0:T(8,128)} %copy-done.4) | copy-start | bytes 3244036
  125.6 9.8 %collective-permute-start.17 = (bf16[64,2112]{1,0:T(8,128)(2,1)}, bf16[64,2112]{1,0:T(8,128)(2,1)}, u32[]{:S(2)}, u32[]{:S(2)}) collective-permute-start(bf16[64,2112]{1,0:T(8,128)(2,1)} %dynamic-slice_convert_fusion.5), channel_id=1, source_target_pairs={{0,8},{4,12},{8,0},{12,4},{16,24},{20,28},{24,16},{28,20},{1,9},{5... | collective-permute-start | bytes 811016 | tf_op jit(solution)/shard_map/ppermute | solution.py:38
  127.5 2.4 %copy-start.7 = (f32[128,2112]{1,0:T(8,128)S(1)}, f32[128,2112]{1,0:T(8,128)}, u32[]{:S(2)}) copy-start(f32[128,2112]{1,0:T(8,128)} %copy-done.6) | copy-start | bytes 3244036
  127.6 7.8 %copy-start.9 = (f32[128,2112]{1,0:T(8,128)S(1)}, f32[128,2112]{1,0:T(8,128)}, u32[]{:S(2)}) copy-start(f32[128,2112]{1,0:T(8,128)} %copy-done.8) | copy-start | bytes 3244036
  127.6 9.6 %collective-permute-start.25 = (bf16[64,2112]{1,0:T(8,128)(2,1)S(1)}, bf16[64,2112]{1,0:T(8,128)(2,1)S(1)}, u32[]{:S(2)}, u32[]{:S(2)}) collective-permute-start(bf16[64,2112]{1,0:T(8,128)(2,1)S(1)} %dynamic-slice_convert_fusion.4), channel_id=1, source_target_pairs={{0,16},{4,20},{8,24},{12,28},{16,0},{20,4},{24,8},{28,12},{1,17},{... | collective-permute-start | bytes 811016 | tf_op jit(solution)/shard_map/ppermute | solution.py:38
  127.9 12.1 %collective-permute-start.2 = (bf16[32,2112]{1,0:T(8,128)(2,1)S(1)}, bf16[32,2112]{1,0:T(8,128)(2,1)S(1)}, u32[]{:S(2)}, u32[]{:S(2)}) collective-permute-start(bf16[32,2112]{1,0:T(8,128)(2,1)S(1)} %dynamic-slice_convert_fusion.11), channel_id=1, source_target_pairs={{0,16},{4,20},{8,24},{12,28},{16,0},{20,4},{24,8},{28,12},{1,17},{... | collective-permute-start | bytes 405512 | tf_op jit(solution)/shard_map/ppermute | solution.py:38
  130.0 12.7 %collective-permute-start.10 = (bf16[32,2112]{1,0:T(8,128)(2,1)S(1)}, bf16[32,2112]{1,0:T(8,128)(2,1)S(1)}, u32[]{:S(2)}, u32[]{:S(2)}) collective-permute-start(bf16[32,2112]{1,0:T(8,128)(2,1)S(1)} %dynamic-slice_convert_fusion.10), channel_id=1, source_target_pairs={{0,8},{4,12},{8,0},{12,4},{16,24},{20,28},{24,16},{28,20},{1,9},{5... | collective-permute-start | bytes 405512 | tf_op jit(solution)/shard_map/ppermute | solution.py:38
  136.5 6.7 %collective-permute-start.18 = (bf16[32,2112]{1,0:T(8,128)(2,1)S(1)}, bf16[32,2112]{1,0:T(8,128)(2,1)S(1)}, u32[]{:S(2)}, u32[]{:S(2)}) collective-permute-start(bf16[32,2112]{1,0:T(8,128)(2,1)S(1)} %dynamic-slice_convert_fusion.9), channel_id=1, source_target_pairs={{0,16},{4,20},{8,24},{12,28},{16,0},{20,4},{24,8},{28,12},{1,17},{... | collective-permute-start | bytes 405512 | tf_op jit(solution)/shard_map/ppermute | solution.py:38
  137.3 8.6 %collective-permute-start.26 = (bf16[32,2112]{1,0:T(8,128)(2,1)S(1)}, bf16[32,2112]{1,0:T(8,128)(2,1)S(1)}, u32[]{:S(2)}, u32[]{:S(2)}) collective-permute-start(bf16[32,2112]{1,0:T(8,128)(2,1)S(1)} %dynamic-slice_convert_fusion.8), channel_id=1, source_target_pairs={{0,8},{4,12},{8,0},{12,4},{16,24},{20,28},{24,16},{28,20},{1,9},{5... | collective-permute-start | bytes 405512 | tf_op jit(solution)/shard_map/ppermute | solution.py:38
  140.1 9.0 %collective-permute-start.3 = (bf16[16,2112]{1,0:T(8,128)(2,1)S(1)}, bf16[16,2112]{1,0:T(8,128)(2,1)S(1)}, u32[]{:S(2)}, u32[]{:S(2)}) collective-permute-start(bf16[16,2112]{1,0:T(8,128)(2,1)S(1)} %dynamic-slice_convert_fusion.15), channel_id=1, source_target_pairs={{0,2},{1,3},{2,0},{3,1},{4,6},{5,7},{6,4},{7,5},{8,10},{9,11},{10,... | collective-permute-start | bytes 202760 | tf_op jit(solution)/shard_map/ppermute | solution.py:38
  142.8 8.4 %collective-permute-start.11 = (bf16[16,2112]{1,0:T(8,128)(2,1)S(1)}, bf16[16,2112]{1,0:T(8,128)(2,1)S(1)}, u32[]{:S(2)}, u32[]{:S(2)}) collective-permute-start(bf16[16,2112]{1,0:T(8,128)(2,1)S(1)} %dynamic-slice_convert_fusion.14), channel_id=1, source_target_pairs={{0,2},{1,3},{2,0},{3,1},{4,6},{5,7},{6,4},{7,5},{8,10},{9,11},{10,... | collective-permute-start | bytes 202760 | tf_op jit(solution)/shard_map/ppermute | solution.py:38
  143.2 9.4 %collective-permute-start.19 = (bf16[16,2112]{1,0:T(8,128)(2,1)S(1)}, bf16[16,2112]{1,0:T(8,128)(2,1)S(1)}, u32[]{:S(2)}, u32[]{:S(2)}) collective-permute-start(bf16[16,2112]{1,0:T(8,128)(2,1)S(1)} %dynamic-slice_convert_fusion.13), channel_id=1, source_target_pairs={{0,2},{1,3},{2,0},{3,1},{4,6},{5,7},{6,4},{7,5},{8,10},{9,11},{10,... | collective-permute-start | bytes 202760 | tf_op jit(solution)/shard_map/ppermute | solution.py:38
  145.9 7.5 %collective-permute-start.27 = (bf16[16,2112]{1,0:T(8,128)(2,1)S(1)}, bf16[16,2112]{1,0:T(8,128)(2,1)S(1)}, u32[]{:S(2)}, u32[]{:S(2)}) collective-permute-start(bf16[16,2112]{1,0:T(8,128)(2,1)S(1)} %dynamic-slice_convert_fusion.12), channel_id=1, source_target_pairs={{0,2},{1,3},{2,0},{3,1},{4,6},{5,7},{6,4},{7,5},{8,10},{9,11},{10,... | collective-permute-start | bytes 202760 | tf_op jit(solution)/shard_map/ppermute | solution.py:38
  149.1 5.8 %collective-permute-start.4 = (bf16[8,2112]{1,0:T(8,128)(2,1)S(1)}, bf16[8,2112]{1,0:T(8,128)(2,1)S(1)}, u32[]{:S(2)}, u32[]{:S(2)}) collective-permute-start(bf16[8,2112]{1,0:T(8,128)(2,1)S(1)} %dynamic-slice_convert_fusion.19), channel_id=1, source_target_pairs={{0,1},{1,0},{2,3},{3,2},{4,5},{5,4},{6,7},{7,6},{8,9},{9,8},{10,11... | collective-permute-start | bytes 101384 | tf_op jit(solution)/shard_map/ppermute | solution.py:38
  151.3 6.0 %collective-permute-start.12 = (bf16[8,2112]{1,0:T(8,128)(2,1)S(1)}, bf16[8,2112]{1,0:T(8,128)(2,1)S(1)}, u32[]{:S(2)}, u32[]{:S(2)}) collective-permute-start(bf16[8,2112]{1,0:T(8,128)(2,1)S(1)} %dynamic-slice_convert_fusion.18), channel_id=1, source_target_pairs={{0,1},{1,0},{2,3},{3,2},{4,5},{5,4},{6,7},{7,6},{8,9},{9,8},{10,11... | collective-permute-start | bytes 101384 | tf_op jit(solution)/shard_map/ppermute | solution.py:38
  152.7 4.6 %collective-permute-start.20 = (bf16[8,2112]{1,0:T(8,128)(2,1)S(1)}, bf16[8,2112]{1,0:T(8,128)(2,1)S(1)}, u32[]{:S(2)}, u32[]{:S(2)}) collective-permute-start(bf16[8,2112]{1,0:T(8,128)(2,1)S(1)} %dynamic-slice_convert_fusion.17), channel_id=1, source_target_pairs={{0,1},{1,0},{2,3},{3,2},{4,5},{5,4},{6,7},{7,6},{8,9},{9,8},{10,11... | collective-permute-start | bytes 101384 | tf_op jit(solution)/shard_map/ppermute | solution.py:38
  153.5 5.5 %collective-permute-start.28 = (bf16[8,2112]{1,0:T(8,128)(2,1)S(1)}, bf16[8,2112]{1,0:T(8,128)(2,1)S(1)}, u32[]{:S(2)}, u32[]{:S(2)}) collective-permute-start(bf16[8,2112]{1,0:T(8,128)(2,1)S(1)} %dynamic-slice_convert_fusion.16), channel_id=1, source_target_pairs={{0,1},{1,0},{2,3},{3,2},{4,5},{5,4},{6,7},{7,6},{8,9},{9,8},{10,11... | collective-permute-start | bytes 101384 | tf_op jit(solution)/shard_map/ppermute | solution.py:38
  154.9 5.5 %collective-permute-start.5 = (bf16[8,2112]{1,0:T(8,128)(2,1)S(1)}, bf16[8,2112]{1,0:T(8,128)(2,1)S(1)}, u32[]{:S(2)}, u32[]{:S(2)}) collective-permute-start(bf16[8,2112]{1,0:T(8,128)(2,1)S(1)} %add_convert_fusion.3), channel_id=1, source_target_pairs={{0,16},{4,20},{8,24},{12,28},{16,0},{20,4},{24,8},{28,12},{1,17},{... | collective-permute-start | bytes 101384 | tf_op jit(solution)/shard_map/ppermute | solution.py:44
  157.2 4.0 %collective-permute-start.13 = (bf16[8,2112]{1,0:T(8,128)(2,1)S(1)}, bf16[8,2112]{1,0:T(8,128)(2,1)S(1)}, u32[]{:S(2)}, u32[]{:S(2)}) collective-permute-start(bf16[8,2112]{1,0:T(8,128)(2,1)S(1)} %add_convert_fusion.2), channel_id=1, source_target_pairs={{0,8},{4,12},{8,0},{12,4},{16,24},{20,28},{24,16},{28,20},{1,9},{5... | collective-permute-start | bytes 101384 | tf_op jit(solution)/shard_map/ppermute | solution.py:44
  157.4 5.1 %collective-permute-start.21 = (bf16[8,2112]{1,0:T(8,128)(2,1)S(1)}, bf16[8,2112]{1,0:T(8,128)(2,1)S(1)}, u32[]{:S(2)}, u32[]{:S(2)}) collective-permute-start(bf16[8,2112]{1,0:T(8,128)(2,1)S(1)} %add_convert_fusion.1), channel_id=1, source_target_pairs={{0,16},{4,20},{8,24},{12,28},{16,0},{20,4},{24,8},{28,12},{1,17},{... | collective-permute-start | bytes 101384 | tf_op jit(solution)/shard_map/ppermute | solution.py:44
  159.0 4.8 %collective-permute-start.29 = (bf16[8,2112]{1,0:T(8,128)(2,1)S(1)}, bf16[8,2112]{1,0:T(8,128)(2,1)S(1)}, u32[]{:S(2)}, u32[]{:S(2)}) collective-permute-start(bf16[8,2112]{1,0:T(8,128)(2,1)S(1)} %add_convert_fusion), channel_id=1, source_target_pairs={{0,8},{4,12},{8,0},{12,4},{16,24},{20,28},{24,16},{28,20},{1,9},{5... | collective-permute-start | bytes 101384 | tf_op jit(solution)/shard_map/ppermute | solution.py:44
  160.4 4.4 %collective-permute-start.6 = (bf16[16,2112]{1,0:T(8,128)(2,1)S(1)}, bf16[16,2112]{1,0:T(8,128)(2,1)S(1)}, u32[]{:S(2)}, u32[]{:S(2)}) collective-permute-start(bf16[16,2112]{1,0:T(8,128)(2,1)S(1)} %maximum_select_fusion.8), channel_id=1, source_target_pairs={{0,8},{4,12},{8,0},{12,4},{16,24},{20,28},{24,16},{28,20},{1,9},{5... | collective-permute-start | bytes 202760 | tf_op jit(solution)/shard_map/ppermute | solution.py:44
  161.3 4.4 %collective-permute-start.14 = (bf16[16,2112]{1,0:T(8,128)(2,1)S(1)}, bf16[16,2112]{1,0:T(8,128)(2,1)S(1)}, u32[]{:S(2)}, u32[]{:S(2)}) collective-permute-start(bf16[16,2112]{1,0:T(8,128)(2,1)S(1)} %maximum_select_fusion.9), channel_id=1, source_target_pairs={{0,16},{4,20},{8,24},{12,28},{16,0},{20,4},{24,8},{28,12},{1,17},{... | collective-permute-start | bytes 202760 | tf_op jit(solution)/shard_map/ppermute | solution.py:44
  162.4 4.4 %collective-permute-start.22 = (bf16[16,2112]{1,0:T(8,128)(2,1)S(1)}, bf16[16,2112]{1,0:T(8,128)(2,1)S(1)}, u32[]{:S(2)}, u32[]{:S(2)}) collective-permute-start(bf16[16,2112]{1,0:T(8,128)(2,1)S(1)} %maximum_select_fusion.10), channel_id=1, source_target_pairs={{0,8},{4,12},{8,0},{12,4},{16,24},{20,28},{24,16},{28,20},{1,9},{5... | collective-permute-start | bytes 202760 | tf_op jit(solution)/shard_map/ppermute | solution.py:44
  163.8 4.4 %collective-permute-start.30 = (bf16[16,2112]{1,0:T(8,128)(2,1)S(1)}, bf16[16,2112]{1,0:T(8,128)(2,1)S(1)}, u32[]{:S(2)}, u32[]{:S(2)}) collective-permute-start(bf16[16,2112]{1,0:T(8,128)(2,1)S(1)} %maximum_select_fusion.11), channel_id=1, source_target_pairs={{0,16},{4,20},{8,24},{12,28},{16,0},{20,4},{24,8},{28,12},{1,17},{... | collective-permute-start | bytes 202760 | tf_op jit(solution)/shard_map/ppermute | solution.py:44
  164.8 3.5 %collective-permute-start.7 = (bf16[32,2112]{1,0:T(8,128)(2,1)S(1)}, bf16[32,2112]{1,0:T(8,128)(2,1)S(1)}, u32[]{:S(2)}, u32[]{:S(2)}) collective-permute-start(bf16[32,2112]{1,0:T(8,128)(2,1)S(1)} %maximum_select_fusion.4), channel_id=1, source_target_pairs={{0,4},{4,0},{8,12},{12,8},{16,20},{20,16},{24,28},{28,24},{1,5},{5... | collective-permute-start | bytes 405512 | tf_op jit(solution)/shard_map/ppermute | solution.py:44
  165.7 2.7 %collective-permute-start.15 = (bf16[32,2112]{1,0:T(8,128)(2,1)S(1)}, bf16[32,2112]{1,0:T(8,128)(2,1)S(1)}, u32[]{:S(2)}, u32[]{:S(2)}) collective-permute-start(bf16[32,2112]{1,0:T(8,128)(2,1)S(1)} %maximum_select_fusion.5), channel_id=1, source_target_pairs={{0,4},{4,0},{8,12},{12,8},{16,20},{20,16},{24,28},{28,24},{1,5},{5... | collective-permute-start | bytes 405512 | tf_op jit(solution)/shard_map/ppermute | solution.py:44
  166.8 1.6 collective-permute-start.23
  168.2 1.4 collective-permute-start.31
  169.7 1.7 %copy-start.1 = (bf16[64,16384]{1,0:T(8,128)(2,1)S(1)}, bf16[64,16384]{1,0:T(8,128)(2,1)}, u32[]{:S(2)}) copy-start(bf16[64,16384]{1,0:T(8,128)(2,1)} %param.7) | copy-start | bytes 6291460

commit v2 on v0

v2 whole, which is shorter than its diff:
```python
import functools

import jax
import jax.numpy as jnp
from jax import lax
from jax.experimental import pallas as pl
from jax.experimental.pallas import tpu as pltpu
from jax.sharding import PartitionSpec as P


SHARES = (4, 2, 2)

F32, BF16 = jnp.float32, jnp.bfloat16
CONTRACT_MINOR = (((1,), (1,)), ((), ()))


def one_hot_columns(index, count):
    numbers = lax.broadcasted_iota(jnp.int32, (count, index.shape[1]), 0)
    return jnp.where(numbers == index, 1.0, 0.0)


def groups(ref, n_col, start, width):
    each = ref.shape[0] // n_col
    return jnp.concatenate([ref[z * each + start : z * each + start + width, :] for z in range(n_col)])


def build_val(first, second, val_ref, val_density):
    grid = val_ref.shape[1]
    step = min(2048, grid)

    @pl.loop(0, grid // step)
    def _(i):
        at = pl.ds(pl.multiple_of(i * step, step), step)
        orbitals = val_ref[:, at]
        a = jnp.dot(first, orbitals, preferred_element_type=F32)
        b = jnp.dot(second, orbitals, preferred_element_type=F32)
        val_density[:, at] = (a * b).astype(BF16)


def build_con(con, rolled, density):
    count, columns = con.shape
    wide = min(512, columns)
    apart = density.shape[0] // count

    @pl.loop(0, columns // wide)
    def _(i):
        at = pl.ds(pl.multiple_of(i * wide, wide), wide)
        one = con[:, at].astype(F32)
        for shift in range(8):
            moved = one if shift == 0 else jnp.concatenate([one[shift:], one[:shift]])
            rolled[0:count, :] = moved
            rolled[count : 2 * count, :] = moved
            for d in range(shift, apart, 8):
                other = rolled[d - shift : d - shift + count, :]
                density[d * count : (d + 1) * count, at] = (one * other).astype(BF16)


def product(numbers, w, density, val_density):
    stripe = w[0].shape[0]
    t = [lax.dot_general(val_density[...], w[s][...], CONTRACT_MINOR, preferred_element_type=F32).astype(BF16) for s in numbers]
    rows = slice(numbers[0] * stripe, (numbers[-1] + 1) * stripe)
    return lax.dot_general(jnp.concatenate(t, axis=1), density[:, rows], CONTRACT_MINOR, preferred_element_type=F32)


def hand_out(n_col, mine, acc, kept, sent):
    half = acc.shape[0] // n_col // 2
    for z in range(n_col):
        to = slice(z * half, (z + 1) * half)
        kept[to, :] = acc[pl.ds(pl.multiple_of((2 * z + mine) * half, half), half), :]
        sent[to, :] = acc[pl.ds(pl.multiple_of((2 * z + 1 - mine) * half, half), half), :].astype(BF16)


def first_kernel(n_col, width, n_stripes, place, pairs, val, con_all, w_hbm, kept, sent, *refs):
    w, refs = refs[:n_stripes], refs[n_stripes:]
    density, hot1, hot2, val_density, acc, pairs_here, val_here, con, rolled, sems, in_sems = refs
    me = place[0] // n_col
    columns, stripe = con.shape[1], w[0].shape[0]
    fetches = [
        pltpu.make_async_copy(pairs, pairs_here, in_sems.at[0]),
        pltpu.make_async_copy(val, val_here, in_sems.at[1]),
        pltpu.make_async_copy(
            con_all.at[:, pl.ds(pl.multiple_of(me * columns, columns), columns)], con, in_sems.at[2]
        ),
    ]
    for fetch in fetches:
        fetch.start()
    copies = []
    for s in range(n_stripes):
        copies.append(pltpu.make_async_copy(w_hbm.at[pl.ds(s * stripe, stripe), :], w[s], sems.at[s]))
        copies[-1].start()
    fetches[0].wait()
    hot1[...] = one_hot_columns(pairs_here[0:1, :], hot1.shape[1]).T.astype(BF16)
    hot2[...] = one_hot_columns(pairs_here[1:2, :], hot2.shape[1]).T.astype(BF16)
    fetches[1].wait()
    build_val(groups(hot1, n_col, 0, width), groups(hot2, n_col, 0, width), val_here, val_density)
    fetches[2].wait()
    build_con(con, rolled, density)
    for s, copy in enumerate(copies):
        copy.wait()
        part = product([s], w, density, val_density)
        if s == 0:
            acc[...] = part
        else:
            acc[...] += part
    hand_out(n_col, me % 2, acc, kept, sent)


def begin_kernel(n_col, start, width, n_stripes, numbers, n_after, *refs):
    w, refs = refs[:n_stripes], refs[n_stripes:]
    (density, hot1, hot2, val), refs = refs[:4], refs[4:]
    acc, val_density, *_ = refs[n_after:]
    build_val(groups(hot1, n_col, start, width), groups(hot2, n_col, start, width), val, val_density)
    acc[...] = product(numbers, w, density, val_density)


def end_kernel(n_col, n_stripes, numbers, n_after, place, *refs):
    w, refs = refs[:n_stripes], refs[n_stripes:]
    (density, before, val_density), refs = refs[:3], refs[3:]
    kept, sent, place_out, acc = *refs[n_after : n_after + 3], refs[-1]
    acc[...] = before[...] + product(numbers, w, density, val_density)
    hand_out(n_col, place[0] // n_col % 2, acc, kept, sent)
    place_out[0] = place[0]


def fold_kernel(n_col, bit, place, kept, got, kept_out, sent_out):
    high = ((place[0] // n_col) >> bit) % 2 == 1
    half = kept_out.shape[0] // n_col
    for z in range(n_col):
        a = slice(2 * z * half, (2 * z + 1) * half)
        b = slice((2 * z + 1) * half, (2 * z + 2) * half)
        to = slice(z * half, (z + 1) * half)
        low_part = kept[a, :] + got[a, :].astype(F32)
        high_part = kept[b, :] + got[b, :].astype(F32)
        kept_out[to, :] = jnp.where(high, high_part, low_part)
        sent_out[to, :] = jnp.where(high, low_part, high_part).astype(BF16)


def pick_kernel(n_col, count, scale, place, pairs, whole, out):
    own = out.shape[0]
    me = place[0] // n_col
    if own % 128:
        every = pairs[...]
        asked = functools.reduce(
            lambda a, i: jnp.where(me == i, every[:, i * own : (i + 1) * own], a), range(pairs.shape[1] // own), every[:, :own]
        )
    else:
        asked = pairs[:, pl.ds(pl.multiple_of(me * own, own), own)]
    c, other = asked[0:1], asked[1:2]
    apart = jnp.where(other >= c, other - c, other - c + count)
    row = jnp.where(apart <= count // 2, apart * count + c, (count - apart) * count + other)
    pick = one_hot_columns(row, whole.shape[1]).astype(BF16)
    out[...] = (jnp.dot(whole[...], pick, preferred_element_type=F32) * scale).T


def swap(x, axis, bit, size):
    return lax.ppermute(x, axis, [(i, i ^ (1 << bit)) for i in range(size)])


def solution(mesh):
    n_row, n_col = mesh.shape["row"], mesh.shape["col"]
    row_bits, col_bits = n_row.bit_length() - 1, n_col.bit_length() - 1

    def per_device(screened, val_orbitals, con_orbitals, val_pairs, con_pairs):
        own_rows, own_columns = screened.shape
        count, grid = con_orbitals.shape
        n_val = val_orbitals.shape[0]
        blocks = count // 2 + 1
        while blocks * count % 128:
            blocks += 1
        unordered = blocks * count
        n_pairs = val_pairs.shape[0]
        per_col = n_pairs // n_col
        shares = SHARES if n_pairs >= 32 * n_row * n_col else (8,)
        widths = [per_col * s // 8 for s in shares]
        starts = [sum(widths[:k]) for k in range(len(widths))]
        place = (lax.axis_index("row") * n_col + lax.axis_index("col")).astype(jnp.int32)[None]
        smem = pl.BlockSpec(memory_space=pltpu.SMEM)
        vmem = pl.BlockSpec(memory_space=pltpu.VMEM)
        anywhere = pl.BlockSpec(memory_space=pl.ANY)
        hbm = pl.BlockSpec(memory_space=pltpu.HBM)

        def params(mib):
            return pltpu.CompilerParams(vmem_limit_bytes=mib << 20)

        def cost(n, rows):
            return pl.CostEstimate(
                flops=2 * n * rows * (own_columns + unordered), bytes_accessed=1 << 20, transcendentals=0
            )

        def outs(rows):
            return [pltpu.VMEM((rows, unordered), F32), pltpu.VMEM((rows, unordered), BF16)]

        stripe = min(512, own_rows)
        hots = [pltpu.VMEM((n_pairs, n_val), BF16)] * 2
        n = n_col * widths[0]
        n_stripes = own_rows // stripe
        held = [pltpu.VMEM((stripe, own_columns), BF16)] * n_stripes + [pltpu.VMEM((unordered, own_rows), BF16)]
        n_held = n_stripes + 1
        kept, sent, *fixed = pl.pallas_call(
            functools.partial(first_kernel, n_col, widths[0], n_stripes),
            in_specs=[smem] + [hbm] * 4,
            out_specs=[vmem] * (2 + n_held + 2),
            out_shape=outs(n // 2) + held + hots,
            scratch_shapes=[
                pltpu.VMEM((n, own_columns), BF16),
                pltpu.VMEM((n, unordered), F32),
                pltpu.VMEM((2, n_pairs), jnp.int32),
                pltpu.VMEM((n_val, own_columns), BF16),
                pltpu.VMEM((count, own_rows), BF16),
                pltpu.VMEM((2 * count, min(512, own_rows)), F32),
                pltpu.SemaphoreType.DMA((n_stripes,)),
                pltpu.SemaphoreType.DMA((3,)),
            ],
            compiler_params=params(18),
            cost_estimate=cost(n, own_rows),
            name="first",
        )(place, *[pltpu.with_memory_space_constraint(x, pltpu.HBM) for x in (val_pairs.T, val_orbitals, con_orbitals, screened)])

        def begin(k, numbers, fixed, after):
            n = n_col * widths[k]
            acc, val_density, *fixed = pl.pallas_call(
                functools.partial(begin_kernel, n_col, starts[k], widths[k], n_stripes, numbers, len(after)),
                in_specs=[vmem] * (n_held + 3) + [anywhere] * len(after),
                out_specs=[vmem] * (2 + n_held + 2),
                out_shape=[pltpu.VMEM((n, unordered), F32), pltpu.VMEM((n, own_columns), BF16)] + held + hots,
                input_output_aliases={i: 2 + i for i in range(n_held + 2)},
                compiler_params=params(7),
                cost_estimate=cost(n, len(numbers) * stripe),
            )(*fixed, val_orbitals, *after)
            return (acc, val_density), fixed

        def end(k, numbers, fixed, before, after):
            n = n_col * widths[k]
            kept, sent, last_place, *same = pl.pallas_call(
                functools.partial(end_kernel, n_col, n_stripes, numbers, len(after)),
                in_specs=[smem] + [vmem] * (n_held + 2) + [anywhere] * len(after),
                out_specs=[vmem] * 2 + [smem] + [vmem] * n_held,
                out_shape=outs(n // 2) + [jax.ShapeDtypeStruct((1,), jnp.int32)] + held,
                scratch_shapes=[pltpu.VMEM((n, unordered), F32)],
                input_output_aliases={1 + i: 3 + i for i in range(n_held)},
                compiler_params=params(9),
                cost_estimate=cost(n, len(numbers) * stripe),
            )(place, *fixed[:n_held], *before, *after)
            return (kept, sent), last_place, same + fixed[n_held:]

        def fold(kept, got, bit):
            return pl.pallas_call(
                functools.partial(fold_kernel, n_col, bit),
                in_specs=[smem] + [vmem] * 2,
                out_specs=[vmem] * 2,
                out_shape=outs(kept.shape[0] // 2),
                compiler_params=params(4),
            )(place, kept, got)

        def step(k, at, kept, sent):
            got = swap(sent, "row", orders[k][at - 1], n_row)
            return fold(kept, got, orders[k][at])

        order = list(range(1, row_bits))
        orders = [[0] + (order if k % 2 == 0 else order[::-1]) for k in range(len(shares))]
        if len(shares) > 1:
            low, high = list(range(n_stripes // 2)), list(range(n_stripes // 2, n_stripes))
            a = kept, sent
            before, fixed = begin(1, low, fixed, [a[1]])
            a = step(0, 1, *a)
            b, last_place, fixed = end(1, high, fixed, before, [a[1]])
            before, fixed = begin(2, low, fixed, [b[1]])
            b = step(1, 1, *b)
            c, last_place, fixed = end(2, high, fixed, before, [b[1]])
            state = [(2, a), (2, b), (1, c)]
        else:
            last_place = place
            state = [(1, (kept, sent))]

        me = last_place[0]
        row, col = me // n_col, me % n_col

        def split(part, where, bit, each):
            size = part.shape[0] // (2 * each)
            mine = (where >> bit) & 1
            part = part.reshape(each, 2, size, unordered)
            take = lambda i: lax.dynamic_slice(
                part, (0, i, 0, 0), (each, 1, size, unordered), allow_negative_indices=False
            ).reshape(each * size, unordered)
            return take(mine), take(1 - mine).astype(BF16)

        def over_row(k, at, kept, sent):
            for at in range(at, row_bits + 1):
                part = kept + swap(sent, "row", orders[k][at - 1], n_row).astype(F32)
                if at < row_bits:
                    kept, sent = split(part, row, orders[k][at], n_col)
            return part

        def finish(parts):
            for bit in reversed(range(col_bits)):
                halves = [split(part, col, bit, 1) for part in parts]
                got = swap(jnp.concatenate([h[1] for h in halves]), "col", bit, n_col).astype(F32)
                parts, used = [], 0
                for kept, _ in halves:
                    parts.append(kept + got[used : used + kept.shape[0]])
                    used += kept.shape[0]
            part = jnp.concatenate(parts).astype(BF16)
            each = part.shape[0]
            for bit in reversed(orders[0]):
                got = swap(part, "row", bit, n_row)
                lower = ((row >> bit) & 1) == 0
                part = jnp.where(lower, jnp.concatenate([part, got]), jnp.concatenate([got, part]))
            out, used = [], 0
            for p in parts:
                out.append(part.reshape(n_row, each, unordered)[:, used : used + p.shape[0]])
                used += p.shape[0]
            return out

        def natural(blocks, k):
            shape = (2,) * row_bits
            axes = [orders[0].index(bit) for bit in orders[k]]
            moved = blocks.reshape(shape + blocks.shape[1:]).transpose(axes + [row_bits, row_bits + 1])
            return moved.reshape(-1, unordered)

        sums = [over_row(k, at, *pair) for k, (at, pair) in enumerate(state)]
        merged = finish(sums[:-1]) + finish(sums[-1:]) if len(sums) > 1 else finish(sums)
        whole = jnp.concatenate([natural(blocks, k) for k, blocks in enumerate(merged)])

        own = con_pairs.shape[0] // n_row
        return pl.pallas_call(
            functools.partial(pick_kernel, n_col, count, float(grid ** (-0.5))),
            in_specs=[smem] + [vmem] * 2,
            out_specs=vmem,
            out_shape=jax.ShapeDtypeStruct((own, per_col), F32),
            compiler_params=params(20),
            name="pick",
        )(place, con_pairs.T, whole)

    in_specs = (P("row", "col"), P(None, "col"), P(), P(), P())

    return jax.shard_map(per_device, mesh=mesh, in_specs=in_specs, out_specs=P("row", "col"), check_vma=False)
```

time: 275 us -> 109 us (0.40)
  waiting for transfers between devices: 185 us -> 34.5 us
  matrix products: 72.6 us -> 0 us
  Pallas kernels: 0 us -> 46.1 us
  starting transfers between devices: 0.04 us -> 18.3 us
  between operations: 13.4 us -> 2.97 us
    reduce_scatter x2 -> x0, waiting for transfers between devices: 185 us -> none  [the longest x1 133 us: per_device(): lax.psum_scatter(partial_sums, 'col', scatter_dimension=1, tiled=True)]
    dot_general x4 -> x0, matrix products: 72.6 us -> none  [the longest x1 31.7 us: per_device(): lax.dot_general(screened, val_density, (((1,), (1,)), ((), ())), preferre...]
    pallas_call x0 -> x8, Pallas kernels: none -> 46.1 us  [the longest x1 23.3 us: per_device(): pl.pallas_call(functools.partial(first_kernel, n_col, widths[0], n_stripe...]
    ppermute x0 -> x19, waiting for transfers between devices: none -> 34.5 us  [swap(): return lax.ppermute(x, axis, [(i, i ^ 1 << bit) for i in range(size)])]
    ppermute x0 -> x19, starting transfers between devices: none -> 18.3 us  [swap(): return lax.ppermute(x, axis, [(i, i ^ 1 << bit) for i in range(size)])]
  transfers between devices with their start and end apart: 2 -> 19, of which waited for: 2 -> 10; matrix products, arithmetic and copies ran while one was open for 5% -> 3% of each run, Pallas kernels for 0% -> 15%
where the time goes in v2:
time: 109 us
  Pallas kernels  46.1 us (42%)
  waiting for transfers between devices  34.5 us (32%)
  starting transfers between devices  18.3 us (17%)
  local copies, waits for them, and re-layouts  3.58 us (3%)
  other arithmetic  3.24 us (3%)
  between operations  2.97 us (3%)
    ppermute x19, waiting for transfers between devices, swap(): return lax.ppermute(x, axis, [(i, i ^ 1 << bit) for i in range(size)])  34.5 us
    pallas_call x1, Pallas kernels, per_device(): pl.pallas_call(functools.partial(first_kernel, n_col, widths[0], n_stripe...  23.3 us
    ppermute x19, starting transfers between devices, swap(): return lax.ppermute(x, axis, [(i, i ^ 1 << bit) for i in range(size)])  18.3 us
    pallas_call x2, Pallas kernels, begin(): pl.pallas_call(functools.partial(begin_kernel, n_col, starts[k], widths[k...  10.6 us
    pallas_call x2, Pallas kernels, end(): pl.pallas_call(functools.partial(end_kernel, n_col, n_stripes, numbers, l...  8.56 us
    unnamed x16, local copies, waits for them, and re-layouts  3.18 us
    add x7, other arithmetic, over_row(): part = kept + swap(sent, 'row', orders[k][at - 1], n_row).astype(F32)  2.61 us
  transfers between devices with their start and end apart: 19, of which 10 were waited for; matrix products, arithmetic and copies ran while one was open for 3% of the time, Pallas kernels for 15%

profile of v2, /device:TPU:0, one launch (start us, length us, event | category | flops | bytes accessed | tf_op | source)
XLA Modules:
  0.0 108.6 jit_solution(8651914256155796609)
XLA Ops:
  0.0 23.3 %first.1 = (f32[256,2176]{1,0:T(8,128)S(1)}, bf16[256,2176]{1,0:T(8,128)(2,1)S(1)}, bf16[512,4096]{1,0:T(8,128)(2,1)S(1)}, bf16[512,4096]{1,0:T(8,128)(2,1)S(1)}...) custom-call(s32[1]{0:T(128)} %bitcast.place, ...), custom_call_target="tpu_custom_call" | custom-call | flops 13153337344 | bytes 1048576 | tf_op jit(solution)/shard_map/first/pallas_call | solution.py:199
  23.3 0.6 collective-permute-start
  23.8 0.0 copy-done
  23.8 5.3 %shard_map.55 = (f32[256,2176]{1,0:T(8,128)S(1)}, bf16[256,4096]{1,0:T(8,128)(2,1)S(1)}, bf16[512,4096]{1,0:T(8,128)(2,1)S(1)}, bf16[512,4096]{1,0:T(8,128)(2,1)...) custom-call(bf16[512,4096]{1,0:T(8,128)(2,1)S(1)} %get-tuple-element, ...), custom_call_target="tpu_custom_call", output_to_operand_aliasing={{2}: (0, {}), {3}: (1, {}), {4}: (2, {}), {5}: (3, {}), {6}... | custom-call | flops 3288334336 | bytes 1048576 | tf_op jit(solution)/shard_map/pallas_call | solution.py:221
  29.1 0.0 collective-permute-done.got
  29.1 1.1 %shard_map.56 = (f32[128,2176]{1,0:T(8,128)S(1)}, bf16[128,2176]{1,0:T(8,128)(2,1)}) custom-call(s32[1]{0:T(128)} %bitcast.place, f32[256,2176]{1,0:T(8,128)S(1)} %get-tuple-element.59.kept, bf16[256,2176]{1,0:T(8,128)(2,1)S(1)} %collective-permute-done.got), custom_call_target="tpu_custom_call" | custom-call | tf_op jit(solution)/shard_map/pallas_call | solution.py:247
  30.2 4.2 %shard_map.57 = (f32[128,2176]{1,0:T(8,128)S(1)}, bf16[128,2176]{1,0:T(8,128)(2,1)S(1)}, s32[1]{0:T(128)}, bf16[512,4096]{1,0:T(8,128)(2,1)S(1)}, bf16[512,4096]...) custom-call(s32[1]{0:T(128)} %bitcast.place, ...), custom_call_target="tpu_custom_call", output_to_operand_aliasing={{3}: (1, {}), {4}: (2, {}), {5}: (3, {}), {6}: (4, {}), {7}... | custom-call | flops 3288334336 | bytes 1048576 | tf_op jit(solution)/shard_map/pallas_call | solution.py:234
  34.4 0.1 collective-permute-start.1
  34.5 3.0 %collective-permute-start.2 = (bf16[128,2176]{1,0:T(8,128)(2,1)}, bf16[128,2176]{1,0:T(8,128)(2,1)}, u32[]{:S(2)}, u32[]{:S(2)}) collective-permute-start(bf16[128,2176]{1,0:T(8,128)(2,1)} %get-tuple-element.60.refs_7_), channel_id=1, source_target_pairs={{0,8},{4,12},{8,0},{12,4},{16,24},{20,28},{24,16},{28,20},{1,9},{5... | collective-permute-start | bytes 1671176 | tf_op jit(solution)/shard_map/ppermute | solution.py:156
  37.5 5.3 %shard_map.58 = (f32[256,2176]{1,0:T(8,128)S(1)}, bf16[256,4096]{1,0:T(8,128)(2,1)S(1)}, bf16[512,4096]{1,0:T(8,128)(2,1)S(1)}, bf16[512,4096]{1,0:T(8,128)(2,1)...) custom-call(bf16[512,4096]{1,0:T(8,128)(2,1)S(1)} %get-tuple-element, ...), custom_call_target="tpu_custom_call", output_to_operand_aliasing={{2}: (0, {}), {3}: (1, {}), {4}: (2, {}), {5}: (3, {}), {6}... | custom-call | flops 3288334336 | bytes 1048576 | tf_op jit(solution)/shard_map/pallas_call | solution.py:221
  42.8 0.0 collective-permute-done.1.got
  42.8 0.8 shard_map.59
  43.7 0.8 copy-done.3
  44.5 1.5 %collective-permute-start.4 = (bf16[64,2176]{1,0:T(8,128)(2,1)}, bf16[64,2176]{1,0:T(8,128)(2,1)}, u32[]{:S(2)}, u32[]{:S(2)}) collective-permute-start(bf16[64,2176]{1,0:T(8,128)(2,1)} %get-tuple-element.77.refs_7_), channel_id=1, source_target_pairs={{0,16},{4,20},{8,24},{12,28},{16,0},{20,4},{24,8},{28,12},{1,17},{... | collective-permute-start | bytes 835592 | tf_op jit(solution)/shard_map/ppermute | solution.py:156
  46.0 4.3 %shard_map.60 = (f32[128,2176]{1,0:T(8,128)S(1)}, bf16[128,2176]{1,0:T(8,128)(2,1)S(1)}, s32[1]{0:T(128)}, bf16[512,4096]{1,0:T(8,128)(2,1)S(1)}, bf16[512,4096]...) custom-call(s32[1]{0:T(128)} %bitcast.place, ...), custom_call_target="tpu_custom_call", output_to_operand_aliasing={{3}: (1, {}), {4}: (2, {}), {5}: (3, {}), {6}: (4, {}), {7}... | custom-call | flops 3288334336 | bytes 1048576 | tf_op jit(solution)/shard_map/pallas_call | solution.py:234
  50.4 0.0 copy-start.1
  50.4 1.0 copy-done.1
  51.4 0.8 copy-done.6
  54.7 0.0 collective-permute-done.2
  54.8 0.0 copy-start.4
  54.8 1.2 %convert_add_fusion.1 = f32[128,2176]{1,0:T(8,128)S(1)} fusion(f32[128,2176]{1,0:T(8,128)S(1)} %get-tuple-element.79, bf16[128,2176]{1,0:T(8,128)(2,1)} %collective-permute-done.2), kind=kLoop, calls=%fused_computation.2 | loop fusion | flops 557056 | bytes 2785280 | tf_op jit(solution)/shard_map/add | solution.py:289
  56.1 0.6 collective-permute-start.3
  56.6 0.0 copy-done.7
  56.6 0.0 collective-permute-start.11
  56.7 0.0 collective-permute-done.4
  56.7 1.1 %convert_add_fusion.2 = f32[64,2176]{1,0:T(8,128)S(1)} fusion(f32[64,2176]{1,0:T(8,128)S(1)} %copy-done.4, bf16[64,2176]{1,0:T(8,128)(2,1)} %collective-permute-done.4), kind=kLoop, calls=%fused_computation.7 | loop fusion | flops 278528 | bytes 1392640 | tf_op jit(solution)/shard_map/add | solution.py:289
  57.8 0.2 collective-permute-start.5
  58.0 6.2 %collective-permute-done.3 = bf16[64,2176]{1,0:T(8,128)(2,1)S(1)} collective-permute-done((bf16[64,2176]{1,0:T(8,128)(2,1)S(1)}, bf16[64,2176]{1,0:T(8,128)(2,1)S(1)}, u32[]{:S(2)}, u32[]{:S(2)}) %collective-permute-start.3) | collective-permute-done | bytes 278560 | tf_op jit(solution)/shard_map/ppermute | solution.py:156
  64.2 0.1 bitcast_add_fusion.1
  64.3 0.0 collective-permute-done.5
  64.4 2.7 %collective-permute-start.6 = (bf16[48,2176]{1,0:T(8,128)(2,1)S(1)}, bf16[48,2176]{1,0:T(8,128)(2,1)S(1)}, u32[]{:S(2)}, u32[]{:S(2)}) collective-permute-start(bf16[48,2176]{1,0:T(8,128)(2,1)S(1)} %pad_maximum_fusion.1), channel_id=1, source_target_pairs={{0,2},{1,3},{2,0},{3,1},{4,6},{5,7},{6,4},{7,5},{8,10},{9,11},{10,... | collective-permute-start | bytes 626696 | tf_op jit(solution)/shard_map/ppermute | solution.py:156
  67.1 0.0 collective-permute-done.11
  67.1 0.1 convert_add_fusion
  67.2 0.6 collective-permute-start.12
  67.8 8.4 %collective-permute-done.6 = bf16[48,2176]{1,0:T(8,128)(2,1)S(1)} collective-permute-done((bf16[48,2176]{1,0:T(8,128)(2,1)S(1)}, bf16[48,2176]{1,0:T(8,128)(2,1)S(1)}, u32[]{:S(2)}, u32[]{:S(2)}) %collective-permute-start.6) | collective-permute-done | bytes 208928 | tf_op jit(solution)/shard_map/ppermute | solution.py:156
  76.4 0.0 collective-permute-done.12
  76.4 0.1 bitcast_add_fusion
  76.5 1.6 %collective-permute-start.13 = (bf16[32,2176]{1,0:T(8,128)(2,1)S(1)}, bf16[32,2176]{1,0:T(8,128)(2,1)S(1)}, u32[]{:S(2)}, u32[]{:S(2)}) collective-permute-start(bf16[32,2176]{1,0:T(8,128)(2,1)S(1)} %fusion.2), channel_id=1, source_target_pairs={{0,16},{4,20},{8,24},{12,28},{16,0},{20,4},{24,8},{28,12},{1,17},{... | collective-permute-start | bytes 417800 | tf_op jit(solution)/shard_map/ppermute | solution.py:156
  78.1 0.7 collective-permute-start.7
  78.8 4.0 %collective-permute-done.7 = bf16[24,2176]{1,0:T(8,128)(2,1)S(1)} collective-permute-done((bf16[24,2176]{1,0:T(8,128)(2,1)S(1)}, bf16[24,2176]{1,0:T(8,128)(2,1)S(1)}, u32[]{:S(2)}, u32[]{:S(2)}) %collective-permute-start.7) | collective-permute-done | bytes 104480 | tf_op jit(solution)/shard_map/ppermute | solution.py:156
  82.9 0.0 collective-permute-done.13
  82.9 2.3 %collective-permute-start.14 = (bf16[16,2176]{1,0:T(8,128)(2,1)S(1)}, bf16[16,2176]{1,0:T(8,128)(2,1)S(1)}, u32[]{:S(2)}, u32[]{:S(2)}) collective-permute-start(bf16[16,2176]{1,0:T(8,128)(2,1)S(1)} %fusion.8), channel_id=1, source_target_pairs={{0,2},{1,3},{2,0},{3,1},{4,6},{5,7},{6,4},{7,5},{8,10},{9,11},{10,... | collective-permute-start | bytes 208904 | tf_op jit(solution)/shard_map/ppermute | solution.py:156
  85.2 3.7 %collective-permute-done.14 = bf16[16,2176]{1,0:T(8,128)(2,1)S(1)} collective-permute-done((bf16[16,2176]{1,0:T(8,128)(2,1)S(1)}, bf16[16,2176]{1,0:T(8,128)(2,1)S(1)}, u32[]{:S(2)}, u32[]{:S(2)}) %collective-permute-start.14) | collective-permute-done | bytes 69664 | tf_op jit(solution)/shard_map/ppermute | solution.py:156
  89.0 0.6 collective-permute-start.15
  89.6 3.4 %collective-permute-done.15 = bf16[8,2176]{1,0:T(8,128)(2,1)S(1)} collective-permute-done((bf16[8,2176]{1,0:T(8,128)(2,1)S(1)}, bf16[8,2176]{1,0:T(8,128)(2,1)S(1)}, u32[]{:S(2)}, u32[]{:S(2)}) %collective-permute-start.15) | collective-permute-done | bytes 34848 | tf_op jit(solution)/shard_map/ppermute | solution.py:156
  93.0 0.1 collective-permute-start.16
  93.1 2.1 %collective-permute-start.8 = (bf16[24,2176]{1,0:T(8,128)(2,1)S(1)}, bf16[24,2176]{1,0:T(8,128)(2,1)S(1)}, u32[]{:S(2)}, u32[]{:S(2)}) collective-permute-start(bf16[24,2176]{1,0:T(8,128)(2,1)S(1)} %pad_maximum_fusion.3), channel_id=1, source_target_pairs={{0,16},{4,20},{8,24},{12,28},{16,0},{20,4},{24,8},{28,12},{1,17},{... | collective-permute-start | bytes 313352 | tf_op jit(solution)/shard_map/ppermute | solution.py:156
  95.2 1.8 %collective-permute-done.16 = bf16[8,2176]{1,0:T(8,128)(2,1)S(1)} collective-permute-done((bf16[8,2176]{1,0:T(8,128)(2,1)S(1)}, bf16[8,2176]{1,0:T(8,128)(2,1)S(1)}, u32[]{:S(2)}, u32[]{:S(2)}) %collective-permute-start.16) | collective-permute-done | bytes 34848 | tf_op jit(solution)/shard_map/ppermute | solution.py:156
  97.0 0.6 collective-permute-start.17
  97.6 0.5 collective-permute-done.8
  98.2 1.1 collective-permute-start.9
  99.2 2.2 %collective-permute-done.17 = bf16[16,2176]{1,0:T(8,128)(2,1)S(1)} collective-permute-done((bf16[16,2176]{1,0:T(8,128)(2,1)S(1)}, bf16[16,2176]{1,0:T(8,128)(2,1)S(1)}, u32[]{:S(2)}, u32[]{:S(2)}) %collective-permute-start.17) | collective-permute-done | bytes 69664 | tf_op jit(solution)/shard_map/ppermute | solution.py:156
  101.4 0.1 collective-permute-start.18
  101.5 2.5 %collective-permute-done.9 = bf16[48,2176]{1,0:T(8,128)(2,1)S(1)} collective-permute-done((bf16[48,2176]{1,0:T(8,128)(2,1)S(1)}, bf16[48,2176]{1,0:T(8,128)(2,1)S(1)}, u32[]{:S(2)}, u32[]{:S(2)}) %collective-permute-start.9) | collective-permute-done | bytes 208928 | tf_op jit(solution)/shard_map/ppermute | solution.py:156
  104.0 0.1 maximum_select_fusion.1
  104.1 0.1 collective-permute-start.10
  104.2 0.0 collective-permute-done.18
  104.2 0.1 maximum_select_fusion.2
  104.3 1.7 %collective-permute-done.10 = bf16[96,2176]{1,0:T(8,128)(2,1)S(1)} collective-permute-done((bf16[96,2176]{1,0:T(8,128)(2,1)S(1)}, bf16[96,2176]{1,0:T(8,128)(2,1)S(1)}, u32[]{:S(2)}, u32[]{:S(2)}) %collective-permute-start.10) | collective-permute-done | bytes 417824 | tf_op jit(solution)/shard_map/ppermute | solution.py:156
  105.9 0.1 maximum_select_fusion
  106.1 0.0 copy-start.5
  106.2 0.1 pad_maximum_fusion.whole
  106.3 0.6 copy-done.5
  106.8 1.7 %pick.1 = f32[512,256]{1,0:T(8,128)} custom-call(s32[1]{0:T(128)} %bitcast.place, s32[2,4096]{1,0:T(2,128)S(1)} %bitcast.70, bf16[256,2176]{1,0:T(8,128)(2,1)S(1)} %pad_maximum_fusion.whole), custom_call_target="tpu_custom_call" | custom-call | tf_op jit(solution)/shard_map/pick/pallas_call | solution.py:325
  (38 shorter events, 0.8 us)
Async XLA Ops:
  0.0 23.8 %copy-start = (bf16[45,4096]{1,0:T(8,128)(2,1)S(1)}, bf16[45,4096]{1,0:T(8,128)(2,1)}, u32[]{:S(2)}) copy-start(bf16[45,4096]{1,0:T(8,128)(2,1)} %refs_7_.3) | copy-start | bytes 1105924
  23.3 5.8 %collective-permute-start = (bf16[256,2176]{1,0:T(8,128)(2,1)S(1)}, bf16[256,2176]{1,0:T(8,128)(2,1)S(1)}, u32[]{:S(2)}, u32[]{:S(2)}) collective-permute-start(bf16[256,2176]{1,0:T(8,128)(2,1)S(1)} %get-tuple-element.51.refs_8_), channel_id=1, source_target_pairs={{0,4},{4,0},{8,12},{12,8},{16,20},{20,16},{24,28},{28,24},{1,5},{5... | collective-permute-start | bytes 3342344 | tf_op jit(solution)/shard_map/ppermute | solution.py:156
  34.4 8.4 %collective-permute-start.1 = (bf16[128,2176]{1,0:T(8,128)(2,1)S(1)}, bf16[128,2176]{1,0:T(8,128)(2,1)S(1)}, u32[]{:S(2)}, u32[]{:S(2)}) collective-permute-start(bf16[128,2176]{1,0:T(8,128)(2,1)S(1)} %get-tuple-element.68.refs_8_), channel_id=1, source_target_pairs={{0,4},{4,0},{8,12},{12,8},{16,20},{20,16},{24,28},{28,24},{1,5},{5... | collective-permute-start | bytes 1671176 | tf_op jit(solution)/shard_map/ppermute | solution.py:156
  34.5 20.2 %collective-permute-start.2 = (bf16[128,2176]{1,0:T(8,128)(2,1)}, bf16[128,2176]{1,0:T(8,128)(2,1)}, u32[]{:S(2)}, u32[]{:S(2)}) collective-permute-start(bf16[128,2176]{1,0:T(8,128)(2,1)} %get-tuple-element.60.refs_7_), channel_id=1, source_target_pairs={{0,8},{4,12},{8,0},{12,4},{16,24},{20,28},{24,16},{28,20},{1,9},{5... | collective-permute-start | bytes 1671176 | tf_op jit(solution)/shard_map/ppermute | solution.py:156
  43.7 0.8 copy-start.3
  44.5 12.2 %collective-permute-start.4 = (bf16[64,2176]{1,0:T(8,128)(2,1)}, bf16[64,2176]{1,0:T(8,128)(2,1)}, u32[]{:S(2)}, u32[]{:S(2)}) collective-permute-start(bf16[64,2176]{1,0:T(8,128)(2,1)} %get-tuple-element.77.refs_7_), channel_id=1, source_target_pairs={{0,16},{4,20},{8,24},{12,28},{16,0},{20,4},{24,8},{28,12},{1,17},{... | collective-permute-start | bytes 835592 | tf_op jit(solution)/shard_map/ppermute | solution.py:156
  50.4 1.0 copy-start.1
  51.4 0.8 copy-start.6
  52.2 4.4 %copy-start.7 = (bf16[128,2176]{1,0:T(8,128)(2,1)S(1)}, bf16[128,2176]{1,0:T(8,128)(2,1)}, u32[]{:S(2)}) copy-start(bf16[128,2176]{1,0:T(8,128)(2,1)} %copy-done.6) | copy-start | bytes 1671172
  54.8 1.9 %copy-start.4 = (f32[64,2176]{1,0:T(8,128)S(1)}, f32[64,2176]{1,0:T(8,128)}, u32[]{:S(2)}) copy-start(f32[64,2176]{1,0:T(8,128)} %copy-done.3) | copy-start | bytes 1671172
  56.1 8.2 %collective-permute-start.3 = (bf16[64,2176]{1,0:T(8,128)(2,1)S(1)}, bf16[64,2176]{1,0:T(8,128)(2,1)S(1)}, u32[]{:S(2)}, u32[]{:S(2)}) collective-permute-start(bf16[64,2176]{1,0:T(8,128)(2,1)S(1)} %bitcast.92), channel_id=1, source_target_pairs={{0,16},{4,20},{8,24},{12,28},{16,0},{20,4},{24,8},{28,12},{1,17},{... | collective-permute-start | bytes 835592 | tf_op jit(solution)/shard_map/ppermute | solution.py:156
  56.6 10.4 %collective-permute-start.11 = (bf16[128,2176]{1,0:T(8,128)(2,1)S(1)}, bf16[128,2176]{1,0:T(8,128)(2,1)S(1)}, u32[]{:S(2)}, u32[]{:S(2)}) collective-permute-start(bf16[128,2176]{1,0:T(8,128)(2,1)S(1)} %copy-done.7), channel_id=1, source_target_pairs={{0,4},{4,0},{8,12},{12,8},{16,20},{20,16},{24,28},{28,24},{1,5},{5... | collective-permute-start | bytes 1671176 | tf_op jit(solution)/shard_map/ppermute | solution.py:156
  56.7 10.4 %copy-start.2 = (f32[128,2176]{1,0:T(8,128)S(1)}, f32[128,2176]{1,0:T(8,128)}, u32[]{:S(2)}) copy-start(f32[128,2176]{1,0:T(8,128)} %copy-done.1) | copy-start | bytes 3342340
  57.8 6.5 %collective-permute-start.5 = (bf16[32,2176]{1,0:T(8,128)(2,1)S(1)}, bf16[32,2176]{1,0:T(8,128)(2,1)S(1)}, u32[]{:S(2)}, u32[]{:S(2)}) collective-permute-start(bf16[32,2176]{1,0:T(8,128)(2,1)S(1)} %fusion.1), channel_id=1, source_target_pairs={{0,8},{4,12},{8,0},{12,4},{16,24},{20,28},{24,16},{28,20},{1,9},{5... | collective-permute-start | bytes 417800 | tf_op jit(solution)/shard_map/ppermute | solution.py:156
  64.4 11.8 %collective-permute-start.6 = (bf16[48,2176]{1,0:T(8,128)(2,1)S(1)}, bf16[48,2176]{1,0:T(8,128)(2,1)S(1)}, u32[]{:S(2)}, u32[]{:S(2)}) collective-permute-start(bf16[48,2176]{1,0:T(8,128)(2,1)S(1)} %pad_maximum_fusion.1), channel_id=1, source_target_pairs={{0,2},{1,3},{2,0},{3,1},{4,6},{5,7},{6,4},{7,5},{8,10},{9,11},{10,... | collective-permute-start | bytes 626696 | tf_op jit(solution)/shard_map/ppermute | solution.py:156
  67.2 9.2 %collective-permute-start.12 = (bf16[64,2176]{1,0:T(8,128)(2,1)S(1)}, bf16[64,2176]{1,0:T(8,128)(2,1)S(1)}, u32[]{:S(2)}, u32[]{:S(2)}) collective-permute-start(bf16[64,2176]{1,0:T(8,128)(2,1)S(1)} %bitcast.93), channel_id=1, source_target_pairs={{0,8},{4,12},{8,0},{12,4},{16,24},{20,28},{24,16},{28,20},{1,9},{5... | collective-permute-start | bytes 835592 | tf_op jit(solution)/shard_map/ppermute | solution.py:156
  76.5 6.4 %collective-permute-start.13 = (bf16[32,2176]{1,0:T(8,128)(2,1)S(1)}, bf16[32,2176]{1,0:T(8,128)(2,1)S(1)}, u32[]{:S(2)}, u32[]{:S(2)}) collective-permute-start(bf16[32,2176]{1,0:T(8,128)(2,1)S(1)} %fusion.2), channel_id=1, source_target_pairs={{0,16},{4,20},{8,24},{12,28},{16,0},{20,4},{24,8},{28,12},{1,17},{... | collective-permute-start | bytes 417800 | tf_op jit(solution)/shard_map/ppermute | solution.py:156
  78.1 4.7 %collective-permute-start.7 = (bf16[24,2176]{1,0:T(8,128)(2,1)S(1)}, bf16[24,2176]{1,0:T(8,128)(2,1)S(1)}, u32[]{:S(2)}, u32[]{:S(2)}) collective-permute-start(bf16[24,2176]{1,0:T(8,128)(2,1)S(1)} %pad_maximum_fusion.2), channel_id=1, source_target_pairs={{0,1},{1,0},{2,3},{3,2},{4,5},{5,4},{6,7},{7,6},{8,9},{9,8},{10,11... | collective-permute-start | bytes 313352 | tf_op jit(solution)/shard_map/ppermute | solution.py:156
  82.9 6.0 %collective-permute-start.14 = (bf16[16,2176]{1,0:T(8,128)(2,1)S(1)}, bf16[16,2176]{1,0:T(8,128)(2,1)S(1)}, u32[]{:S(2)}, u32[]{:S(2)}) collective-permute-start(bf16[16,2176]{1,0:T(8,128)(2,1)S(1)} %fusion.8), channel_id=1, source_target_pairs={{0,2},{1,3},{2,0},{3,1},{4,6},{5,7},{6,4},{7,5},{8,10},{9,11},{10,... | collective-permute-start | bytes 208904 | tf_op jit(solution)/shard_map/ppermute | solution.py:156
  89.0 4.0 %collective-permute-start.15 = (bf16[8,2176]{1,0:T(8,128)(2,1)S(1)}, bf16[8,2176]{1,0:T(8,128)(2,1)S(1)}, u32[]{:S(2)}, u32[]{:S(2)}) collective-permute-start(bf16[8,2176]{1,0:T(8,128)(2,1)S(1)} %fusion.12), channel_id=1, source_target_pairs={{0,1},{1,0},{2,3},{3,2},{4,5},{5,4},{6,7},{7,6},{8,9},{9,8},{10,11... | collective-permute-start | bytes 104456 | tf_op jit(solution)/shard_map/ppermute | solution.py:156
  93.0 4.0 %collective-permute-start.16 = (bf16[8,2176]{1,0:T(8,128)(2,1)S(1)}, bf16[8,2176]{1,0:T(8,128)(2,1)S(1)}, u32[]{:S(2)}, u32[]{:S(2)}) collective-permute-start(bf16[8,2176]{1,0:T(8,128)(2,1)S(1)} %fusion.10), channel_id=1, source_target_pairs={{0,16},{4,20},{8,24},{12,28},{16,0},{20,4},{24,8},{28,12},{1,17},{... | collective-permute-start | bytes 104456 | tf_op jit(solution)/shard_map/ppermute | solution.py:156
  93.1 5.0 %collective-permute-start.8 = (bf16[24,2176]{1,0:T(8,128)(2,1)S(1)}, bf16[24,2176]{1,0:T(8,128)(2,1)S(1)}, u32[]{:S(2)}, u32[]{:S(2)}) collective-permute-start(bf16[24,2176]{1,0:T(8,128)(2,1)S(1)} %pad_maximum_fusion.3), channel_id=1, source_target_pairs={{0,16},{4,20},{8,24},{12,28},{16,0},{20,4},{24,8},{28,12},{1,17},{... | collective-permute-start | bytes 313352 | tf_op jit(solution)/shard_map/ppermute | solution.py:156
  97.0 4.4 %collective-permute-start.17 = (bf16[16,2176]{1,0:T(8,128)(2,1)S(1)}, bf16[16,2176]{1,0:T(8,128)(2,1)S(1)}, u32[]{:S(2)}, u32[]{:S(2)}) collective-permute-start(bf16[16,2176]{1,0:T(8,128)(2,1)S(1)} %maximum_select_fusion.5), channel_id=1, source_target_pairs={{0,8},{4,12},{8,0},{12,4},{16,24},{20,28},{24,16},{28,20},{1,9},{5... | collective-permute-start | bytes 208904 | tf_op jit(solution)/shard_map/ppermute | solution.py:156
  98.2 5.9 %collective-permute-start.9 = (bf16[48,2176]{1,0:T(8,128)(2,1)S(1)}, bf16[48,2176]{1,0:T(8,128)(2,1)S(1)}, u32[]{:S(2)}, u32[]{:S(2)}) collective-permute-start(bf16[48,2176]{1,0:T(8,128)(2,1)S(1)} %maximum_select_fusion.3), channel_id=1, source_target_pairs={{0,8},{4,12},{8,0},{12,4},{16,24},{20,28},{24,16},{28,20},{1,9},{5... | collective-permute-start | bytes 626696 | tf_op jit(solution)/shard_map/ppermute | solution.py:156
  101.4 2.8 %collective-permute-start.18 = (bf16[32,2176]{1,0:T(8,128)(2,1)S(1)}, bf16[32,2176]{1,0:T(8,128)(2,1)S(1)}, u32[]{:S(2)}, u32[]{:S(2)}) collective-permute-start(bf16[32,2176]{1,0:T(8,128)(2,1)S(1)} %maximum_select_fusion.4), channel_id=1, source_target_pairs={{0,4},{4,0},{8,12},{12,8},{16,20},{20,16},{24,28},{28,24},{1,5},{5... | collective-permute-start | bytes 417800 | tf_op jit(solution)/shard_map/ppermute | solution.py:156
  104.1 1.8 %collective-permute-start.10 = (bf16[96,2176]{1,0:T(8,128)(2,1)S(1)}, bf16[96,2176]{1,0:T(8,128)(2,1)S(1)}, u32[]{:S(2)}, u32[]{:S(2)}) collective-permute-start(bf16[96,2176]{1,0:T(8,128)(2,1)S(1)} %maximum_select_fusion.1), channel_id=1, source_target_pairs={{0,4},{4,0},{8,12},{12,8},{16,20},{20,16},{24,28},{28,24},{1,5},{5... | collective-permute-start | bytes 1253384 | tf_op jit(solution)/shard_map/ppermute | solution.py:156
  106.1 0.8 copy-start.5

commit v3 on v2

v3 whole, which is shorter than its diff:
```python
import functools

import jax
import jax.numpy as jnp
from jax import lax
from jax.experimental import pallas as pl
from jax.experimental.pallas import tpu as pltpu
from jax.sharding import PartitionSpec as P


CHUNKS = 4

F32, BF16 = jnp.float32, jnp.bfloat16
CONTRACT_MINOR = (((1,), (1,)), ((), ()))


def one_hot_columns(index, count):
    numbers = lax.broadcasted_iota(jnp.int32, (count, index.shape[1]), 0)
    return jnp.where(numbers == index, 1.0, 0.0)


def groups(ref, n_col, start, width):
    each = ref.shape[0] // n_col
    return jnp.concatenate([ref[z * each + start : z * each + start + width, :] for z in range(n_col)])


def build_val(first, second, val_ref, val_density):
    grid = val_ref.shape[1]
    step = min(2048, grid)

    @pl.loop(0, grid // step)
    def _(i):
        at = pl.ds(pl.multiple_of(i * step, step), step)
        orbitals = val_ref[:, at]
        a = jnp.dot(first, orbitals, preferred_element_type=F32)
        b = jnp.dot(second, orbitals, preferred_element_type=F32)
        val_density[:, at] = (a * b).astype(BF16)


def build_con(con, rolled, density):
    count, columns = con.shape
    wide = min(512, columns)
    apart = density.shape[0] // count

    @pl.loop(0, columns // wide)
    def _(i):
        at = pl.ds(pl.multiple_of(i * wide, wide), wide)
        one = con[:, at].astype(F32)
        for shift in range(8):
            moved = one if shift == 0 else jnp.concatenate([one[shift:], one[:shift]])
            rolled[0:count, :] = moved
            rolled[count : 2 * count, :] = moved
            for d in range(shift, apart, 8):
                other = rolled[d - shift : d - shift + count, :]
                density[d * count : (d + 1) * count, at] = (one * other).astype(BF16)


def product(numbers, w, density, val_density):
    stripe = w[0].shape[0]
    t = [lax.dot_general(val_density[...], w[s][...], CONTRACT_MINOR, preferred_element_type=F32).astype(BF16) for s in numbers]
    rows = slice(numbers[0] * stripe, (numbers[-1] + 1) * stripe)
    return lax.dot_general(jnp.concatenate(t, axis=1), density[:, rows], CONTRACT_MINOR, preferred_element_type=F32)


def hand_out(n_col, mine, acc, kept, sent):
    half = kept[0].shape[0] // n_col
    for c, own in enumerate(kept):
        for z in range(n_col):
            first = (z * len(kept) + c) * 2
            to = slice(z * half, (z + 1) * half)
            own[to, :] = acc[pl.ds(pl.multiple_of((first + mine) * half, half), half), :]
            to = slice((c * n_col + z) * half, (c * n_col + z + 1) * half)
            sent[to, :] = acc[pl.ds(pl.multiple_of((first + 1 - mine) * half, half), half), :].astype(BF16)


def first_kernel(n_col, width, n_stripes, n_chunks, place, pairs, val, con_all, w_hbm, *refs):
    kept, sent, refs = refs[:n_chunks], refs[n_chunks], refs[n_chunks + 1 :]
    w, refs = refs[:n_stripes], refs[n_stripes:]
    density, hot1, hot2, val_density, acc, pairs_here, val_here, con, rolled, sems, in_sems = refs
    me = place[0] // n_col
    columns, stripe = con.shape[1], w[0].shape[0]
    fetches = [
        pltpu.make_async_copy(pairs, pairs_here, in_sems.at[0]),
        pltpu.make_async_copy(val, val_here, in_sems.at[1]),
        pltpu.make_async_copy(
            con_all.at[:, pl.ds(pl.multiple_of(me * columns, columns), columns)], con, in_sems.at[2]
        ),
    ]
    for fetch in fetches:
        fetch.start()
    copies = []
    for s in range(n_stripes):
        copies.append(pltpu.make_async_copy(w_hbm.at[pl.ds(s * stripe, stripe), :], w[s], sems.at[s]))
        copies[-1].start()
    fetches[0].wait()
    hot1[...] = one_hot_columns(pairs_here[0:1, :], hot1.shape[1]).T.astype(BF16)
    hot2[...] = one_hot_columns(pairs_here[1:2, :], hot2.shape[1]).T.astype(BF16)
    fetches[1].wait()
    build_val(groups(hot1, n_col, 0, width), groups(hot2, n_col, 0, width), val_here, val_density)
    fetches[2].wait()
    build_con(con, rolled, density)
    at_once = 2 - n_stripes % 2
    for s in range(0, n_stripes, at_once):
        for copy in copies[s : s + at_once]:
            copy.wait()
        part = product(list(range(s, s + at_once)), w, density, val_density)
        if s == 0:
            acc[...] = part
        else:
            acc[...] += part
    hand_out(n_col, me % 2, acc, kept, sent)


def begin_kernel(n_col, start, width, n_stripes, numbers, n_after, *refs):
    w, refs = refs[:n_stripes], refs[n_stripes:]
    (density, hot1, hot2, val), refs = refs[:4], refs[4:]
    acc, val_density, *_ = refs[n_after:]
    build_val(groups(hot1, n_col, start, width), groups(hot2, n_col, start, width), val, val_density)
    acc[...] = product(numbers, w, density, val_density)


def end_kernel(n_col, n_stripes, numbers, n_after, place, *refs):
    w, refs = refs[:n_stripes], refs[n_stripes:]
    (density, before, val_density), refs = refs[:3], refs[3:]
    kept, sent, acc = *refs[n_after : n_after + 2], refs[-1]
    acc[...] = before[...] + product(numbers, w, density, val_density)
    hand_out(n_col, place[0] // n_col % 2, acc, [kept], sent)


def fold_kernel(n_col, targets, got_groups, sent_groups, place, *refs):
    n = len(targets)
    kept, got = refs[:n], refs[n : n + len(got_groups)]
    out = refs[n + len(got_groups) :]
    halves, sent = out[: len(out) - len(sent_groups)], out[len(out) - len(sent_groups) :]
    source, sink = {}, {}
    for array, group in zip(got, got_groups):
        at = 0
        for c in group:
            source[c] = array, at
            at += kept[c].shape[0]
    for array, group in zip(sent, sent_groups):
        at = 0
        for c in group:
            sink[c] = array, at
            at += kept[c].shape[0] // (2 if targets[c] else 1)
    for c, target in enumerate(targets):
        part, rows = kept[c], kept[c].shape[0]
        (array, at), (other, to) = source[c], sink[c]
        if target is None:
            other[to : to + rows, :] = (part[...] + array[at : at + rows, :].astype(F32)).astype(BF16)
            continue
        axis, bit, each = target
        me = place[0] // n_col if axis == "row" else place[0] % n_col
        high = (me >> bit) % 2 == 1
        half = rows // each // 2
        for z in range(each):
            a, b = 2 * z * half, (2 * z + 1) * half
            low_part = part[a : a + half, :] + array[at + a : at + a + half, :].astype(F32)
            high_part = part[b : b + half, :] + array[at + b : at + b + half, :].astype(F32)
            halves[c][z * half : (z + 1) * half, :] = jnp.where(high, high_part, low_part)
            other[to + z * half : to + (z + 1) * half, :] = jnp.where(high, low_part, high_part).astype(BF16)


def pick_kernel(n_col, count, scale, gathers, place, pairs, *refs):
    arrays, (out, whole) = refs[: len(gathers)], refs[len(gathers) :]
    own = out.shape[0]
    me = place[0] // n_col
    for array, (steps, chunks) in zip(arrays, gathers):
        each = sum(rows for _, rows, _ in chunks)
        for j in range(array.shape[0] // each):
            block = sum((((me ^ j) >> bit) % 2) << s for s, bit in enumerate(steps))
            used = 0
            for start, rows, order in chunks:
                spot = sum(((j >> bit) & 1) << (len(order) - 1 - s) for s, bit in enumerate(order))
                to = start + spot * rows
                whole[to : to + rows, :] = array[pl.ds(block * each + used, rows), :]
                used += rows
    if own % 128:
        every = pairs[...]
        asked = functools.reduce(
            lambda a, i: jnp.where(me == i, every[:, i * own : (i + 1) * own], a), range(pairs.shape[1] // own), every[:, :own]
        )
    else:
        asked = pairs[:, pl.ds(pl.multiple_of(me * own, own), own)]
    c, other = asked[0:1], asked[1:2]
    apart = jnp.where(other >= c, other - c, other - c + count)
    row = jnp.where(apart <= count // 2, apart * count + c, (count - apart) * count + other)
    pick = one_hot_columns(row, whole.shape[1]).astype(BF16)
    out[...] = (jnp.dot(whole[...].astype(BF16), pick, preferred_element_type=F32) * scale).T


def swap(x, axis, bit, size):
    return lax.ppermute(x, axis, [(i, i ^ (1 << bit)) for i in range(size)])


def solution(mesh):
    n_row, n_col = mesh.shape["row"], mesh.shape["col"]
    row_bits, col_bits = n_row.bit_length() - 1, n_col.bit_length() - 1

    def per_device(screened, val_orbitals, con_orbitals, val_pairs, con_pairs):
        own_rows, own_columns = screened.shape
        count, grid = con_orbitals.shape
        n_val = val_orbitals.shape[0]
        blocks = count // 2 + 1
        while blocks * count % 128:
            blocks += 1
        unordered = blocks * count
        n_pairs = val_pairs.shape[0]
        per_col = n_pairs // n_col
        chunks = CHUNKS if n_pairs >= 8 * CHUNKS * n_row * n_col and row_bits > 2 else 1
        width = per_col // chunks
        starts = [k * width for k in range(chunks)]
        place = (lax.axis_index("row") * n_col + lax.axis_index("col")).astype(jnp.int32)[None]
        smem = pl.BlockSpec(memory_space=pltpu.SMEM)
        vmem = pl.BlockSpec(memory_space=pltpu.VMEM)
        anywhere = pl.BlockSpec(memory_space=pl.ANY)
        hbm = pl.BlockSpec(memory_space=pltpu.HBM)

        def params(mib):
            return pltpu.CompilerParams(vmem_limit_bytes=mib << 20)

        def cost(n, rows):
            return pl.CostEstimate(
                flops=2 * n * rows * (own_columns + unordered), bytes_accessed=1 << 20, transcendentals=0
            )

        def outs(rows):
            return [pltpu.VMEM((rows, unordered), F32), pltpu.VMEM((rows, unordered), BF16)]

        stripe = min(512, own_rows)
        hots = [pltpu.VMEM((n_pairs, n_val), BF16)] * 2
        n_first = min(chunks, 2)
        n = n_col * width * n_first
        n_stripes = own_rows // stripe
        held = [pltpu.VMEM((stripe, own_columns), BF16)] * n_stripes + [pltpu.VMEM((unordered, own_rows), BF16)]
        n_held = n_stripes + 1
        *kept, sent = [pltpu.VMEM((n // n_first // 2, unordered), F32)] * n_first + [pltpu.VMEM((n // 2, unordered), BF16)]
        out = pl.pallas_call(
            functools.partial(first_kernel, n_col, width * n_first, n_stripes, n_first),
            in_specs=[smem] + [hbm] * 4,
            out_specs=[vmem] * (n_first + 1 + n_held + 2),
            out_shape=kept + [sent] + held + hots,
            scratch_shapes=[
                pltpu.VMEM((n, own_columns), BF16),
                pltpu.VMEM((n, unordered), F32),
                pltpu.VMEM((2, n_pairs), jnp.int32),
                pltpu.VMEM((n_val, own_columns), BF16),
                pltpu.VMEM((count, own_rows), BF16),
                pltpu.VMEM((2 * count, min(512, own_rows)), F32),
                pltpu.SemaphoreType.DMA((n_stripes,)),
                pltpu.SemaphoreType.DMA((3,)),
            ],
            compiler_params=params(18),
            cost_estimate=cost(n, own_rows),
            name="first",
        )(place, *[pltpu.with_memory_space_constraint(x, pltpu.HBM) for x in (val_pairs.T, val_orbitals, con_orbitals, screened)])
        kept, sent, fixed = list(out[:n_first]), out[n_first], list(out[n_first + 1 :])

        def begin(k, numbers, fixed, after):
            n = n_col * width
            acc, val_density, *fixed = pl.pallas_call(
                functools.partial(begin_kernel, n_col, starts[k], width, n_stripes, numbers, len(after)),
                in_specs=[vmem] * (n_held + 3) + [anywhere] * len(after),
                out_specs=[vmem] * (2 + n_held + 2),
                out_shape=[pltpu.VMEM((n, unordered), F32), pltpu.VMEM((n, own_columns), BF16)] + held + hots,
                input_output_aliases={i: 2 + i for i in range(n_held + 2)},
                compiler_params=params(7),
                cost_estimate=cost(n, len(numbers) * stripe),
            )(*fixed, val_orbitals, *after)
            return (acc, val_density), fixed

        def end(numbers, fixed, before, after):
            n = n_col * width
            kept, sent, *same = pl.pallas_call(
                functools.partial(end_kernel, n_col, n_stripes, numbers, len(after)),
                in_specs=[smem] + [vmem] * (n_held + 2) + [anywhere] * len(after),
                out_specs=[vmem] * (2 + n_held),
                out_shape=outs(n // 2) + held,
                scratch_shapes=[pltpu.VMEM((n, unordered), F32)],
                input_output_aliases={1 + i: 2 + i for i in range(n_held)},
                compiler_params=params(9),
                cost_estimate=cost(n, len(numbers) * stripe),
            )(place, *fixed[:n_held], *before, *after)
            return (kept, sent), same + fixed[n_held:]

        def fold(kept, got, targets, got_groups=None, sent_groups=None):
            everything = [list(range(len(kept)))]
            got_groups, sent_groups = got_groups or everything, sent_groups or everything
            rows = [k.shape[0] // (2 if t else 1) for k, t in zip(kept, targets)]
            shapes = [pltpu.VMEM((r, unordered), F32) for r, t in zip(rows, targets) if t]
            n_kept = len(shapes)
            shapes += [pltpu.VMEM((sum(rows[c] for c in g), unordered), BF16) for g in sent_groups]
            out = pl.pallas_call(
                functools.partial(fold_kernel, n_col, targets, got_groups, sent_groups),
                in_specs=[smem] + [vmem] * (len(kept) + len(got)),
                out_specs=[vmem] * len(shapes),
                out_shape=shapes,
                compiler_params=params(4),
            )(place, *kept, *got)
            return list(out[:n_kept]), list(out[n_kept:])

        order = list(range(1, row_bits))
        orders = [[0] + (order if k % 2 == 0 else order[::-1]) for k in range(chunks)]
        steps = [
            [("row", bit, n_col) for bit in orders[k]] + [("col", bit, 1) for bit in reversed(range(col_bits))] + [None]
            for k in range(chunks)
        ]
        n_steps = row_bits + col_bits
        sizes = {"row": n_row, "col": n_col}

        def send(k, at, sent):
            axis, bit, _ = steps[k][at]
            return swap(sent, axis, bit, sizes[axis])

        def run(k, at, until, kept, sent):
            for s in range(at, until):
                got = send(k, s, sent)
                kept, (sent,) = fold(kept, [got], [steps[k][s + 1]] * len(kept))
            return kept, sent

        def gather(part, bits):
            for bit in bits:
                part = jnp.concatenate([part, swap(part, "row", bit, n_row)])
            return part.astype(F32)

        if chunks > 1:
            low, high = list(range(n_stripes // 2)), list(range(n_stripes // 2, n_stripes))
            apart = [[0], [1]]
            before, fixed = begin(2, low, fixed, [sent])
            got = [send(0, 0, sent)]
            kept, sents = fold(kept, got, [steps[0][1], steps[1][1]], None, apart)
            m, fixed = end(high, fixed, before, sents)
            got = [send(k, 1, sents[k]) for k in range(2)]
            before, fixed = begin(3, low, fixed, [m[1]])
            kept, sents = fold(kept, got, [steps[0][2], steps[1][2]], apart, apart)
            m = run(2, 0, 1, [m[0]], m[1])
            b, fixed = end(high, fixed, before, sents + [m[1]])
            b = [b[0]], b[1]
            for s in range(2, row_bits):
                got = [send(k, s, sents[k]) for k in range(2)]
                ends = apart if s < row_bits - 1 else None
                kept, sents = fold(kept, got, [steps[0][s + 1], steps[1][s + 1]], apart, ends)
            a, sent = run(0, row_bits, n_steps - 1, kept, sents[0])
            m, m_sent = run(2, 1, n_steps - 1, *m)
            got = [send(0, n_steps - 1, sent), send(2, n_steps - 1, m_sent)]
            _, (early,) = fold(a + m, got, [None] * 3, [[0, 1], [2]], None)
            _, late = run(3, 0, n_steps, *b)
            early_bits, late_bits = order + [0], order[::-1] + [0]
            arrays = [gather(early, early_bits), gather(late, late_bits)]
            gathers = [(early_bits, [0, 1, 2]), (late_bits, [3])]
        else:
            _, late = run(0, 0, n_steps, kept, sent)
            late_bits = order[::-1] + [0]
            arrays, gathers = [gather(late, late_bits)], [(late_bits, [0])]
        gathers = [(bits, [(starts[k], width // n_row, orders[k]) for k in ks]) for bits, ks in gathers]

        own = con_pairs.shape[0] // n_row
        return pl.pallas_call(
            functools.partial(pick_kernel, n_col, count, float(grid ** (-0.5)), gathers),
            in_specs=[smem] + [vmem] * (1 + len(arrays)),
            out_specs=vmem,
            out_shape=jax.ShapeDtypeStruct((own, per_col), F32),
            scratch_shapes=[pltpu.VMEM((per_col, unordered), F32)],
            compiler_params=params(20),
            name="pick",
        )(place, con_pairs.T, *arrays)

    in_specs = (P("row", "col"), P(None, "col"), P(), P(), P())

    return jax.shard_map(per_device, mesh=mesh, in_specs=in_specs, out_specs=P("row", "col"), check_vma=False)
```

time: 109 us -> 105 us (0.963)
  starting transfers between devices: 18.3 us -> 28.7 us
  local copies, waits for them, and re-layouts: 3.58 us -> 0.01 us
  waiting for transfers between devices: 34.5 us -> 31.1 us
  other arithmetic: 3.24 us -> 0.23 us
  between operations: 2.97 us -> 0.2 us
  Pallas kernels: 46.1 us -> 44.1 us
    ppermute x19 -> x23, starting transfers between devices: 18.3 us -> 28.7 us  [swap(): return lax.ppermute(x, axis, [(i, i ^ 1 << bit) for i in range(size)])]
    ppermute x19 -> x23, waiting for transfers between devices: 34.5 us -> 31.1 us  [swap(): return lax.ppermute(x, axis, [(i, i ^ 1 << bit) for i in range(size)])]
    unnamed x16 -> x4, local copies, waits for them, and re-layouts: 3.18 us -> 0.01 us
    add x8 -> x0, other arithmetic: 2.65 us -> none  [the longest x7 2.61 us: over_row(): part = kept + swap(sent, 'row', orders[k][at - 1], n_row).astype(F32)]
    pallas_call x5 -> x17, Pallas kernels: 35.8 us -> 34.3 us  [the longest x1 22.6 us: per_device(): pl.pallas_call(functools.partial(first_kernel, n_col, width * n_first, n_...]
  transfers between devices with their start and end apart: 19 -> 23, of which waited for: 10 -> 14; matrix products, arithmetic and copies ran while one was open for 3% -> 0% of each run, Pallas kernels for 15% -> 11%
where the time goes in v3:
time: 105 us; the launch traced here: 104 us
  Pallas kernels  44.1 us (42%)
  waiting for transfers between devices  31.1 us (30%)
  starting transfers between devices  28.7 us (27%)
    ppermute x23, waiting for transfers between devices, swap(): return lax.ppermute(x, axis, [(i, i ^ 1 << bit) for i in range(size)])  31.1 us
    ppermute x23, starting transfers between devices, swap(): return lax.ppermute(x, axis, [(i, i ^ 1 << bit) for i in range(size)])  28.7 us
    pallas_call x1, Pallas kernels, per_device(): pl.pallas_call(functools.partial(first_kernel, n_col, width * n_first, n_...  22.6 us
    pallas_call x2, Pallas kernels, begin(): pl.pallas_call(functools.partial(begin_kernel, n_col, starts[k], width, n...  10.6 us
    pallas_call x2, Pallas kernels, end(): pl.pallas_call(functools.partial(end_kernel, n_col, n_stripes, numbers, l...  8.04 us
  transfers between devices with their start and end apart: 23, of which 14 were waited for; matrix products, arithmetic and copies ran while one was open for 0% of the time, Pallas kernels for 11%

profile of v3, /device:TPU:0, one launch (start us, length us, event | category | flops | bytes accessed | tf_op | source)
XLA Modules:
  0.0 104.4 jit_solution(2684533213027735754)
XLA Ops:
  0.0 0.0 copy-start
  0.0 22.6 %first.1 = (f32[128,2176]{1,0:T(8,128)S(1)}, f32[128,2176]{1,0:T(8,128)S(1)}, bf16[256,2176]{1,0:T(8,128)(2,1)S(1)}, bf16[512,4096]{1,0:T(8,128)(2,1)S(1)}, bf16...) custom-call(s32[1]{0:T(128)} %bitcast.place, ...), custom_call_target="tpu_custom_call" | custom-call | flops 13153337344 | bytes 1048576 | tf_op jit(solution)/shard_map/first/pallas_call | solution.py:238
  22.6 0.6 collective-permute-start
  23.2 0.0 copy-done
  23.2 5.3 %shard_map.59 = (f32[256,2176]{1,0:T(8,128)S(1)}, bf16[256,4096]{1,0:T(8,128)(2,1)S(1)}, bf16[512,4096]{1,0:T(8,128)(2,1)S(1)}, bf16[512,4096]{1,0:T(8,128)(2,1)...) custom-call(bf16[512,4096]{1,0:T(8,128)(2,1)S(1)} %get-tuple-element, ...), custom_call_target="tpu_custom_call", output_to_operand_aliasing={{2}: (0, {}), {3}: (1, {}), {4}: (2, {}), {5}: (3, {}), {6}... | custom-call | flops 3288334336 | bytes 1048576 | tf_op jit(solution)/shard_map/pallas_call | solution.py:261
  28.5 0.0 collective-permute-done.refs_2_
  28.5 0.3 shard_map.55
  28.8 4.0 %shard_map.60 = (f32[128,2176]{1,0:T(8,128)S(1)}, bf16[128,2176]{1,0:T(8,128)(2,1)S(1)}, bf16[512,4096]{1,0:T(8,128)(2,1)S(1)}, bf16[512,4096]{1,0:T(8,128)(2,1)...) custom-call(s32[1]{0:T(128)} %bitcast.place, ...), custom_call_target="tpu_custom_call", output_to_operand_aliasing={{2}: (1, {}), {3}: (2, {}), {4}: (3, {}), {5}: (4, {}), {6}... | custom-call | flops 3288334336 | bytes 1048576 | tf_op jit(solution)/shard_map/pallas_call | solution.py:274
  32.8 0.1 collective-permute-start.6
  32.9 3.0 %collective-permute-start.1 = (bf16[64,2176]{1,0:T(8,128)(2,1)S(1)}, bf16[64,2176]{1,0:T(8,128)(2,1)S(1)}, u32[]{:S(2)}, u32[]{:S(2)}) collective-permute-start(bf16[64,2176]{1,0:T(8,128)(2,1)S(1)} %get-tuple-element.75.refs_7_), channel_id=1, source_target_pairs={{0,8},{4,12},{8,0},{12,4},{16,24},{20,28},{24,16},{28,20},{1,9},{5... | collective-permute-start | bytes 835592 | tf_op jit(solution)/shard_map/ppermute | solution.py:193
  35.8 1.5 %collective-permute-start.2 = (bf16[64,2176]{1,0:T(8,128)(2,1)S(1)}, bf16[64,2176]{1,0:T(8,128)(2,1)S(1)}, u32[]{:S(2)}, u32[]{:S(2)}) collective-permute-start(bf16[64,2176]{1,0:T(8,128)(2,1)S(1)} %get-tuple-element.76.refs_8_), channel_id=1, source_target_pairs={{0,16},{4,20},{8,24},{12,28},{16,0},{20,4},{24,8},{28,12},{1,17},{... | collective-permute-start | bytes 835592 | tf_op jit(solution)/shard_map/ppermute | solution.py:193
  37.4 5.3 %shard_map.66 = (f32[256,2176]{1,0:T(8,128)S(1)}, bf16[256,4096]{1,0:T(8,128)(2,1)S(1)}, bf16[512,4096]{1,0:T(8,128)(2,1)S(1)}, bf16[512,4096]{1,0:T(8,128)(2,1)...) custom-call(bf16[512,4096]{1,0:T(8,128)(2,1)S(1)} %get-tuple-element, ...), custom_call_target="tpu_custom_call", output_to_operand_aliasing={{2}: (0, {}), {3}: (1, {}), {4}: (2, {}), {5}: (3, {}), {6}... | custom-call | flops 3288334336 | bytes 1048576 | tf_op jit(solution)/shard_map/pallas_call | solution.py:261
  42.7 0.1 collective-permute-done.1.refs_2_
  42.7 1.5 %collective-permute-done.2.refs_3_ = bf16[64,2176]{1,0:T(8,128)(2,1)S(1)} collective-permute-done((bf16[64,2176]{1,0:T(8,128)(2,1)S(1)}, bf16[64,2176]{1,0:T(8,128)(2,1)S(1)}, u32[]{:S(2)}, u32[]{:S(2)}) %collective-permute-start.2) | collective-permute-done | bytes 278560 | tf_op jit(solution)/shard_map/ppermute | solution.py:193
  44.2 0.1 shard_map.56
  44.3 0.0 collective-permute-done.6.refs_1_
  44.3 0.2 shard_map.61
  44.5 4.0 %shard_map.67 = (f32[128,2176]{1,0:T(8,128)S(1)}, bf16[128,2176]{1,0:T(8,128)(2,1)S(1)}, bf16[512,4096]{1,0:T(8,128)(2,1)S(1)}, bf16[512,4096]{1,0:T(8,128)(2,1)...) custom-call(s32[1]{0:T(128)} %bitcast.place, ...), custom_call_target="tpu_custom_call", output_to_operand_aliasing={{2}: (1, {}), {3}: (2, {}), {4}: (3, {}), {5}: (4, {}), {6}... | custom-call | flops 3288334336 | bytes 1048576 | tf_op jit(solution)/shard_map/pallas_call | solution.py:274
  48.5 0.1 collective-permute-start.15
  48.6 0.4 collective-permute-start.7
  49.0 1.7 %collective-permute-start.3 = (bf16[32,2176]{1,0:T(8,128)(2,1)S(1)}, bf16[32,2176]{1,0:T(8,128)(2,1)S(1)}, u32[]{:S(2)}, u32[]{:S(2)}) collective-permute-start(bf16[32,2176]{1,0:T(8,128)(2,1)S(1)} %get-tuple-element.79.refs_7_), channel_id=1, source_target_pairs={{0,16},{4,20},{8,24},{12,28},{16,0},{20,4},{24,8},{28,12},{1,17},{... | collective-permute-start | bytes 417800 | tf_op jit(solution)/shard_map/ppermute | solution.py:193
  50.7 1.5 %collective-permute-start.4 = (bf16[32,2176]{1,0:T(8,128)(2,1)S(1)}, bf16[32,2176]{1,0:T(8,128)(2,1)S(1)}, u32[]{:S(2)}, u32[]{:S(2)}) collective-permute-start(bf16[32,2176]{1,0:T(8,128)(2,1)S(1)} %get-tuple-element.80.refs_8_), channel_id=1, source_target_pairs={{0,8},{4,12},{8,0},{12,4},{16,24},{20,28},{24,16},{28,20},{1,9},{5... | collective-permute-start | bytes 417800 | tf_op jit(solution)/shard_map/ppermute | solution.py:193
  52.2 6.0 %collective-permute-done.7.refs_1_ = bf16[64,2176]{1,0:T(8,128)(2,1)S(1)} collective-permute-done((bf16[64,2176]{1,0:T(8,128)(2,1)S(1)}, bf16[64,2176]{1,0:T(8,128)(2,1)S(1)}, u32[]{:S(2)}, u32[]{:S(2)}) %collective-permute-start.7) | collective-permute-done | bytes 278560 | tf_op jit(solution)/shard_map/ppermute | solution.py:193
  58.2 0.1 shard_map.62
  58.3 1.6 %collective-permute-start.8 = (bf16[32,2176]{1,0:T(8,128)(2,1)S(1)}, bf16[32,2176]{1,0:T(8,128)(2,1)S(1)}, u32[]{:S(2)}, u32[]{:S(2)}) collective-permute-start(bf16[32,2176]{1,0:T(8,128)(2,1)S(1)} %get-tuple-element.105), channel_id=1, source_target_pairs={{0,16},{4,20},{8,24},{12,28},{16,0},{20,4},{24,8},{28,12},{1,17},{... | collective-permute-start | bytes 417800 | tf_op jit(solution)/shard_map/ppermute | solution.py:193
  59.9 0.0 collective-permute-done.3.refs_2_
  59.9 0.8 collective-permute-done.4.refs_3_
  60.7 0.1 shard_map.57
  60.7 2.6 %collective-permute-start.5 = (bf16[32,2176]{1,0:T(8,128)(2,1)S(1)}, bf16[32,2176]{1,0:T(8,128)(2,1)S(1)}, u32[]{:S(2)}, u32[]{:S(2)}) collective-permute-start(bf16[32,2176]{1,0:T(8,128)(2,1)S(1)} %get-tuple-element.83), channel_id=1, source_target_pairs={{0,2},{1,3},{2,0},{3,1},{4,6},{5,7},{6,4},{7,5},{8,10},{9,11},{10,... | collective-permute-start | bytes 417800 | tf_op jit(solution)/shard_map/ppermute | solution.py:193
  63.4 0.0 collective-permute-done.15.refs_1_
  63.4 0.1 shard_map.68
  63.5 0.0 copy-start.1
  63.5 1.6 %collective-permute-start.16 = (bf16[64,2176]{1,0:T(8,128)(2,1)S(1)}, bf16[64,2176]{1,0:T(8,128)(2,1)S(1)}, u32[]{:S(2)}, u32[]{:S(2)}) collective-permute-start(bf16[64,2176]{1,0:T(8,128)(2,1)S(1)} %get-tuple-element.128), channel_id=1, source_target_pairs={{0,16},{4,20},{8,24},{12,28},{16,0},{20,4},{24,8},{28,12},{1,17},{... | collective-permute-start | bytes 835592 | tf_op jit(solution)/shard_map/ppermute | solution.py:193
  65.1 0.0 collective-permute-done.8.refs_1_
  65.2 1.0 collective-permute-start.9
  66.2 5.9 %collective-permute-done.5.refs_2_ = bf16[32,2176]{1,0:T(8,128)(2,1)S(1)} collective-permute-done((bf16[32,2176]{1,0:T(8,128)(2,1)S(1)}, bf16[32,2176]{1,0:T(8,128)(2,1)S(1)}, u32[]{:S(2)}, u32[]{:S(2)}) %collective-permute-start.5) | collective-permute-done | bytes 139296 | tf_op jit(solution)/shard_map/ppermute | solution.py:193
  72.1 0.1 collective-permute-start.10
  72.2 0.6 collective-permute-done.9.refs_1_
  72.9 1.5 %collective-permute-start.11 = (bf16[8,2176]{1,0:T(8,128)(2,1)S(1)}, bf16[8,2176]{1,0:T(8,128)(2,1)S(1)}, u32[]{:S(2)}, u32[]{:S(2)}) collective-permute-start(bf16[8,2176]{1,0:T(8,128)(2,1)S(1)} %get-tuple-element.110), channel_id=1, source_target_pairs={{0,1},{1,0},{2,3},{3,2},{4,5},{5,4},{6,7},{7,6},{8,9},{9,8},{10,11... | collective-permute-start | bytes 104456 | tf_op jit(solution)/shard_map/ppermute | solution.py:193
  74.3 2.2 %collective-permute-done.10.refs_3_ = bf16[16,2176]{1,0:T(8,128)(2,1)S(1)} collective-permute-done((bf16[16,2176]{1,0:T(8,128)(2,1)S(1)}, bf16[16,2176]{1,0:T(8,128)(2,1)S(1)}, u32[]{:S(2)}, u32[]{:S(2)}) %collective-permute-start.10) | collective-permute-done | bytes 69664 | tf_op jit(solution)/shard_map/ppermute | solution.py:193
  76.5 0.4 collective-permute-done.11.refs_4_
  76.9 0.5 collective-permute-start.12
  77.4 0.0 collective-permute-done.16.refs_1_
  77.4 0.1 shard_map.69
  77.5 1.6 %collective-permute-start.17 = (bf16[32,2176]{1,0:T(8,128)(2,1)S(1)}, bf16[32,2176]{1,0:T(8,128)(2,1)S(1)}, u32[]{:S(2)}, u32[]{:S(2)}) collective-permute-start(bf16[32,2176]{1,0:T(8,128)(2,1)S(1)} %get-tuple-element.130), channel_id=1, source_target_pairs={{0,8},{4,12},{8,0},{12,4},{16,24},{20,28},{24,16},{28,20},{1,9},{5... | collective-permute-start | bytes 417800 | tf_op jit(solution)/shard_map/ppermute | solution.py:193
  79.2 2.5 %collective-permute-done.12 = bf16[24,2176]{1,0:T(8,128)(2,1)S(1)} collective-permute-done((bf16[24,2176]{1,0:T(8,128)(2,1)S(1)}, bf16[24,2176]{1,0:T(8,128)(2,1)S(1)}, u32[]{:S(2)}, u32[]{:S(2)}) %collective-permute-start.12) | collective-permute-done | bytes 104480 | tf_op jit(solution)/shard_map/ppermute | solution.py:193
  81.7 1.6 %collective-permute-start.13 = (bf16[48,2176]{1,0:T(8,128)(2,1)S(1)}, bf16[48,2176]{1,0:T(8,128)(2,1)S(1)}, u32[]{:S(2)}, u32[]{:S(2)}) collective-permute-start(bf16[48,2176]{1,0:T(8,128)(2,1)S(1)} %pad_maximum_fusion.1), channel_id=1, source_target_pairs={{0,16},{4,20},{8,24},{12,28},{16,0},{20,4},{24,8},{28,12},{1,17},{... | collective-permute-start | bytes 626696 | tf_op jit(solution)/shard_map/ppermute | solution.py:193
  83.3 0.0 collective-permute-done.17.refs_1_
  83.3 3.0 %collective-permute-start.18 = (bf16[16,2176]{1,0:T(8,128)(2,1)S(1)}, bf16[16,2176]{1,0:T(8,128)(2,1)S(1)}, u32[]{:S(2)}, u32[]{:S(2)}) collective-permute-start(bf16[16,2176]{1,0:T(8,128)(2,1)S(1)} %get-tuple-element.132), channel_id=1, source_target_pairs={{0,2},{1,3},{2,0},{3,1},{4,6},{5,7},{6,4},{7,5},{8,10},{9,11},{10,... | collective-permute-start | bytes 208904 | tf_op jit(solution)/shard_map/ppermute | solution.py:193
  86.3 2.4 %collective-permute-done.18.refs_1_ = bf16[16,2176]{1,0:T(8,128)(2,1)S(1)} collective-permute-done((bf16[16,2176]{1,0:T(8,128)(2,1)S(1)}, bf16[16,2176]{1,0:T(8,128)(2,1)S(1)}, u32[]{:S(2)}, u32[]{:S(2)}) %collective-permute-start.18) | collective-permute-done | bytes 69664 | tf_op jit(solution)/shard_map/ppermute | solution.py:193
  88.7 2.1 %collective-permute-start.19 = (bf16[8,2176]{1,0:T(8,128)(2,1)S(1)}, bf16[8,2176]{1,0:T(8,128)(2,1)S(1)}, u32[]{:S(2)}, u32[]{:S(2)}) collective-permute-start(bf16[8,2176]{1,0:T(8,128)(2,1)S(1)} %get-tuple-element.134), channel_id=1, source_target_pairs={{0,1},{1,0},{2,3},{3,2},{4,5},{5,4},{6,7},{7,6},{8,9},{9,8},{10,11... | collective-permute-start | bytes 104456 | tf_op jit(solution)/shard_map/ppermute | solution.py:193
  90.9 1.9 %collective-permute-done.19.refs_1_ = bf16[8,2176]{1,0:T(8,128)(2,1)S(1)} collective-permute-done((bf16[8,2176]{1,0:T(8,128)(2,1)S(1)}, bf16[8,2176]{1,0:T(8,128)(2,1)S(1)}, u32[]{:S(2)}, u32[]{:S(2)}) %collective-permute-start.19) | collective-permute-done | bytes 34848 | tf_op jit(solution)/shard_map/ppermute | solution.py:193
  92.8 1.5 %collective-permute-start.20 = (bf16[8,2176]{1,0:T(8,128)(2,1)S(1)}, bf16[8,2176]{1,0:T(8,128)(2,1)S(1)}, u32[]{:S(2)}, u32[]{:S(2)}) collective-permute-start(bf16[8,2176]{1,0:T(8,128)(2,1)S(1)} %shard_map.72), channel_id=1, source_target_pairs={{0,16},{4,20},{8,24},{12,28},{16,0},{20,4},{24,8},{28,12},{1,17},{... | collective-permute-start | bytes 104456 | tf_op jit(solution)/shard_map/ppermute | solution.py:193
  94.3 0.0 collective-permute-done.13
  94.4 0.1 collective-permute-start.14
  94.5 2.3 %collective-permute-done.20 = bf16[8,2176]{1,0:T(8,128)(2,1)S(1)} collective-permute-done((bf16[8,2176]{1,0:T(8,128)(2,1)S(1)}, bf16[8,2176]{1,0:T(8,128)(2,1)S(1)}, u32[]{:S(2)}, u32[]{:S(2)}) %collective-permute-start.20) | collective-permute-done | bytes 34848 | tf_op jit(solution)/shard_map/ppermute | solution.py:193
  96.8 1.0 collective-permute-start.21
  97.8 3.3 %collective-permute-done.21 = bf16[16,2176]{1,0:T(8,128)(2,1)S(1)} collective-permute-done((bf16[16,2176]{1,0:T(8,128)(2,1)S(1)}, bf16[16,2176]{1,0:T(8,128)(2,1)S(1)}, u32[]{:S(2)}, u32[]{:S(2)}) %collective-permute-start.21) | collective-permute-done | bytes 69664 | tf_op jit(solution)/shard_map/ppermute | solution.py:193
  101.1 0.1 collective-permute-start.22
  101.2 0.0 collective-permute-done.14
  101.2 0.1 maximum_convert_fusion.refs_0_
  101.3 1.2 %collective-permute-done.22 = bf16[32,2176]{1,0:T(8,128)(2,1)S(1)} collective-permute-done((bf16[32,2176]{1,0:T(8,128)(2,1)S(1)}, bf16[32,2176]{1,0:T(8,128)(2,1)S(1)}, u32[]{:S(2)}, u32[]{:S(2)}) %collective-permute-start.22) | collective-permute-done | bytes 139296 | tf_op jit(solution)/shard_map/ppermute | solution.py:193
  102.6 0.0 copy-done.1
  102.6 1.8 %pick.1 = f32[512,256]{1,0:T(8,128)} custom-call(s32[1]{0:T(128)} %bitcast.place, s32[2,4096]{1,0:T(2,128)S(1)} %bitcast.3, f32[192,2176]{1,0:T(8,128)S(1)} %maximum_convert_fusion.refs_0_, f32[64,2176]{1,0:T(8,128)S(1)} %maximum_convert_fusion.1.refs_1_), custom_call_target="tpu_custom_call" | custom-call | tf_op jit(solution)/shard_map/pick/pallas_call | solution.py:358
  (12 shorter events, 0.3 us)
Async XLA Ops:
  0.0 23.2 %copy-start = (bf16[45,4096]{1,0:T(8,128)(2,1)S(1)}, bf16[45,4096]{1,0:T(8,128)(2,1)}, u32[]{:S(2)}) copy-start(bf16[45,4096]{1,0:T(8,128)(2,1)} %refs_7_.3) | copy-start | bytes 1105924
  22.6 5.8 %collective-permute-start = (bf16[256,2176]{1,0:T(8,128)(2,1)S(1)}, bf16[256,2176]{1,0:T(8,128)(2,1)S(1)}, u32[]{:S(2)}, u32[]{:S(2)}) collective-permute-start(bf16[256,2176]{1,0:T(8,128)(2,1)S(1)} %get-tuple-element.72.refs_8_), channel_id=1, source_target_pairs={{0,4},{4,0},{8,12},{12,8},{16,20},{20,16},{24,28},{28,24},{1,5},{5... | collective-permute-start | bytes 3342344 | tf_op jit(solution)/shard_map/ppermute | solution.py:193
  32.8 11.6 %collective-permute-start.6 = (bf16[128,2176]{1,0:T(8,128)(2,1)S(1)}, bf16[128,2176]{1,0:T(8,128)(2,1)S(1)}, u32[]{:S(2)}, u32[]{:S(2)}) collective-permute-start(bf16[128,2176]{1,0:T(8,128)(2,1)S(1)} %get-tuple-element.101.refs_8_), channel_id=1, source_target_pairs={{0,4},{4,0},{8,12},{12,8},{16,20},{20,16},{24,28},{28,24},{1,5},{5... | collective-permute-start | bytes 1671176 | tf_op jit(solution)/shard_map/ppermute | solution.py:193
  32.9 9.9 %collective-permute-start.1 = (bf16[64,2176]{1,0:T(8,128)(2,1)S(1)}, bf16[64,2176]{1,0:T(8,128)(2,1)S(1)}, u32[]{:S(2)}, u32[]{:S(2)}) collective-permute-start(bf16[64,2176]{1,0:T(8,128)(2,1)S(1)} %get-tuple-element.75.refs_7_), channel_id=1, source_target_pairs={{0,8},{4,12},{8,0},{12,4},{16,24},{20,28},{24,16},{28,20},{1,9},{5... | collective-permute-start | bytes 835592 | tf_op jit(solution)/shard_map/ppermute | solution.py:193
  35.8 8.4 %collective-permute-start.2 = (bf16[64,2176]{1,0:T(8,128)(2,1)S(1)}, bf16[64,2176]{1,0:T(8,128)(2,1)S(1)}, u32[]{:S(2)}, u32[]{:S(2)}) collective-permute-start(bf16[64,2176]{1,0:T(8,128)(2,1)S(1)} %get-tuple-element.76.refs_8_), channel_id=1, source_target_pairs={{0,16},{4,20},{8,24},{12,28},{16,0},{20,4},{24,8},{28,12},{1,17},{... | collective-permute-start | bytes 835592 | tf_op jit(solution)/shard_map/ppermute | solution.py:193
  48.5 14.8 %collective-permute-start.15 = (bf16[128,2176]{1,0:T(8,128)(2,1)S(1)}, bf16[128,2176]{1,0:T(8,128)(2,1)S(1)}, u32[]{:S(2)}, u32[]{:S(2)}) collective-permute-start(bf16[128,2176]{1,0:T(8,128)(2,1)S(1)} %get-tuple-element.126), channel_id=1, source_target_pairs={{0,4},{4,0},{8,12},{12,8},{16,20},{20,16},{24,28},{28,24},{1,5},{5... | collective-permute-start | bytes 1671176 | tf_op jit(solution)/shard_map/ppermute | solution.py:193
  48.6 9.6 %collective-permute-start.7 = (bf16[64,2176]{1,0:T(8,128)(2,1)S(1)}, bf16[64,2176]{1,0:T(8,128)(2,1)S(1)}, u32[]{:S(2)}, u32[]{:S(2)}) collective-permute-start(bf16[64,2176]{1,0:T(8,128)(2,1)S(1)} %get-tuple-element.103.refs_9_), channel_id=1, source_target_pairs={{0,8},{4,12},{8,0},{12,4},{16,24},{20,28},{24,16},{28,20},{1,9},{5... | collective-permute-start | bytes 835592 | tf_op jit(solution)/shard_map/ppermute | solution.py:193
  49.0 10.8 %collective-permute-start.3 = (bf16[32,2176]{1,0:T(8,128)(2,1)S(1)}, bf16[32,2176]{1,0:T(8,128)(2,1)S(1)}, u32[]{:S(2)}, u32[]{:S(2)}) collective-permute-start(bf16[32,2176]{1,0:T(8,128)(2,1)S(1)} %get-tuple-element.79.refs_7_), channel_id=1, source_target_pairs={{0,16},{4,20},{8,24},{12,28},{16,0},{20,4},{24,8},{28,12},{1,17},{... | collective-permute-start | bytes 417800 | tf_op jit(solution)/shard_map/ppermute | solution.py:193
  50.7 9.9 %collective-permute-start.4 = (bf16[32,2176]{1,0:T(8,128)(2,1)S(1)}, bf16[32,2176]{1,0:T(8,128)(2,1)S(1)}, u32[]{:S(2)}, u32[]{:S(2)}) collective-permute-start(bf16[32,2176]{1,0:T(8,128)(2,1)S(1)} %get-tuple-element.80.refs_8_), channel_id=1, source_target_pairs={{0,8},{4,12},{8,0},{12,4},{16,24},{20,28},{24,16},{28,20},{1,9},{5... | collective-permute-start | bytes 417800 | tf_op jit(solution)/shard_map/ppermute | solution.py:193
  58.3 6.9 %collective-permute-start.8 = (bf16[32,2176]{1,0:T(8,128)(2,1)S(1)}, bf16[32,2176]{1,0:T(8,128)(2,1)S(1)}, u32[]{:S(2)}, u32[]{:S(2)}) collective-permute-start(bf16[32,2176]{1,0:T(8,128)(2,1)S(1)} %get-tuple-element.105), channel_id=1, source_target_pairs={{0,16},{4,20},{8,24},{12,28},{16,0},{20,4},{24,8},{28,12},{1,17},{... | collective-permute-start | bytes 417800 | tf_op jit(solution)/shard_map/ppermute | solution.py:193
  60.7 11.3 %collective-permute-start.5 = (bf16[32,2176]{1,0:T(8,128)(2,1)S(1)}, bf16[32,2176]{1,0:T(8,128)(2,1)S(1)}, u32[]{:S(2)}, u32[]{:S(2)}) collective-permute-start(bf16[32,2176]{1,0:T(8,128)(2,1)S(1)} %get-tuple-element.83), channel_id=1, source_target_pairs={{0,2},{1,3},{2,0},{3,1},{4,6},{5,7},{6,4},{7,5},{8,10},{9,11},{10,... | collective-permute-start | bytes 417800 | tf_op jit(solution)/shard_map/ppermute | solution.py:193
  63.5 39.1 %copy-start.1 = (s32[4096,2]{0,1:T(2,128)S(1)}, s32[4096,2]{0,1:T(2,128)}, u32[]{:S(2)}) copy-start(s32[4096,2]{0,1:T(2,128)} %param.9) | copy-start | bytes 98308
  63.5 13.9 %collective-permute-start.16 = (bf16[64,2176]{1,0:T(8,128)(2,1)S(1)}, bf16[64,2176]{1,0:T(8,128)(2,1)S(1)}, u32[]{:S(2)}, u32[]{:S(2)}) collective-permute-start(bf16[64,2176]{1,0:T(8,128)(2,1)S(1)} %get-tuple-element.128), channel_id=1, source_target_pairs={{0,16},{4,20},{8,24},{12,28},{16,0},{20,4},{24,8},{28,12},{1,17},{... | collective-permute-start | bytes 835592 | tf_op jit(solution)/shard_map/ppermute | solution.py:193
  65.2 7.6 %collective-permute-start.9 = (bf16[16,2176]{1,0:T(8,128)(2,1)S(1)}, bf16[16,2176]{1,0:T(8,128)(2,1)S(1)}, u32[]{:S(2)}, u32[]{:S(2)}) collective-permute-start(bf16[16,2176]{1,0:T(8,128)(2,1)S(1)} %get-tuple-element.107), channel_id=1, source_target_pairs={{0,2},{1,3},{2,0},{3,1},{4,6},{5,7},{6,4},{7,5},{8,10},{9,11},{10,... | collective-permute-start | bytes 208904 | tf_op jit(solution)/shard_map/ppermute | solution.py:193
  72.1 4.4 %collective-permute-start.10 = (bf16[16,2176]{1,0:T(8,128)(2,1)S(1)}, bf16[16,2176]{1,0:T(8,128)(2,1)S(1)}, u32[]{:S(2)}, u32[]{:S(2)}) collective-permute-start(bf16[16,2176]{1,0:T(8,128)(2,1)S(1)} %get-tuple-element.109), channel_id=1, source_target_pairs={{0,1},{1,0},{2,3},{3,2},{4,5},{5,4},{6,7},{7,6},{8,9},{9,8},{10,11... | collective-permute-start | bytes 208904 | tf_op jit(solution)/shard_map/ppermute | solution.py:193
  72.9 4.0 %collective-permute-start.11 = (bf16[8,2176]{1,0:T(8,128)(2,1)S(1)}, bf16[8,2176]{1,0:T(8,128)(2,1)S(1)}, u32[]{:S(2)}, u32[]{:S(2)}) collective-permute-start(bf16[8,2176]{1,0:T(8,128)(2,1)S(1)} %get-tuple-element.110), channel_id=1, source_target_pairs={{0,1},{1,0},{2,3},{3,2},{4,5},{5,4},{6,7},{7,6},{8,9},{9,8},{10,11... | collective-permute-start | bytes 104456 | tf_op jit(solution)/shard_map/ppermute | solution.py:193
  76.9 4.7 %collective-permute-start.12 = (bf16[24,2176]{1,0:T(8,128)(2,1)S(1)}, bf16[24,2176]{1,0:T(8,128)(2,1)S(1)}, u32[]{:S(2)}, u32[]{:S(2)}) collective-permute-start(bf16[24,2176]{1,0:T(8,128)(2,1)S(1)} %shard_map.65), channel_id=1, source_target_pairs={{0,8},{4,12},{8,0},{12,4},{16,24},{20,28},{24,16},{28,20},{1,9},{5... | collective-permute-start | bytes 313352 | tf_op jit(solution)/shard_map/ppermute | solution.py:193
  77.5 5.7 %collective-permute-start.17 = (bf16[32,2176]{1,0:T(8,128)(2,1)S(1)}, bf16[32,2176]{1,0:T(8,128)(2,1)S(1)}, u32[]{:S(2)}, u32[]{:S(2)}) collective-permute-start(bf16[32,2176]{1,0:T(8,128)(2,1)S(1)} %get-tuple-element.130), channel_id=1, source_target_pairs={{0,8},{4,12},{8,0},{12,4},{16,24},{20,28},{24,16},{28,20},{1,9},{5... | collective-permute-start | bytes 417800 | tf_op jit(solution)/shard_map/ppermute | solution.py:193
  81.7 12.7 %collective-permute-start.13 = (bf16[48,2176]{1,0:T(8,128)(2,1)S(1)}, bf16[48,2176]{1,0:T(8,128)(2,1)S(1)}, u32[]{:S(2)}, u32[]{:S(2)}) collective-permute-start(bf16[48,2176]{1,0:T(8,128)(2,1)S(1)} %pad_maximum_fusion.1), channel_id=1, source_target_pairs={{0,16},{4,20},{8,24},{12,28},{16,0},{20,4},{24,8},{28,12},{1,17},{... | collective-permute-start | bytes 626696 | tf_op jit(solution)/shard_map/ppermute | solution.py:193
  83.3 5.4 %collective-permute-start.18 = (bf16[16,2176]{1,0:T(8,128)(2,1)S(1)}, bf16[16,2176]{1,0:T(8,128)(2,1)S(1)}, u32[]{:S(2)}, u32[]{:S(2)}) collective-permute-start(bf16[16,2176]{1,0:T(8,128)(2,1)S(1)} %get-tuple-element.132), channel_id=1, source_target_pairs={{0,2},{1,3},{2,0},{3,1},{4,6},{5,7},{6,4},{7,5},{8,10},{9,11},{10,... | collective-permute-start | bytes 208904 | tf_op jit(solution)/shard_map/ppermute | solution.py:193
  88.7 4.1 %collective-permute-start.19 = (bf16[8,2176]{1,0:T(8,128)(2,1)S(1)}, bf16[8,2176]{1,0:T(8,128)(2,1)S(1)}, u32[]{:S(2)}, u32[]{:S(2)}) collective-permute-start(bf16[8,2176]{1,0:T(8,128)(2,1)S(1)} %get-tuple-element.134), channel_id=1, source_target_pairs={{0,1},{1,0},{2,3},{3,2},{4,5},{5,4},{6,7},{7,6},{8,9},{9,8},{10,11... | collective-permute-start | bytes 104456 | tf_op jit(solution)/shard_map/ppermute | solution.py:193
  92.8 4.0 %collective-permute-start.20 = (bf16[8,2176]{1,0:T(8,128)(2,1)S(1)}, bf16[8,2176]{1,0:T(8,128)(2,1)S(1)}, u32[]{:S(2)}, u32[]{:S(2)}) collective-permute-start(bf16[8,2176]{1,0:T(8,128)(2,1)S(1)} %shard_map.72), channel_id=1, source_target_pairs={{0,16},{4,20},{8,24},{12,28},{16,0},{20,4},{24,8},{28,12},{1,17},{... | collective-permute-start | bytes 104456 | tf_op jit(solution)/shard_map/ppermute | solution.py:193
  94.4 6.8 %collective-permute-start.14 = (bf16[96,2176]{1,0:T(8,128)(2,1)S(1)}, bf16[96,2176]{1,0:T(8,128)(2,1)S(1)}, u32[]{:S(2)}, u32[]{:S(2)}) collective-permute-start(bf16[96,2176]{1,0:T(8,128)(2,1)S(1)} %pad_maximum_fusion), channel_id=1, source_target_pairs={{0,4},{4,0},{8,12},{12,8},{16,20},{20,16},{24,28},{28,24},{1,5},{5... | collective-permute-start | bytes 1253384 | tf_op jit(solution)/shard_map/ppermute | solution.py:193
  96.8 4.3 %collective-permute-start.21 = (bf16[16,2176]{1,0:T(8,128)(2,1)S(1)}, bf16[16,2176]{1,0:T(8,128)(2,1)S(1)}, u32[]{:S(2)}, u32[]{:S(2)}) collective-permute-start(bf16[16,2176]{1,0:T(8,128)(2,1)S(1)} %pad_maximum_fusion.3), channel_id=1, source_target_pairs={{0,8},{4,12},{8,0},{12,4},{16,24},{20,28},{24,16},{28,20},{1,9},{5... | collective-permute-start | bytes 208904 | tf_op jit(solution)/shard_map/ppermute | solution.py:193
  101.1 1.4 %collective-permute-start.22 = (bf16[32,2176]{1,0:T(8,128)(2,1)S(1)}, bf16[32,2176]{1,0:T(8,128)(2,1)S(1)}, u32[]{:S(2)}, u32[]{:S(2)}) collective-permute-start(bf16[32,2176]{1,0:T(8,128)(2,1)S(1)} %pad_maximum_fusion.2), channel_id=1, source_target_pairs={{0,4},{4,0},{8,12},{12,8},{16,20},{20,16},{24,28},{28,24},{1,5},{5... | collective-permute-start | bytes 417800 | tf_op jit(solution)/shard_map/ppermute | solution.py:193

commit v4 on v3

v4 whole, which is shorter than its diff:
```python
import functools

import jax
import jax.numpy as jnp
from jax import lax
from jax.experimental import pallas as pl
from jax.experimental.pallas import tpu as pltpu
from jax.sharding import PartitionSpec as P


CHUNKS = 4

F32, BF16 = jnp.float32, jnp.bfloat16
CONTRACT_MINOR = (((1,), (1,)), ((), ()))


def one_hot_columns(index, count):
    numbers = lax.broadcasted_iota(jnp.int32, (count, index.shape[1]), 0)
    return jnp.where(numbers == index, 1.0, 0.0)


def groups(ref, n_col, start, width):
    each = ref.shape[0] // n_col
    return jnp.concatenate([ref[z * each + start : z * each + start + width, :] for z in range(n_col)])


def build_val(first, second, val_ref, val_density):
    grid = val_ref.shape[1]
    step = min(2048, grid)

    @pl.loop(0, grid // step)
    def _(i):
        at = pl.ds(pl.multiple_of(i * step, step), step)
        orbitals = val_ref[:, at]
        a = jnp.dot(first, orbitals, preferred_element_type=F32)
        b = jnp.dot(second, orbitals, preferred_element_type=F32)
        val_density[:, at] = (a * b).astype(BF16)


def build_con(con, rolled, density):
    count, columns = con.shape
    wide = min(512, columns)
    apart = density.shape[0] // count

    @pl.loop(0, columns // wide)
    def _(i):
        at = pl.ds(pl.multiple_of(i * wide, wide), wide)
        one = con[:, at].astype(F32)
        for shift in range(8):
            moved = one if shift == 0 else jnp.concatenate([one[shift:], one[:shift]])
            rolled[0:count, :] = moved
            rolled[count : 2 * count, :] = moved
            for d in range(shift, apart, 8):
                other = rolled[d - shift : d - shift + count, :]
                density[d * count : (d + 1) * count, at] = (one * other).astype(BF16)


def product(numbers, w, density, val_density):
    stripe = w[0].shape[0]
    t = [lax.dot_general(val_density[...], w[s][...], CONTRACT_MINOR, preferred_element_type=F32).astype(BF16) for s in numbers]
    rows = slice(numbers[0] * stripe, (numbers[-1] + 1) * stripe)
    return lax.dot_general(jnp.concatenate(t, axis=1), density[:, rows], CONTRACT_MINOR, preferred_element_type=F32)


def hand_out(n_col, mine, acc, kept, sent):
    half = kept[0].shape[0] // n_col
    for c, own in enumerate(kept):
        for z in range(n_col):
            first = (z * len(kept) + c) * 2
            to = slice(z * half, (z + 1) * half)
            own[to, :] = acc[pl.ds(pl.multiple_of((first + mine) * half, half), half), :]
            to = slice((c * n_col + z) * half, (c * n_col + z + 1) * half)
            sent[to, :] = acc[pl.ds(pl.multiple_of((first + 1 - mine) * half, half), half), :].astype(BF16)


def fetch_all(n_col, n_stripes, place, hbm, vmem, sems, in_sems):
    pairs, val, con_all, w_hbm = hbm
    pairs_here, val_here, con, w = vmem
    columns, stripe = con.shape[1], w[0].shape[0]
    mine = pl.ds(pl.multiple_of((place[0] // n_col) * columns, columns), columns)
    fetches = [
        pltpu.make_async_copy(pairs, pairs_here, in_sems.at[0]),
        pltpu.make_async_copy(val, val_here, in_sems.at[1]),
        pltpu.make_async_copy(con_all.at[:, mine], con, in_sems.at[2]),
    ]
    fetches += [
        pltpu.make_async_copy(w_hbm.at[pl.ds(s * stripe, stripe), :], w[s], sems.at[s]) for s in range(n_stripes)
    ]
    for fetch in fetches:
        fetch.start()
    return fetches[:3], fetches[3:]


def make_hot(pairs, hot1, hot2):
    hot1[...] = one_hot_columns(pairs[0:1, :], hot1.shape[1]).T.astype(BF16)
    hot2[...] = one_hot_columns(pairs[1:2, :], hot2.shape[1]).T.astype(BF16)


def single_kernel(n_col, n_stripes, place, pairs, val, con_all, w_hbm, kept, sent, val_density, acc, density, hot1, hot2, pairs_here, val_here, con, rolled, sems, in_sems, *w):
    inputs, stripes = fetch_all(n_col, n_stripes, place, (pairs, val, con_all, w_hbm), (pairs_here, val_here, con, w), sems, in_sems)
    for fetch in inputs:
        fetch.wait()
    make_hot(pairs_here, hot1, hot2)
    build_val(hot1[...], hot2[...], val_here, val_density)
    build_con(con, rolled, density)
    for fetch in stripes:
        fetch.wait()
    acc[...] = product(list(range(n_stripes)), w, density, val_density)
    hand_out(n_col, place[0] // n_col % 2, acc, [kept], sent)


def load_kernel(n_col, start, width, n_stripes, place, pairs, val, con_all, w_hbm, kept, sent, val_a, *refs):
    w, refs = refs[:n_stripes], refs[n_stripes:]
    density, hot1, hot2, val_b, pairs_here, val_here, con, rolled, sems, in_sems = refs
    inputs, stripes = fetch_all(n_col, n_stripes, place, (pairs, val, con_all, w_hbm), (pairs_here, val_here, con, w), sems, in_sems)
    inputs[0].wait()
    make_hot(pairs_here, hot1, hot2)
    inputs[1].wait()
    build_val(groups(hot1, n_col, start, width), groups(hot2, n_col, start, width), val_here, val_b)
    build_val(groups(hot1, n_col, 0, 2 * width), groups(hot2, n_col, 0, 2 * width), val_here, val_a)
    inputs[2].wait()
    build_con(con, rolled, density)
    high = place[0] % n_col % 2 == 1
    for s, fetch in enumerate(stripes):
        fetch.wait()
        stripe = w[s].shape[0]
        at = slice(s * stripe, (s + 1) * stripe)
        t = lax.dot_general(val_b[...], w[s][...], CONTRACT_MINOR, preferred_element_type=F32)
        for z in range(n_col // 2):
            to = slice(z * width, (z + 1) * width)
            low_part = t[2 * z * width : (2 * z + 1) * width, :]
            high_part = t[(2 * z + 1) * width : (2 * z + 2) * width, :]
            kept[to, at] = jnp.where(high, high_part, low_part)
            sent[to, at] = jnp.where(high, low_part, high_part).astype(BF16)


def pair_kernel(n_col, n_stripes, n_after, place, *refs):
    w, refs = refs[:n_stripes], refs[n_stripes:]
    (density, val_density), refs = refs[:2], refs[2 + n_after :]
    kept, sent, acc = refs[:2], refs[2], refs[-1]
    at_once = 2 - n_stripes % 2
    for s in range(0, n_stripes, at_once):
        part = product(list(range(s, s + at_once)), w, density, val_density)
        if s == 0:
            acc[...] = part
        else:
            acc[...] += part
    hand_out(n_col, place[0] // n_col % 2, acc, kept, sent)


def last_kernel(n_col, n_after, place, density, t, *refs):
    kept, sent, acc = refs[n_after:]
    acc[...] = lax.dot_general(t[...], density[...], CONTRACT_MINOR, preferred_element_type=F32)
    hand_out(1, place[0] // n_col % 2, acc, [kept], sent)


def begin_kernel(n_col, start, width, n_stripes, numbers, n_after, *refs):
    w, refs = refs[:n_stripes], refs[n_stripes:]
    (density, hot1, hot2, val), refs = refs[:4], refs[4:]
    acc, val_density, *_ = refs[n_after:]
    build_val(groups(hot1, n_col, start, width), groups(hot2, n_col, start, width), val, val_density)
    acc[...] = product(numbers, w, density, val_density)


def end_kernel(n_col, n_stripes, numbers, n_after, place, *refs):
    w, refs = refs[:n_stripes], refs[n_stripes:]
    (density, before, val_density), refs = refs[:3], refs[3:]
    kept, sent, acc = *refs[n_after : n_after + 2], refs[-1]
    acc[...] = before[...] + product(numbers, w, density, val_density)
    hand_out(n_col, place[0] // n_col % 2, acc, [kept], sent)


def fold_kernel(n_col, targets, got_groups, sent_groups, place, *refs):
    n = len(targets)
    kept, got = refs[:n], refs[n : n + len(got_groups)]
    out = refs[n + len(got_groups) :]
    halves, sent = out[: len(out) - len(sent_groups)], out[len(out) - len(sent_groups) :]
    source, sink = {}, {}
    for array, group in zip(got, got_groups):
        at = 0
        for c in group:
            source.setdefault(c, []).append((array, at))
            at += kept[c].shape[0]
    for array, group in zip(sent, sent_groups):
        at = 0
        for c in group:
            sink[c] = array, at
            at += kept[c].shape[0] // (2 if targets[c] else 1)
    for c, target in enumerate(targets):
        rows, (other, to) = kept[c].shape[0], sink[c]

        def part(first, size, c=c):
            total = kept[c][first : first + size, :]
            for array, at in source[c]:
                total = total + array[at + first : at + first + size, :].astype(F32)
            return total

        if target is None:
            other[to : to + rows, :] = part(0, rows).astype(BF16)
            continue
        axis, bit, each = target
        me = place[0] // n_col if axis == "row" else place[0] % n_col
        high = (me >> bit) % 2 == 1
        half = rows // each // 2
        for z in range(each):
            a, b = 2 * z * half, (2 * z + 1) * half
            low_part, high_part = part(a, half), part(b, half)
            halves[c][z * half : (z + 1) * half, :] = jnp.where(high, high_part, low_part)
            other[to + z * half : to + (z + 1) * half, :] = jnp.where(high, low_part, high_part).astype(BF16)


def quarter_kernel(n_col, bits, place, kept, got, kept_out, *refs):
    *sent, part = refs
    part[...] = kept[...] + got[...].astype(F32)
    me = place[0] // n_col
    first, second = (me >> bits[0]) % 2, (me >> bits[1]) % 2
    size = kept_out.shape[0] // n_col
    for flip, out in enumerate([kept_out, *sent]):
        at = ((first + flip // 2) % 2 * 2 + (second + flip % 2) % 2) * size
        for z in range(n_col):
            rows = part[pl.ds(pl.multiple_of(z * 4 * size + at, size), size), :]
            out[z * size : (z + 1) * size, :] = rows.astype(out.dtype)


def hot_kernel(n_col, count, n_after, place, pairs, *refs):
    pick = refs[n_after]
    own = pick.shape[1]
    me = place[0] // n_col
    if own % 128:
        every = pairs[...]
        asked = functools.reduce(
            lambda a, i: jnp.where(me == i, every[:, i * own : (i + 1) * own], a), range(pairs.shape[1] // own), every[:, :own]
        )
    else:
        asked = pairs[:, pl.ds(pl.multiple_of(me * own, own), own)]
    c, other = asked[0:1], asked[1:2]
    apart = jnp.where(other >= c, other - c, other - c + count)
    row = jnp.where(apart <= count // 2, apart * count + c, (count - apart) * count + other)
    pick[...] = one_hot_columns(row, pick.shape[0]).astype(BF16)


def pick_kernel(n_col, scale, gathers, place, pick, *refs):
    arrays, (out, whole) = refs[: len(gathers)], refs[len(gathers) :]
    me = place[0] // n_col
    for array, (steps, chunks) in zip(arrays, gathers):
        each = sum(rows for _, rows, _ in chunks)
        for j in range(array.shape[0] // each):
            block = sum((((me ^ j) >> bit) % 2) << s for s, bit in enumerate(steps))
            used = 0
            for start, rows, order in chunks:
                spot = sum(((j >> bit) & 1) << (len(order) - 1 - s) for s, bit in enumerate(order))
                to = start + spot * rows
                whole[to : to + rows, :] = array[pl.ds(block * each + used, rows), :]
                used += rows
    out[...] = (jnp.dot(whole[...].astype(BF16), pick[...], preferred_element_type=F32) * scale).T


def swap(x, axis, bits, size):
    return lax.ppermute(x, axis, [(i, i ^ bits) for i in range(size)])


def solution(mesh):
    n_row, n_col = mesh.shape["row"], mesh.shape["col"]
    row_bits, col_bits = n_row.bit_length() - 1, n_col.bit_length() - 1

    def per_device(screened, val_orbitals, con_orbitals, val_pairs, con_pairs):
        own_rows, own_columns = screened.shape
        count, grid = con_orbitals.shape
        n_val = val_orbitals.shape[0]
        blocks = count // 2 + 1
        while blocks * count % 128:
            blocks += 1
        unordered = blocks * count
        n_pairs = val_pairs.shape[0]
        per_col = n_pairs // n_col
        chunks = CHUNKS if n_pairs >= 8 * CHUNKS * n_row * n_col and row_bits > 2 else 1
        width = per_col // chunks
        starts = [k * width for k in range(chunks)]
        place = (lax.axis_index("row") * n_col + lax.axis_index("col")).astype(jnp.int32)[None]
        smem = pl.BlockSpec(memory_space=pltpu.SMEM)
        vmem = pl.BlockSpec(memory_space=pltpu.VMEM)
        anywhere = pl.BlockSpec(memory_space=pl.ANY)
        hbm = pl.BlockSpec(memory_space=pltpu.HBM)

        def params(mib):
            return pltpu.CompilerParams(vmem_limit_bytes=mib << 20)

        def cost(n, rows):
            return pl.CostEstimate(
                flops=2 * n * rows * (own_columns + unordered), bytes_accessed=1 << 20, transcendentals=0
            )

        def outs(rows):
            return [pltpu.VMEM((rows, unordered), F32), pltpu.VMEM((rows, unordered), BF16)]

        stripe = min(512, own_rows)
        n_stripes = own_rows // stripe
        held = [pltpu.VMEM((stripe, own_columns), BF16)] * n_stripes + [pltpu.VMEM((unordered, own_rows), BF16)]
        hots = [pltpu.VMEM((n_pairs, n_val), BF16)] * 2
        n_held = n_stripes + 1
        arguments = (place, *[pltpu.with_memory_space_constraint(x, pltpu.HBM) for x in (val_pairs.T, val_orbitals, con_orbitals, screened)])
        inputs = [
            pltpu.VMEM((2, n_pairs), jnp.int32),
            pltpu.VMEM((n_val, own_columns), BF16),
            pltpu.VMEM((count, own_rows), BF16),
            pltpu.VMEM((2 * count, min(512, own_rows)), F32),
            pltpu.SemaphoreType.DMA((n_stripes,)),
            pltpu.SemaphoreType.DMA((3,)),
        ]
        n = n_col * width

        def single():
            return pl.pallas_call(
                functools.partial(single_kernel, n_col, n_stripes),
                in_specs=[smem] + [hbm] * 4,
                out_specs=[vmem] * 2,
                out_shape=outs(n // 2),
                scratch_shapes=[pltpu.VMEM((n, own_columns), BF16), pltpu.VMEM((n, unordered), F32), held[-1], *hots, *inputs, *held[:-1]],
                compiler_params=params(40),
                name="single",
            )(*arguments)

        def load():
            kept, sent, val_density, *fixed = pl.pallas_call(
                functools.partial(load_kernel, n_col, starts[3], width, n_stripes),
                in_specs=[smem] + [hbm] * 4,
                out_specs=[vmem] * (3 + n_held + 2),
                out_shape=[
                    pltpu.VMEM((n // 2, own_rows), F32),
                    pltpu.VMEM((n // 2, own_rows), BF16),
                    pltpu.VMEM((2 * n, own_columns), BF16),
                    *held,
                    *hots,
                ],
                scratch_shapes=[pltpu.VMEM((n, own_columns), BF16), *inputs],
                compiler_params=params(10),
                cost_estimate=cost(n, own_rows),
                name="load",
            )(*arguments)
            return kept, sent, val_density, fixed

        def pair(fixed, val_density, after):
            *out, sent = pl.pallas_call(
                functools.partial(pair_kernel, n_col, n_stripes, len(after)),
                in_specs=[smem] + [vmem] * (n_held + 1) + [anywhere] * len(after),
                out_specs=[vmem] * (3 + n_held),
                out_shape=[outs(n // 2)[0]] * 2 + [outs(n)[1]] + held,
                scratch_shapes=[pltpu.VMEM((2 * n, unordered), F32)],
                input_output_aliases={1 + i: 3 + i for i in range(n_held)},
                compiler_params=params(12),
                cost_estimate=cost(2 * n, own_rows),
                name="pair",
            )(place, *fixed[:n_held], val_density, *after), None
            out = out[0]
            return list(out[:2]), out[2], list(out[3:]) + fixed[n_held:]

        def last(density, t, after):
            rows = t.shape[0]
            return pl.pallas_call(
                functools.partial(last_kernel, n_col, len(after)),
                in_specs=[smem] + [vmem] * 2 + [anywhere] * len(after),
                out_specs=[vmem] * 2,
                out_shape=outs(rows // 2),
                scratch_shapes=[pltpu.VMEM((rows, unordered), F32)],
                compiler_params=params(8),
                cost_estimate=cost(rows, own_rows),
                name="last",
            )(place, density, t, *after)

        def begin(k, numbers, fixed, after):
            n = n_col * width
            acc, val_density, *fixed = pl.pallas_call(
                functools.partial(begin_kernel, n_col, starts[k], width, n_stripes, numbers, len(after)),
                in_specs=[vmem] * (n_held + 3) + [anywhere] * len(after),
                out_specs=[vmem] * (2 + n_held),
                out_shape=[pltpu.VMEM((n, unordered), F32), pltpu.VMEM((n, own_columns), BF16)] + held,
                input_output_aliases={i: 2 + i for i in range(n_held)},
                compiler_params=params(7),
                cost_estimate=cost(n, len(numbers) * stripe),
            )(*fixed, val_orbitals, *after)
            return (acc, val_density), fixed

        def end(numbers, fixed, before, after):
            n = n_col * width
            kept, sent, *same = pl.pallas_call(
                functools.partial(end_kernel, n_col, n_stripes, numbers, len(after)),
                in_specs=[smem] + [vmem] * (n_held + 2) + [anywhere] * len(after),
                out_specs=[vmem] * 3,
                out_shape=outs(n // 2) + held[-1:],
                scratch_shapes=[pltpu.VMEM((n, unordered), F32)],
                input_output_aliases={n_held: 2},
                compiler_params=params(7),
                cost_estimate=cost(n, len(numbers) * stripe),
            )(place, *fixed[:n_held], *before, *after)
            return (kept, sent), same[0]

        def fold(kept, got, targets, got_groups=None, sent_groups=None):
            everything = [list(range(len(kept)))]
            got_groups, sent_groups = got_groups or everything, sent_groups or everything
            rows = [k.shape[0] // (2 if t else 1) for k, t in zip(kept, targets)]
            minor = kept[0].shape[1]
            shapes = [pltpu.VMEM((r, minor), F32) for r, t in zip(rows, targets) if t]
            n_kept = len(shapes)
            shapes += [pltpu.VMEM((sum(rows[c] for c in g), minor), BF16) for g in sent_groups]
            out = pl.pallas_call(
                functools.partial(fold_kernel, n_col, targets, got_groups, sent_groups),
                in_specs=[smem] + [vmem] * (len(kept) + len(got)),
                out_specs=[vmem] * len(shapes),
                out_shape=shapes,
                compiler_params=params(4),
            )(place, *kept, *got)
            return list(out[:n_kept]), list(out[n_kept:])

        def quarters(kept, got, bits):
            rows = kept.shape[0] // 4
            kept, *sent = pl.pallas_call(
                functools.partial(quarter_kernel, n_col, bits),
                in_specs=[smem] + [vmem] * 2,
                out_specs=[vmem] * 4,
                out_shape=[pltpu.VMEM((rows, unordered), F32)] + [pltpu.VMEM((rows, unordered), BF16)] * 3,
                scratch_shapes=[pltpu.VMEM(kept.shape, F32)],
                compiler_params=params(4),
            )(place, kept, got)
            return kept, sent

        order = list(range(1, row_bits))
        orders = [[0] + (order if k % 2 == 0 else order[::-1]) for k in range(chunks)]
        col_steps = [("col", bit, n_col >> (bit + 1)) for bit in range(col_bits)]
        steps = [
            [("row", bit, n_col) for bit in orders[k]] + col_steps + [None] if k < 3
            else col_steps + [None] + [("row", bit, 1) for bit in orders[k]] + [None]
            for k in range(chunks)
        ]
        n_steps = row_bits + col_bits
        sizes = {"row": n_row, "col": n_col}

        def send(k, at, sent):
            axis, bit, _ = steps[k][at]
            return swap(sent, axis, 1 << bit, sizes[axis])

        def run(k, at, until, kept, sent):
            for s in range(at, until):
                got = send(k, s, sent)
                kept, (sent,) = fold(kept, [got], [steps[k][s + 1]] * len(kept))
            return kept, sent

        def gather(part, bits):
            for bit in bits:
                part = jnp.concatenate([part, swap(part, "row", 1 << bit, n_row)])
            return part.astype(F32)

        if chunks > 1:
            low, high = list(range(n_stripes // 2)), list(range(n_stripes // 2, n_stripes))
            apart = [[0], [1]]
            kept, b_sent, val_density, fixed = load()
            b = [kept], b_sent
            kept, sent, fixed = pair(fixed, val_density, [b_sent])
            b = run(3, 0, 1, *b)
            got = [send(0, 0, sent)]
            kept, sents = fold(kept, got, [steps[0][1], steps[1][1]], None, apart)
            before, fixed = begin(2, low, fixed, [b[1], *sents])
            m, density = end(high, fixed, before, [])
            m_kept, m_sent = quarters(m[0], send(2, 0, m[1]), orders[2][1:3])
            for s in range(1, row_bits):
                got = [send(k, s, sents[k]) for k in range(2)]
                ends = apart if s < row_bits - 1 else None
                kept, sents = fold(kept, got, [steps[0][s + 1], steps[1][s + 1]], apart, ends)
                if s == 1:
                    hold = sents
            b = run(3, 1, col_bits, *b)
            b_kept, b_sent = last(density, b[1], hold + m_sent)
            b = [b_kept], b_sent
            when = [b_sent]
            axis_steps = len(steps[3]) - 1
            for s in range(col_bits + 1, axis_steps):
                axis, bit, _ = steps[3][s]
                got = swap(b[1], axis, 1 << bit, sizes[axis])
                kept_b, (sent_b,) = fold(b[0], [got], [steps[3][s + 1]])
                b = kept_b, sent_b
            _, a_sums = run(0, row_bits, n_steps, kept, sents[0])
            flips = [1 << orders[2][2], 1 << orders[2][1], 1 << orders[2][1] | 1 << orders[2][2]]
            got = [swap(x, "row", flip, n_row) for x, flip in zip(m_sent, flips)]
            m_kept, m_sent = fold([m_kept], got, [steps[2][3]], [[0]] * 3)
            _, m_sums = run(2, 3, n_steps, m_kept, m_sent[0])
            up, down = order + [0], order[::-1] + [0]
            arrays = [gather(a_sums, down), gather(b[1], up), gather(m_sums, up)]
            gathers = [(down, [0, 1]), (up, [3]), (up, [2])]
        else:
            kept, sent = single()
            when = []
            _, late = run(0, 0, n_steps, [kept], sent)
            late_bits = order[::-1] + [0]
            arrays, gathers = [gather(late, late_bits)], [(late_bits, [0])]
        gathers = [(bits, [(starts[k], width // n_row, orders[k]) for k in ks]) for bits, ks in gathers]

        own = con_pairs.shape[0] // n_row
        pick = pl.pallas_call(
            functools.partial(hot_kernel, n_col, count, len(when)),
            in_specs=[smem, vmem] + [anywhere] * len(when),
            out_specs=vmem,
            out_shape=pltpu.VMEM((unordered, own), BF16),
            compiler_params=params(8),
            name="hot",
        )(place, con_pairs.T, *when)
        return pl.pallas_call(
            functools.partial(pick_kernel, n_col, float(grid ** (-0.5)), gathers),
            in_specs=[smem] + [vmem] * (1 + len(arrays)),
            out_specs=vmem,
            out_shape=jax.ShapeDtypeStruct((own, per_col), F32),
            scratch_shapes=[pltpu.VMEM((per_col, unordered), F32)],
            compiler_params=params(20),
            name="pick",
        )(place, pick, *arrays)

    in_specs = (P("row", "col"), P(None, "col"), P(), P(), P())

    return jax.shard_map(per_device, mesh=mesh, in_specs=in_specs, out_specs=P("row", "col"), check_vma=False)
```

time: 105 us -> 111 us (1.057)
  starting transfers between devices: 28.7 us -> 32.6 us
  waiting for transfers between devices: 31.1 us -> 33.1 us
    pallas_call x2 -> x6, Pallas kernels: 24.4 us -> 34.9 us  [the longest x1 15.7 us: pair(): pl.pallas_call(functools.partial(pair_kernel, n_col, n_stripes, len(after...]
    pallas_call x2 -> x1, Pallas kernels: 10.6 us -> 5.1 us  [begin(): pl.pallas_call(functools.partial(begin_kernel, n_col, starts[k], width, n...]
    pallas_call x2 -> x1, Pallas kernels: 8.04 us -> 4.02 us  [end(): pl.pallas_call(functools.partial(end_kernel, n_col, n_stripes, numbers, l...]
    ppermute x23 -> x27, starting transfers between devices: 28.7 us -> 32.6 us  [swap(): return lax.ppermute(x, axis, [(i, i ^ bits) for i in range(size)])]
    ppermute x23 -> x27, waiting for transfers between devices: 31.1 us -> 33.1 us  [swap(): return lax.ppermute(x, axis, [(i, i ^ bits) for i in range(size)])]
  transfers between devices with their start and end apart: 23 -> 27, of which waited for: 14 -> 14; matrix products, arithmetic and copies ran while one was open for 0% -> 0% of each run, Pallas kernels for 11% -> 12%
where the time goes in v4:
time: 111 us
  Pallas kernels  44.9 us (40%)
  waiting for transfers between devices  33.1 us (30%)
  starting transfers between devices  32.6 us (29%)
    ppermute x27, waiting for transfers between devices, swap(): return lax.ppermute(x, axis, [(i, i ^ bits) for i in range(size)])  33.1 us
    ppermute x27, starting transfers between devices, swap(): return lax.ppermute(x, axis, [(i, i ^ bits) for i in range(size)])  32.6 us
    pallas_call x1, Pallas kernels, pair(): pl.pallas_call(functools.partial(pair_kernel, n_col, n_stripes, len(after...  15.7 us
    pallas_call x1, Pallas kernels, load(): pl.pallas_call(functools.partial(load_kernel, n_col, starts[3], width, n_...  13.9 us
    pallas_call x1, Pallas kernels, begin(): pl.pallas_call(functools.partial(begin_kernel, n_col, starts[k], width, n...  5.1 us
    pallas_call x1, Pallas kernels, end(): pl.pallas_call(functools.partial(end_kernel, n_col, n_stripes, numbers, l...  4.02 us
    pallas_call x1, Pallas kernels, last(): pl.pallas_call(functools.partial(last_kernel, n_col, len(after)), in_spec...  2.86 us
  transfers between devices with their start and end apart: 27, of which 14 were waited for; matrix products, arithmetic and copies ran while one was open for 0% of the time, Pallas kernels for 12%

profile of v4, /device:TPU:0, one launch (start us, length us, event | category | flops | bytes accessed | tf_op | source)
XLA Modules:
  0.0 111.1 jit_solution(5116180727727821272)
XLA Ops:
  0.0 13.9 %load.1 = (f32[128,2048]{1,0:T(8,128)S(1)}, bf16[128,2048]{1,0:T(8,128)(2,1)S(1)}, bf16[512,4096]{1,0:T(8,128)(2,1)S(1)}, bf16[512,4096]{1,0:T(8,128)(2,1)S(1)},...) custom-call(s32[1]{0:T(128)} %bitcast.place, ...), custom_call_target="tpu_custom_call" | custom-call | flops 6576668672 | bytes 1048576 | tf_op jit(solution)/shard_map/load/pallas_call | solution.py:324
  13.9 15.7 %pair.1 = (f32[128,2176]{1,0:T(8,128)S(1)}, f32[128,2176]{1,0:T(8,128)S(1)}, bf16[256,2176]{1,0:T(8,128)(2,1)S(1)}, bf16[512,4096]{1,0:T(8,128)(2,1)S(1)}, bf16[...) custom-call(s32[1]{0:T(128)} %bitcast.place, ...), custom_call_target="tpu_custom_call", output_to_operand_aliasing={{3}: (1, {}), {4}: (2, {}), {5}: (3, {}), {6}: (4, {}), {7}... | custom-call | flops 13153337344 | bytes 1048576 | tf_op jit(solution)/shard_map/pair/pallas_call | solution.py:343
  29.6 0.0 copy-start
  29.6 0.5 collective-permute-start.1
  30.2 2.6 %collective-permute-start = (bf16[128,2048]{1,0:T(8,128)(2,1)S(1)}, bf16[128,2048]{1,0:T(8,128)(2,1)S(1)}, u32[]{:S(2)}, u32[]{:S(2)}) collective-permute-start(bf16[128,2048]{1,0:T(8,128)(2,1)S(1)} %get-tuple-element.69.refs_6_), channel_id=1, source_target_pairs={{0,1},{1,0},{2,3},{3,2},{4,5},{5,4},{6,7},{7,6},{8,9},{9,8},{10,11... | collective-permute-start | bytes 1572872 | tf_op jit(solution)/shard_map/ppermute | solution.py:259
  32.8 12.5 %collective-permute-done.refs_1_ = bf16[128,2048]{1,0:T(8,128)(2,1)S(1)} collective-permute-done((bf16[128,2048]{1,0:T(8,128)(2,1)S(1)}, bf16[128,2048]{1,0:T(8,128)(2,1)S(1)}, u32[]{:S(2)}, u32[]{:S(2)}) %collective-permute-start) | collective-permute-done | bytes 524320 | tf_op jit(solution)/shard_map/ppermute | solution.py:259
  45.3 0.1 shard_map.55
  45.5 0.0 collective-permute-done.1.refs_2_
  45.5 0.3 shard_map.56
  45.8 1.7 %collective-permute-start.3 = (bf16[64,2176]{1,0:T(8,128)(2,1)S(1)}, bf16[64,2176]{1,0:T(8,128)(2,1)S(1)}, u32[]{:S(2)}, u32[]{:S(2)}) collective-permute-start(bf16[64,2176]{1,0:T(8,128)(2,1)S(1)} %get-tuple-element.82.refs_9_), channel_id=1, source_target_pairs={{0,8},{4,12},{8,0},{12,4},{16,24},{20,28},{24,16},{28,20},{1,9},{5... | collective-permute-start | bytes 835592 | tf_op jit(solution)/shard_map/ppermute | solution.py:259
  47.5 1.5 %collective-permute-start.4 = (bf16[64,2176]{1,0:T(8,128)(2,1)S(1)}, bf16[64,2176]{1,0:T(8,128)(2,1)S(1)}, u32[]{:S(2)}, u32[]{:S(2)}) collective-permute-start(bf16[64,2176]{1,0:T(8,128)(2,1)S(1)} %get-tuple-element.83.refs_10_), channel_id=1, source_target_pairs={{0,16},{4,20},{8,24},{12,28},{16,0},{20,4},{24,8},{28,12},{1,17},{... | collective-permute-start | bytes 835592 | tf_op jit(solution)/shard_map/ppermute | solution.py:259
  49.0 5.1 %shard_map.57 = (f32[256,2176]{1,0:T(8,128)S(1)}, bf16[256,4096]{1,0:T(8,128)(2,1)S(1)}, bf16[512,4096]{1,0:T(8,128)(2,1)S(1)}, bf16[512,4096]{1,0:T(8,128)(2,1)...) custom-call(bf16[512,4096]{1,0:T(8,128)(2,1)S(1)} %get-tuple-element, ...), custom_call_target="tpu_custom_call", output_to_operand_aliasing={{2}: (0, {}), {3}: (1, {}), {4}: (2, {}), {5}: (3, {}), {6}... | custom-call | flops 3288334336 | bytes 1048576 | tf_op jit(solution)/shard_map/pallas_call | solution.py:372
  54.1 4.0 %shard_map.58 = (f32[128,2176]{1,0:T(8,128)S(1)}, bf16[128,2176]{1,0:T(8,128)(2,1)S(1)}, bf16[2176,2048]{1,0:T(8,128)(2,1)S(1)}) custom-call(s32[1]{0:T(128)} %bitcast.place, bf16[512,4096]{1,0:T(8,128)(2,1)S(1)} %get-tuple-element.84.refs_0_, bf16[512,4096]{1,0:T(8,128)(2,1)S(1)} %get-tuple-element.85.refs_1_, ...), custom_call_target="tpu_custom_call", output_to_operand_aliasing={{2}: (5, {})} | custom-call | flops 3288334336 | bytes 1048576 | tf_op jit(solution)/shard_map/pallas_call | solution.py:385
  58.2 0.1 collective-permute-start.5
  58.2 0.0 collective-permute-done.3.refs_2_
  58.3 0.1 shard_map.60
  58.4 0.6 collective-permute-start.6
  59.0 0.4 collective-permute-start.7
  59.3 2.8 %collective-permute-start.2 = (bf16[64,2048]{1,0:T(8,128)(2,1)S(1)}, bf16[64,2048]{1,0:T(8,128)(2,1)S(1)}, u32[]{:S(2)}, u32[]{:S(2)}) collective-permute-start(bf16[64,2048]{1,0:T(8,128)(2,1)S(1)} %get-tuple-element.78.refs_8_), channel_id=1, source_target_pairs={{0,2},{1,3},{2,0},{3,1},{4,6},{5,7},{6,4},{7,5},{8,10},{9,11},{10,... | collective-permute-start | bytes 786440 | tf_op jit(solution)/shard_map/ppermute | solution.py:259
  62.1 2.4 %collective-permute-done.6.refs_2_ = bf16[32,2176]{1,0:T(8,128)(2,1)S(1)} collective-permute-done((bf16[32,2176]{1,0:T(8,128)(2,1)S(1)}, bf16[32,2176]{1,0:T(8,128)(2,1)S(1)}, u32[]{:S(2)}, u32[]{:S(2)}) %collective-permute-start.6) | collective-permute-done | bytes 139296 | tf_op jit(solution)/shard_map/ppermute | solution.py:259
  64.5 0.2 collective-permute-done.7.refs_3_
  64.8 0.1 shard_map.62
  64.8 1.6 %collective-permute-start.8 = (bf16[32,2176]{1,0:T(8,128)(2,1)S(1)}, bf16[32,2176]{1,0:T(8,128)(2,1)S(1)}, u32[]{:S(2)}, u32[]{:S(2)}) collective-permute-start(bf16[32,2176]{1,0:T(8,128)(2,1)S(1)} %get-tuple-element.107), channel_id=1, source_target_pairs={{0,1},{1,0},{2,3},{3,2},{4,5},{5,4},{6,7},{7,6},{8,9},{9,8},{10,11... | collective-permute-start | bytes 417800 | tf_op jit(solution)/shard_map/ppermute | solution.py:259
  66.5 8.7 %collective-permute-done.8.refs_2_ = bf16[32,2176]{1,0:T(8,128)(2,1)S(1)} collective-permute-done((bf16[32,2176]{1,0:T(8,128)(2,1)S(1)}, bf16[32,2176]{1,0:T(8,128)(2,1)S(1)}, u32[]{:S(2)}, u32[]{:S(2)}) %collective-permute-start.8) | collective-permute-done | bytes 139296 | tf_op jit(solution)/shard_map/ppermute | solution.py:259
  75.2 2.0 %collective-permute-start.9 = (bf16[16,2176]{1,0:T(8,128)(2,1)S(1)}, bf16[16,2176]{1,0:T(8,128)(2,1)S(1)}, u32[]{:S(2)}, u32[]{:S(2)}) collective-permute-start(bf16[16,2176]{1,0:T(8,128)(2,1)S(1)} %get-tuple-element.110), channel_id=1, source_target_pairs={{0,2},{1,3},{2,0},{3,1},{4,6},{5,7},{6,4},{7,5},{8,10},{9,11},{10,... | collective-permute-start | bytes 208904 | tf_op jit(solution)/shard_map/ppermute | solution.py:259
  77.3 0.0 collective-permute-done.5.got
  77.3 0.2 shard_map.61
  77.5 1.5 %collective-permute-start.19 = (bf16[32,2176]{1,0:T(8,128)(2,1)S(1)}, bf16[32,2176]{1,0:T(8,128)(2,1)S(1)}, u32[]{:S(2)}, u32[]{:S(2)}) collective-permute-start(bf16[32,2176]{1,0:T(8,128)(2,1)S(1)} %get-tuple-element.99.refs_2_), channel_id=1, source_target_pairs={{0,16},{4,20},{8,24},{12,28},{16,0},{20,4},{24,8},{28,12},{1,17},{... | collective-permute-start | bytes 417800 | tf_op jit(solution)/shard_map/ppermute | solution.py:259
  79.0 0.0 collective-permute-start.20
  79.0 2.0 %collective-permute-start.21 = (bf16[32,2176]{1,0:T(8,128)(2,1)S(1)}, bf16[32,2176]{1,0:T(8,128)(2,1)S(1)}, u32[]{:S(2)}, u32[]{:S(2)}) collective-permute-start(bf16[32,2176]{1,0:T(8,128)(2,1)S(1)} %get-tuple-element.101.refs_4_), channel_id=1, source_target_pairs={{0,24},{4,28},{8,16},{12,20},{16,8},{20,12},{24,0},{28,4},{1,25},{... | collective-permute-start | bytes 417800 | tf_op jit(solution)/shard_map/ppermute | solution.py:259
  81.0 0.0 collective-permute-done.9.refs_2_
  81.1 1.5 %collective-permute-start.10 = (bf16[16,2176]{1,0:T(8,128)(2,1)S(1)}, bf16[16,2176]{1,0:T(8,128)(2,1)S(1)}, u32[]{:S(2)}, u32[]{:S(2)}) collective-permute-start(bf16[16,2176]{1,0:T(8,128)(2,1)S(1)} %shard_map.64), channel_id=1, source_target_pairs={{0,16},{4,20},{8,24},{12,28},{16,0},{20,4},{24,8},{28,12},{1,17},{... | collective-permute-start | bytes 208904 | tf_op jit(solution)/shard_map/ppermute | solution.py:259
  82.6 2.9 %last.1 = (f32[32,2176]{1,0:T(8,128)S(1)}, bf16[32,2176]{1,0:T(8,128)(2,1)S(1)}) custom-call(s32[1]{0:T(128)} %bitcast.place, bf16[2176,2048]{1,0:T(8,128)(2,1)S(1)} %get-tuple-element.91.density, bf16[64,2048]{1,0:T(8,128)(2,1)S(1)} %shard_map.59.t, bf16[32,2176]{1,0:T(8,128)(2,1)S(1)} %get-tuple-element.95.refs_0_, ...), custom_call_target="tpu_custom_call" | custom-call | flops 1644167168 | bytes 1048576 | tf_op jit(solution)/shard_map/last/pallas_call | solution.py:359
  85.5 0.1 collective-permute-start.13
  85.5 0.8 collective-permute-done.10
  86.3 0.1 collective-permute-start.11
  86.4 0.5 collective-permute-done.13.refs_1_
  86.9 1.6 %collective-permute-start.14 = (bf16[16,2176]{1,0:T(8,128)(2,1)S(1)}, bf16[16,2176]{1,0:T(8,128)(2,1)S(1)}, u32[]{:S(2)}, u32[]{:S(2)}) collective-permute-start(bf16[16,2176]{1,0:T(8,128)(2,1)S(1)} %get-tuple-element.113), channel_id=1, source_target_pairs={{0,16},{4,20},{8,24},{12,28},{16,0},{20,4},{24,8},{28,12},{1,17},{... | collective-permute-start | bytes 208904 | tf_op jit(solution)/shard_map/ppermute | solution.py:259
  88.5 0.0 collective-permute-done.19.refs_1_
  88.5 0.0 collective-permute-done.20.refs_2_
  88.5 0.1 shard_map.68
  88.6 2.6 %collective-permute-start.22 = (bf16[16,2176]{1,0:T(8,128)(2,1)S(1)}, bf16[16,2176]{1,0:T(8,128)(2,1)S(1)}, u32[]{:S(2)}, u32[]{:S(2)}) collective-permute-start(bf16[16,2176]{1,0:T(8,128)(2,1)S(1)} %get-tuple-element.118), channel_id=1, source_target_pairs={{0,1},{1,0},{2,3},{3,2},{4,5},{5,4},{6,7},{7,6},{8,9},{9,8},{10,11... | collective-permute-start | bytes 208904 | tf_op jit(solution)/shard_map/ppermute | solution.py:259
  91.2 0.1 collective-permute-done.14.refs_1_
  91.3 1.8 %collective-permute-start.15 = (bf16[8,2176]{1,0:T(8,128)(2,1)S(1)}, bf16[8,2176]{1,0:T(8,128)(2,1)S(1)}, u32[]{:S(2)}, u32[]{:S(2)}) collective-permute-start(bf16[8,2176]{1,0:T(8,128)(2,1)S(1)} %get-tuple-element.115), channel_id=1, source_target_pairs={{0,8},{4,12},{8,0},{12,4},{16,24},{20,28},{24,16},{28,20},{1,9},{5... | collective-permute-start | bytes 104456 | tf_op jit(solution)/shard_map/ppermute | solution.py:259
  93.1 0.3 collective-permute-done.22.refs_1_
  93.5 1.8 %collective-permute-start.23 = (bf16[8,2176]{1,0:T(8,128)(2,1)S(1)}, bf16[8,2176]{1,0:T(8,128)(2,1)S(1)}, u32[]{:S(2)}, u32[]{:S(2)}) collective-permute-start(bf16[8,2176]{1,0:T(8,128)(2,1)S(1)} %get-tuple-element.120), channel_id=1, source_target_pairs={{0,2},{1,3},{2,0},{3,1},{4,6},{5,7},{6,4},{7,5},{8,10},{9,11},{10,... | collective-permute-start | bytes 104456 | tf_op jit(solution)/shard_map/ppermute | solution.py:259
  95.3 0.4 hot.1.pick
  95.7 0.0 collective-permute-done.15.refs_1_
  95.7 1.5 %collective-permute-start.16 = (bf16[8,2176]{1,0:T(8,128)(2,1)S(1)}, bf16[8,2176]{1,0:T(8,128)(2,1)S(1)}, u32[]{:S(2)}, u32[]{:S(2)}) collective-permute-start(bf16[8,2176]{1,0:T(8,128)(2,1)S(1)} %shard_map.67), channel_id=1, source_target_pairs={{0,8},{4,12},{8,0},{12,4},{16,24},{20,28},{24,16},{28,20},{1,9},{5... | collective-permute-start | bytes 104456 | tf_op jit(solution)/shard_map/ppermute | solution.py:259
  97.3 1.1 %collective-permute-done.23.refs_1_ = bf16[8,2176]{1,0:T(8,128)(2,1)S(1)} collective-permute-done((bf16[8,2176]{1,0:T(8,128)(2,1)S(1)}, bf16[8,2176]{1,0:T(8,128)(2,1)S(1)}, u32[]{:S(2)}, u32[]{:S(2)}) %collective-permute-start.23) | collective-permute-done | bytes 34848 | tf_op jit(solution)/shard_map/ppermute | solution.py:259
  98.4 1.9 %collective-permute-start.24 = (bf16[8,2176]{1,0:T(8,128)(2,1)S(1)}, bf16[8,2176]{1,0:T(8,128)(2,1)S(1)}, u32[]{:S(2)}, u32[]{:S(2)}) collective-permute-start(bf16[8,2176]{1,0:T(8,128)(2,1)S(1)} %shard_map.70), channel_id=1, source_target_pairs={{0,8},{4,12},{8,0},{12,4},{16,24},{20,28},{24,16},{28,20},{1,9},{5... | collective-permute-start | bytes 104456 | tf_op jit(solution)/shard_map/ppermute | solution.py:259
  100.3 0.0 collective-permute-done.11
  100.4 0.1 collective-permute-start.12
  100.5 2.0 %collective-permute-done.24 = bf16[8,2176]{1,0:T(8,128)(2,1)S(1)} collective-permute-done((bf16[8,2176]{1,0:T(8,128)(2,1)S(1)}, bf16[8,2176]{1,0:T(8,128)(2,1)S(1)}, u32[]{:S(2)}, u32[]{:S(2)}) %collective-permute-start.24) | collective-permute-done | bytes 34848 | tf_op jit(solution)/shard_map/ppermute | solution.py:259
  102.4 0.9 collective-permute-start.25
  103.4 1.2 %collective-permute-start.17 = (bf16[16,2176]{1,0:T(8,128)(2,1)S(1)}, bf16[16,2176]{1,0:T(8,128)(2,1)S(1)}, u32[]{:S(2)}, u32[]{:S(2)}) collective-permute-start(bf16[16,2176]{1,0:T(8,128)(2,1)S(1)} %pad_maximum_fusion.4), channel_id=1, source_target_pairs={{0,16},{4,20},{8,24},{12,28},{16,0},{20,4},{24,8},{28,12},{1,17},{... | collective-permute-start | bytes 208904 | tf_op jit(solution)/shard_map/ppermute | solution.py:259
  104.5 2.2 %collective-permute-done.25 = bf16[16,2176]{1,0:T(8,128)(2,1)S(1)} collective-permute-done((bf16[16,2176]{1,0:T(8,128)(2,1)S(1)}, bf16[16,2176]{1,0:T(8,128)(2,1)S(1)}, u32[]{:S(2)}, u32[]{:S(2)}) %collective-permute-start.25) | collective-permute-done | bytes 69664 | tf_op jit(solution)/shard_map/ppermute | solution.py:259
  106.7 0.1 collective-permute-start.26
  106.8 0.9 collective-permute-done.17
  107.7 0.1 collective-permute-start.18
  107.8 0.3 collective-permute-done.26
  108.2 1.0 collective-permute-done.18
  109.2 0.1 maximum_convert_fusion.refs_0_
  109.3 1.8 %pick.1 = f32[512,256]{1,0:T(8,128)} custom-call(s32[1]{0:T(128)} %bitcast.place, bf16[2176,512]{1,0:T(8,128)(2,1)S(1)} %hot.1.pick, f32[128,2176]{1,0:T(8,128)S(1)} %maximum_convert_fusion.refs_0_, f32[64,2176]{1,0:T(8,128)S(1)} %maximum_convert_fusion.1.refs_1_, f32[64,2176]{1,0:T(8,128)S(1)} %maximum_convert_fusion.2.refs_2_), custom_call_target="tpu_custom_call" | custom-call | tf_op jit(solution)/shard_map/pick/pallas_call | solution.py:505
  (24 shorter events, 0.4 us)
Async XLA Ops:
  29.6 19.4 %copy-start = (bf16[45,4096]{1,0:T(8,128)(2,1)S(1)}, bf16[45,4096]{1,0:T(8,128)(2,1)}, u32[]{:S(2)}) copy-start(bf16[45,4096]{1,0:T(8,128)(2,1)} %refs_7_.1) | copy-start | bytes 1105924
  29.6 15.9 %collective-permute-start.1 = (bf16[256,2176]{1,0:T(8,128)(2,1)S(1)}, bf16[256,2176]{1,0:T(8,128)(2,1)S(1)}, u32[]{:S(2)}, u32[]{:S(2)}) collective-permute-start(bf16[256,2176]{1,0:T(8,128)(2,1)S(1)} %get-tuple-element.81), channel_id=1, source_target_pairs={{0,4},{4,0},{8,12},{12,8},{16,20},{20,16},{24,28},{28,24},{1,5},{5... | collective-permute-start | bytes 3342344 | tf_op jit(solution)/shard_map/ppermute | solution.py:259
  30.2 15.2 %collective-permute-start = (bf16[128,2048]{1,0:T(8,128)(2,1)S(1)}, bf16[128,2048]{1,0:T(8,128)(2,1)S(1)}, u32[]{:S(2)}, u32[]{:S(2)}) collective-permute-start(bf16[128,2048]{1,0:T(8,128)(2,1)S(1)} %get-tuple-element.69.refs_6_), channel_id=1, source_target_pairs={{0,1},{1,0},{2,3},{3,2},{4,5},{5,4},{6,7},{7,6},{8,9},{9,8},{10,11... | collective-permute-start | bytes 1572872 | tf_op jit(solution)/shard_map/ppermute | solution.py:259
  45.8 12.5 %collective-permute-start.3 = (bf16[64,2176]{1,0:T(8,128)(2,1)S(1)}, bf16[64,2176]{1,0:T(8,128)(2,1)S(1)}, u32[]{:S(2)}, u32[]{:S(2)}) collective-permute-start(bf16[64,2176]{1,0:T(8,128)(2,1)S(1)} %get-tuple-element.82.refs_9_), channel_id=1, source_target_pairs={{0,8},{4,12},{8,0},{12,4},{16,24},{20,28},{24,16},{28,20},{1,9},{5... | collective-permute-start | bytes 835592 | tf_op jit(solution)/shard_map/ppermute | solution.py:259
  47.5 10.7 %collective-permute-start.4 = (bf16[64,2176]{1,0:T(8,128)(2,1)S(1)}, bf16[64,2176]{1,0:T(8,128)(2,1)S(1)}, u32[]{:S(2)}, u32[]{:S(2)}) collective-permute-start(bf16[64,2176]{1,0:T(8,128)(2,1)S(1)} %get-tuple-element.83.refs_10_), channel_id=1, source_target_pairs={{0,16},{4,20},{8,24},{12,28},{16,0},{20,4},{24,8},{28,12},{1,17},{... | collective-permute-start | bytes 835592 | tf_op jit(solution)/shard_map/ppermute | solution.py:259
  58.2 19.1 %collective-permute-start.5 = (bf16[128,2176]{1,0:T(8,128)(2,1)S(1)}, bf16[128,2176]{1,0:T(8,128)(2,1)S(1)}, u32[]{:S(2)}, u32[]{:S(2)}) collective-permute-start(bf16[128,2176]{1,0:T(8,128)(2,1)S(1)} %get-tuple-element.98), channel_id=1, source_target_pairs={{0,4},{4,0},{8,12},{12,8},{16,20},{20,16},{24,28},{28,24},{1,5},{5... | collective-permute-start | bytes 1671176 | tf_op jit(solution)/shard_map/ppermute | solution.py:259
  58.4 6.1 %collective-permute-start.6 = (bf16[32,2176]{1,0:T(8,128)(2,1)S(1)}, bf16[32,2176]{1,0:T(8,128)(2,1)S(1)}, u32[]{:S(2)}, u32[]{:S(2)}) collective-permute-start(bf16[32,2176]{1,0:T(8,128)(2,1)S(1)} %get-tuple-element.95.refs_0_), channel_id=1, source_target_pairs={{0,16},{4,20},{8,24},{12,28},{16,0},{20,4},{24,8},{28,12},{1,17},{... | collective-permute-start | bytes 417800 | tf_op jit(solution)/shard_map/ppermute | solution.py:259
  59.0 5.8 %collective-permute-start.7 = (bf16[32,2176]{1,0:T(8,128)(2,1)S(1)}, bf16[32,2176]{1,0:T(8,128)(2,1)S(1)}, u32[]{:S(2)}, u32[]{:S(2)}) collective-permute-start(bf16[32,2176]{1,0:T(8,128)(2,1)S(1)} %get-tuple-element.96.refs_1_), channel_id=1, source_target_pairs={{0,8},{4,12},{8,0},{12,4},{16,24},{20,28},{24,16},{28,20},{1,9},{5... | collective-permute-start | bytes 417800 | tf_op jit(solution)/shard_map/ppermute | solution.py:259
  59.3 17.9 %collective-permute-start.2 = (bf16[64,2048]{1,0:T(8,128)(2,1)S(1)}, bf16[64,2048]{1,0:T(8,128)(2,1)S(1)}, u32[]{:S(2)}, u32[]{:S(2)}) collective-permute-start(bf16[64,2048]{1,0:T(8,128)(2,1)S(1)} %get-tuple-element.78.refs_8_), channel_id=1, source_target_pairs={{0,2},{1,3},{2,0},{3,1},{4,6},{5,7},{6,4},{7,5},{8,10},{9,11},{10,... | collective-permute-start | bytes 786440 | tf_op jit(solution)/shard_map/ppermute | solution.py:259
  64.8 10.3 %collective-permute-start.8 = (bf16[32,2176]{1,0:T(8,128)(2,1)S(1)}, bf16[32,2176]{1,0:T(8,128)(2,1)S(1)}, u32[]{:S(2)}, u32[]{:S(2)}) collective-permute-start(bf16[32,2176]{1,0:T(8,128)(2,1)S(1)} %get-tuple-element.107), channel_id=1, source_target_pairs={{0,1},{1,0},{2,3},{3,2},{4,5},{5,4},{6,7},{7,6},{8,9},{9,8},{10,11... | collective-permute-start | bytes 417800 | tf_op jit(solution)/shard_map/ppermute | solution.py:259
  75.2 5.8 %collective-permute-start.9 = (bf16[16,2176]{1,0:T(8,128)(2,1)S(1)}, bf16[16,2176]{1,0:T(8,128)(2,1)S(1)}, u32[]{:S(2)}, u32[]{:S(2)}) collective-permute-start(bf16[16,2176]{1,0:T(8,128)(2,1)S(1)} %get-tuple-element.110), channel_id=1, source_target_pairs={{0,2},{1,3},{2,0},{3,1},{4,6},{5,7},{6,4},{7,5},{8,10},{9,11},{10,... | collective-permute-start | bytes 208904 | tf_op jit(solution)/shard_map/ppermute | solution.py:259
  77.5 11.0 %collective-permute-start.19 = (bf16[32,2176]{1,0:T(8,128)(2,1)S(1)}, bf16[32,2176]{1,0:T(8,128)(2,1)S(1)}, u32[]{:S(2)}, u32[]{:S(2)}) collective-permute-start(bf16[32,2176]{1,0:T(8,128)(2,1)S(1)} %get-tuple-element.99.refs_2_), channel_id=1, source_target_pairs={{0,16},{4,20},{8,24},{12,28},{16,0},{20,4},{24,8},{28,12},{1,17},{... | collective-permute-start | bytes 417800 | tf_op jit(solution)/shard_map/ppermute | solution.py:259
  79.0 9.5 %collective-permute-start.20 = (bf16[32,2176]{1,0:T(8,128)(2,1)S(1)}, bf16[32,2176]{1,0:T(8,128)(2,1)S(1)}, u32[]{:S(2)}, u32[]{:S(2)}) collective-permute-start(bf16[32,2176]{1,0:T(8,128)(2,1)S(1)} %get-tuple-element.100.refs_3_), channel_id=1, source_target_pairs={{0,8},{4,12},{8,0},{12,4},{16,24},{20,28},{24,16},{28,20},{1,9},{5... | collective-permute-start | bytes 417800 | tf_op jit(solution)/shard_map/ppermute | solution.py:259
  79.0 9.5 %collective-permute-start.21 = (bf16[32,2176]{1,0:T(8,128)(2,1)S(1)}, bf16[32,2176]{1,0:T(8,128)(2,1)S(1)}, u32[]{:S(2)}, u32[]{:S(2)}) collective-permute-start(bf16[32,2176]{1,0:T(8,128)(2,1)S(1)} %get-tuple-element.101.refs_4_), channel_id=1, source_target_pairs={{0,24},{4,28},{8,16},{12,20},{16,8},{20,12},{24,0},{28,4},{1,25},{... | collective-permute-start | bytes 417800 | tf_op jit(solution)/shard_map/ppermute | solution.py:259
  81.1 5.2 %collective-permute-start.10 = (bf16[16,2176]{1,0:T(8,128)(2,1)S(1)}, bf16[16,2176]{1,0:T(8,128)(2,1)S(1)}, u32[]{:S(2)}, u32[]{:S(2)}) collective-permute-start(bf16[16,2176]{1,0:T(8,128)(2,1)S(1)} %shard_map.64), channel_id=1, source_target_pairs={{0,16},{4,20},{8,24},{12,28},{16,0},{20,4},{24,8},{28,12},{1,17},{... | collective-permute-start | bytes 208904 | tf_op jit(solution)/shard_map/ppermute | solution.py:259
  82.6 12.7 %copy-start.1 = (s32[4096,2]{0,1:T(2,128)S(1)}, s32[4096,2]{0,1:T(2,128)}, u32[]{:S(2)}) copy-start(s32[4096,2]{0,1:T(2,128)} %param.9) | copy-start | bytes 98308
  85.5 1.4 %collective-permute-start.13 = (bf16[32,2176]{1,0:T(8,128)(2,1)S(1)}, bf16[32,2176]{1,0:T(8,128)(2,1)S(1)}, u32[]{:S(2)}, u32[]{:S(2)}) collective-permute-start(bf16[32,2176]{1,0:T(8,128)(2,1)S(1)} %get-tuple-element.102.refs_0_), channel_id=1, source_target_pairs={{0,4},{4,0},{8,12},{12,8},{16,20},{20,16},{24,28},{28,24},{1,5},{5... | collective-permute-start | bytes 417800 | tf_op jit(solution)/shard_map/ppermute | solution.py:259
  86.3 14.0 %collective-permute-start.11 = (bf16[32,2176]{1,0:T(8,128)(2,1)S(1)}, bf16[32,2176]{1,0:T(8,128)(2,1)S(1)}, u32[]{:S(2)}, u32[]{:S(2)}) collective-permute-start(bf16[32,2176]{1,0:T(8,128)(2,1)S(1)} %pad_maximum_fusion.1), channel_id=1, source_target_pairs={{0,8},{4,12},{8,0},{12,4},{16,24},{20,28},{24,16},{28,20},{1,9},{5... | collective-permute-start | bytes 417800 | tf_op jit(solution)/shard_map/ppermute | solution.py:259
  86.9 4.4 %collective-permute-start.14 = (bf16[16,2176]{1,0:T(8,128)(2,1)S(1)}, bf16[16,2176]{1,0:T(8,128)(2,1)S(1)}, u32[]{:S(2)}, u32[]{:S(2)}) collective-permute-start(bf16[16,2176]{1,0:T(8,128)(2,1)S(1)} %get-tuple-element.113), channel_id=1, source_target_pairs={{0,16},{4,20},{8,24},{12,28},{16,0},{20,4},{24,8},{28,12},{1,17},{... | collective-permute-start | bytes 208904 | tf_op jit(solution)/shard_map/ppermute | solution.py:259
  88.6 4.9 %collective-permute-start.22 = (bf16[16,2176]{1,0:T(8,128)(2,1)S(1)}, bf16[16,2176]{1,0:T(8,128)(2,1)S(1)}, u32[]{:S(2)}, u32[]{:S(2)}) collective-permute-start(bf16[16,2176]{1,0:T(8,128)(2,1)S(1)} %get-tuple-element.118), channel_id=1, source_target_pairs={{0,1},{1,0},{2,3},{3,2},{4,5},{5,4},{6,7},{7,6},{8,9},{9,8},{10,11... | collective-permute-start | bytes 208904 | tf_op jit(solution)/shard_map/ppermute | solution.py:259
  91.3 4.4 %collective-permute-start.15 = (bf16[8,2176]{1,0:T(8,128)(2,1)S(1)}, bf16[8,2176]{1,0:T(8,128)(2,1)S(1)}, u32[]{:S(2)}, u32[]{:S(2)}) collective-permute-start(bf16[8,2176]{1,0:T(8,128)(2,1)S(1)} %get-tuple-element.115), channel_id=1, source_target_pairs={{0,8},{4,12},{8,0},{12,4},{16,24},{20,28},{24,16},{28,20},{1,9},{5... | collective-permute-start | bytes 104456 | tf_op jit(solution)/shard_map/ppermute | solution.py:259
  93.5 4.9 %collective-permute-start.23 = (bf16[8,2176]{1,0:T(8,128)(2,1)S(1)}, bf16[8,2176]{1,0:T(8,128)(2,1)S(1)}, u32[]{:S(2)}, u32[]{:S(2)}) collective-permute-start(bf16[8,2176]{1,0:T(8,128)(2,1)S(1)} %get-tuple-element.120), channel_id=1, source_target_pairs={{0,2},{1,3},{2,0},{3,1},{4,6},{5,7},{6,4},{7,5},{8,10},{9,11},{10,... | collective-permute-start | bytes 104456 | tf_op jit(solution)/shard_map/ppermute | solution.py:259
  95.7 7.6 %collective-permute-start.16 = (bf16[8,2176]{1,0:T(8,128)(2,1)S(1)}, bf16[8,2176]{1,0:T(8,128)(2,1)S(1)}, u32[]{:S(2)}, u32[]{:S(2)}) collective-permute-start(bf16[8,2176]{1,0:T(8,128)(2,1)S(1)} %shard_map.67), channel_id=1, source_target_pairs={{0,8},{4,12},{8,0},{12,4},{16,24},{20,28},{24,16},{28,20},{1,9},{5... | collective-permute-start | bytes 104456 | tf_op jit(solution)/shard_map/ppermute | solution.py:259
  98.4 4.0 %collective-permute-start.24 = (bf16[8,2176]{1,0:T(8,128)(2,1)S(1)}, bf16[8,2176]{1,0:T(8,128)(2,1)S(1)}, u32[]{:S(2)}, u32[]{:S(2)}) collective-permute-start(bf16[8,2176]{1,0:T(8,128)(2,1)S(1)} %shard_map.70), channel_id=1, source_target_pairs={{0,8},{4,12},{8,0},{12,4},{16,24},{20,28},{24,16},{28,20},{1,9},{5... | collective-permute-start | bytes 104456 | tf_op jit(solution)/shard_map/ppermute | solution.py:259
  100.4 8.8 %collective-permute-start.12 = (bf16[64,2176]{1,0:T(8,128)(2,1)S(1)}, bf16[64,2176]{1,0:T(8,128)(2,1)S(1)}, u32[]{:S(2)}, u32[]{:S(2)}) collective-permute-start(bf16[64,2176]{1,0:T(8,128)(2,1)S(1)} %pad_maximum_fusion), channel_id=1, source_target_pairs={{0,4},{4,0},{8,12},{12,8},{16,20},{20,16},{24,28},{28,24},{1,5},{5... | collective-permute-start | bytes 835592 | tf_op jit(solution)/shard_map/ppermute | solution.py:259
  102.4 4.3 %collective-permute-start.25 = (bf16[16,2176]{1,0:T(8,128)(2,1)S(1)}, bf16[16,2176]{1,0:T(8,128)(2,1)S(1)}, u32[]{:S(2)}, u32[]{:S(2)}) collective-permute-start(bf16[16,2176]{1,0:T(8,128)(2,1)S(1)} %pad_maximum_fusion.5), channel_id=1, source_target_pairs={{0,16},{4,20},{8,24},{12,28},{16,0},{20,4},{24,8},{28,12},{1,17},{... | collective-permute-start | bytes 208904 | tf_op jit(solution)/shard_map/ppermute | solution.py:259
  103.4 4.4 %collective-permute-start.17 = (bf16[16,2176]{1,0:T(8,128)(2,1)S(1)}, bf16[16,2176]{1,0:T(8,128)(2,1)S(1)}, u32[]{:S(2)}, u32[]{:S(2)}) collective-permute-start(bf16[16,2176]{1,0:T(8,128)(2,1)S(1)} %pad_maximum_fusion.4), channel_id=1, source_target_pairs={{0,16},{4,20},{8,24},{12,28},{16,0},{20,4},{24,8},{28,12},{1,17},{... | collective-permute-start | bytes 208904 | tf_op jit(solution)/shard_map/ppermute | solution.py:259
  106.7 1.4 %collective-permute-start.26 = (bf16[32,2176]{1,0:T(8,128)(2,1)S(1)}, bf16[32,2176]{1,0:T(8,128)(2,1)S(1)}, u32[]{:S(2)}, u32[]{:S(2)}) collective-permute-start(bf16[32,2176]{1,0:T(8,128)(2,1)S(1)} %pad_maximum_fusion.3), channel_id=1, source_target_pairs={{0,4},{4,0},{8,12},{12,8},{16,20},{20,16},{24,28},{28,24},{1,5},{5... | collective-permute-start | bytes 417800 | tf_op jit(solution)/shard_map/ppermute | solution.py:259
  107.7 1.4 %collective-permute-start.18 = (bf16[32,2176]{1,0:T(8,128)(2,1)S(1)}, bf16[32,2176]{1,0:T(8,128)(2,1)S(1)}, u32[]{:S(2)}, u32[]{:S(2)}) collective-permute-start(bf16[32,2176]{1,0:T(8,128)(2,1)S(1)} %pad_maximum_fusion.2), channel_id=1, source_target_pairs={{0,4},{4,0},{8,12},{12,8},{16,20},{20,16},{24,28},{28,24},{1,5},{5... | collective-permute-start | bytes 417800 | tf_op jit(solution)/shard_map/ppermute | solution.py:259

commit v5 on v4

--- a/solution.py
+++ b/solution.py
@@ -86,7 +86,7 @@
     fetches += [
         pltpu.make_async_copy(w_hbm.at[pl.ds(s * stripe, stripe), :], w[s], sems.at[s]) for s in range(n_stripes)
     ]
-    for fetch in fetches:
+    for fetch in fetches[:3]:
         fetch.start()
     return fetches[:3], fetches[3:]
 
@@ -98,6 +98,8 @@
 
 def single_kernel(n_col, n_stripes, place, pairs, val, con_all, w_hbm, kept, sent, val_density, acc, density, hot1, hot2, pairs_here, val_here, con, rolled, sems, in_sems, *w):
     inputs, stripes = fetch_all(n_col, n_stripes, place, (pairs, val, con_all, w_hbm), (pairs_here, val_here, con, w), sems, in_sems)
+    for fetch in stripes:
+        fetch.start()
     for fetch in inputs:
         fetch.wait()
     make_hot(pairs_here, hot1, hot2)
@@ -114,8 +116,10 @@
     density, hot1, hot2, val_b, pairs_here, val_here, con, rolled, sems, in_sems = refs
     inputs, stripes = fetch_all(n_col, n_stripes, place, (pairs, val, con_all, w_hbm), (pairs_here, val_here, con, w), sems, in_sems)
     inputs[0].wait()
+    inputs[1].wait()
+    for fetch in stripes:
+        fetch.start()
     make_hot(pairs_here, hot1, hot2)
-    inputs[1].wait()
     build_val(groups(hot1, n_col, start, width), groups(hot2, n_col, start, width), val_here, val_b)
     build_val(groups(hot1, n_col, 0, 2 * width), groups(hot2, n_col, 0, 2 * width), val_here, val_a)
     inputs[2].wait()
@@ -209,17 +213,21 @@
             other[to + z * half : to + (z + 1) * half, :] = jnp.where(high, low_part, high_part).astype(BF16)
 
 
-def quarter_kernel(n_col, bits, place, kept, got, kept_out, *refs):
-    *sent, part = refs
-    part[...] = kept[...] + got[...].astype(F32)
+def quarter_kernel(n_col, bits, n_chunks, place, *refs):
+    kept, got, refs = refs[:n_chunks], refs[n_chunks], refs[n_chunks + 1 :]
+    kept_out, (*sent, part) = refs[:n_chunks], refs[n_chunks:]
     me = place[0] // n_col
     first, second = (me >> bits[0]) % 2, (me >> bits[1]) % 2
-    size = kept_out.shape[0] // n_col
-    for flip, out in enumerate([kept_out, *sent]):
-        at = ((first + flip // 2) % 2 * 2 + (second + flip % 2) % 2) * size
-        for z in range(n_col):
-            rows = part[pl.ds(pl.multiple_of(z * 4 * size + at, size), size), :]
-            out[z * size : (z + 1) * size, :] = rows.astype(out.dtype)
+    rows = kept[0].shape[0]
+    size = rows // 4 // n_col
+    for c in range(n_chunks):
+        part[...] = kept[c][...] + got[c * rows : (c + 1) * rows, :].astype(F32)
+        for flip, out in enumerate([kept_out[c], *sent]):
+            at = ((first + flip // 2) % 2 * 2 + (second + flip % 2) % 2) * size
+            base = c * n_col * size if flip else 0
+            for z in range(n_col):
+                mine = part[pl.ds(pl.multiple_of(z * 4 * size + at, size), size), :]
+                out[base + z * size : base + (z + 1) * size, :] = mine.astype(out.dtype)
 
 
 def hot_kernel(n_col, count, n_after, place, pairs, *refs):
@@ -273,7 +281,7 @@
         unordered = blocks * count
         n_pairs = val_pairs.shape[0]
         per_col = n_pairs // n_col
-        chunks = CHUNKS if n_pairs >= 8 * CHUNKS * n_row * n_col and row_bits > 2 else 1
+        chunks = CHUNKS if n_pairs >= 8 * CHUNKS * n_row * n_col and row_bits == 3 else 1
         width = per_col // chunks
         starts = [k * width for k in range(chunks)]
         place = (lax.axis_index("row") * n_col + lax.axis_index("col")).astype(jnp.int32)[None]
@@ -412,19 +420,23 @@
             return list(out[:n_kept]), list(out[n_kept:])
 
         def quarters(kept, got, bits):
-            rows = kept.shape[0] // 4
-            kept, *sent = pl.pallas_call(
-                functools.partial(quarter_kernel, n_col, bits),
-                in_specs=[smem] + [vmem] * 2,
-                out_specs=[vmem] * 4,
-                out_shape=[pltpu.VMEM((rows, unordered), F32)] + [pltpu.VMEM((rows, unordered), BF16)] * 3,
-                scratch_shapes=[pltpu.VMEM(kept.shape, F32)],
-                compiler_params=params(4),
-            )(place, kept, got)
-            return kept, sent
+            rows = kept[0].shape[0] // 4
+            out = pl.pallas_call(
+                functools.partial(quarter_kernel, n_col, bits, len(kept)),
+                in_specs=[smem] + [vmem] * (len(kept) + 1),
+                out_specs=[vmem] * (len(kept) + 3),
+                out_shape=[pltpu.VMEM((rows, unordered), F32)] * len(kept)
+                + [pltpu.VMEM((rows * len(kept), unordered), BF16)] * 3,
+                scratch_shapes=[pltpu.VMEM(kept[0].shape, F32)],
+                compiler_params=params(6),
+            )(place, *kept, got)
+            sent = list(out[len(kept) :])
+            flips = [1 << bits[1], 1 << bits[0], 1 << bits[0] | 1 << bits[1]]
+            got = [swap(x, "row", flip, n_row) for x, flip in zip(sent, flips)]
+            return list(out[: len(kept)]), got, sent
 
         order = list(range(1, row_bits))
-        orders = [[0] + (order if k % 2 == 0 else order[::-1]) for k in range(chunks)]
+        orders = [[0] + order for _ in range(chunks)]
         col_steps = [("col", bit, n_col >> (bit + 1)) for bit in range(col_bits)]
         steps = [
             [("row", bit, n_col) for bit in orders[k]] + col_steps + [None] if k < 3
@@ -451,24 +463,17 @@
 
         if chunks > 1:
             low, high = list(range(n_stripes // 2)), list(range(n_stripes // 2, n_stripes))
-            apart = [[0], [1]]
             kept, b_sent, val_density, fixed = load()
             b = [kept], b_sent
             kept, sent, fixed = pair(fixed, val_density, [b_sent])
             b = run(3, 0, 1, *b)
-            got = [send(0, 0, sent)]
-            kept, sents = fold(kept, got, [steps[0][1], steps[1][1]], None, apart)
-            before, fixed = begin(2, low, fixed, [b[1], *sents])
+            kept, a_got, a_sent = quarters(kept, send(0, 0, sent), orders[0][1:3])
+            before, fixed = begin(2, low, fixed, [b[1], *a_sent])
             m, density = end(high, fixed, before, [])
-            m_kept, m_sent = quarters(m[0], send(2, 0, m[1]), orders[2][1:3])
-            for s in range(1, row_bits):
-                got = [send(k, s, sents[k]) for k in range(2)]
-                ends = apart if s < row_bits - 1 else None
-                kept, sents = fold(kept, got, [steps[0][s + 1], steps[1][s + 1]], apart, ends)
-                if s == 1:
-                    hold = sents
+            m_kept, m_got, m_sent = quarters([m[0]], send(2, 0, m[1]), orders[2][1:3])
+            kept, (sent,) = fold(kept, a_got, [steps[0][3]] * 2, [[0, 1]] * 3)
             b = run(3, 1, col_bits, *b)
-            b_kept, b_sent = last(density, b[1], hold + m_sent)
+            b_kept, b_sent = last(density, b[1], [])
             b = [b_kept], b_sent
             when = [b_sent]
             axis_steps = len(steps[3]) - 1
@@ -477,10 +482,8 @@
                 got = swap(b[1], axis, 1 << bit, sizes[axis])
                 kept_b, (sent_b,) = fold(b[0], [got], [steps[3][s + 1]])
                 b = kept_b, sent_b
-            _, a_sums = run(0, row_bits, n_steps, kept, sents[0])
-            flips = [1 << orders[2][2], 1 << orders[2][1], 1 << orders[2][1] | 1 << orders[2][2]]
-            got = [swap(x, "row", flip, n_row) for x, flip in zip(m_sent, flips)]
-            m_kept, m_sent = fold([m_kept], got, [steps[2][3]], [[0]] * 3)
+            _, a_sums = run(0, 3, n_steps, kept, sent)
+            m_kept, m_sent = fold(m_kept, m_got, [steps[2][3]], [[0]] * 3)
             _, m_sums = run(2, 3, n_steps, m_kept, m_sent[0])
             up, down = order + [0], order[::-1] + [0]
             arrays = [gather(a_sums, down), gather(b[1], up), gather(m_sums, up)]

time: 111 us -> 127 us (1.14)
  waiting for transfers between devices: 33.1 us -> 51 us
  Pallas kernels: 44.9 us -> 42.8 us
    ppermute x27 -> x26, waiting for transfers between devices: 33.1 us -> 51 us  [swap(): return lax.ppermute(x, axis, [(i, i ^ bits) for i in range(size)])]
    pallas_call x1, Pallas kernels: 13.9 us -> 11.7 us  [load(): pl.pallas_call(functools.partial(load_kernel, n_col, starts[3], width, n_...]
    ppermute x27 -> x26, starting transfers between devices: 32.6 us -> 32.4 us  [swap(): return lax.ppermute(x, axis, [(i, i ^ bits) for i in range(size)])]
  transfers between devices with their start and end apart: 27 -> 26, of which waited for: 14 -> 16; matrix products, arithmetic and copies ran while one was open for 0% -> 0% of each run, Pallas kernels for 12% -> 1%
where the time goes in v5:
time: 127 us
  waiting for transfers between devices  51 us (40%)
  Pallas kernels  42.8 us (34%)
  starting transfers between devices  32.4 us (26%)
    ppermute x26, waiting for transfers between devices, swap(): return lax.ppermute(x, axis, [(i, i ^ bits) for i in range(size)])  51 us
    ppermute x26, starting transfers between devices, swap(): return lax.ppermute(x, axis, [(i, i ^ bits) for i in range(size)])  32.4 us
    pallas_call x1, Pallas kernels, pair(): pl.pallas_call(functools.partial(pair_kernel, n_col, n_stripes, len(after...  15.7 us
    pallas_call x1, Pallas kernels, load(): pl.pallas_call(functools.partial(load_kernel, n_col, starts[3], width, n_...  11.7 us
    pallas_call x1, Pallas kernels, begin(): pl.pallas_call(functools.partial(begin_kernel, n_col, starts[k], width, n...  5.1 us
    pallas_call x1, Pallas kernels, end(): pl.pallas_call(functools.partial(end_kernel, n_col, n_stripes, numbers, l...  4.02 us
    pallas_call x1, Pallas kernels, last(): pl.pallas_call(functools.partial(last_kernel, n_col, len(after)), in_spec...  2.86 us
  transfers between devices with their start and end apart: 26, of which 16 were waited for; matrix products, arithmetic and copies ran while one was open for 0% of the time, Pallas kernels for 1%

profile of v5, /device:TPU:0, one launch (start us, length us, event | category | flops | bytes accessed | tf_op | source)
XLA Modules:
  0.0 126.7 jit_solution(639646645115568984)
XLA Ops:
  0.0 11.7 %load.1 = (f32[128,2048]{1,0:T(8,128)S(1)}, bf16[128,2048]{1,0:T(8,128)(2,1)S(1)}, bf16[512,4096]{1,0:T(8,128)(2,1)S(1)}, bf16[512,4096]{1,0:T(8,128)(2,1)S(1)},...) custom-call(s32[1]{0:T(128)} %bitcast.place, ...), custom_call_target="tpu_custom_call" | custom-call | flops 6576668672 | bytes 1048576 | tf_op jit(solution)/shard_map/load/pallas_call | solution.py:332
  11.7 15.7 %pair.1 = (f32[128,2176]{1,0:T(8,128)S(1)}, f32[128,2176]{1,0:T(8,128)S(1)}, bf16[256,2176]{1,0:T(8,128)(2,1)S(1)}, bf16[512,4096]{1,0:T(8,128)(2,1)S(1)}, bf16[...) custom-call(s32[1]{0:T(128)} %bitcast.place, ...), custom_call_target="tpu_custom_call", output_to_operand_aliasing={{3}: (1, {}), {4}: (2, {}), {5}: (3, {}), {6}: (4, {}), {7}... | custom-call | flops 13153337344 | bytes 1048576 | tf_op jit(solution)/shard_map/pair/pallas_call | solution.py:351
  27.4 0.0 copy-start
  27.4 0.5 collective-permute-start.1
  28.0 2.6 %collective-permute-start = (bf16[128,2048]{1,0:T(8,128)(2,1)S(1)}, bf16[128,2048]{1,0:T(8,128)(2,1)S(1)}, u32[]{:S(2)}, u32[]{:S(2)}) collective-permute-start(bf16[128,2048]{1,0:T(8,128)(2,1)S(1)} %get-tuple-element.66.refs_6_), channel_id=1, source_target_pairs={{0,1},{1,0},{2,3},{3,2},{4,5},{5,4},{6,7},{7,6},{8,9},{9,8},{10,11... | collective-permute-start | bytes 1572872 | tf_op jit(solution)/shard_map/ppermute | solution.py:267
  30.6 12.5 %collective-permute-done.refs_1_ = bf16[128,2048]{1,0:T(8,128)(2,1)S(1)} collective-permute-done((bf16[128,2048]{1,0:T(8,128)(2,1)S(1)}, bf16[128,2048]{1,0:T(8,128)(2,1)S(1)}, u32[]{:S(2)}, u32[]{:S(2)}) %collective-permute-start) | collective-permute-done | bytes 524320 | tf_op jit(solution)/shard_map/ppermute | solution.py:267
  43.1 0.1 shard_map.55
  43.3 2.8 %collective-permute-start.2 = (bf16[64,2048]{1,0:T(8,128)(2,1)S(1)}, bf16[64,2048]{1,0:T(8,128)(2,1)S(1)}, u32[]{:S(2)}, u32[]{:S(2)}) collective-permute-start(bf16[64,2048]{1,0:T(8,128)(2,1)S(1)} %get-tuple-element.75.refs_8_), channel_id=1, source_target_pairs={{0,2},{1,3},{2,0},{3,1},{4,6},{5,7},{6,4},{7,5},{8,10},{9,11},{10,... | collective-permute-start | bytes 786440 | tf_op jit(solution)/shard_map/ppermute | solution.py:267
  46.1 11.8 %collective-permute-done.2.refs_1_ = bf16[64,2048]{1,0:T(8,128)(2,1)S(1)} collective-permute-done((bf16[64,2048]{1,0:T(8,128)(2,1)S(1)}, bf16[64,2048]{1,0:T(8,128)(2,1)S(1)}, u32[]{:S(2)}, u32[]{:S(2)}) %collective-permute-start.2) | collective-permute-done | bytes 262176 | tf_op jit(solution)/shard_map/ppermute | solution.py:267
  57.9 0.1 shard_map.59.t
  58.0 0.0 collective-permute-done.1.refs_2_
  58.0 0.4 shard_map.56
  58.4 5.1 %shard_map.57 = (f32[256,2176]{1,0:T(8,128)S(1)}, bf16[256,4096]{1,0:T(8,128)(2,1)S(1)}, bf16[512,4096]{1,0:T(8,128)(2,1)S(1)}, bf16[512,4096]{1,0:T(8,128)(2,1)...) custom-call(bf16[512,4096]{1,0:T(8,128)(2,1)S(1)} %get-tuple-element, ...), custom_call_target="tpu_custom_call", output_to_operand_aliasing={{2}: (0, {}), {3}: (1, {}), {4}: (2, {}), {5}: (3, {}), {6}... | custom-call | flops 3288334336 | bytes 1048576 | tf_op jit(solution)/shard_map/pallas_call | solution.py:380
  63.5 4.0 %shard_map.58 = (f32[128,2176]{1,0:T(8,128)S(1)}, bf16[128,2176]{1,0:T(8,128)(2,1)S(1)}, bf16[2176,2048]{1,0:T(8,128)(2,1)S(1)}) custom-call(s32[1]{0:T(128)} %bitcast.place, bf16[512,4096]{1,0:T(8,128)(2,1)S(1)} %get-tuple-element.82.refs_0_, bf16[512,4096]{1,0:T(8,128)(2,1)S(1)} %get-tuple-element.83.refs_1_, ...), custom_call_target="tpu_custom_call", output_to_operand_aliasing={{2}: (5, {})} | custom-call | flops 3288334336 | bytes 1048576 | tf_op jit(solution)/shard_map/pallas_call | solution.py:393
  67.5 2.9 %last.1 = (f32[32,2176]{1,0:T(8,128)S(1)}, bf16[32,2176]{1,0:T(8,128)(2,1)S(1)}) custom-call(s32[1]{0:T(128)} %bitcast.place, bf16[2176,2048]{1,0:T(8,128)(2,1)S(1)} %get-tuple-element.89.density, bf16[64,2048]{1,0:T(8,128)(2,1)S(1)} %shard_map.59.t), custom_call_target="tpu_custom_call" | custom-call | flops 1644167168 | bytes 1048576 | tf_op jit(solution)/shard_map/last/pallas_call | solution.py:367
  70.4 0.0 copy-start.1
  70.4 0.1 collective-permute-start.11
  70.5 0.5 collective-permute-start.17
  71.0 0.8 collective-permute-done.11.refs_1_
  71.9 1.4 %collective-permute-start.12 = (bf16[16,2176]{1,0:T(8,128)(2,1)S(1)}, bf16[16,2176]{1,0:T(8,128)(2,1)S(1)}, u32[]{:S(2)}, u32[]{:S(2)}) collective-permute-start(bf16[16,2176]{1,0:T(8,128)(2,1)S(1)} %get-tuple-element.102), channel_id=1, source_target_pairs={{0,8},{4,12},{8,0},{12,4},{16,24},{20,28},{24,16},{28,20},{1,9},{5... | collective-permute-start | bytes 208904 | tf_op jit(solution)/shard_map/ppermute | solution.py:267
  73.4 2.9 %collective-permute-done.12.refs_1_ = bf16[16,2176]{1,0:T(8,128)(2,1)S(1)} collective-permute-done((bf16[16,2176]{1,0:T(8,128)(2,1)S(1)}, bf16[16,2176]{1,0:T(8,128)(2,1)S(1)}, u32[]{:S(2)}, u32[]{:S(2)}) %collective-permute-start.12) | collective-permute-done | bytes 69664 | tf_op jit(solution)/shard_map/ppermute | solution.py:267
  76.3 1.5 %collective-permute-start.13 = (bf16[8,2176]{1,0:T(8,128)(2,1)S(1)}, bf16[8,2176]{1,0:T(8,128)(2,1)S(1)}, u32[]{:S(2)}, u32[]{:S(2)}) collective-permute-start(bf16[8,2176]{1,0:T(8,128)(2,1)S(1)} %get-tuple-element.104), channel_id=1, source_target_pairs={{0,16},{4,20},{8,24},{12,28},{16,0},{20,4},{24,8},{28,12},{1,17},{... | collective-permute-start | bytes 104456 | tf_op jit(solution)/shard_map/ppermute | solution.py:267
  77.8 2.5 %collective-permute-done.13.refs_1_ = bf16[8,2176]{1,0:T(8,128)(2,1)S(1)} collective-permute-done((bf16[8,2176]{1,0:T(8,128)(2,1)S(1)}, bf16[8,2176]{1,0:T(8,128)(2,1)S(1)}, u32[]{:S(2)}, u32[]{:S(2)}) %collective-permute-start.13) | collective-permute-done | bytes 34848 | tf_op jit(solution)/shard_map/ppermute | solution.py:267
  80.3 1.4 %collective-permute-start.14 = (bf16[8,2176]{1,0:T(8,128)(2,1)S(1)}, bf16[8,2176]{1,0:T(8,128)(2,1)S(1)}, u32[]{:S(2)}, u32[]{:S(2)}) collective-permute-start(bf16[8,2176]{1,0:T(8,128)(2,1)S(1)} %shard_map.65), channel_id=1, source_target_pairs={{0,8},{4,12},{8,0},{12,4},{16,24},{20,28},{24,16},{28,20},{1,9},{5... | collective-permute-start | bytes 104456 | tf_op jit(solution)/shard_map/ppermute | solution.py:267
  81.8 1.5 %collective-permute-start.3 = (bf16[64,2176]{1,0:T(8,128)(2,1)S(1)}, bf16[64,2176]{1,0:T(8,128)(2,1)S(1)}, u32[]{:S(2)}, u32[]{:S(2)}) collective-permute-start(bf16[64,2176]{1,0:T(8,128)(2,1)S(1)} %get-tuple-element.79.refs_9_), channel_id=1, source_target_pairs={{0,16},{4,20},{8,24},{12,28},{16,0},{20,4},{24,8},{28,12},{1,17},{... | collective-permute-start | bytes 835592 | tf_op jit(solution)/shard_map/ppermute | solution.py:267
  83.3 0.5 collective-permute-start.4
  83.8 1.4 %collective-permute-start.5 = (bf16[64,2176]{1,0:T(8,128)(2,1)S(1)}, bf16[64,2176]{1,0:T(8,128)(2,1)S(1)}, u32[]{:S(2)}, u32[]{:S(2)}) collective-permute-start(bf16[64,2176]{1,0:T(8,128)(2,1)S(1)} %get-tuple-element.81.refs_11_), channel_id=1, source_target_pairs={{0,24},{4,28},{8,16},{12,20},{16,8},{20,12},{24,0},{28,4},{1,25},{... | collective-permute-start | bytes 835592 | tf_op jit(solution)/shard_map/ppermute | solution.py:267
  85.3 1.6 %collective-permute-start.15 = (bf16[16,2176]{1,0:T(8,128)(2,1)S(1)}, bf16[16,2176]{1,0:T(8,128)(2,1)S(1)}, u32[]{:S(2)}, u32[]{:S(2)}) collective-permute-start(bf16[16,2176]{1,0:T(8,128)(2,1)S(1)} %pad_maximum_fusion.4), channel_id=1, source_target_pairs={{0,16},{4,20},{8,24},{12,28},{16,0},{20,4},{24,8},{28,12},{1,17},{... | collective-permute-start | bytes 208904 | tf_op jit(solution)/shard_map/ppermute | solution.py:267
  86.9 4.3 %collective-permute-done.3.refs_2_ = bf16[64,2176]{1,0:T(8,128)(2,1)S(1)} collective-permute-done((bf16[64,2176]{1,0:T(8,128)(2,1)S(1)}, bf16[64,2176]{1,0:T(8,128)(2,1)S(1)}, u32[]{:S(2)}, u32[]{:S(2)}) %collective-permute-start.3) | collective-permute-done | bytes 278560 | tf_op jit(solution)/shard_map/ppermute | solution.py:267
  91.1 1.4 %collective-permute-done.4.refs_3_ = bf16[64,2176]{1,0:T(8,128)(2,1)S(1)} collective-permute-done((bf16[64,2176]{1,0:T(8,128)(2,1)S(1)}, bf16[64,2176]{1,0:T(8,128)(2,1)S(1)}, u32[]{:S(2)}, u32[]{:S(2)}) %collective-permute-start.4) | collective-permute-done | bytes 278560 | tf_op jit(solution)/shard_map/ppermute | solution.py:267
  92.5 2.9 %collective-permute-done.5.refs_4_ = bf16[64,2176]{1,0:T(8,128)(2,1)S(1)} collective-permute-done((bf16[64,2176]{1,0:T(8,128)(2,1)S(1)}, bf16[64,2176]{1,0:T(8,128)(2,1)S(1)}, u32[]{:S(2)}, u32[]{:S(2)}) %collective-permute-start.5) | collective-permute-done | bytes 278560 | tf_op jit(solution)/shard_map/ppermute | solution.py:267
  95.4 0.2 shard_map.60
  95.6 0.7 collective-permute-start.6
  96.3 0.2 shard_map.66
  96.5 1.6 %collective-permute-start.18 = (bf16[32,2176]{1,0:T(8,128)(2,1)S(1)}, bf16[32,2176]{1,0:T(8,128)(2,1)S(1)}, u32[]{:S(2)}, u32[]{:S(2)}) collective-permute-start(bf16[32,2176]{1,0:T(8,128)(2,1)S(1)} %get-tuple-element.108), channel_id=1, source_target_pairs={{0,16},{4,20},{8,24},{12,28},{16,0},{20,4},{24,8},{28,12},{1,17},{... | collective-permute-start | bytes 417800 | tf_op jit(solution)/shard_map/ppermute | solution.py:267
  98.1 0.5 collective-permute-start.19
  98.6 1.4 %collective-permute-start.20 = (bf16[32,2176]{1,0:T(8,128)(2,1)S(1)}, bf16[32,2176]{1,0:T(8,128)(2,1)S(1)}, u32[]{:S(2)}, u32[]{:S(2)}) collective-permute-start(bf16[32,2176]{1,0:T(8,128)(2,1)S(1)} %get-tuple-element.110), channel_id=1, source_target_pairs={{0,24},{4,28},{8,16},{12,20},{16,8},{20,12},{24,0},{28,4},{1,25},{... | collective-permute-start | bytes 417800 | tf_op jit(solution)/shard_map/ppermute | solution.py:267
  100.1 0.1 collective-permute-start.16
  100.2 0.5 collective-permute-done.6.refs_2_
  100.8 2.9 %collective-permute-start.7 = (bf16[16,2176]{1,0:T(8,128)(2,1)S(1)}, bf16[16,2176]{1,0:T(8,128)(2,1)S(1)}, u32[]{:S(2)}, u32[]{:S(2)}) collective-permute-start(bf16[16,2176]{1,0:T(8,128)(2,1)S(1)} %get-tuple-element.99), channel_id=1, source_target_pairs={{0,2},{1,3},{2,0},{3,1},{4,6},{5,7},{6,4},{7,5},{8,10},{9,11},{10,... | collective-permute-start | bytes 208904 | tf_op jit(solution)/shard_map/ppermute | solution.py:267
  103.7 0.0 collective-permute-done.18.refs_1_
  103.7 0.0 collective-permute-done.19.refs_2_
  103.7 0.9 collective-permute-done.20.refs_3_
  104.6 0.1 shard_map.67
  104.7 1.4 %collective-permute-start.21 = (bf16[16,2176]{1,0:T(8,128)(2,1)S(1)}, bf16[16,2176]{1,0:T(8,128)(2,1)S(1)}, u32[]{:S(2)}, u32[]{:S(2)}) collective-permute-start(bf16[16,2176]{1,0:T(8,128)(2,1)S(1)} %get-tuple-element.112), channel_id=1, source_target_pairs={{0,1},{1,0},{2,3},{3,2},{4,5},{5,4},{6,7},{7,6},{8,9},{9,8},{10,11... | collective-permute-start | bytes 208904 | tf_op jit(solution)/shard_map/ppermute | solution.py:267
  106.1 0.4 hot.1.pick
  106.5 1.6 %collective-permute-done.7.refs_2_ = bf16[16,2176]{1,0:T(8,128)(2,1)S(1)} collective-permute-done((bf16[16,2176]{1,0:T(8,128)(2,1)S(1)}, bf16[16,2176]{1,0:T(8,128)(2,1)S(1)}, u32[]{:S(2)}, u32[]{:S(2)}) %collective-permute-start.7) | collective-permute-done | bytes 69664 | tf_op jit(solution)/shard_map/ppermute | solution.py:267
  108.1 1.6 %collective-permute-start.8 = (bf16[16,2176]{1,0:T(8,128)(2,1)S(1)}, bf16[16,2176]{1,0:T(8,128)(2,1)S(1)}, u32[]{:S(2)}, u32[]{:S(2)}) collective-permute-start(bf16[16,2176]{1,0:T(8,128)(2,1)S(1)} %shard_map.62), channel_id=1, source_target_pairs={{0,16},{4,20},{8,24},{12,28},{16,0},{20,4},{24,8},{28,12},{1,17},{... | collective-permute-start | bytes 208904 | tf_op jit(solution)/shard_map/ppermute | solution.py:267
  109.7 2.8 %collective-permute-start.22 = (bf16[8,2176]{1,0:T(8,128)(2,1)S(1)}, bf16[8,2176]{1,0:T(8,128)(2,1)S(1)}, u32[]{:S(2)}, u32[]{:S(2)}) collective-permute-start(bf16[8,2176]{1,0:T(8,128)(2,1)S(1)} %get-tuple-element.114), channel_id=1, source_target_pairs={{0,2},{1,3},{2,0},{3,1},{4,6},{5,7},{6,4},{7,5},{8,10},{9,11},{10,... | collective-permute-start | bytes 104456 | tf_op jit(solution)/shard_map/ppermute | solution.py:267
  112.6 0.0 collective-permute-done.16
  112.6 2.4 %collective-permute-done.22.refs_1_ = bf16[8,2176]{1,0:T(8,128)(2,1)S(1)} collective-permute-done((bf16[8,2176]{1,0:T(8,128)(2,1)S(1)}, bf16[8,2176]{1,0:T(8,128)(2,1)S(1)}, u32[]{:S(2)}, u32[]{:S(2)}) %collective-permute-start.22) | collective-permute-done | bytes 34848 | tf_op jit(solution)/shard_map/ppermute | solution.py:267
  115.0 1.5 %collective-permute-start.23 = (bf16[8,2176]{1,0:T(8,128)(2,1)S(1)}, bf16[8,2176]{1,0:T(8,128)(2,1)S(1)}, u32[]{:S(2)}, u32[]{:S(2)}) collective-permute-start(bf16[8,2176]{1,0:T(8,128)(2,1)S(1)} %shard_map.69), channel_id=1, source_target_pairs={{0,8},{4,12},{8,0},{12,4},{16,24},{20,28},{24,16},{28,20},{1,9},{5... | collective-permute-start | bytes 104456 | tf_op jit(solution)/shard_map/ppermute | solution.py:267
  116.5 0.0 collective-permute-done.8
  116.5 0.7 collective-permute-start.9
  117.2 1.8 %collective-permute-done.23 = bf16[8,2176]{1,0:T(8,128)(2,1)S(1)} collective-permute-done((bf16[8,2176]{1,0:T(8,128)(2,1)S(1)}, bf16[8,2176]{1,0:T(8,128)(2,1)S(1)}, u32[]{:S(2)}, u32[]{:S(2)}) %collective-permute-start.23) | collective-permute-done | bytes 34848 | tf_op jit(solution)/shard_map/ppermute | solution.py:267
  119.0 1.0 collective-permute-start.24
  120.0 1.6 %collective-permute-done.9 = bf16[32,2176]{1,0:T(8,128)(2,1)S(1)} collective-permute-done((bf16[32,2176]{1,0:T(8,128)(2,1)S(1)}, bf16[32,2176]{1,0:T(8,128)(2,1)S(1)}, u32[]{:S(2)}, u32[]{:S(2)}) %collective-permute-start.9) | collective-permute-done | bytes 139296 | tf_op jit(solution)/shard_map/ppermute | solution.py:267
  121.7 0.1 collective-permute-start.10
  121.8 1.6 %collective-permute-done.24 = bf16[16,2176]{1,0:T(8,128)(2,1)S(1)} collective-permute-done((bf16[16,2176]{1,0:T(8,128)(2,1)S(1)}, bf16[16,2176]{1,0:T(8,128)(2,1)S(1)}, u32[]{:S(2)}, u32[]{:S(2)}) %collective-permute-start.24) | collective-permute-done | bytes 69664 | tf_op jit(solution)/shard_map/ppermute | solution.py:267
  123.4 0.1 collective-permute-start.25
  123.4 0.0 collective-permute-done.10
  123.4 0.1 maximum_convert_fusion.refs_0_
  123.5 1.2 collective-permute-done.25
  124.8 1.8 %pick.1 = f32[512,256]{1,0:T(8,128)} custom-call(s32[1]{0:T(128)} %bitcast.place, bf16[2176,512]{1,0:T(8,128)(2,1)S(1)} %hot.1.pick, f32[128,2176]{1,0:T(8,128)S(1)} %maximum_convert_fusion.refs_0_, f32[64,2176]{1,0:T(8,128)S(1)} %maximum_convert_fusion.1.refs_1_, f32[64,2176]{1,0:T(8,128)S(1)} %maximum_convert_fusion.2.refs_2_), custom_call_target="tpu_custom_call" | custom-call | tf_op jit(solution)/shard_map/pick/pallas_call | solution.py:508
  (21 shorter events, 0.3 us)
Async XLA Ops:
  27.4 31.0 %copy-start = (bf16[45,4096]{1,0:T(8,128)(2,1)S(1)}, bf16[45,4096]{1,0:T(8,128)(2,1)}, u32[]{:S(2)}) copy-start(bf16[45,4096]{1,0:T(8,128)(2,1)} %refs_7_.1) | copy-start | bytes 1105924
  27.4 30.6 %collective-permute-start.1 = (bf16[256,2176]{1,0:T(8,128)(2,1)S(1)}, bf16[256,2176]{1,0:T(8,128)(2,1)S(1)}, u32[]{:S(2)}, u32[]{:S(2)}) collective-permute-start(bf16[256,2176]{1,0:T(8,128)(2,1)S(1)} %get-tuple-element.78), channel_id=1, source_target_pairs={{0,4},{4,0},{8,12},{12,8},{16,20},{20,16},{24,28},{28,24},{1,5},{5... | collective-permute-start | bytes 3342344 | tf_op jit(solution)/shard_map/ppermute | solution.py:267
  28.0 15.2 %collective-permute-start = (bf16[128,2048]{1,0:T(8,128)(2,1)S(1)}, bf16[128,2048]{1,0:T(8,128)(2,1)S(1)}, u32[]{:S(2)}, u32[]{:S(2)}) collective-permute-start(bf16[128,2048]{1,0:T(8,128)(2,1)S(1)} %get-tuple-element.66.refs_6_), channel_id=1, source_target_pairs={{0,1},{1,0},{2,3},{3,2},{4,5},{5,4},{6,7},{7,6},{8,9},{9,8},{10,11... | collective-permute-start | bytes 1572872 | tf_op jit(solution)/shard_map/ppermute | solution.py:267
  43.3 14.6 %collective-permute-start.2 = (bf16[64,2048]{1,0:T(8,128)(2,1)S(1)}, bf16[64,2048]{1,0:T(8,128)(2,1)S(1)}, u32[]{:S(2)}, u32[]{:S(2)}) collective-permute-start(bf16[64,2048]{1,0:T(8,128)(2,1)S(1)} %get-tuple-element.75.refs_8_), channel_id=1, source_target_pairs={{0,2},{1,3},{2,0},{3,1},{4,6},{5,7},{6,4},{7,5},{8,10},{9,11},{10,... | collective-permute-start | bytes 786440 | tf_op jit(solution)/shard_map/ppermute | solution.py:267
  70.4 35.7 %copy-start.1 = (s32[4096,2]{0,1:T(2,128)S(1)}, s32[4096,2]{0,1:T(2,128)}, u32[]{:S(2)}) copy-start(s32[4096,2]{0,1:T(2,128)} %param.9) | copy-start | bytes 98308
  70.4 1.4 %collective-permute-start.11 = (bf16[32,2176]{1,0:T(8,128)(2,1)S(1)}, bf16[32,2176]{1,0:T(8,128)(2,1)S(1)}, u32[]{:S(2)}, u32[]{:S(2)}) collective-permute-start(bf16[32,2176]{1,0:T(8,128)(2,1)S(1)} %get-tuple-element.91.refs_0_), channel_id=1, source_target_pairs={{0,4},{4,0},{8,12},{12,8},{16,20},{20,16},{24,28},{28,24},{1,5},{5... | collective-permute-start | bytes 417800 | tf_op jit(solution)/shard_map/ppermute | solution.py:267
  70.5 25.8 %collective-permute-start.17 = (bf16[128,2176]{1,0:T(8,128)(2,1)S(1)}, bf16[128,2176]{1,0:T(8,128)(2,1)S(1)}, u32[]{:S(2)}, u32[]{:S(2)}) collective-permute-start(bf16[128,2176]{1,0:T(8,128)(2,1)S(1)} %get-tuple-element.106), channel_id=1, source_target_pairs={{0,4},{4,0},{8,12},{12,8},{16,20},{20,16},{24,28},{28,24},{1,5},{5... | collective-permute-start | bytes 1671176 | tf_op jit(solution)/shard_map/ppermute | solution.py:267
  71.9 4.4 %collective-permute-start.12 = (bf16[16,2176]{1,0:T(8,128)(2,1)S(1)}, bf16[16,2176]{1,0:T(8,128)(2,1)S(1)}, u32[]{:S(2)}, u32[]{:S(2)}) collective-permute-start(bf16[16,2176]{1,0:T(8,128)(2,1)S(1)} %get-tuple-element.102), channel_id=1, source_target_pairs={{0,8},{4,12},{8,0},{12,4},{16,24},{20,28},{24,16},{28,20},{1,9},{5... | collective-permute-start | bytes 208904 | tf_op jit(solution)/shard_map/ppermute | solution.py:267
  76.3 4.0 %collective-permute-start.13 = (bf16[8,2176]{1,0:T(8,128)(2,1)S(1)}, bf16[8,2176]{1,0:T(8,128)(2,1)S(1)}, u32[]{:S(2)}, u32[]{:S(2)}) collective-permute-start(bf16[8,2176]{1,0:T(8,128)(2,1)S(1)} %get-tuple-element.104), channel_id=1, source_target_pairs={{0,16},{4,20},{8,24},{12,28},{16,0},{20,4},{24,8},{28,12},{1,17},{... | collective-permute-start | bytes 104456 | tf_op jit(solution)/shard_map/ppermute | solution.py:267
  80.3 4.9 %collective-permute-start.14 = (bf16[8,2176]{1,0:T(8,128)(2,1)S(1)}, bf16[8,2176]{1,0:T(8,128)(2,1)S(1)}, u32[]{:S(2)}, u32[]{:S(2)}) collective-permute-start(bf16[8,2176]{1,0:T(8,128)(2,1)S(1)} %shard_map.65), channel_id=1, source_target_pairs={{0,8},{4,12},{8,0},{12,4},{16,24},{20,28},{24,16},{28,20},{1,9},{5... | collective-permute-start | bytes 104456 | tf_op jit(solution)/shard_map/ppermute | solution.py:267
  81.8 9.4 %collective-permute-start.3 = (bf16[64,2176]{1,0:T(8,128)(2,1)S(1)}, bf16[64,2176]{1,0:T(8,128)(2,1)S(1)}, u32[]{:S(2)}, u32[]{:S(2)}) collective-permute-start(bf16[64,2176]{1,0:T(8,128)(2,1)S(1)} %get-tuple-element.79.refs_9_), channel_id=1, source_target_pairs={{0,16},{4,20},{8,24},{12,28},{16,0},{20,4},{24,8},{28,12},{1,17},{... | collective-permute-start | bytes 835592 | tf_op jit(solution)/shard_map/ppermute | solution.py:267
  83.3 9.2 %collective-permute-start.4 = (bf16[64,2176]{1,0:T(8,128)(2,1)S(1)}, bf16[64,2176]{1,0:T(8,128)(2,1)S(1)}, u32[]{:S(2)}, u32[]{:S(2)}) collective-permute-start(bf16[64,2176]{1,0:T(8,128)(2,1)S(1)} %get-tuple-element.80.refs_10_), channel_id=1, source_target_pairs={{0,8},{4,12},{8,0},{12,4},{16,24},{20,28},{24,16},{28,20},{1,9},{5... | collective-permute-start | bytes 835592 | tf_op jit(solution)/shard_map/ppermute | solution.py:267
  83.8 11.6 %collective-permute-start.5 = (bf16[64,2176]{1,0:T(8,128)(2,1)S(1)}, bf16[64,2176]{1,0:T(8,128)(2,1)S(1)}, u32[]{:S(2)}, u32[]{:S(2)}) collective-permute-start(bf16[64,2176]{1,0:T(8,128)(2,1)S(1)} %get-tuple-element.81.refs_11_), channel_id=1, source_target_pairs={{0,24},{4,28},{8,16},{12,20},{16,8},{20,12},{24,0},{28,4},{1,25},{... | collective-permute-start | bytes 835592 | tf_op jit(solution)/shard_map/ppermute | solution.py:267
  85.3 14.8 %collective-permute-start.15 = (bf16[16,2176]{1,0:T(8,128)(2,1)S(1)}, bf16[16,2176]{1,0:T(8,128)(2,1)S(1)}, u32[]{:S(2)}, u32[]{:S(2)}) collective-permute-start(bf16[16,2176]{1,0:T(8,128)(2,1)S(1)} %pad_maximum_fusion.4), channel_id=1, source_target_pairs={{0,16},{4,20},{8,24},{12,28},{16,0},{20,4},{24,8},{28,12},{1,17},{... | collective-permute-start | bytes 208904 | tf_op jit(solution)/shard_map/ppermute | solution.py:267
  95.6 5.1 %collective-permute-start.6 = (bf16[32,2176]{1,0:T(8,128)(2,1)S(1)}, bf16[32,2176]{1,0:T(8,128)(2,1)S(1)}, u32[]{:S(2)}, u32[]{:S(2)}) collective-permute-start(bf16[32,2176]{1,0:T(8,128)(2,1)S(1)} %get-tuple-element.96), channel_id=1, source_target_pairs={{0,1},{1,0},{2,3},{3,2},{4,5},{5,4},{6,7},{7,6},{8,9},{9,8},{10,11... | collective-permute-start | bytes 417800 | tf_op jit(solution)/shard_map/ppermute | solution.py:267
  96.5 7.2 %collective-permute-start.18 = (bf16[32,2176]{1,0:T(8,128)(2,1)S(1)}, bf16[32,2176]{1,0:T(8,128)(2,1)S(1)}, u32[]{:S(2)}, u32[]{:S(2)}) collective-permute-start(bf16[32,2176]{1,0:T(8,128)(2,1)S(1)} %get-tuple-element.108), channel_id=1, source_target_pairs={{0,16},{4,20},{8,24},{12,28},{16,0},{20,4},{24,8},{28,12},{1,17},{... | collective-permute-start | bytes 417800 | tf_op jit(solution)/shard_map/ppermute | solution.py:267
  98.1 5.6 %collective-permute-start.19 = (bf16[32,2176]{1,0:T(8,128)(2,1)S(1)}, bf16[32,2176]{1,0:T(8,128)(2,1)S(1)}, u32[]{:S(2)}, u32[]{:S(2)}) collective-permute-start(bf16[32,2176]{1,0:T(8,128)(2,1)S(1)} %get-tuple-element.109), channel_id=1, source_target_pairs={{0,8},{4,12},{8,0},{12,4},{16,24},{20,28},{24,16},{28,20},{1,9},{5... | collective-permute-start | bytes 417800 | tf_op jit(solution)/shard_map/ppermute | solution.py:267
  98.6 6.0 %collective-permute-start.20 = (bf16[32,2176]{1,0:T(8,128)(2,1)S(1)}, bf16[32,2176]{1,0:T(8,128)(2,1)S(1)}, u32[]{:S(2)}, u32[]{:S(2)}) collective-permute-start(bf16[32,2176]{1,0:T(8,128)(2,1)S(1)} %get-tuple-element.110), channel_id=1, source_target_pairs={{0,24},{4,28},{8,16},{12,20},{16,8},{20,12},{24,0},{28,4},{1,25},{... | collective-permute-start | bytes 417800 | tf_op jit(solution)/shard_map/ppermute | solution.py:267
  100.1 12.5 %collective-permute-start.16 = (bf16[32,2176]{1,0:T(8,128)(2,1)S(1)}, bf16[32,2176]{1,0:T(8,128)(2,1)S(1)}, u32[]{:S(2)}, u32[]{:S(2)}) collective-permute-start(bf16[32,2176]{1,0:T(8,128)(2,1)S(1)} %pad_maximum_fusion.2), channel_id=1, source_target_pairs={{0,4},{4,0},{8,12},{12,8},{16,20},{20,16},{24,28},{28,24},{1,5},{5... | collective-permute-start | bytes 417800 | tf_op jit(solution)/shard_map/ppermute | solution.py:267
  100.8 7.3 %collective-permute-start.7 = (bf16[16,2176]{1,0:T(8,128)(2,1)S(1)}, bf16[16,2176]{1,0:T(8,128)(2,1)S(1)}, u32[]{:S(2)}, u32[]{:S(2)}) collective-permute-start(bf16[16,2176]{1,0:T(8,128)(2,1)S(1)} %get-tuple-element.99), channel_id=1, source_target_pairs={{0,2},{1,3},{2,0},{3,1},{4,6},{5,7},{6,4},{7,5},{8,10},{9,11},{10,... | collective-permute-start | bytes 208904 | tf_op jit(solution)/shard_map/ppermute | solution.py:267
  104.7 5.0 %collective-permute-start.21 = (bf16[16,2176]{1,0:T(8,128)(2,1)S(1)}, bf16[16,2176]{1,0:T(8,128)(2,1)S(1)}, u32[]{:S(2)}, u32[]{:S(2)}) collective-permute-start(bf16[16,2176]{1,0:T(8,128)(2,1)S(1)} %get-tuple-element.112), channel_id=1, source_target_pairs={{0,1},{1,0},{2,3},{3,2},{4,5},{5,4},{6,7},{7,6},{8,9},{9,8},{10,11... | collective-permute-start | bytes 208904 | tf_op jit(solution)/shard_map/ppermute | solution.py:267
  108.1 8.4 %collective-permute-start.8 = (bf16[16,2176]{1,0:T(8,128)(2,1)S(1)}, bf16[16,2176]{1,0:T(8,128)(2,1)S(1)}, u32[]{:S(2)}, u32[]{:S(2)}) collective-permute-start(bf16[16,2176]{1,0:T(8,128)(2,1)S(1)} %shard_map.62), channel_id=1, source_target_pairs={{0,16},{4,20},{8,24},{12,28},{16,0},{20,4},{24,8},{28,12},{1,17},{... | collective-permute-start | bytes 208904 | tf_op jit(solution)/shard_map/ppermute | solution.py:267
  109.7 5.3 %collective-permute-start.22 = (bf16[8,2176]{1,0:T(8,128)(2,1)S(1)}, bf16[8,2176]{1,0:T(8,128)(2,1)S(1)}, u32[]{:S(2)}, u32[]{:S(2)}) collective-permute-start(bf16[8,2176]{1,0:T(8,128)(2,1)S(1)} %get-tuple-element.114), channel_id=1, source_target_pairs={{0,2},{1,3},{2,0},{3,1},{4,6},{5,7},{6,4},{7,5},{8,10},{9,11},{10,... | collective-permute-start | bytes 104456 | tf_op jit(solution)/shard_map/ppermute | solution.py:267
  115.0 4.0 %collective-permute-start.23 = (bf16[8,2176]{1,0:T(8,128)(2,1)S(1)}, bf16[8,2176]{1,0:T(8,128)(2,1)S(1)}, u32[]{:S(2)}, u32[]{:S(2)}) collective-permute-start(bf16[8,2176]{1,0:T(8,128)(2,1)S(1)} %shard_map.69), channel_id=1, source_target_pairs={{0,8},{4,12},{8,0},{12,4},{16,24},{20,28},{24,16},{28,20},{1,9},{5... | collective-permute-start | bytes 104456 | tf_op jit(solution)/shard_map/ppermute | solution.py:267
  116.5 5.1 %collective-permute-start.9 = (bf16[32,2176]{1,0:T(8,128)(2,1)S(1)}, bf16[32,2176]{1,0:T(8,128)(2,1)S(1)}, u32[]{:S(2)}, u32[]{:S(2)}) collective-permute-start(bf16[32,2176]{1,0:T(8,128)(2,1)S(1)} %pad_maximum_fusion.1), channel_id=1, source_target_pairs={{0,8},{4,12},{8,0},{12,4},{16,24},{20,28},{24,16},{28,20},{1,9},{5... | collective-permute-start | bytes 417800 | tf_op jit(solution)/shard_map/ppermute | solution.py:267
  119.0 4.3 %collective-permute-start.24 = (bf16[16,2176]{1,0:T(8,128)(2,1)S(1)}, bf16[16,2176]{1,0:T(8,128)(2,1)S(1)}, u32[]{:S(2)}, u32[]{:S(2)}) collective-permute-start(bf16[16,2176]{1,0:T(8,128)(2,1)S(1)} %pad_maximum_fusion.5), channel_id=1, source_target_pairs={{0,16},{4,20},{8,24},{12,28},{16,0},{20,4},{24,8},{28,12},{1,17},{... | collective-permute-start | bytes 208904 | tf_op jit(solution)/shard_map/ppermute | solution.py:267
  121.7 1.8 %collective-permute-start.10 = (bf16[64,2176]{1,0:T(8,128)(2,1)S(1)}, bf16[64,2176]{1,0:T(8,128)(2,1)S(1)}, u32[]{:S(2)}, u32[]{:S(2)}) collective-permute-start(bf16[64,2176]{1,0:T(8,128)(2,1)S(1)} %pad_maximum_fusion), channel_id=1, source_target_pairs={{0,4},{4,0},{8,12},{12,8},{16,20},{20,16},{24,28},{28,24},{1,5},{5... | collective-permute-start | bytes 835592 | tf_op jit(solution)/shard_map/ppermute | solution.py:267
  123.4 1.4 %collective-permute-start.25 = (bf16[32,2176]{1,0:T(8,128)(2,1)S(1)}, bf16[32,2176]{1,0:T(8,128)(2,1)S(1)}, u32[]{:S(2)}, u32[]{:S(2)}) collective-permute-start(bf16[32,2176]{1,0:T(8,128)(2,1)S(1)} %pad_maximum_fusion.3), channel_id=1, source_target_pairs={{0,4},{4,0},{8,12},{12,8},{16,20},{20,16},{24,28},{28,24},{1,5},{5... | collective-permute-start | bytes 417800 | tf_op jit(solution)/shard_map/ppermute | solution.py:267

commit v6 on v5

--- a/solution.py
+++ b/solution.py
@@ -71,6 +71,14 @@
             own[to, :] = acc[pl.ds(pl.multiple_of((first + mine) * half, half), half), :]
             to = slice((c * n_col + z) * half, (c * n_col + z + 1) * half)
             sent[to, :] = acc[pl.ds(pl.multiple_of((first + 1 - mine) * half, half), half), :].astype(BF16)
+
+
+def deal(index, ways, each, size, source, base, outs, starts):
+    for flip, (out, start) in enumerate(zip(outs, starts)):
+        for g in range(each):
+            at = base + g * ways * size + (index ^ flip) * size
+            rows = source[pl.ds(pl.multiple_of(at, size), size), :]
+            out[start + g * size : start + (g + 1) * size, :] = rows.astype(out.dtype)
 
 
 def fetch_all(n_col, n_stripes, place, hbm, vmem, sems, in_sems):
@@ -111,9 +119,10 @@
     hand_out(n_col, place[0] // n_col % 2, acc, [kept], sent)
 
 
-def load_kernel(n_col, start, width, n_stripes, place, pairs, val, con_all, w_hbm, kept, sent, val_a, *refs):
+def load_kernel(n_col, start, width, n_stripes, place, pairs, val, con_all, w_hbm, kept, *refs):
+    sent, (val_a, *refs) = refs[: n_col - 1], refs[n_col - 1 :]
     w, refs = refs[:n_stripes], refs[n_stripes:]
-    density, hot1, hot2, val_b, pairs_here, val_here, con, rolled, sems, in_sems = refs
+    density, hot1, hot2, val_b, acc, pairs_here, val_here, con, rolled, sems, in_sems = refs
     inputs, stripes = fetch_all(n_col, n_stripes, place, (pairs, val, con_all, w_hbm), (pairs_here, val_here, con, w), sems, in_sems)
     inputs[0].wait()
     inputs[1].wait()
@@ -124,18 +133,12 @@
     build_val(groups(hot1, n_col, 0, 2 * width), groups(hot2, n_col, 0, 2 * width), val_here, val_a)
     inputs[2].wait()
     build_con(con, rolled, density)
-    high = place[0] % n_col % 2 == 1
     for s, fetch in enumerate(stripes):
         fetch.wait()
         stripe = w[s].shape[0]
-        at = slice(s * stripe, (s + 1) * stripe)
         t = lax.dot_general(val_b[...], w[s][...], CONTRACT_MINOR, preferred_element_type=F32)
-        for z in range(n_col // 2):
-            to = slice(z * width, (z + 1) * width)
-            low_part = t[2 * z * width : (2 * z + 1) * width, :]
-            high_part = t[(2 * z + 1) * width : (2 * z + 2) * width, :]
-            kept[to, at] = jnp.where(high, high_part, low_part)
-            sent[to, at] = jnp.where(high, low_part, high_part).astype(BF16)
+        acc[:, s * stripe : (s + 1) * stripe] = t
+    deal(place[0] % n_col, n_col, 1, width, acc, 0, [kept, *sent], [0] * n_col)
 
 
 def pair_kernel(n_col, n_stripes, n_after, place, *refs):
@@ -152,26 +155,54 @@
     hand_out(n_col, place[0] // n_col % 2, acc, kept, sent)
 
 
-def last_kernel(n_col, n_after, place, density, t, *refs):
-    kept, sent, acc = refs[n_after:]
-    acc[...] = lax.dot_general(t[...], density[...], CONTRACT_MINOR, preferred_element_type=F32)
-    hand_out(1, place[0] // n_col % 2, acc, [kept], sent)
-
-
-def begin_kernel(n_col, start, width, n_stripes, numbers, n_after, *refs):
-    w, refs = refs[:n_stripes], refs[n_stripes:]
-    (density, hot1, hot2, val), refs = refs[:4], refs[4:]
-    acc, val_density, *_ = refs[n_after:]
-    build_val(groups(hot1, n_col, start, width), groups(hot2, n_col, start, width), val, val_density)
-    acc[...] = product(numbers, w, density, val_density)
-
-
-def end_kernel(n_col, n_stripes, numbers, n_after, place, *refs):
-    w, refs = refs[:n_stripes], refs[n_stripes:]
-    (density, before, val_density), refs = refs[:3], refs[3:]
-    kept, sent, acc = *refs[n_after : n_after + 2], refs[-1]
-    acc[...] = before[...] + product(numbers, w, density, val_density)
-    hand_out(n_col, place[0] // n_col % 2, acc, [kept], sent)
+def val_kernel(n_col, start, width, n_after, hot1, hot2, val, *refs):
+    build_val(groups(hot1, n_col, start, width), groups(hot2, n_col, start, width), val, refs[n_after])
+
+
+def grid_kernel(n_stripes, n_after, *refs):
+    w, val_density, t = refs[:n_stripes], refs[n_stripes], refs[n_stripes + 1 + n_after]
+    stripe = w[0].shape[0]
+    for s in range(n_stripes):
+        part = lax.dot_general(val_density[...], w[s][...], CONTRACT_MINOR, preferred_element_type=F32)
+        t[:, s * stripe : (s + 1) * stripe] = part.astype(BF16)
+
+
+def con_kernel(n_col, place, density, t_m, t_b, kept_m, kept_b, sent, acc):
+    both = jnp.concatenate([t_m[...], t_b[...]])
+    acc[...] = lax.dot_general(both, density[...], CONTRACT_MINOR, preferred_element_type=F32)
+    mine = place[0] // n_col % 2
+    rows, size = t_m.shape[0], t_b.shape[0] // 2
+    deal(mine, 2, n_col, size, acc, 0, [kept_m, sent], [0, 0])
+    deal(mine, 2, 1, size, acc, rows, [kept_b, sent], [0, rows // 2])
+
+
+def spread_kernel(n_col, axis, bits, eaches, offsets, n_got, place, *refs):
+    n, ways = len(eaches), 1 << len(bits)
+    kept, got, refs = refs[:n], refs[n : n + n_got], refs[n + n_got :]
+    kept_out, sent, part = refs[:n], refs[n:-1], refs[-1]
+    me = place[0] // n_col if axis == "row" else place[0] % n_col
+    index = sum(((me >> bit) & 1) << (len(bits) - 1 - k) for k, bit in enumerate(bits))
+    to = 0
+    for c, (each, at) in enumerate(zip(eaches, offsets)):
+        rows = kept[c].shape[0]
+        total = kept[c][...]
+        for arrived in got:
+            total = total + arrived[at : at + rows, :].astype(F32)
+        part[0:rows, :] = total
+        deal(index, ways, each, rows // ways // each, part, 0, [kept_out[c], *sent], [0] + [to] * (ways - 1))
+        to += rows // ways
+
+
+def sum_kernel(offsets, *refs):
+    kept, got, out = refs[: len(offsets)], refs[len(offsets) : -1], refs[-1]
+    to = 0
+    for part, at in zip(kept, offsets):
+        rows = part.shape[0]
+        total = part[...]
+        for arrived in got:
+            total = total + arrived[at : at + rows, :].astype(F32)
+        out[to : to + rows, :] = total.astype(BF16)
+        to += rows
 
 
 def fold_kernel(n_col, targets, got_groups, sent_groups, place, *refs):
@@ -213,23 +244,6 @@
             other[to + z * half : to + (z + 1) * half, :] = jnp.where(high, low_part, high_part).astype(BF16)
 
 
-def quarter_kernel(n_col, bits, n_chunks, place, *refs):
-    kept, got, refs = refs[:n_chunks], refs[n_chunks], refs[n_chunks + 1 :]
-    kept_out, (*sent, part) = refs[:n_chunks], refs[n_chunks:]
-    me = place[0] // n_col
-    first, second = (me >> bits[0]) % 2, (me >> bits[1]) % 2
-    rows = kept[0].shape[0]
-    size = rows // 4 // n_col
-    for c in range(n_chunks):
-        part[...] = kept[c][...] + got[c * rows : (c + 1) * rows, :].astype(F32)
-        for flip, out in enumerate([kept_out[c], *sent]):
-            at = ((first + flip // 2) % 2 * 2 + (second + flip % 2) % 2) * size
-            base = c * n_col * size if flip else 0
-            for z in range(n_col):
-                mine = part[pl.ds(pl.multiple_of(z * 4 * size + at, size), size), :]
-                out[base + z * size : base + (z + 1) * size, :] = mine.astype(out.dtype)
-
-
 def hot_kernel(n_col, count, n_after, place, pairs, *refs):
     pick = refs[n_after]
     own = pick.shape[1]
@@ -248,8 +262,11 @@
 
 
 def pick_kernel(n_col, scale, gathers, place, pick, *refs):
-    arrays, (out, whole) = refs[: len(gathers)], refs[len(gathers) :]
+    arrays, (out, found, turned) = refs[: len(gathers)], refs[len(gathers) :]
     me = place[0] // n_col
+    whole = jnp.concatenate([array[...] for array in arrays])
+    found[...] = jnp.dot(whole, pick[...], preferred_element_type=F32) * scale
+    base = 0
     for array, (steps, chunks) in zip(arrays, gathers):
         each = sum(rows for _, rows, _ in chunks)
         for j in range(array.shape[0] // each):
@@ -258,9 +275,10 @@
             for start, rows, order in chunks:
                 spot = sum(((j >> bit) & 1) << (len(order) - 1 - s) for s, bit in enumerate(order))
                 to = start + spot * rows
-                whole[to : to + rows, :] = array[pl.ds(block * each + used, rows), :]
+                turned[to : to + rows, :] = found[pl.ds(base + block * each + used, rows), :]
                 used += rows
-    out[...] = (jnp.dot(whole[...].astype(BF16), pick[...], preferred_element_type=F32) * scale).T
+        base += array.shape[0]
+    out[...] = turned[...].T
 
 
 def swap(x, axis, bits, size):
@@ -293,11 +311,6 @@
         def params(mib):
             return pltpu.CompilerParams(vmem_limit_bytes=mib << 20)
 
-        def cost(n, rows):
-            return pl.CostEstimate(
-                flops=2 * n * rows * (own_columns + unordered), bytes_accessed=1 << 20, transcendentals=0
-            )
-
         def outs(rows):
             return [pltpu.VMEM((rows, unordered), F32), pltpu.VMEM((rows, unordered), BF16)]
 
@@ -328,79 +341,74 @@
                 name="single",
             )(*arguments)
 
+        def call(kernel, in_specs, out_shape, operands, after=(), scratch=(), aliases={}, mib=8, flops=0):
+            return pl.pallas_call(
+                kernel,
+                in_specs=in_specs + [anywhere] * len(after),
+                out_specs=[vmem] * len(out_shape),
+                out_shape=out_shape,
+                scratch_shapes=list(scratch),
+                input_output_aliases=aliases,
+                compiler_params=params(mib),
+                cost_estimate=pl.CostEstimate(flops=flops, bytes_accessed=1 << 20, transcendentals=0),
+            )(*operands, *after)
+
         def load():
-            kept, sent, val_density, *fixed = pl.pallas_call(
+            kept, *rest = call(
                 functools.partial(load_kernel, n_col, starts[3], width, n_stripes),
-                in_specs=[smem] + [hbm] * 4,
-                out_specs=[vmem] * (3 + n_held + 2),
-                out_shape=[
-                    pltpu.VMEM((n // 2, own_rows), F32),
-                    pltpu.VMEM((n // 2, own_rows), BF16),
-                    pltpu.VMEM((2 * n, own_columns), BF16),
-                    *held,
-                    *hots,
-                ],
-                scratch_shapes=[pltpu.VMEM((n, own_columns), BF16), *inputs],
-                compiler_params=params(10),
-                cost_estimate=cost(n, own_rows),
-                name="load",
-            )(*arguments)
-            return kept, sent, val_density, fixed
+                [smem] + [hbm] * 4,
+                [pltpu.VMEM((width, own_rows), F32)]
+                + [pltpu.VMEM((width, own_rows), BF16)] * (n_col - 1)
+                + [pltpu.VMEM((2 * n, own_columns), BF16), *held, *hots],
+                arguments,
+                scratch=[pltpu.VMEM((n, own_columns), BF16), pltpu.VMEM((n, own_rows), F32), *inputs],
+                mib=12,
+                flops=2 * n * own_rows * own_columns,
+            )
+            return kept, rest[: n_col - 1], rest[n_col - 1], rest[n_col : n_col + n_held], rest[n_col + n_held :]
 
         def pair(fixed, val_density, after):
-            *out, sent = pl.pallas_call(
+            out = call(
                 functools.partial(pair_kernel, n_col, n_stripes, len(after)),
-                in_specs=[smem] + [vmem] * (n_held + 1) + [anywhere] * len(after),
-                out_specs=[vmem] * (3 + n_held),
-                out_shape=[outs(n // 2)[0]] * 2 + [outs(n)[1]] + held,
-                scratch_shapes=[pltpu.VMEM((2 * n, unordered), F32)],
-                input_output_aliases={1 + i: 3 + i for i in range(n_held)},
-                compiler_params=params(12),
-                cost_estimate=cost(2 * n, own_rows),
-                name="pair",
-            )(place, *fixed[:n_held], val_density, *after), None
-            out = out[0]
-            return list(out[:2]), out[2], list(out[3:]) + fixed[n_held:]
-
-        def last(density, t, after):
-            rows = t.shape[0]
-            return pl.pallas_call(
-                functools.partial(last_kernel, n_col, len(after)),
-                in_specs=[smem] + [vmem] * 2 + [anywhere] * len(after),
-                out_specs=[vmem] * 2,
-                out_shape=outs(rows // 2),
-                scratch_shapes=[pltpu.VMEM((rows, unordered), F32)],
-                compiler_params=params(8),
-                cost_estimate=cost(rows, own_rows),
-                name="last",
-            )(place, density, t, *after)
-
-        def begin(k, numbers, fixed, after):
-            n = n_col * width
-            acc, val_density, *fixed = pl.pallas_call(
-                functools.partial(begin_kernel, n_col, starts[k], width, n_stripes, numbers, len(after)),
-                in_specs=[vmem] * (n_held + 3) + [anywhere] * len(after),
-                out_specs=[vmem] * (2 + n_held),
-                out_shape=[pltpu.VMEM((n, unordered), F32), pltpu.VMEM((n, own_columns), BF16)] + held,
-                input_output_aliases={i: 2 + i for i in range(n_held)},
-                compiler_params=params(7),
-                cost_estimate=cost(n, len(numbers) * stripe),
-            )(*fixed, val_orbitals, *after)
-            return (acc, val_density), fixed
-
-        def end(numbers, fixed, before, after):
-            n = n_col * width
-            kept, sent, *same = pl.pallas_call(
-                functools.partial(end_kernel, n_col, n_stripes, numbers, len(after)),
-                in_specs=[smem] + [vmem] * (n_held + 2) + [anywhere] * len(after),
-                out_specs=[vmem] * 3,
-                out_shape=outs(n // 2) + held[-1:],
-                scratch_shapes=[pltpu.VMEM((n, unordered), F32)],
-                input_output_aliases={n_held: 2},
-                compiler_params=params(7),
-                cost_estimate=cost(n, len(numbers) * stripe),
-            )(place, *fixed[:n_held], *before, *after)
-            return (kept, sent), same[0]
+                [smem] + [vmem] * (n_held + 1),
+                [outs(n // 2)[0]] * 2 + [outs(n)[1]] + held,
+                (place, *fixed, val_density),
+                after,
+                [pltpu.VMEM((2 * n, unordered), F32)],
+                {1 + i: 3 + i for i in range(n_held)},
+                12,
+                4 * n * own_rows * (own_columns + unordered),
+            )
+            return list(out[:2]), out[2], list(out[3:])
+
+        def scatter(sent, axis, bits):
+            got = []
+            for flip, x in enumerate(sent, 1):
+                mask = sum(((flip >> (len(bits) - 1 - k)) & 1) << bit for k, bit in enumerate(bits))
+                got.append(swap(x, axis, mask, mesh.shape[axis]))
+            return got
+
+        def spread(kept, got, axis, bits, eaches, offsets):
+            ways = 1 << len(bits)
+            rows = [k.shape[0] // ways for k in kept]
+            out = call(
+                functools.partial(spread_kernel, n_col, axis, bits, eaches, offsets, len(got)),
+                [smem] + [vmem] * (len(kept) + len(got)),
+                [pltpu.VMEM((r, unordered), F32) for r in rows] + [pltpu.VMEM((sum(rows), unordered), BF16)] * (ways - 1),
+                (place, *kept, *got),
+                scratch=[pltpu.VMEM((max(rows) * ways, unordered), F32)],
+                mib=6,
+            )
+            return list(out[: len(kept)]), list(out[len(kept) :])
+
+        def total(kept, got, offsets):
+            return call(
+                functools.partial(sum_kernel, offsets),
+                [vmem] * (len(kept) + len(got)),
+                [pltpu.VMEM((sum(k.shape[0] for k in kept), kept[0].shape[1]), BF16)],
+                (*kept, *got),
+                mib=6,
+            )[0]
 
         def fold(kept, got, targets, got_groups=None, sent_groups=None):
             everything = [list(range(len(kept)))]
@@ -419,29 +427,10 @@
             )(place, *kept, *got)
             return list(out[:n_kept]), list(out[n_kept:])
 
-        def quarters(kept, got, bits):
-            rows = kept[0].shape[0] // 4
-            out = pl.pallas_call(
-                functools.partial(quarter_kernel, n_col, bits, len(kept)),
-                in_specs=[smem] + [vmem] * (len(kept) + 1),
-                out_specs=[vmem] * (len(kept) + 3),
-                out_shape=[pltpu.VMEM((rows, unordered), F32)] * len(kept)
-                + [pltpu.VMEM((rows * len(kept), unordered), BF16)] * 3,
-                scratch_shapes=[pltpu.VMEM(kept[0].shape, F32)],
-                compiler_params=params(6),
-            )(place, *kept, got)
-            sent = list(out[len(kept) :])
-            flips = [1 << bits[1], 1 << bits[0], 1 << bits[0] | 1 << bits[1]]
-            got = [swap(x, "row", flip, n_row) for x, flip in zip(sent, flips)]
-            return list(out[: len(kept)]), got, sent
-
         order = list(range(1, row_bits))
         orders = [[0] + order for _ in range(chunks)]
-        col_steps = [("col", bit, n_col >> (bit + 1)) for bit in range(col_bits)]
         steps = [
-            [("row", bit, n_col) for bit in orders[k]] + col_steps + [None] if k < 3
-            else col_steps + [None] + [("row", bit, 1) for bit in orders[k]] + [None]
-            for k in range(chunks)
+            [("row", bit, n_col) for bit in orders[0]] + [("col", bit, n_col >> (bit + 1)) for bit in range(col_bits)] + [None]
         ]
         n_steps = row_bits + col_bits
         sizes = {"row": n_row, "col": n_col}
@@ -456,44 +445,57 @@
                 kept, (sent,) = fold(kept, [got], [steps[k][s + 1]] * len(kept))
             return kept, sent
 
-        def gather(part, bits):
-            for bit in bits:
-                part = jnp.concatenate([part, swap(part, "row", 1 << bit, n_row)])
-            return part.astype(F32)
+        def gather(part, steps):
+            for bits in steps:
+                flips = [1 << bits[0]] if len(bits) == 1 else [1 << bits[0], 1 << bits[1], 1 << bits[0] | 1 << bits[1]]
+                got = [swap(part, "row", flip, n_row) for flip in flips]
+                part = jnp.concatenate([part, *got])
+            return part
 
         if chunks > 1:
-            low, high = list(range(n_stripes // 2)), list(range(n_stripes // 2, n_stripes))
-            kept, b_sent, val_density, fixed = load()
-            b = [kept], b_sent
-            kept, sent, fixed = pair(fixed, val_density, [b_sent])
-            b = run(3, 0, 1, *b)
-            kept, a_got, a_sent = quarters(kept, send(0, 0, sent), orders[0][1:3])
-            before, fixed = begin(2, low, fixed, [b[1], *a_sent])
-            m, density = end(high, fixed, before, [])
-            m_kept, m_got, m_sent = quarters([m[0]], send(2, 0, m[1]), orders[2][1:3])
-            kept, (sent,) = fold(kept, a_got, [steps[0][3]] * 2, [[0, 1]] * 3)
-            b = run(3, 1, col_bits, *b)
-            b_kept, b_sent = last(density, b[1], [])
-            b = [b_kept], b_sent
-            when = [b_sent]
-            axis_steps = len(steps[3]) - 1
-            for s in range(col_bits + 1, axis_steps):
-                axis, bit, _ = steps[3][s]
-                got = swap(b[1], axis, 1 << bit, sizes[axis])
-                kept_b, (sent_b,) = fold(b[0], [got], [steps[3][s + 1]])
-                b = kept_b, sent_b
-            _, a_sums = run(0, 3, n_steps, kept, sent)
-            m_kept, m_sent = fold(m_kept, m_got, [steps[2][3]], [[0]] * 3)
-            _, m_sums = run(2, 3, n_steps, m_kept, m_sent[0])
-            up, down = order + [0], order[::-1] + [0]
-            arrays = [gather(a_sums, down), gather(b[1], up), gather(m_sums, up)]
-            gathers = [(down, [0, 1]), (up, [3]), (up, [2])]
+            cols = tuple(reversed(range(col_bits)))
+            half = n // 2
+            b_kept, b_sent, val_a, fixed, hot = load()
+            b_got = scatter(b_sent, "col", cols)
+            a_kept, a_sent, fixed = pair(fixed, val_a, b_sent)
+            a_got = [swap(a_sent, "row", 1, n_row)]
+            when = [a_sent]
+            val_m = call(
+                functools.partial(val_kernel, n_col, starts[2], width, 1), [vmem] * 3,
+                [pltpu.VMEM((n, own_columns), BF16)], (*hot, val_orbitals), when, mib=6,
+            )[0]
+            a_kept, a_sent = spread(a_kept, a_got, "row", tuple(order), [n_col] * 2, [0, half])
+            a_got = scatter(a_sent, "row", order)
+            t_m = call(
+                functools.partial(grid_kernel, n_stripes, len(a_sent)), [vmem] * (n_stripes + 1),
+                [pltpu.VMEM((n, own_rows), BF16)], (*fixed[:-1], val_m), a_sent, mib=8, flops=2 * n * own_rows * own_columns,
+            )[0]
+            t_b = total([b_kept], b_got, [0])
+            m_kept, b_kept, sent = call(
+                functools.partial(con_kernel, n_col), [smem] + [vmem] * 3,
+                [outs(half)[0], outs(width // 2)[0], outs(half + width // 2)[1]], (place, fixed[-1], t_m, t_b),
+                scratch=[pltpu.VMEM((n + width, unordered), F32)], mib=12, flops=2 * (n + width) * own_rows * unordered,
+            )
+            got = [swap(sent, "row", 1, n_row)]
+            (m_kept, b_kept), sent = spread([m_kept, b_kept], got, "row", tuple(order), [n_col, 1], [0, half])
+            mb_got = scatter(sent, "row", order)
+            a_kept, a_sent = spread(a_kept, a_got, "col", cols, [1, 1], [0, a_kept[0].shape[0]])
+            a_got = scatter(a_sent, "col", cols)
+            rows = m_kept.shape[0]
+            m_kept, m_sent = spread([m_kept], mb_got, "col", cols, [1], [0])
+            m_got = scatter(m_sent, "col", cols)
+            b_sums = total([b_kept], mb_got, [rows])
+            a_sums = total(a_kept, a_got, [0, a_kept[0].shape[0]])
+            m_sums = total(m_kept, m_got, [0])
+            square = [order, [0]]
+            arrays = [gather(jnp.concatenate([a_sums, b_sums]), square), gather(m_sums, square)]
+            gathers = [(order + [0], [0, 1, 3]), (order + [0], [2])]
         else:
             kept, sent = single()
             when = []
             _, late = run(0, 0, n_steps, [kept], sent)
             late_bits = order[::-1] + [0]
-            arrays, gathers = [gather(late, late_bits)], [(late_bits, [0])]
+            arrays, gathers = [gather(late, [[bit] for bit in late_bits])], [(late_bits, [0])]
         gathers = [(bits, [(starts[k], width // n_row, orders[k]) for k in ks]) for bits, ks in gathers]
 
         own = con_pairs.shape[0] // n_row
@@ -510,7 +512,7 @@
             in_specs=[smem] + [vmem] * (1 + len(arrays)),
             out_specs=vmem,
             out_shape=jax.ShapeDtypeStruct((own, per_col), F32),
-            scratch_shapes=[pltpu.VMEM((per_col, unordered), F32)],
+            scratch_shapes=[pltpu.VMEM((per_col, own), F32)] * 2,
             compiler_params=params(20),
             name="pick",
         )(place, pick, *arrays)

time: 127 us -> 129 us (1.016)
  local copies, waits for them, and re-layouts: 0.01 us -> 3.7 us
  Pallas kernels: 42.8 us -> 40.3 us
    unnamed x4 -> x20, local copies, waits for them, and re-layouts: 0.01 us -> 3.62 us
    pallas_call x18 -> x13, Pallas kernels: 40.6 us -> 38.2 us  [call(): pl.pallas_call(kernel, in_specs=in_specs + [anywhere] * len(after), out_s...]
    ppermute x26 -> x25, waiting for transfers between devices: 51 us -> 51.9 us  [swap(): return lax.ppermute(x, axis, [(i, i ^ bits) for i in range(size)])]
    ppermute x26 -> x25, starting transfers between devices: 32.4 us -> 32.8 us  [swap(): return lax.ppermute(x, axis, [(i, i ^ bits) for i in range(size)])]
  transfers between devices with their start and end apart: 26 -> 25, of which waited for: 16 -> 15; matrix products, arithmetic and copies ran while one was open for 0% -> 0% of each run, Pallas kernels for 1% -> 2%
where the time goes in v6:
time: 129 us
  waiting for transfers between devices  51.9 us (40%)
  Pallas kernels  40.3 us (31%)
  starting transfers between devices  32.8 us (25%)
  local copies, waits for them, and re-layouts  3.7 us (3%)
    ppermute x25, waiting for transfers between devices, swap(): return lax.ppermute(x, axis, [(i, i ^ bits) for i in range(size)])  51.9 us
    pallas_call x13, Pallas kernels, call(): pl.pallas_call(kernel, in_specs=in_specs + [anywhere] * len(after), out_s...  38.2 us
    ppermute x25, starting transfers between devices, swap(): return lax.ppermute(x, axis, [(i, i ^ bits) for i in range(size)])  32.8 us
    unnamed x20, local copies, waits for them, and re-layouts  3.62 us
  transfers between devices with their start and end apart: 25, of which 15 were waited for; matrix products, arithmetic and copies ran while one was open for 0% of the time, Pallas kernels for 2%

profile of v6, /device:TPU:0, one launch (start us, length us, event | category | flops | bytes accessed | tf_op | source)
XLA Modules:
  0.0 129.1 jit_solution(14967342638210329580)
XLA Ops:
  0.0 11.8 %shard_map.55 = (f32[64,2048]{1,0:T(8,128)S(1)}, bf16[64,2048]{1,0:T(8,128)(2,1)S(1)}, bf16[64,2048]{1,0:T(8,128)(2,1)S(1)}, bf16[64,2048]{1,0:T(8,128)(2,1)S(1)...) custom-call(s32[1]{0:T(128)} %bitcast.place, ...), custom_call_target="tpu_custom_call" | custom-call | flops 4294967296 | bytes 1048576 | tf_op jit(solution)/shard_map/pallas_call | solution.py:345
  11.8 0.0 copy-start
  11.8 15.7 %shard_map.56 = (f32[128,2176]{1,0:T(8,128)S(1)}, f32[128,2176]{1,0:T(8,128)S(1)}, bf16[256,2176]{1,0:T(8,128)(2,1)S(1)}, bf16[512,4096]{1,0:T(8,128)(2,1)S(1)},...) custom-call(s32[1]{0:T(128)} %bitcast.place, ...), custom_call_target="tpu_custom_call", output_to_operand_aliasing={{3}: (1, {}), {4}: (2, {}), {5}: (3, {}), {6}: (4, {}), {7}... | custom-call | flops 13153337344 | bytes 1048576 | tf_op jit(solution)/shard_map/pallas_call | solution.py:345
  27.5 3.5 %copy-done.2 = bf16[2176,2048]{1,0:T(8,128)(2,1)} copy-done((bf16[2176,2048]{1,0:T(8,128)(2,1)}, bf16[2176,2048]{1,0:T(8,128)(2,1)S(1)}, u32[]{:S(2)}) %copy-start.2) | copy-done | bytes 8912920
  31.0 0.5 collective-permute-start
  31.5 2.6 %collective-permute-start.7 = (bf16[64,2048]{1,0:T(8,128)(2,1)S(1)}, bf16[64,2048]{1,0:T(8,128)(2,1)S(1)}, u32[]{:S(2)}, u32[]{:S(2)}) collective-permute-start(bf16[64,2048]{1,0:T(8,128)(2,1)S(1)} %get-tuple-element.53.refs_6_), channel_id=1, source_target_pairs={{0,1},{1,0},{2,3},{3,2},{4,5},{5,4},{6,7},{7,6},{8,9},{9,8},{10,11... | collective-permute-start | bytes 786440 | tf_op jit(solution)/shard_map/ppermute | solution.py:285
  34.0 2.6 %collective-permute-start.8 = (bf16[64,2048]{1,0:T(8,128)(2,1)S(1)}, bf16[64,2048]{1,0:T(8,128)(2,1)S(1)}, u32[]{:S(2)}, u32[]{:S(2)}) collective-permute-start(bf16[64,2048]{1,0:T(8,128)(2,1)S(1)} %get-tuple-element.54.refs_7_), channel_id=1, source_target_pairs={{0,2},{1,3},{2,0},{3,1},{4,6},{5,7},{6,4},{7,5},{8,10},{9,11},{10,... | collective-permute-start | bytes 786440 | tf_op jit(solution)/shard_map/ppermute | solution.py:285
  36.6 1.4 %shard_map.60.refs_4_ = bf16[256,4096]{1,0:T(8,128)(2,1)S(1)} custom-call(bf16[1024,45]{1,0:T(8,128)(2,1)S(1)} %get-tuple-element.74.hot1, bf16[1024,45]{1,0:T(8,128)(2,1)S(1)} %get-tuple-element.75.hot2, bf16[45,4096]{1,0:T(8,128)(2,1)S(1)} %copy-done, bf16[256,2176]{1,0:T(8,128)(2,1)S(1)} %get-tuple-element.56.refs_0_), custom_call_target="tpu_custom_call" | custom-call | bytes 1048576 | tf_op jit(solution)/shard_map/pallas_call | solution.py:345
  38.0 8.2 %collective-permute-done.7.refs_1_ = bf16[64,2048]{1,0:T(8,128)(2,1)S(1)} collective-permute-done((bf16[64,2048]{1,0:T(8,128)(2,1)S(1)}, bf16[64,2048]{1,0:T(8,128)(2,1)S(1)}, u32[]{:S(2)}, u32[]{:S(2)}) %collective-permute-start.7) | collective-permute-done | bytes 262176 | tf_op jit(solution)/shard_map/ppermute | solution.py:285
  46.2 9.2 %collective-permute-done.8.refs_2_ = bf16[64,2048]{1,0:T(8,128)(2,1)S(1)} collective-permute-done((bf16[64,2048]{1,0:T(8,128)(2,1)S(1)}, bf16[64,2048]{1,0:T(8,128)(2,1)S(1)}, u32[]{:S(2)}, u32[]{:S(2)}) %collective-permute-start.8) | collective-permute-done | bytes 262176 | tf_op jit(solution)/shard_map/ppermute | solution.py:285
  55.4 0.0 collective-permute-done.9.refs_3_
  55.4 0.1 shard_map.62.t_b
  55.5 0.0 collective-permute-done.refs_2_
  55.5 0.0 slice-start
  55.5 0.5 shard_map.57
  56.0 0.0 slice-start.2
  56.0 4.5 %shard_map.61.t_m = bf16[256,2048]{1,0:T(8,128)(2,1)S(1)} custom-call(bf16[512,4096]{1,0:T(8,128)(2,1)S(1)} %get-tuple-element.70.refs_0_, bf16[512,4096]{1,0:T(8,128)(2,1)S(1)} %get-tuple-element.71.refs_1_, bf16[512,4096]{1,0:T(8,128)(2,1)S(1)} %get-tuple-element.72.refs_2_, bf16[512,4096]{1,0:T(8,128)(2,1)S(1)} %get-tuple-element.73.refs_3_, ...), custom_call_target="tpu_custom_call" | custom-call | flops 4294967296 | bytes 1048576 | tf_op jit(solution)/shard_map/pallas_call | solution.py:345
  60.6 0.0 copy-start.1
  60.6 3.6 %shard_map.63 = (f32[128,2176]{1,0:T(8,128)S(1)}, f32[32,2176]{1,0:T(8,128)S(1)}, bf16[160,2176]{1,0:T(8,128)(2,1)S(1)}) custom-call(s32[1]{0:T(128)} %bitcast.place, bf16[2176,2048]{1,0:T(8,128)(2,1)S(1)} %bitcast.5, bf16[256,2048]{1,0:T(8,128)(2,1)S(1)} %shard_map.61.t_m, bf16[64,2048]{1,0:T(8,128)(2,1)S(1)} %shard_map.62.t_b), custom_call_target="tpu_custom_call" | custom-call | flops 2852126720 | bytes 1048576 | tf_op jit(solution)/shard_map/pallas_call | solution.py:345
  64.1 0.1 collective-permute-start.10
  64.2 1.6 %collective-permute-start.1 = (bf16[64,2176]{1,0:T(8,128)(2,1)S(1)}, bf16[64,2176]{1,0:T(8,128)(2,1)S(1)}, u32[]{:S(2)}, u32[]{:S(2)}) collective-permute-start(bf16[64,2176]{1,0:T(8,128)(2,1)S(1)} %get-tuple-element.61.refs_5_), channel_id=1, source_target_pairs={{0,16},{4,20},{8,24},{12,28},{16,0},{20,4},{24,8},{28,12},{1,17},{... | collective-permute-start | bytes 835592 | tf_op jit(solution)/shard_map/ppermute | solution.py:285
  65.8 1.5 %collective-permute-start.2 = (bf16[64,2176]{1,0:T(8,128)(2,1)S(1)}, bf16[64,2176]{1,0:T(8,128)(2,1)S(1)}, u32[]{:S(2)}, u32[]{:S(2)}) collective-permute-start(bf16[64,2176]{1,0:T(8,128)(2,1)S(1)} %get-tuple-element.62.refs_6_), channel_id=1, source_target_pairs={{0,8},{4,12},{8,0},{12,4},{16,24},{20,28},{24,16},{28,20},{1,9},{5... | collective-permute-start | bytes 835592 | tf_op jit(solution)/shard_map/ppermute | solution.py:285
  67.3 0.5 collective-permute-start.3
  67.8 5.5 %collective-permute-done.1.refs_2_ = bf16[64,2176]{1,0:T(8,128)(2,1)S(1)} collective-permute-done((bf16[64,2176]{1,0:T(8,128)(2,1)S(1)}, bf16[64,2176]{1,0:T(8,128)(2,1)S(1)}, u32[]{:S(2)}, u32[]{:S(2)}) %collective-permute-start.1) | collective-permute-done | bytes 278560 | tf_op jit(solution)/shard_map/ppermute | solution.py:285
  73.3 2.1 %collective-permute-done.2.refs_3_ = bf16[64,2176]{1,0:T(8,128)(2,1)S(1)} collective-permute-done((bf16[64,2176]{1,0:T(8,128)(2,1)S(1)}, bf16[64,2176]{1,0:T(8,128)(2,1)S(1)}, u32[]{:S(2)}, u32[]{:S(2)}) %collective-permute-start.2) | collective-permute-done | bytes 278560 | tf_op jit(solution)/shard_map/ppermute | solution.py:285
  75.4 5.1 %collective-permute-done.3.refs_4_ = bf16[64,2176]{1,0:T(8,128)(2,1)S(1)} collective-permute-done((bf16[64,2176]{1,0:T(8,128)(2,1)S(1)}, bf16[64,2176]{1,0:T(8,128)(2,1)S(1)}, u32[]{:S(2)}, u32[]{:S(2)}) %collective-permute-start.3) | collective-permute-done | bytes 278560 | tf_op jit(solution)/shard_map/ppermute | solution.py:285
  80.4 0.2 shard_map.58
  80.6 5.5 %collective-permute-start.4 = (bf16[16,2176]{1,0:T(8,128)(2,1)S(1)}, bf16[16,2176]{1,0:T(8,128)(2,1)S(1)}, u32[]{:S(2)}, u32[]{:S(2)}) collective-permute-start(bf16[16,2176]{1,0:T(8,128)(2,1)S(1)} %get-tuple-element.66), channel_id=1, source_target_pairs={{0,1},{1,0},{2,3},{3,2},{4,5},{5,4},{6,7},{7,6},{8,9},{9,8},{10,11... | collective-permute-start | bytes 208904 | tf_op jit(solution)/shard_map/ppermute | solution.py:285
  86.1 1.1 collective-permute-start.5
  87.2 1.4 %collective-permute-start.6 = (bf16[16,2176]{1,0:T(8,128)(2,1)S(1)}, bf16[16,2176]{1,0:T(8,128)(2,1)S(1)}, u32[]{:S(2)}, u32[]{:S(2)}) collective-permute-start(bf16[16,2176]{1,0:T(8,128)(2,1)S(1)} %get-tuple-element.68), channel_id=1, source_target_pairs={{0,3},{1,2},{2,1},{3,0},{4,7},{5,6},{6,5},{7,4},{8,11},{9,10},{10,... | collective-permute-start | bytes 208904 | tf_op jit(solution)/shard_map/ppermute | solution.py:285
  88.6 0.4 hot.1.pick
  89.0 0.0 collective-permute-done.4.refs_2_
  89.1 4.8 %collective-permute-done.5.refs_3_ = bf16[16,2176]{1,0:T(8,128)(2,1)S(1)} collective-permute-done((bf16[16,2176]{1,0:T(8,128)(2,1)S(1)}, bf16[16,2176]{1,0:T(8,128)(2,1)S(1)}, u32[]{:S(2)}, u32[]{:S(2)}) %collective-permute-start.5) | collective-permute-done | bytes 69664 | tf_op jit(solution)/shard_map/ppermute | solution.py:285
  93.9 0.0 collective-permute-done.10.refs_2_
  93.9 0.3 shard_map.64
  94.2 1.6 %collective-permute-start.11 = (bf16[40,2176]{1,0:T(8,128)(2,1)S(1)}, bf16[40,2176]{1,0:T(8,128)(2,1)S(1)}, u32[]{:S(2)}, u32[]{:S(2)}) collective-permute-start(bf16[40,2176]{1,0:T(8,128)(2,1)S(1)} %get-tuple-element.81), channel_id=1, source_target_pairs={{0,16},{4,20},{8,24},{12,28},{16,0},{20,4},{24,8},{28,12},{1,17},{... | collective-permute-start | bytes 522248 | tf_op jit(solution)/shard_map/ppermute | solution.py:285
  95.8 1.5 %collective-permute-start.12 = (bf16[40,2176]{1,0:T(8,128)(2,1)S(1)}, bf16[40,2176]{1,0:T(8,128)(2,1)S(1)}, u32[]{:S(2)}, u32[]{:S(2)}) collective-permute-start(bf16[40,2176]{1,0:T(8,128)(2,1)S(1)} %get-tuple-element.82), channel_id=1, source_target_pairs={{0,8},{4,12},{8,0},{12,4},{16,24},{20,28},{24,16},{28,20},{1,9},{5... | collective-permute-start | bytes 522248 | tf_op jit(solution)/shard_map/ppermute | solution.py:285
  97.3 0.5 collective-permute-start.13
  97.8 3.8 %collective-permute-done.11.refs_1_ = bf16[40,2176]{1,0:T(8,128)(2,1)S(1)} collective-permute-done((bf16[40,2176]{1,0:T(8,128)(2,1)S(1)}, bf16[40,2176]{1,0:T(8,128)(2,1)S(1)}, u32[]{:S(2)}, u32[]{:S(2)}) %collective-permute-start.11) | collective-permute-done | bytes 174112 | tf_op jit(solution)/shard_map/ppermute | solution.py:285
  101.6 0.4 collective-permute-done.12.refs_2_
  102.0 2.1 %collective-permute-done.13.refs_3_ = bf16[40,2176]{1,0:T(8,128)(2,1)S(1)} collective-permute-done((bf16[40,2176]{1,0:T(8,128)(2,1)S(1)}, bf16[40,2176]{1,0:T(8,128)(2,1)S(1)}, u32[]{:S(2)}, u32[]{:S(2)}) %collective-permute-start.13) | collective-permute-done | bytes 174112 | tf_op jit(solution)/shard_map/ppermute | solution.py:285
  104.1 2.3 %collective-permute-start.16 = (bf16[24,2176]{1,0:T(8,128)(2,1)S(1)}, bf16[24,2176]{1,0:T(8,128)(2,1)S(1)}, u32[]{:S(2)}, u32[]{:S(2)}) collective-permute-start(bf16[24,2176]{1,0:T(8,128)(2,1)S(1)} %pad_maximum_fusion.1), channel_id=1, source_target_pairs={{0,24},{4,28},{8,16},{12,20},{16,8},{20,12},{24,0},{28,4},{1,25},{... | collective-permute-start | bytes 313352 | tf_op jit(solution)/shard_map/ppermute | solution.py:285
  106.3 0.5 collective-permute-start.15
  106.8 0.1 shard_map.66
  106.9 1.8 %collective-permute-start.18 = (bf16[8,2176]{1,0:T(8,128)(2,1)S(1)}, bf16[8,2176]{1,0:T(8,128)(2,1)S(1)}, u32[]{:S(2)}, u32[]{:S(2)}) collective-permute-start(bf16[8,2176]{1,0:T(8,128)(2,1)S(1)} %get-tuple-element.86), channel_id=1, source_target_pairs={{0,1},{1,0},{2,3},{3,2},{4,5},{5,4},{6,7},{7,6},{8,9},{9,8},{10,11... | collective-permute-start | bytes 104456 | tf_op jit(solution)/shard_map/ppermute | solution.py:285
  108.7 1.4 %collective-permute-start.19 = (bf16[8,2176]{1,0:T(8,128)(2,1)S(1)}, bf16[8,2176]{1,0:T(8,128)(2,1)S(1)}, u32[]{:S(2)}, u32[]{:S(2)}) collective-permute-start(bf16[8,2176]{1,0:T(8,128)(2,1)S(1)} %get-tuple-element.87), channel_id=1, source_target_pairs={{0,2},{1,3},{2,0},{3,1},{4,6},{5,7},{6,4},{7,5},{8,10},{9,11},{10,... | collective-permute-start | bytes 104456 | tf_op jit(solution)/shard_map/ppermute | solution.py:285
  110.0 1.4 %collective-permute-start.20 = (bf16[8,2176]{1,0:T(8,128)(2,1)S(1)}, bf16[8,2176]{1,0:T(8,128)(2,1)S(1)}, u32[]{:S(2)}, u32[]{:S(2)}) collective-permute-start(bf16[8,2176]{1,0:T(8,128)(2,1)S(1)} %get-tuple-element.88), channel_id=1, source_target_pairs={{0,3},{1,2},{2,1},{3,0},{4,7},{5,6},{6,5},{7,4},{8,11},{9,10},{10,... | collective-permute-start | bytes 104456 | tf_op jit(solution)/shard_map/ppermute | solution.py:285
  111.4 0.0 collective-permute-done.18.refs_1_
  111.4 2.5 %collective-permute-done.19.refs_2_ = bf16[8,2176]{1,0:T(8,128)(2,1)S(1)} collective-permute-done((bf16[8,2176]{1,0:T(8,128)(2,1)S(1)}, bf16[8,2176]{1,0:T(8,128)(2,1)S(1)}, u32[]{:S(2)}, u32[]{:S(2)}) %collective-permute-start.19) | collective-permute-done | bytes 34848 | tf_op jit(solution)/shard_map/ppermute | solution.py:285
  113.9 1.9 %collective-permute-done.20.refs_3_ = bf16[8,2176]{1,0:T(8,128)(2,1)S(1)} collective-permute-done((bf16[8,2176]{1,0:T(8,128)(2,1)S(1)}, bf16[8,2176]{1,0:T(8,128)(2,1)S(1)}, u32[]{:S(2)}, u32[]{:S(2)}) %collective-permute-start.20) | collective-permute-done | bytes 34848 | tf_op jit(solution)/shard_map/ppermute | solution.py:285
  115.8 1.5 %collective-permute-start.23 = (bf16[8,2176]{1,0:T(8,128)(2,1)S(1)}, bf16[8,2176]{1,0:T(8,128)(2,1)S(1)}, u32[]{:S(2)}, u32[]{:S(2)}) collective-permute-start(bf16[8,2176]{1,0:T(8,128)(2,1)S(1)} %shard_map.67), channel_id=1, source_target_pairs={{0,24},{4,28},{8,16},{12,20},{16,8},{20,12},{24,0},{28,4},{1,25},{... | collective-permute-start | bytes 104456 | tf_op jit(solution)/shard_map/ppermute | solution.py:285
  117.3 1.1 collective-permute-start.22
  118.4 1.0 collective-permute-start.21
  119.4 1.3 %collective-permute-done.23 = bf16[8,2176]{1,0:T(8,128)(2,1)S(1)} collective-permute-done((bf16[8,2176]{1,0:T(8,128)(2,1)S(1)}, bf16[8,2176]{1,0:T(8,128)(2,1)S(1)}, u32[]{:S(2)}, u32[]{:S(2)}) %collective-permute-start.23) | collective-permute-done | bytes 34848 | tf_op jit(solution)/shard_map/ppermute | solution.py:285
  120.7 1.1 collective-permute-start.14
  121.8 0.0 collective-permute-done.22
  121.8 0.6 collective-permute-done.21
  122.4 0.1 collective-permute-start.24
  122.5 2.9 %collective-permute-done.14 = bf16[24,2176]{1,0:T(8,128)(2,1)S(1)} collective-permute-done((bf16[24,2176]{1,0:T(8,128)(2,1)S(1)}, bf16[24,2176]{1,0:T(8,128)(2,1)S(1)}, u32[]{:S(2)}, u32[]{:S(2)}) %collective-permute-start.14) | collective-permute-done | bytes 104480 | tf_op jit(solution)/shard_map/ppermute | solution.py:285
  125.4 0.0 collective-permute-done.15
  125.5 0.0 collective-permute-done.16
  125.5 0.1 collective-permute-start.17
  125.6 1.7 %collective-permute-done.17 = bf16[96,2176]{1,0:T(8,128)(2,1)S(1)} collective-permute-done((bf16[96,2176]{1,0:T(8,128)(2,1)S(1)}, bf16[96,2176]{1,0:T(8,128)(2,1)S(1)}, u32[]{:S(2)}, u32[]{:S(2)}) %collective-permute-start.17) | collective-permute-done | bytes 417824 | tf_op jit(solution)/shard_map/ppermute | solution.py:285
  127.4 1.8 %pick.1 = f32[512,256]{1,0:T(8,128)} custom-call(s32[1]{0:T(128)} %bitcast.place, bf16[2176,512]{1,0:T(8,128)(2,1)S(1)} %hot.1.pick, bf16[192,2176]{1,0:T(8,128)(2,1)S(1)} %constant_dynamic-update-slice_fusion.5.refs_0_, bf16[64,2176]{1,0:T(8,128)(2,1)S(1)} %constant_dynamic-update-slice_fusion.11.refs_1_), custom_call_target="tpu_custom_call" | custom-call | tf_op jit(solution)/shard_map/pick/pallas_call | solution.py:510
  (27 shorter events, 0.3 us)
Async XLA Ops:
  11.8 24.9 %copy-start = (bf16[45,4096]{1,0:T(8,128)(2,1)S(1)}, bf16[45,4096]{1,0:T(8,128)(2,1)}, u32[]{:S(2)}) copy-start(bf16[45,4096]{1,0:T(8,128)(2,1)} %val.3) | copy-start | bytes 1105924
  27.5 3.5 %copy-start.2 = (bf16[2176,2048]{1,0:T(8,128)(2,1)}, bf16[2176,2048]{1,0:T(8,128)(2,1)S(1)}, u32[]{:S(2)}) copy-start(bf16[2176,2048]{1,0:T(8,128)(2,1)S(1)} %get-tuple-element.69.density) | copy-start | bytes 26738692
  31.0 24.5 %collective-permute-start = (bf16[256,2176]{1,0:T(8,128)(2,1)S(1)}, bf16[256,2176]{1,0:T(8,128)(2,1)S(1)}, u32[]{:S(2)}, u32[]{:S(2)}) collective-permute-start(bf16[256,2176]{1,0:T(8,128)(2,1)S(1)} %get-tuple-element.56.refs_0_), channel_id=1, source_target_pairs={{0,4},{4,0},{8,12},{12,8},{16,20},{20,16},{24,28},{28,24},{1,5},{5... | collective-permute-start | bytes 3342344 | tf_op jit(solution)/shard_map/ppermute | solution.py:285
  31.5 14.7 %collective-permute-start.7 = (bf16[64,2048]{1,0:T(8,128)(2,1)S(1)}, bf16[64,2048]{1,0:T(8,128)(2,1)S(1)}, u32[]{:S(2)}, u32[]{:S(2)}) collective-permute-start(bf16[64,2048]{1,0:T(8,128)(2,1)S(1)} %get-tuple-element.53.refs_6_), channel_id=1, source_target_pairs={{0,1},{1,0},{2,3},{3,2},{4,5},{5,4},{6,7},{7,6},{8,9},{9,8},{10,11... | collective-permute-start | bytes 786440 | tf_op jit(solution)/shard_map/ppermute | solution.py:285
  34.0 21.4 %collective-permute-start.8 = (bf16[64,2048]{1,0:T(8,128)(2,1)S(1)}, bf16[64,2048]{1,0:T(8,128)(2,1)S(1)}, u32[]{:S(2)}, u32[]{:S(2)}) collective-permute-start(bf16[64,2048]{1,0:T(8,128)(2,1)S(1)} %get-tuple-element.54.refs_7_), channel_id=1, source_target_pairs={{0,2},{1,3},{2,0},{3,1},{4,6},{5,7},{6,4},{7,5},{8,10},{9,11},{10,... | collective-permute-start | bytes 786440 | tf_op jit(solution)/shard_map/ppermute | solution.py:285
  36.6 18.8 %collective-permute-start.9 = (bf16[64,2048]{1,0:T(8,128)(2,1)S(1)}, bf16[64,2048]{1,0:T(8,128)(2,1)S(1)}, u32[]{:S(2)}, u32[]{:S(2)}) collective-permute-start(bf16[64,2048]{1,0:T(8,128)(2,1)S(1)} %get-tuple-element.55.refs_8_), channel_id=1, source_target_pairs={{0,3},{1,2},{2,1},{3,0},{4,7},{5,6},{6,5},{7,4},{8,11},{9,10},{10,... | collective-permute-start | bytes 786440 | tf_op jit(solution)/shard_map/ppermute | solution.py:285
  55.5 5.0 %slice-start = ((s8[8912896]{0:T(1024)(128)(4,1)}), s8[4194304]{0:T(1024)(128)(4,1)S(1)}, s32[]{:S(2)}) async-start(s8[8912896]{0:T(1024)(128)(4,1)} %bitcast.4), calls=%async_computation | async-start | bytes 8388608
  56.0 4.6 %slice-start.1 = ((s8[8912896]{0:T(1024)(128)(4,1)}), s8[4194304]{0:T(1024)(128)(4,1)S(1)}, s32[]{:S(2)}) async-start(s8[8912896]{0:T(1024)(128)(4,1)} %bitcast.4), calls=%async_computation.1 | async-start | bytes 8388608
  56.0 4.6 %slice-start.2 = ((s8[8912896]{0:T(1024)(128)(4,1)}), s8[524288]{0:T(1024)(128)(4,1)S(1)}, s32[]{:S(2)}) async-start(s8[8912896]{0:T(1024)(128)(4,1)} %bitcast.4), calls=%async_computation.2 | async-start | bytes 1048576
  60.6 28.1 %copy-start.1 = (s32[4096,2]{0,1:T(2,128)S(1)}, s32[4096,2]{0,1:T(2,128)}, u32[]{:S(2)}) copy-start(s32[4096,2]{0,1:T(2,128)} %param.9) | copy-start | bytes 98308
  64.1 29.8 %collective-permute-start.10 = (bf16[160,2176]{1,0:T(8,128)(2,1)S(1)}, bf16[160,2176]{1,0:T(8,128)(2,1)S(1)}, u32[]{:S(2)}, u32[]{:S(2)}) collective-permute-start(bf16[160,2176]{1,0:T(8,128)(2,1)S(1)} %get-tuple-element.79), channel_id=1, source_target_pairs={{0,4},{4,0},{8,12},{12,8},{16,20},{20,16},{24,28},{28,24},{1,5},{5... | collective-permute-start | bytes 2088968 | tf_op jit(solution)/shard_map/ppermute | solution.py:285
  64.2 9.1 %collective-permute-start.1 = (bf16[64,2176]{1,0:T(8,128)(2,1)S(1)}, bf16[64,2176]{1,0:T(8,128)(2,1)S(1)}, u32[]{:S(2)}, u32[]{:S(2)}) collective-permute-start(bf16[64,2176]{1,0:T(8,128)(2,1)S(1)} %get-tuple-element.61.refs_5_), channel_id=1, source_target_pairs={{0,16},{4,20},{8,24},{12,28},{16,0},{20,4},{24,8},{28,12},{1,17},{... | collective-permute-start | bytes 835592 | tf_op jit(solution)/shard_map/ppermute | solution.py:285
  65.8 9.5 %collective-permute-start.2 = (bf16[64,2176]{1,0:T(8,128)(2,1)S(1)}, bf16[64,2176]{1,0:T(8,128)(2,1)S(1)}, u32[]{:S(2)}, u32[]{:S(2)}) collective-permute-start(bf16[64,2176]{1,0:T(8,128)(2,1)S(1)} %get-tuple-element.62.refs_6_), channel_id=1, source_target_pairs={{0,8},{4,12},{8,0},{12,4},{16,24},{20,28},{24,16},{28,20},{1,9},{5... | collective-permute-start | bytes 835592 | tf_op jit(solution)/shard_map/ppermute | solution.py:285
  67.3 13.1 %collective-permute-start.3 = (bf16[64,2176]{1,0:T(8,128)(2,1)S(1)}, bf16[64,2176]{1,0:T(8,128)(2,1)S(1)}, u32[]{:S(2)}, u32[]{:S(2)}) collective-permute-start(bf16[64,2176]{1,0:T(8,128)(2,1)S(1)} %get-tuple-element.63.refs_7_), channel_id=1, source_target_pairs={{0,24},{4,28},{8,16},{12,20},{16,8},{20,12},{24,0},{28,4},{1,25},{... | collective-permute-start | bytes 835592 | tf_op jit(solution)/shard_map/ppermute | solution.py:285
  80.6 8.4 %collective-permute-start.4 = (bf16[16,2176]{1,0:T(8,128)(2,1)S(1)}, bf16[16,2176]{1,0:T(8,128)(2,1)S(1)}, u32[]{:S(2)}, u32[]{:S(2)}) collective-permute-start(bf16[16,2176]{1,0:T(8,128)(2,1)S(1)} %get-tuple-element.66), channel_id=1, source_target_pairs={{0,1},{1,0},{2,3},{3,2},{4,5},{5,4},{6,7},{7,6},{8,9},{9,8},{10,11... | collective-permute-start | bytes 208904 | tf_op jit(solution)/shard_map/ppermute | solution.py:285
  86.1 7.7 %collective-permute-start.5 = (bf16[16,2176]{1,0:T(8,128)(2,1)S(1)}, bf16[16,2176]{1,0:T(8,128)(2,1)S(1)}, u32[]{:S(2)}, u32[]{:S(2)}) collective-permute-start(bf16[16,2176]{1,0:T(8,128)(2,1)S(1)} %get-tuple-element.67), channel_id=1, source_target_pairs={{0,2},{1,3},{2,0},{3,1},{4,6},{5,7},{6,4},{7,5},{8,10},{9,11},{10,... | collective-permute-start | bytes 208904 | tf_op jit(solution)/shard_map/ppermute | solution.py:285
  87.2 6.6 %collective-permute-start.6 = (bf16[16,2176]{1,0:T(8,128)(2,1)S(1)}, bf16[16,2176]{1,0:T(8,128)(2,1)S(1)}, u32[]{:S(2)}, u32[]{:S(2)}) collective-permute-start(bf16[16,2176]{1,0:T(8,128)(2,1)S(1)} %get-tuple-element.68), channel_id=1, source_target_pairs={{0,3},{1,2},{2,1},{3,0},{4,7},{5,6},{6,5},{7,4},{8,11},{9,10},{10,... | collective-permute-start | bytes 208904 | tf_op jit(solution)/shard_map/ppermute | solution.py:285
  94.2 7.4 %collective-permute-start.11 = (bf16[40,2176]{1,0:T(8,128)(2,1)S(1)}, bf16[40,2176]{1,0:T(8,128)(2,1)S(1)}, u32[]{:S(2)}, u32[]{:S(2)}) collective-permute-start(bf16[40,2176]{1,0:T(8,128)(2,1)S(1)} %get-tuple-element.81), channel_id=1, source_target_pairs={{0,16},{4,20},{8,24},{12,28},{16,0},{20,4},{24,8},{28,12},{1,17},{... | collective-permute-start | bytes 522248 | tf_op jit(solution)/shard_map/ppermute | solution.py:285
  95.8 6.1 %collective-permute-start.12 = (bf16[40,2176]{1,0:T(8,128)(2,1)S(1)}, bf16[40,2176]{1,0:T(8,128)(2,1)S(1)}, u32[]{:S(2)}, u32[]{:S(2)}) collective-permute-start(bf16[40,2176]{1,0:T(8,128)(2,1)S(1)} %get-tuple-element.82), channel_id=1, source_target_pairs={{0,8},{4,12},{8,0},{12,4},{16,24},{20,28},{24,16},{28,20},{1,9},{5... | collective-permute-start | bytes 522248 | tf_op jit(solution)/shard_map/ppermute | solution.py:285
  97.3 6.7 %collective-permute-start.13 = (bf16[40,2176]{1,0:T(8,128)(2,1)S(1)}, bf16[40,2176]{1,0:T(8,128)(2,1)S(1)}, u32[]{:S(2)}, u32[]{:S(2)}) collective-permute-start(bf16[40,2176]{1,0:T(8,128)(2,1)S(1)} %get-tuple-element.83), channel_id=1, source_target_pairs={{0,24},{4,28},{8,16},{12,20},{16,8},{20,12},{24,0},{28,4},{1,25},{... | collective-permute-start | bytes 522248 | tf_op jit(solution)/shard_map/ppermute | solution.py:285
  104.1 21.4 %collective-permute-start.16 = (bf16[24,2176]{1,0:T(8,128)(2,1)S(1)}, bf16[24,2176]{1,0:T(8,128)(2,1)S(1)}, u32[]{:S(2)}, u32[]{:S(2)}) collective-permute-start(bf16[24,2176]{1,0:T(8,128)(2,1)S(1)} %pad_maximum_fusion.1), channel_id=1, source_target_pairs={{0,24},{4,28},{8,16},{12,20},{16,8},{20,12},{24,0},{28,4},{1,25},{... | collective-permute-start | bytes 313352 | tf_op jit(solution)/shard_map/ppermute | solution.py:285
  106.3 19.1 %collective-permute-start.15 = (bf16[24,2176]{1,0:T(8,128)(2,1)S(1)}, bf16[24,2176]{1,0:T(8,128)(2,1)S(1)}, u32[]{:S(2)}, u32[]{:S(2)}) collective-permute-start(bf16[24,2176]{1,0:T(8,128)(2,1)S(1)} %pad_maximum_fusion.1), channel_id=1, source_target_pairs={{0,16},{4,20},{8,24},{12,28},{16,0},{20,4},{24,8},{28,12},{1,17},{... | collective-permute-start | bytes 313352 | tf_op jit(solution)/shard_map/ppermute | solution.py:285
  106.9 4.5 %collective-permute-start.18 = (bf16[8,2176]{1,0:T(8,128)(2,1)S(1)}, bf16[8,2176]{1,0:T(8,128)(2,1)S(1)}, u32[]{:S(2)}, u32[]{:S(2)}) collective-permute-start(bf16[8,2176]{1,0:T(8,128)(2,1)S(1)} %get-tuple-element.86), channel_id=1, source_target_pairs={{0,1},{1,0},{2,3},{3,2},{4,5},{5,4},{6,7},{7,6},{8,9},{9,8},{10,11... | collective-permute-start | bytes 104456 | tf_op jit(solution)/shard_map/ppermute | solution.py:285
  108.7 5.2 %collective-permute-start.19 = (bf16[8,2176]{1,0:T(8,128)(2,1)S(1)}, bf16[8,2176]{1,0:T(8,128)(2,1)S(1)}, u32[]{:S(2)}, u32[]{:S(2)}) collective-permute-start(bf16[8,2176]{1,0:T(8,128)(2,1)S(1)} %get-tuple-element.87), channel_id=1, source_target_pairs={{0,2},{1,3},{2,0},{3,1},{4,6},{5,7},{6,4},{7,5},{8,10},{9,11},{10,... | collective-permute-start | bytes 104456 | tf_op jit(solution)/shard_map/ppermute | solution.py:285
  110.0 5.7 %collective-permute-start.20 = (bf16[8,2176]{1,0:T(8,128)(2,1)S(1)}, bf16[8,2176]{1,0:T(8,128)(2,1)S(1)}, u32[]{:S(2)}, u32[]{:S(2)}) collective-permute-start(bf16[8,2176]{1,0:T(8,128)(2,1)S(1)} %get-tuple-element.88), channel_id=1, source_target_pairs={{0,3},{1,2},{2,1},{3,0},{4,7},{5,6},{6,5},{7,4},{8,11},{9,10},{10,... | collective-permute-start | bytes 104456 | tf_op jit(solution)/shard_map/ppermute | solution.py:285
  115.8 4.9 %collective-permute-start.23 = (bf16[8,2176]{1,0:T(8,128)(2,1)S(1)}, bf16[8,2176]{1,0:T(8,128)(2,1)S(1)}, u32[]{:S(2)}, u32[]{:S(2)}) collective-permute-start(bf16[8,2176]{1,0:T(8,128)(2,1)S(1)} %shard_map.67), channel_id=1, source_target_pairs={{0,24},{4,28},{8,16},{12,20},{16,8},{20,12},{24,0},{28,4},{1,25},{... | collective-permute-start | bytes 104456 | tf_op jit(solution)/shard_map/ppermute | solution.py:285
  117.3 4.4 %collective-permute-start.22 = (bf16[8,2176]{1,0:T(8,128)(2,1)S(1)}, bf16[8,2176]{1,0:T(8,128)(2,1)S(1)}, u32[]{:S(2)}, u32[]{:S(2)}) collective-permute-start(bf16[8,2176]{1,0:T(8,128)(2,1)S(1)} %shard_map.67), channel_id=1, source_target_pairs={{0,16},{4,20},{8,24},{12,28},{16,0},{20,4},{24,8},{28,12},{1,17},{... | collective-permute-start | bytes 104456 | tf_op jit(solution)/shard_map/ppermute | solution.py:285
  118.4 3.9 %collective-permute-start.21 = (bf16[8,2176]{1,0:T(8,128)(2,1)S(1)}, bf16[8,2176]{1,0:T(8,128)(2,1)S(1)}, u32[]{:S(2)}, u32[]{:S(2)}) collective-permute-start(bf16[8,2176]{1,0:T(8,128)(2,1)S(1)} %shard_map.67), channel_id=1, source_target_pairs={{0,8},{4,12},{8,0},{12,4},{16,24},{20,28},{24,16},{28,20},{1,9},{5... | collective-permute-start | bytes 104456 | tf_op jit(solution)/shard_map/ppermute | solution.py:285
  120.7 4.7 %collective-permute-start.14 = (bf16[24,2176]{1,0:T(8,128)(2,1)S(1)}, bf16[24,2176]{1,0:T(8,128)(2,1)S(1)}, u32[]{:S(2)}, u32[]{:S(2)}) collective-permute-start(bf16[24,2176]{1,0:T(8,128)(2,1)S(1)} %pad_maximum_fusion.1), channel_id=1, source_target_pairs={{0,8},{4,12},{8,0},{12,4},{16,24},{20,28},{24,16},{28,20},{1,9},{5... | collective-permute-start | bytes 313352 | tf_op jit(solution)/shard_map/ppermute | solution.py:285
  122.4 3.2 %collective-permute-start.24 = (bf16[32,2176]{1,0:T(8,128)(2,1)S(1)}, bf16[32,2176]{1,0:T(8,128)(2,1)S(1)}, u32[]{:S(2)}, u32[]{:S(2)}) collective-permute-start(bf16[32,2176]{1,0:T(8,128)(2,1)S(1)} %pad_maximum_fusion), channel_id=1, source_target_pairs={{0,4},{4,0},{8,12},{12,8},{16,20},{20,16},{24,28},{28,24},{1,5},{5... | collective-permute-start | bytes 417800 | tf_op jit(solution)/shard_map/ppermute | solution.py:285
  125.5 1.8 %collective-permute-start.17 = (bf16[96,2176]{1,0:T(8,128)(2,1)S(1)}, bf16[96,2176]{1,0:T(8,128)(2,1)S(1)}, u32[]{:S(2)}, u32[]{:S(2)}) collective-permute-start(bf16[96,2176]{1,0:T(8,128)(2,1)S(1)} %get-tuple-element.89), channel_id=1, source_target_pairs={{0,4},{4,0},{8,12},{12,8},{16,20},{20,16},{24,28},{28,24},{1,5},{5... | collective-permute-start | bytes 1253384 | tf_op jit(solution)/shard_map/ppermute | solution.py:285

commit v7 on v6

--- a/solution.py
+++ b/solution.py
@@ -167,9 +167,11 @@
         t[:, s * stripe : (s + 1) * stripe] = part.astype(BF16)
 
 
-def con_kernel(n_col, place, density, t_m, t_b, kept_m, kept_b, sent, acc):
+def con_kernel(n_col, first, size_of_cut, n_same, place, density, t_m, t_b, kept_m, kept_b, sent, *refs):
+    acc = refs[n_same]
     both = jnp.concatenate([t_m[...], t_b[...]])
-    acc[...] = lax.dot_general(both, density[...], CONTRACT_MINOR, preferred_element_type=F32)
+    rows_of_cut = density[first : first + size_of_cut, :]
+    acc[...] = lax.dot_general(both, rows_of_cut, CONTRACT_MINOR, preferred_element_type=F32)
     mine = place[0] // n_col % 2
     rows, size = t_m.shape[0], t_b.shape[0] // 2
     deal(mine, 2, n_col, size, acc, 0, [kept_m, sent], [0, 0])
@@ -390,13 +392,13 @@
 
         def spread(kept, got, axis, bits, eaches, offsets):
             ways = 1 << len(bits)
-            rows = [k.shape[0] // ways for k in kept]
+            rows, minor = [k.shape[0] // ways for k in kept], kept[0].shape[1]
             out = call(
                 functools.partial(spread_kernel, n_col, axis, bits, eaches, offsets, len(got)),
                 [smem] + [vmem] * (len(kept) + len(got)),
-                [pltpu.VMEM((r, unordered), F32) for r in rows] + [pltpu.VMEM((sum(rows), unordered), BF16)] * (ways - 1),
+                [pltpu.VMEM((r, minor), F32) for r in rows] + [pltpu.VMEM((sum(rows), minor), BF16)] * (ways - 1),
                 (place, *kept, *got),
-                scratch=[pltpu.VMEM((max(rows) * ways, unordered), F32)],
+                scratch=[pltpu.VMEM((max(rows) * ways, minor), F32)],
                 mib=6,
             )
             return list(out[: len(kept)]), list(out[len(kept) :])
@@ -471,16 +473,26 @@
                 [pltpu.VMEM((n, own_rows), BF16)], (*fixed[:-1], val_m), a_sent, mib=8, flops=2 * n * own_rows * own_columns,
             )[0]
             t_b = total([b_kept], b_got, [0])
-            m_kept, b_kept, sent = call(
-                functools.partial(con_kernel, n_col), [smem] + [vmem] * 3,
-                [outs(half)[0], outs(width // 2)[0], outs(half + width // 2)[1]], (place, fixed[-1], t_m, t_b),
-                scratch=[pltpu.VMEM((n + width, unordered), F32)], mib=12, flops=2 * (n + width) * own_rows * unordered,
-            )
-            got = [swap(sent, "row", 1, n_row)]
-            (m_kept, b_kept), sent = spread([m_kept, b_kept], got, "row", tuple(order), [n_col, 1], [0, half])
-            mb_got = scatter(sent, "row", order)
+            cut = (unordered // 256 + 1) * 128
+            same = [held[-1], pltpu.VMEM(t_m.shape, BF16), pltpu.VMEM(t_b.shape, BF16)]
+            operands, parts = [fixed[-1], t_m, t_b], []
+            for first, size, name in ((0, cut, "l"), (cut, unordered - cut, "r")):
+                again = same if name == "l" else []
+                m_kept, b_kept, sent, *operands = call(
+                    functools.partial(con_kernel, n_col, first, size, len(again)), [smem] + [vmem] * 3,
+                    [pltpu.VMEM((half, size), F32), pltpu.VMEM((width // 2, size), F32), pltpu.VMEM((half + width // 2, size), BF16)] + again,
+                    (place, *operands), scratch=[pltpu.VMEM((n + width, size), F32)], mib=10,
+                    aliases={1 + i: 3 + i for i in range(len(again))}, flops=2 * (n + width) * own_rows * size,
+                )
+                parts.append(([m_kept, b_kept], [swap(sent, "row", 1, n_row)]))
+            cuts = []
+            for name, (kept, got) in zip("lr", parts):
+                kept, sent = spread(kept, got, "row", tuple(order), [n_col, 1], [0, half])
+                cuts.append((kept, scatter(sent, "row", order)))
             a_kept, a_sent = spread(a_kept, a_got, "col", cols, [1, 1], [0, a_kept[0].shape[0]])
             a_got = scatter(a_sent, "col", cols)
+            join = lambda a, b: jnp.concatenate([a, b], axis=1)
+            (m_kept, b_kept), mb_got = [[join(a, b) for a, b in zip(*x)] for x in zip(*cuts)]
             rows = m_kept.shape[0]
             m_kept, m_sent = spread([m_kept], mb_got, "col", cols, [1], [0])
             m_got = scatter(m_sent, "col", cols)

time: 129 us -> 118 us (0.915)
  waiting for transfers between devices: 51.9 us -> 37.4 us
  starting transfers between devices: 32.8 us -> 38.8 us
  local copies, waits for them, and re-layouts: 3.7 us -> 0.25 us
    ppermute x25 -> x29, waiting for transfers between devices: 51.9 us -> 37.4 us  [swap(): return lax.ppermute(x, axis, [(i, i ^ bits) for i in range(size)])]
    ppermute x25 -> x29, starting transfers between devices: 32.8 us -> 38.8 us  [swap(): return lax.ppermute(x, axis, [(i, i ^ bits) for i in range(size)])]
    unnamed x20 -> x15, local copies, waits for them, and re-layouts: 3.62 us -> 0.14 us
    pallas_call x13 -> x15, Pallas kernels: 38.2 us -> 38.3 us  [call(): pl.pallas_call(kernel, in_specs=in_specs + [anywhere] * len(after), out_s...]
  transfers between devices with their start and end apart: 25 -> 29, of which waited for: 15 -> 11; matrix products, arithmetic and copies ran while one was open for 0% -> 0% of each run, Pallas kernels for 2% -> 9%
where the time goes in v7:
time: 118 us; the launch traced here: 117 us
  Pallas kernels  40.5 us (34%)
  starting transfers between devices  38.8 us (33%)
  waiting for transfers between devices  37.4 us (32%)
    ppermute x29, starting transfers between devices, swap(): return lax.ppermute(x, axis, [(i, i ^ bits) for i in range(size)])  38.8 us
    pallas_call x15, Pallas kernels, call(): pl.pallas_call(kernel, in_specs=in_specs + [anywhere] * len(after), out_s...  38.3 us
    ppermute x29, waiting for transfers between devices, swap(): return lax.ppermute(x, axis, [(i, i ^ bits) for i in range(size)])  37.4 us
  transfers between devices with their start and end apart: 29, of which 11 were waited for; matrix products, arithmetic and copies ran while one was open for 0% of the time, Pallas kernels for 9%

profile of v7, /device:TPU:0, one launch (start us, length us, event | category | flops | bytes accessed | tf_op | source)
XLA Modules:
  0.0 117.4 jit_solution(10240416285840391507)
XLA Ops:
  0.0 11.8 %shard_map.55 = (f32[64,2048]{1,0:T(8,128)S(1)}, bf16[64,2048]{1,0:T(8,128)(2,1)S(1)}, bf16[64,2048]{1,0:T(8,128)(2,1)S(1)}, bf16[64,2048]{1,0:T(8,128)(2,1)S(1)...) custom-call(s32[1]{0:T(128)} %bitcast.place, ...), custom_call_target="tpu_custom_call" | custom-call | flops 4294967296 | bytes 1048576 | tf_op jit(solution)/shard_map/pallas_call | solution.py:347
  11.8 0.0 copy-start
  11.8 15.7 %shard_map.56 = (f32[128,2176]{1,0:T(8,128)S(1)}, f32[128,2176]{1,0:T(8,128)S(1)}, bf16[256,2176]{1,0:T(8,128)(2,1)S(1)}, bf16[512,4096]{1,0:T(8,128)(2,1)S(1)},...) custom-call(s32[1]{0:T(128)} %bitcast.place, ...), custom_call_target="tpu_custom_call", output_to_operand_aliasing={{3}: (1, {}), {4}: (2, {}), {5}: (3, {}), {6}: (4, {}), {7}... | custom-call | flops 13153337344 | bytes 1048576 | tf_op jit(solution)/shard_map/pallas_call | solution.py:347
  27.5 0.6 collective-permute-start
  28.1 2.6 %collective-permute-start.7 = (bf16[64,2048]{1,0:T(8,128)(2,1)S(1)}, bf16[64,2048]{1,0:T(8,128)(2,1)S(1)}, u32[]{:S(2)}, u32[]{:S(2)}) collective-permute-start(bf16[64,2048]{1,0:T(8,128)(2,1)S(1)} %get-tuple-element.64.refs_6_), channel_id=1, source_target_pairs={{0,1},{1,0},{2,3},{3,2},{4,5},{5,4},{6,7},{7,6},{8,9},{9,8},{10,11... | collective-permute-start | bytes 786440 | tf_op jit(solution)/shard_map/ppermute | solution.py:287
  30.7 2.6 %collective-permute-start.8 = (bf16[64,2048]{1,0:T(8,128)(2,1)S(1)}, bf16[64,2048]{1,0:T(8,128)(2,1)S(1)}, u32[]{:S(2)}, u32[]{:S(2)}) collective-permute-start(bf16[64,2048]{1,0:T(8,128)(2,1)S(1)} %get-tuple-element.65.refs_7_), channel_id=1, source_target_pairs={{0,2},{1,3},{2,0},{3,1},{4,6},{5,7},{6,4},{7,5},{8,10},{9,11},{10,... | collective-permute-start | bytes 786440 | tf_op jit(solution)/shard_map/ppermute | solution.py:287
  33.3 0.0 collective-permute-start.9
  33.3 1.4 %shard_map.60.refs_4_ = bf16[256,4096]{1,0:T(8,128)(2,1)S(1)} custom-call(bf16[1024,45]{1,0:T(8,128)(2,1)S(1)} %get-tuple-element.85.hot1, bf16[1024,45]{1,0:T(8,128)(2,1)S(1)} %get-tuple-element.86.hot2, bf16[45,4096]{1,0:T(8,128)(2,1)S(1)} %copy-done, bf16[256,2176]{1,0:T(8,128)(2,1)S(1)} %get-tuple-element.67.refs_0_), custom_call_target="tpu_custom_call" | custom-call | bytes 1048576 | tf_op jit(solution)/shard_map/pallas_call | solution.py:347
  34.7 8.1 %collective-permute-done.7.refs_1_ = bf16[64,2048]{1,0:T(8,128)(2,1)S(1)} collective-permute-done((bf16[64,2048]{1,0:T(8,128)(2,1)S(1)}, bf16[64,2048]{1,0:T(8,128)(2,1)S(1)}, u32[]{:S(2)}, u32[]{:S(2)}) %collective-permute-start.7) | collective-permute-done | bytes 262176 | tf_op jit(solution)/shard_map/ppermute | solution.py:287
  42.8 9.3 %collective-permute-done.8.refs_2_ = bf16[64,2048]{1,0:T(8,128)(2,1)S(1)} collective-permute-done((bf16[64,2048]{1,0:T(8,128)(2,1)S(1)}, bf16[64,2048]{1,0:T(8,128)(2,1)S(1)}, u32[]{:S(2)}, u32[]{:S(2)}) %collective-permute-start.8) | collective-permute-done | bytes 262176 | tf_op jit(solution)/shard_map/ppermute | solution.py:287
  52.1 0.0 collective-permute-done.9.refs_3_
  52.1 0.1 shard_map.62.t_b
  52.2 0.0 collective-permute-done.refs_2_
  52.2 0.5 shard_map.57
  52.7 1.6 %collective-permute-start.1 = (bf16[64,2176]{1,0:T(8,128)(2,1)S(1)}, bf16[64,2176]{1,0:T(8,128)(2,1)S(1)}, u32[]{:S(2)}, u32[]{:S(2)}) collective-permute-start(bf16[64,2176]{1,0:T(8,128)(2,1)S(1)} %get-tuple-element.72.refs_5_), channel_id=1, source_target_pairs={{0,16},{4,20},{8,24},{12,28},{16,0},{20,4},{24,8},{28,12},{1,17},{... | collective-permute-start | bytes 835592 | tf_op jit(solution)/shard_map/ppermute | solution.py:287
  54.3 1.5 %collective-permute-start.2 = (bf16[64,2176]{1,0:T(8,128)(2,1)S(1)}, bf16[64,2176]{1,0:T(8,128)(2,1)S(1)}, u32[]{:S(2)}, u32[]{:S(2)}) collective-permute-start(bf16[64,2176]{1,0:T(8,128)(2,1)S(1)} %get-tuple-element.73.refs_6_), channel_id=1, source_target_pairs={{0,8},{4,12},{8,0},{12,4},{16,24},{20,28},{24,16},{28,20},{1,9},{5... | collective-permute-start | bytes 835592 | tf_op jit(solution)/shard_map/ppermute | solution.py:287
  55.7 0.5 collective-permute-start.3
  56.2 4.5 %shard_map.61.t_m = bf16[256,2048]{1,0:T(8,128)(2,1)S(1)} custom-call(bf16[512,4096]{1,0:T(8,128)(2,1)S(1)} %get-tuple-element.81.refs_0_, bf16[512,4096]{1,0:T(8,128)(2,1)S(1)} %get-tuple-element.82.refs_1_, bf16[512,4096]{1,0:T(8,128)(2,1)S(1)} %get-tuple-element.83.refs_2_, bf16[512,4096]{1,0:T(8,128)(2,1)S(1)} %get-tuple-element.84.refs_3_, ...), custom_call_target="tpu_custom_call" | custom-call | flops 4294967296 | bytes 1048576 | tf_op jit(solution)/shard_map/pallas_call | solution.py:347
  60.7 2.1 %shard_map.63 = (f32[128,1152]{1,0:T(8,128)S(1)}, f32[32,1152]{1,0:T(8,128)S(1)}, bf16[160,1152]{1,0:T(8,128)(2,1)S(1)}, bf16[2176,2048]{1,0:T(8,128)(2,1)S(1)},...) custom-call(s32[1]{0:T(128)} %bitcast.place, ...), custom_call_target="tpu_custom_call", output_to_operand_aliasing={{3}: (1, {}), {4}: (2, {}), {5}: (3, {})} | custom-call | flops 1509949440 | bytes 1048576 | tf_op jit(solution)/shard_map/pallas_call | solution.py:347
  62.8 0.0 copy-start.1
  62.8 1.7 %shard_map.65 = (f32[128,1024]{1,0:T(8,128)S(1)}, f32[32,1024]{1,0:T(8,128)S(1)}, bf16[160,1024]{1,0:T(8,128)(2,1)S(1)}) custom-call(s32[1]{0:T(128)} %bitcast.place, bf16[2176,2048]{1,0:T(8,128)(2,1)S(1)} %get-tuple-element.92.density, bf16[256,2048]{1,0:T(8,128)(2,1)S(1)} %get-tuple-element.93.t_m, bf16[64,2048]{1,0:T(8,128)(2,1)S(1)} %get-tuple-element.94.t_b), custom_call_target="tpu_custom_call" | custom-call | flops 1342177280 | bytes 1048576 | tf_op jit(solution)/shard_map/pallas_call | solution.py:347
  64.5 0.1 collective-permute-start.11
  64.6 0.0 collective-permute-done.1.refs_2_
  64.6 0.0 collective-permute-done.2.refs_3_
  64.6 2.5 %collective-permute-done.3.refs_4_ = bf16[64,2176]{1,0:T(8,128)(2,1)S(1)} collective-permute-done((bf16[64,2176]{1,0:T(8,128)(2,1)S(1)}, bf16[64,2176]{1,0:T(8,128)(2,1)S(1)}, u32[]{:S(2)}, u32[]{:S(2)}) %collective-permute-start.3) | collective-permute-done | bytes 278560 | tf_op jit(solution)/shard_map/ppermute | solution.py:287
  67.0 0.2 shard_map.58
  67.2 6.1 %collective-permute-start.4 = (bf16[16,2176]{1,0:T(8,128)(2,1)S(1)}, bf16[16,2176]{1,0:T(8,128)(2,1)S(1)}, u32[]{:S(2)}, u32[]{:S(2)}) collective-permute-start(bf16[16,2176]{1,0:T(8,128)(2,1)S(1)} %get-tuple-element.77), channel_id=1, source_target_pairs={{0,1},{1,0},{2,3},{3,2},{4,5},{5,4},{6,7},{7,6},{8,9},{9,8},{10,11... | collective-permute-start | bytes 208904 | tf_op jit(solution)/shard_map/ppermute | solution.py:287
  73.3 1.1 collective-permute-start.5
  74.4 1.4 %collective-permute-start.6 = (bf16[16,2176]{1,0:T(8,128)(2,1)S(1)}, bf16[16,2176]{1,0:T(8,128)(2,1)S(1)}, u32[]{:S(2)}, u32[]{:S(2)}) collective-permute-start(bf16[16,2176]{1,0:T(8,128)(2,1)S(1)} %get-tuple-element.79), channel_id=1, source_target_pairs={{0,3},{1,2},{2,1},{3,0},{4,7},{5,6},{6,5},{7,4},{8,11},{9,10},{10,... | collective-permute-start | bytes 208904 | tf_op jit(solution)/shard_map/ppermute | solution.py:287
  75.8 0.4 hot.1.pick
  76.3 0.0 collective-permute-done.11.refs_2_
  76.3 0.1 shard_map.66
  76.4 1.6 %collective-permute-start.13 = (bf16[40,1024]{1,0:T(8,128)(2,1)S(1)}, bf16[40,1024]{1,0:T(8,128)(2,1)S(1)}, u32[]{:S(2)}, u32[]{:S(2)}) collective-permute-start(bf16[40,1024]{1,0:T(8,128)(2,1)S(1)} %get-tuple-element.100), channel_id=1, source_target_pairs={{0,16},{4,20},{8,24},{12,28},{16,0},{20,4},{24,8},{28,12},{1,17},{... | collective-permute-start | bytes 245768 | tf_op jit(solution)/shard_map/ppermute | solution.py:287
  78.0 0.0 collective-permute-done.4.refs_2_
  78.0 1.5 %collective-permute-start.15 = (bf16[40,1024]{1,0:T(8,128)(2,1)S(1)}, bf16[40,1024]{1,0:T(8,128)(2,1)S(1)}, u32[]{:S(2)}, u32[]{:S(2)}) collective-permute-start(bf16[40,1024]{1,0:T(8,128)(2,1)S(1)} %get-tuple-element.102), channel_id=1, source_target_pairs={{0,8},{4,12},{8,0},{12,4},{16,24},{20,28},{24,16},{28,20},{1,9},{5... | collective-permute-start | bytes 245768 | tf_op jit(solution)/shard_map/ppermute | solution.py:287
  79.5 0.0 collective-permute-done.5.refs_3_
  79.5 2.3 %collective-permute-start.17 = (bf16[40,1024]{1,0:T(8,128)(2,1)S(1)}, bf16[40,1024]{1,0:T(8,128)(2,1)S(1)}, u32[]{:S(2)}, u32[]{:S(2)}) collective-permute-start(bf16[40,1024]{1,0:T(8,128)(2,1)S(1)} %get-tuple-element.104), channel_id=1, source_target_pairs={{0,24},{4,28},{8,16},{12,20},{16,8},{20,12},{24,0},{28,4},{1,25},{... | collective-permute-start | bytes 245768 | tf_op jit(solution)/shard_map/ppermute | solution.py:287
  81.8 0.0 collective-permute-done.6.refs_4_
  81.8 0.0 collective-permute-done.10.refs_2_
  81.8 0.2 shard_map.64
  82.0 0.6 collective-permute-start.12
  82.6 1.4 %collective-permute-start.14 = (bf16[40,1152]{1,0:T(8,128)(2,1)S(1)}, bf16[40,1152]{1,0:T(8,128)(2,1)S(1)}, u32[]{:S(2)}, u32[]{:S(2)}) collective-permute-start(bf16[40,1152]{1,0:T(8,128)(2,1)S(1)} %get-tuple-element.101), channel_id=1, source_target_pairs={{0,8},{4,12},{8,0},{12,4},{16,24},{20,28},{24,16},{28,20},{1,9},{5... | collective-permute-start | bytes 276488 | tf_op jit(solution)/shard_map/ppermute | solution.py:287
  84.0 2.6 %collective-permute-done.12 = bf16[40,1152]{1,0:T(8,128)(2,1)S(1)} collective-permute-done((bf16[40,1152]{1,0:T(8,128)(2,1)S(1)}, bf16[40,1152]{1,0:T(8,128)(2,1)S(1)}, u32[]{:S(2)}, u32[]{:S(2)}) %collective-permute-start.12) | collective-permute-done | bytes 92192 | tf_op jit(solution)/shard_map/ppermute | solution.py:287
  86.7 1.8 %collective-permute-start.16 = (bf16[40,1152]{1,0:T(8,128)(2,1)S(1)}, bf16[40,1152]{1,0:T(8,128)(2,1)S(1)}, u32[]{:S(2)}, u32[]{:S(2)}) collective-permute-start(bf16[40,1152]{1,0:T(8,128)(2,1)S(1)} %get-tuple-element.103), channel_id=1, source_target_pairs={{0,24},{4,28},{8,16},{12,20},{16,8},{20,12},{24,0},{28,4},{1,25},{... | collective-permute-start | bytes 276488 | tf_op jit(solution)/shard_map/ppermute | solution.py:287
  88.5 3.6 %collective-permute-done.16 = bf16[40,1152]{1,0:T(8,128)(2,1)S(1)} collective-permute-done((bf16[40,1152]{1,0:T(8,128)(2,1)S(1)}, bf16[40,1152]{1,0:T(8,128)(2,1)S(1)}, u32[]{:S(2)}, u32[]{:S(2)}) %collective-permute-start.16) | collective-permute-done | bytes 92192 | tf_op jit(solution)/shard_map/ppermute | solution.py:287
  92.2 1.9 %collective-permute-start.20 = (bf16[24,2176]{1,0:T(8,128)(2,1)S(1)}, bf16[24,2176]{1,0:T(8,128)(2,1)S(1)}, u32[]{:S(2)}, u32[]{:S(2)}) collective-permute-start(bf16[24,2176]{1,0:T(8,128)(2,1)S(1)} %pad_maximum_fusion.2), channel_id=1, source_target_pairs={{0,24},{4,28},{8,16},{12,20},{16,8},{20,12},{24,0},{28,4},{1,25},{... | collective-permute-start | bytes 313352 | tf_op jit(solution)/shard_map/ppermute | solution.py:287
  94.1 0.6 collective-permute-start.19
  94.7 0.1 shard_map.68
  94.8 1.0 collective-permute-start.22
  95.8 2.6 %collective-permute-start.23 = (bf16[8,2176]{1,0:T(8,128)(2,1)S(1)}, bf16[8,2176]{1,0:T(8,128)(2,1)S(1)}, u32[]{:S(2)}, u32[]{:S(2)}) collective-permute-start(bf16[8,2176]{1,0:T(8,128)(2,1)S(1)} %get-tuple-element.109), channel_id=1, source_target_pairs={{0,2},{1,3},{2,0},{3,1},{4,6},{5,7},{6,4},{7,5},{8,10},{9,11},{10,... | collective-permute-start | bytes 104456 | tf_op jit(solution)/shard_map/ppermute | solution.py:287
  98.3 0.9 collective-permute-start.24
  99.3 1.3 %collective-permute-done.23.refs_2_ = bf16[8,2176]{1,0:T(8,128)(2,1)S(1)} collective-permute-done((bf16[8,2176]{1,0:T(8,128)(2,1)S(1)}, bf16[8,2176]{1,0:T(8,128)(2,1)S(1)}, u32[]{:S(2)}, u32[]{:S(2)}) %collective-permute-start.23) | collective-permute-done | bytes 34848 | tf_op jit(solution)/shard_map/ppermute | solution.py:287
  100.6 3.5 %collective-permute-done.24.refs_3_ = bf16[8,2176]{1,0:T(8,128)(2,1)S(1)} collective-permute-done((bf16[8,2176]{1,0:T(8,128)(2,1)S(1)}, bf16[8,2176]{1,0:T(8,128)(2,1)S(1)}, u32[]{:S(2)}, u32[]{:S(2)}) %collective-permute-start.24) | collective-permute-done | bytes 34848 | tf_op jit(solution)/shard_map/ppermute | solution.py:287
  104.1 1.5 %collective-permute-start.27 = (bf16[8,2176]{1,0:T(8,128)(2,1)S(1)}, bf16[8,2176]{1,0:T(8,128)(2,1)S(1)}, u32[]{:S(2)}, u32[]{:S(2)}) collective-permute-start(bf16[8,2176]{1,0:T(8,128)(2,1)S(1)} %shard_map.69), channel_id=1, source_target_pairs={{0,24},{4,28},{8,16},{12,20},{16,8},{20,12},{24,0},{28,4},{1,25},{... | collective-permute-start | bytes 104456 | tf_op jit(solution)/shard_map/ppermute | solution.py:287
  105.7 1.1 collective-permute-start.26
  106.7 0.9 collective-permute-start.25
  107.7 1.3 %collective-permute-done.27 = bf16[8,2176]{1,0:T(8,128)(2,1)S(1)} collective-permute-done((bf16[8,2176]{1,0:T(8,128)(2,1)S(1)}, bf16[8,2176]{1,0:T(8,128)(2,1)S(1)}, u32[]{:S(2)}, u32[]{:S(2)}) %collective-permute-start.27) | collective-permute-done | bytes 34848 | tf_op jit(solution)/shard_map/ppermute | solution.py:287
  109.0 1.1 collective-permute-start.18
  110.1 0.6 collective-permute-done.25
  110.7 0.1 collective-permute-start.28
  110.8 2.9 %collective-permute-done.18 = bf16[24,2176]{1,0:T(8,128)(2,1)S(1)} collective-permute-done((bf16[24,2176]{1,0:T(8,128)(2,1)S(1)}, bf16[24,2176]{1,0:T(8,128)(2,1)S(1)}, u32[]{:S(2)}, u32[]{:S(2)}) %collective-permute-start.18) | collective-permute-done | bytes 104480 | tf_op jit(solution)/shard_map/ppermute | solution.py:287
  113.8 0.1 collective-permute-start.21
  113.9 1.7 %collective-permute-done.21 = bf16[96,2176]{1,0:T(8,128)(2,1)S(1)} collective-permute-done((bf16[96,2176]{1,0:T(8,128)(2,1)S(1)}, bf16[96,2176]{1,0:T(8,128)(2,1)S(1)}, u32[]{:S(2)}, u32[]{:S(2)}) %collective-permute-start.21) | collective-permute-done | bytes 417824 | tf_op jit(solution)/shard_map/ppermute | solution.py:287
  115.6 1.8 %pick.1 = f32[512,256]{1,0:T(8,128)} custom-call(s32[1]{0:T(128)} %bitcast.place, bf16[2176,512]{1,0:T(8,128)(2,1)S(1)} %hot.1.pick, bf16[192,2176]{1,0:T(8,128)(2,1)S(1)} %constant_dynamic-update-slice_fusion.11.refs_0_, bf16[64,2176]{1,0:T(8,128)(2,1)S(1)} %constant_dynamic-update-slice_fusion.17.refs_1_), custom_call_target="tpu_custom_call" | custom-call | tf_op jit(solution)/shard_map/pick/pallas_call | solution.py:522
  (36 shorter events, 0.4 us)
Async XLA Ops:
  11.8 21.5 %copy-start = (bf16[45,4096]{1,0:T(8,128)(2,1)S(1)}, bf16[45,4096]{1,0:T(8,128)(2,1)}, u32[]{:S(2)}) copy-start(bf16[45,4096]{1,0:T(8,128)(2,1)} %val.3) | copy-start | bytes 1105924
  27.5 24.7 %collective-permute-start = (bf16[256,2176]{1,0:T(8,128)(2,1)S(1)}, bf16[256,2176]{1,0:T(8,128)(2,1)S(1)}, u32[]{:S(2)}, u32[]{:S(2)}) collective-permute-start(bf16[256,2176]{1,0:T(8,128)(2,1)S(1)} %get-tuple-element.67.refs_0_), channel_id=1, source_target_pairs={{0,4},{4,0},{8,12},{12,8},{16,20},{20,16},{24,28},{28,24},{1,5},{5... | collective-permute-start | bytes 3342344 | tf_op jit(solution)/shard_map/ppermute | solution.py:287
  28.1 14.7 %collective-permute-start.7 = (bf16[64,2048]{1,0:T(8,128)(2,1)S(1)}, bf16[64,2048]{1,0:T(8,128)(2,1)S(1)}, u32[]{:S(2)}, u32[]{:S(2)}) collective-permute-start(bf16[64,2048]{1,0:T(8,128)(2,1)S(1)} %get-tuple-element.64.refs_6_), channel_id=1, source_target_pairs={{0,1},{1,0},{2,3},{3,2},{4,5},{5,4},{6,7},{7,6},{8,9},{9,8},{10,11... | collective-permute-start | bytes 786440 | tf_op jit(solution)/shard_map/ppermute | solution.py:287
  30.7 21.4 %collective-permute-start.8 = (bf16[64,2048]{1,0:T(8,128)(2,1)S(1)}, bf16[64,2048]{1,0:T(8,128)(2,1)S(1)}, u32[]{:S(2)}, u32[]{:S(2)}) collective-permute-start(bf16[64,2048]{1,0:T(8,128)(2,1)S(1)} %get-tuple-element.65.refs_7_), channel_id=1, source_target_pairs={{0,2},{1,3},{2,0},{3,1},{4,6},{5,7},{6,4},{7,5},{8,10},{9,11},{10,... | collective-permute-start | bytes 786440 | tf_op jit(solution)/shard_map/ppermute | solution.py:287
  33.3 18.8 %collective-permute-start.9 = (bf16[64,2048]{1,0:T(8,128)(2,1)S(1)}, bf16[64,2048]{1,0:T(8,128)(2,1)S(1)}, u32[]{:S(2)}, u32[]{:S(2)}) collective-permute-start(bf16[64,2048]{1,0:T(8,128)(2,1)S(1)} %get-tuple-element.66.refs_8_), channel_id=1, source_target_pairs={{0,3},{1,2},{2,1},{3,0},{4,7},{5,6},{6,5},{7,4},{8,11},{9,10},{10,... | collective-permute-start | bytes 786440 | tf_op jit(solution)/shard_map/ppermute | solution.py:287
  52.7 11.9 %collective-permute-start.1 = (bf16[64,2176]{1,0:T(8,128)(2,1)S(1)}, bf16[64,2176]{1,0:T(8,128)(2,1)S(1)}, u32[]{:S(2)}, u32[]{:S(2)}) collective-permute-start(bf16[64,2176]{1,0:T(8,128)(2,1)S(1)} %get-tuple-element.72.refs_5_), channel_id=1, source_target_pairs={{0,16},{4,20},{8,24},{12,28},{16,0},{20,4},{24,8},{28,12},{1,17},{... | collective-permute-start | bytes 835592 | tf_op jit(solution)/shard_map/ppermute | solution.py:287
  54.3 10.3 %collective-permute-start.2 = (bf16[64,2176]{1,0:T(8,128)(2,1)S(1)}, bf16[64,2176]{1,0:T(8,128)(2,1)S(1)}, u32[]{:S(2)}, u32[]{:S(2)}) collective-permute-start(bf16[64,2176]{1,0:T(8,128)(2,1)S(1)} %get-tuple-element.73.refs_6_), channel_id=1, source_target_pairs={{0,8},{4,12},{8,0},{12,4},{16,24},{20,28},{24,16},{28,20},{1,9},{5... | collective-permute-start | bytes 835592 | tf_op jit(solution)/shard_map/ppermute | solution.py:287
  55.7 11.3 %collective-permute-start.3 = (bf16[64,2176]{1,0:T(8,128)(2,1)S(1)}, bf16[64,2176]{1,0:T(8,128)(2,1)S(1)}, u32[]{:S(2)}, u32[]{:S(2)}) collective-permute-start(bf16[64,2176]{1,0:T(8,128)(2,1)S(1)} %get-tuple-element.74.refs_7_), channel_id=1, source_target_pairs={{0,24},{4,28},{8,16},{12,20},{16,8},{20,12},{24,0},{28,4},{1,25},{... | collective-permute-start | bytes 835592 | tf_op jit(solution)/shard_map/ppermute | solution.py:287
  62.8 13.1 %copy-start.1 = (s32[4096,2]{0,1:T(2,128)S(1)}, s32[4096,2]{0,1:T(2,128)}, u32[]{:S(2)}) copy-start(s32[4096,2]{0,1:T(2,128)} %param.9) | copy-start | bytes 98308
  64.5 11.8 %collective-permute-start.11 = (bf16[160,1024]{1,0:T(8,128)(2,1)S(1)}, bf16[160,1024]{1,0:T(8,128)(2,1)S(1)}, u32[]{:S(2)}, u32[]{:S(2)}) collective-permute-start(bf16[160,1024]{1,0:T(8,128)(2,1)S(1)} %get-tuple-element.97), channel_id=1, source_target_pairs={{0,4},{4,0},{8,12},{12,8},{16,20},{20,16},{24,28},{28,24},{1,5},{5... | collective-permute-start | bytes 983048 | tf_op jit(solution)/shard_map/ppermute | solution.py:287
  67.2 10.8 %collective-permute-start.4 = (bf16[16,2176]{1,0:T(8,128)(2,1)S(1)}, bf16[16,2176]{1,0:T(8,128)(2,1)S(1)}, u32[]{:S(2)}, u32[]{:S(2)}) collective-permute-start(bf16[16,2176]{1,0:T(8,128)(2,1)S(1)} %get-tuple-element.77), channel_id=1, source_target_pairs={{0,1},{1,0},{2,3},{3,2},{4,5},{5,4},{6,7},{7,6},{8,9},{9,8},{10,11... | collective-permute-start | bytes 208904 | tf_op jit(solution)/shard_map/ppermute | solution.py:287
  73.3 6.1 %collective-permute-start.5 = (bf16[16,2176]{1,0:T(8,128)(2,1)S(1)}, bf16[16,2176]{1,0:T(8,128)(2,1)S(1)}, u32[]{:S(2)}, u32[]{:S(2)}) collective-permute-start(bf16[16,2176]{1,0:T(8,128)(2,1)S(1)} %get-tuple-element.78), channel_id=1, source_target_pairs={{0,2},{1,3},{2,0},{3,1},{4,6},{5,7},{6,4},{7,5},{8,10},{9,11},{10,... | collective-permute-start | bytes 208904 | tf_op jit(solution)/shard_map/ppermute | solution.py:287
  74.4 7.3 %collective-permute-start.6 = (bf16[16,2176]{1,0:T(8,128)(2,1)S(1)}, bf16[16,2176]{1,0:T(8,128)(2,1)S(1)}, u32[]{:S(2)}, u32[]{:S(2)}) collective-permute-start(bf16[16,2176]{1,0:T(8,128)(2,1)S(1)} %get-tuple-element.79), channel_id=1, source_target_pairs={{0,3},{1,2},{2,1},{3,0},{4,7},{5,6},{6,5},{7,4},{8,11},{9,10},{10,... | collective-permute-start | bytes 208904 | tf_op jit(solution)/shard_map/ppermute | solution.py:287
  75.8 6.0 %collective-permute-start.10 = (bf16[160,1152]{1,0:T(8,128)(2,1)S(1)}, bf16[160,1152]{1,0:T(8,128)(2,1)S(1)}, u32[]{:S(2)}, u32[]{:S(2)}) collective-permute-start(bf16[160,1152]{1,0:T(8,128)(2,1)S(1)} %get-tuple-element.90), channel_id=1, source_target_pairs={{0,4},{4,0},{8,12},{12,8},{16,20},{20,16},{24,28},{28,24},{1,5},{5... | collective-permute-start | bytes 1105928 | tf_op jit(solution)/shard_map/ppermute | solution.py:287
  76.4 15.7 %collective-permute-start.13 = (bf16[40,1024]{1,0:T(8,128)(2,1)S(1)}, bf16[40,1024]{1,0:T(8,128)(2,1)S(1)}, u32[]{:S(2)}, u32[]{:S(2)}) collective-permute-start(bf16[40,1024]{1,0:T(8,128)(2,1)S(1)} %get-tuple-element.100), channel_id=1, source_target_pairs={{0,16},{4,20},{8,24},{12,28},{16,0},{20,4},{24,8},{28,12},{1,17},{... | collective-permute-start | bytes 245768 | tf_op jit(solution)/shard_map/ppermute | solution.py:287
  78.0 14.2 %collective-permute-start.15 = (bf16[40,1024]{1,0:T(8,128)(2,1)S(1)}, bf16[40,1024]{1,0:T(8,128)(2,1)S(1)}, u32[]{:S(2)}, u32[]{:S(2)}) collective-permute-start(bf16[40,1024]{1,0:T(8,128)(2,1)S(1)} %get-tuple-element.102), channel_id=1, source_target_pairs={{0,8},{4,12},{8,0},{12,4},{16,24},{20,28},{24,16},{28,20},{1,9},{5... | collective-permute-start | bytes 245768 | tf_op jit(solution)/shard_map/ppermute | solution.py:287
  79.5 12.7 %collective-permute-start.17 = (bf16[40,1024]{1,0:T(8,128)(2,1)S(1)}, bf16[40,1024]{1,0:T(8,128)(2,1)S(1)}, u32[]{:S(2)}, u32[]{:S(2)}) collective-permute-start(bf16[40,1024]{1,0:T(8,128)(2,1)S(1)} %get-tuple-element.104), channel_id=1, source_target_pairs={{0,24},{4,28},{8,16},{12,20},{16,8},{20,12},{24,0},{28,4},{1,25},{... | collective-permute-start | bytes 245768 | tf_op jit(solution)/shard_map/ppermute | solution.py:287
  82.0 4.7 %collective-permute-start.12 = (bf16[40,1152]{1,0:T(8,128)(2,1)S(1)}, bf16[40,1152]{1,0:T(8,128)(2,1)S(1)}, u32[]{:S(2)}, u32[]{:S(2)}) collective-permute-start(bf16[40,1152]{1,0:T(8,128)(2,1)S(1)} %get-tuple-element.99), channel_id=1, source_target_pairs={{0,16},{4,20},{8,24},{12,28},{16,0},{20,4},{24,8},{28,12},{1,17},{... | collective-permute-start | bytes 276488 | tf_op jit(solution)/shard_map/ppermute | solution.py:287
  82.6 5.9 %collective-permute-start.14 = (bf16[40,1152]{1,0:T(8,128)(2,1)S(1)}, bf16[40,1152]{1,0:T(8,128)(2,1)S(1)}, u32[]{:S(2)}, u32[]{:S(2)}) collective-permute-start(bf16[40,1152]{1,0:T(8,128)(2,1)S(1)} %get-tuple-element.101), channel_id=1, source_target_pairs={{0,8},{4,12},{8,0},{12,4},{16,24},{20,28},{24,16},{28,20},{1,9},{5... | collective-permute-start | bytes 276488 | tf_op jit(solution)/shard_map/ppermute | solution.py:287
  86.7 5.5 %collective-permute-start.16 = (bf16[40,1152]{1,0:T(8,128)(2,1)S(1)}, bf16[40,1152]{1,0:T(8,128)(2,1)S(1)}, u32[]{:S(2)}, u32[]{:S(2)}) collective-permute-start(bf16[40,1152]{1,0:T(8,128)(2,1)S(1)} %get-tuple-element.103), channel_id=1, source_target_pairs={{0,24},{4,28},{8,16},{12,20},{16,8},{20,12},{24,0},{28,4},{1,25},{... | collective-permute-start | bytes 276488 | tf_op jit(solution)/shard_map/ppermute | solution.py:287
  92.2 21.5 %collective-permute-start.20 = (bf16[24,2176]{1,0:T(8,128)(2,1)S(1)}, bf16[24,2176]{1,0:T(8,128)(2,1)S(1)}, u32[]{:S(2)}, u32[]{:S(2)}) collective-permute-start(bf16[24,2176]{1,0:T(8,128)(2,1)S(1)} %pad_maximum_fusion.2), channel_id=1, source_target_pairs={{0,24},{4,28},{8,16},{12,20},{16,8},{20,12},{24,0},{28,4},{1,25},{... | collective-permute-start | bytes 313352 | tf_op jit(solution)/shard_map/ppermute | solution.py:287
  94.1 19.6 %collective-permute-start.19 = (bf16[24,2176]{1,0:T(8,128)(2,1)S(1)}, bf16[24,2176]{1,0:T(8,128)(2,1)S(1)}, u32[]{:S(2)}, u32[]{:S(2)}) collective-permute-start(bf16[24,2176]{1,0:T(8,128)(2,1)S(1)} %pad_maximum_fusion.2), channel_id=1, source_target_pairs={{0,16},{4,20},{8,24},{12,28},{16,0},{20,4},{24,8},{28,12},{1,17},{... | collective-permute-start | bytes 313352 | tf_op jit(solution)/shard_map/ppermute | solution.py:287
  94.8 4.5 %collective-permute-start.22 = (bf16[8,2176]{1,0:T(8,128)(2,1)S(1)}, bf16[8,2176]{1,0:T(8,128)(2,1)S(1)}, u32[]{:S(2)}, u32[]{:S(2)}) collective-permute-start(bf16[8,2176]{1,0:T(8,128)(2,1)S(1)} %get-tuple-element.108), channel_id=1, source_target_pairs={{0,1},{1,0},{2,3},{3,2},{4,5},{5,4},{6,7},{7,6},{8,9},{9,8},{10,11... | collective-permute-start | bytes 104456 | tf_op jit(solution)/shard_map/ppermute | solution.py:287
  95.8 4.8 %collective-permute-start.23 = (bf16[8,2176]{1,0:T(8,128)(2,1)S(1)}, bf16[8,2176]{1,0:T(8,128)(2,1)S(1)}, u32[]{:S(2)}, u32[]{:S(2)}) collective-permute-start(bf16[8,2176]{1,0:T(8,128)(2,1)S(1)} %get-tuple-element.109), channel_id=1, source_target_pairs={{0,2},{1,3},{2,0},{3,1},{4,6},{5,7},{6,4},{7,5},{8,10},{9,11},{10,... | collective-permute-start | bytes 104456 | tf_op jit(solution)/shard_map/ppermute | solution.py:287
  98.3 5.7 %collective-permute-start.24 = (bf16[8,2176]{1,0:T(8,128)(2,1)S(1)}, bf16[8,2176]{1,0:T(8,128)(2,1)S(1)}, u32[]{:S(2)}, u32[]{:S(2)}) collective-permute-start(bf16[8,2176]{1,0:T(8,128)(2,1)S(1)} %get-tuple-element.110), channel_id=1, source_target_pairs={{0,3},{1,2},{2,1},{3,0},{4,7},{5,6},{6,5},{7,4},{8,11},{9,10},{10,... | collective-permute-start | bytes 104456 | tf_op jit(solution)/shard_map/ppermute | solution.py:287
  104.1 4.9 %collective-permute-start.27 = (bf16[8,2176]{1,0:T(8,128)(2,1)S(1)}, bf16[8,2176]{1,0:T(8,128)(2,1)S(1)}, u32[]{:S(2)}, u32[]{:S(2)}) collective-permute-start(bf16[8,2176]{1,0:T(8,128)(2,1)S(1)} %shard_map.69), channel_id=1, source_target_pairs={{0,24},{4,28},{8,16},{12,20},{16,8},{20,12},{24,0},{28,4},{1,25},{... | collective-permute-start | bytes 104456 | tf_op jit(solution)/shard_map/ppermute | solution.py:287
  105.7 4.5 %collective-permute-start.26 = (bf16[8,2176]{1,0:T(8,128)(2,1)S(1)}, bf16[8,2176]{1,0:T(8,128)(2,1)S(1)}, u32[]{:S(2)}, u32[]{:S(2)}) collective-permute-start(bf16[8,2176]{1,0:T(8,128)(2,1)S(1)} %shard_map.69), channel_id=1, source_target_pairs={{0,16},{4,20},{8,24},{12,28},{16,0},{20,4},{24,8},{28,12},{1,17},{... | collective-permute-start | bytes 104456 | tf_op jit(solution)/shard_map/ppermute | solution.py:287
  106.7 3.9 %collective-permute-start.25 = (bf16[8,2176]{1,0:T(8,128)(2,1)S(1)}, bf16[8,2176]{1,0:T(8,128)(2,1)S(1)}, u32[]{:S(2)}, u32[]{:S(2)}) collective-permute-start(bf16[8,2176]{1,0:T(8,128)(2,1)S(1)} %shard_map.69), channel_id=1, source_target_pairs={{0,8},{4,12},{8,0},{12,4},{16,24},{20,28},{24,16},{28,20},{1,9},{5... | collective-permute-start | bytes 104456 | tf_op jit(solution)/shard_map/ppermute | solution.py:287
  109.0 4.7 %collective-permute-start.18 = (bf16[24,2176]{1,0:T(8,128)(2,1)S(1)}, bf16[24,2176]{1,0:T(8,128)(2,1)S(1)}, u32[]{:S(2)}, u32[]{:S(2)}) collective-permute-start(bf16[24,2176]{1,0:T(8,128)(2,1)S(1)} %pad_maximum_fusion.2), channel_id=1, source_target_pairs={{0,8},{4,12},{8,0},{12,4},{16,24},{20,28},{24,16},{28,20},{1,9},{5... | collective-permute-start | bytes 313352 | tf_op jit(solution)/shard_map/ppermute | solution.py:287
  110.7 3.2 %collective-permute-start.28 = (bf16[32,2176]{1,0:T(8,128)(2,1)S(1)}, bf16[32,2176]{1,0:T(8,128)(2,1)S(1)}, u32[]{:S(2)}, u32[]{:S(2)}) collective-permute-start(bf16[32,2176]{1,0:T(8,128)(2,1)S(1)} %pad_maximum_fusion.1), channel_id=1, source_target_pairs={{0,4},{4,0},{8,12},{12,8},{16,20},{20,16},{24,28},{28,24},{1,5},{5... | collective-permute-start | bytes 417800 | tf_op jit(solution)/shard_map/ppermute | solution.py:287
  113.8 1.8 %collective-permute-start.21 = (bf16[96,2176]{1,0:T(8,128)(2,1)S(1)}, bf16[96,2176]{1,0:T(8,128)(2,1)S(1)}, u32[]{:S(2)}, u32[]{:S(2)}) collective-permute-start(bf16[96,2176]{1,0:T(8,128)(2,1)S(1)} %get-tuple-element.111), channel_id=1, source_target_pairs={{0,4},{4,0},{8,12},{12,8},{16,20},{20,16},{24,28},{28,24},{1,5},{5... | collective-permute-start | bytes 1253384 | tf_op jit(solution)/shard_map/ppermute | solution.py:287

commit v8 on v7

--- a/solution.py
+++ b/solution.py
@@ -264,23 +264,34 @@
 
 
 def pick_kernel(n_col, scale, gathers, place, pick, *refs):
-    arrays, (out, found, turned) = refs[: len(gathers)], refs[len(gathers) :]
+    arrays, (out, found, turned, done, sems) = refs[: len(gathers)], refs[len(gathers) :]
     me = place[0] // n_col
     whole = jnp.concatenate([array[...] for array in arrays])
-    found[...] = jnp.dot(whole, pick[...], preferred_element_type=F32) * scale
-    base = 0
-    for array, (steps, chunks) in zip(arrays, gathers):
-        each = sum(rows for _, rows, _ in chunks)
-        for j in range(array.shape[0] // each):
-            block = sum((((me ^ j) >> bit) % 2) << s for s, bit in enumerate(steps))
-            used = 0
-            for start, rows, order in chunks:
-                spot = sum(((j >> bit) & 1) << (len(order) - 1 - s) for s, bit in enumerate(order))
-                to = start + spot * rows
-                turned[to : to + rows, :] = found[pl.ds(base + block * each + used, rows), :]
-                used += rows
-        base += array.shape[0]
-    out[...] = turned[...].T
+    own = done.shape[0]
+    pieces = 2 if own % 256 == 0 else 1
+    size = own // pieces
+    copies = []
+    for piece in range(pieces):
+        at = slice(piece * size, (piece + 1) * size)
+        found[:, at] = jnp.dot(whole, pick[:, at], preferred_element_type=F32) * scale
+        base = 0
+        for array, (steps, chunks) in zip(arrays, gathers):
+            each = sum(rows for _, rows, _ in chunks)
+            for j in range(array.shape[0] // each):
+                block = sum((((me ^ j) >> bit) % 2) << s for s, bit in enumerate(steps))
+                used = 0
+                for start, rows, order in chunks:
+                    spot = sum(((j >> bit) & 1) << (len(order) - 1 - s) for s, bit in enumerate(order))
+                    to = start + spot * rows
+                    turned[to : to + rows, at] = found[pl.ds(base + block * each + used, rows), at]
+                    used += rows
+            base += array.shape[0]
+        done[at, :] = turned[:, at].T
+        rows = pl.ds(piece * size, size)
+        copies.append(pltpu.make_async_copy(done.at[rows, :], out.at[rows, :], sems.at[piece]))
+        copies[-1].start()
+    for copy in copies:
+        copy.wait()
 
 
 def swap(x, axis, bits, size):
@@ -522,9 +533,10 @@
         return pl.pallas_call(
             functools.partial(pick_kernel, n_col, float(grid ** (-0.5)), gathers),
             in_specs=[smem] + [vmem] * (1 + len(arrays)),
-            out_specs=vmem,
+            out_specs=anywhere,
             out_shape=jax.ShapeDtypeStruct((own, per_col), F32),
-            scratch_shapes=[pltpu.VMEM((per_col, own), F32)] * 2,
+            scratch_shapes=[pltpu.VMEM((per_col, own), F32)] * 2
+            + [pltpu.VMEM((own, per_col), F32), pltpu.SemaphoreType.DMA((2,))],
             compiler_params=params(20),
             name="pick",
         )(place, pick, *arrays)

time: 118 us -> 118 us (level)
  no operation moved by 1% of the time
where the time goes in v8:
time: 118 us
  Pallas kernels  40.5 us (34%)
  starting transfers between devices  38.8 us (33%)
  waiting for transfers between devices  37.4 us (32%)
    ppermute x29, starting transfers between devices, swap(): return lax.ppermute(x, axis, [(i, i ^ bits) for i in range(size)])  38.8 us
    pallas_call x15, Pallas kernels, call(): pl.pallas_call(kernel, in_specs=in_specs + [anywhere] * len(after), out_s...  38.3 us
    ppermute x29, waiting for transfers between devices, swap(): return lax.ppermute(x, axis, [(i, i ^ bits) for i in range(size)])  37.4 us
  transfers between devices with their start and end apart: 29, of which 11 were waited for; matrix products, arithmetic and copies ran while one was open for 0% of the time, Pallas kernels for 9%

profile of v8, /device:TPU:0, one launch (start us, length us, event | category | flops | bytes accessed | tf_op | source)
XLA Modules:
  0.0 117.6 jit_solution(14904648223343914739)
XLA Ops:
  0.0 11.8 %shard_map.55 = (f32[64,2048]{1,0:T(8,128)S(1)}, bf16[64,2048]{1,0:T(8,128)(2,1)S(1)}, bf16[64,2048]{1,0:T(8,128)(2,1)S(1)}, bf16[64,2048]{1,0:T(8,128)(2,1)S(1)...) custom-call(s32[1]{0:T(128)} %bitcast.place, ...), custom_call_target="tpu_custom_call" | custom-call | flops 4294967296 | bytes 1048576 | tf_op jit(solution)/shard_map/pallas_call | solution.py:358
  11.8 0.0 copy-start
  11.8 15.7 %shard_map.56 = (f32[128,2176]{1,0:T(8,128)S(1)}, f32[128,2176]{1,0:T(8,128)S(1)}, bf16[256,2176]{1,0:T(8,128)(2,1)S(1)}, bf16[512,4096]{1,0:T(8,128)(2,1)S(1)},...) custom-call(s32[1]{0:T(128)} %bitcast.place, ...), custom_call_target="tpu_custom_call", output_to_operand_aliasing={{3}: (1, {}), {4}: (2, {}), {5}: (3, {}), {6}: (4, {}), {7}... | custom-call | flops 13153337344 | bytes 1048576 | tf_op jit(solution)/shard_map/pallas_call | solution.py:358
  27.5 0.6 collective-permute-start
  28.1 2.6 %collective-permute-start.7 = (bf16[64,2048]{1,0:T(8,128)(2,1)S(1)}, bf16[64,2048]{1,0:T(8,128)(2,1)S(1)}, u32[]{:S(2)}, u32[]{:S(2)}) collective-permute-start(bf16[64,2048]{1,0:T(8,128)(2,1)S(1)} %get-tuple-element.64.refs_6_), channel_id=1, source_target_pairs={{0,1},{1,0},{2,3},{3,2},{4,5},{5,4},{6,7},{7,6},{8,9},{9,8},{10,11... | collective-permute-start | bytes 786440 | tf_op jit(solution)/shard_map/ppermute | solution.py:298
  30.7 2.6 %collective-permute-start.8 = (bf16[64,2048]{1,0:T(8,128)(2,1)S(1)}, bf16[64,2048]{1,0:T(8,128)(2,1)S(1)}, u32[]{:S(2)}, u32[]{:S(2)}) collective-permute-start(bf16[64,2048]{1,0:T(8,128)(2,1)S(1)} %get-tuple-element.65.refs_7_), channel_id=1, source_target_pairs={{0,2},{1,3},{2,0},{3,1},{4,6},{5,7},{6,4},{7,5},{8,10},{9,11},{10,... | collective-permute-start | bytes 786440 | tf_op jit(solution)/shard_map/ppermute | solution.py:298
  33.3 0.0 collective-permute-start.9
  33.3 1.4 %shard_map.60.refs_4_ = bf16[256,4096]{1,0:T(8,128)(2,1)S(1)} custom-call(bf16[1024,45]{1,0:T(8,128)(2,1)S(1)} %get-tuple-element.85.hot1, bf16[1024,45]{1,0:T(8,128)(2,1)S(1)} %get-tuple-element.86.hot2, bf16[45,4096]{1,0:T(8,128)(2,1)S(1)} %copy-done, bf16[256,2176]{1,0:T(8,128)(2,1)S(1)} %get-tuple-element.67.refs_0_), custom_call_target="tpu_custom_call" | custom-call | bytes 1048576 | tf_op jit(solution)/shard_map/pallas_call | solution.py:358
  34.7 8.1 %collective-permute-done.7.refs_1_ = bf16[64,2048]{1,0:T(8,128)(2,1)S(1)} collective-permute-done((bf16[64,2048]{1,0:T(8,128)(2,1)S(1)}, bf16[64,2048]{1,0:T(8,128)(2,1)S(1)}, u32[]{:S(2)}, u32[]{:S(2)}) %collective-permute-start.7) | collective-permute-done | bytes 262176 | tf_op jit(solution)/shard_map/ppermute | solution.py:298
  42.8 9.3 %collective-permute-done.8.refs_2_ = bf16[64,2048]{1,0:T(8,128)(2,1)S(1)} collective-permute-done((bf16[64,2048]{1,0:T(8,128)(2,1)S(1)}, bf16[64,2048]{1,0:T(8,128)(2,1)S(1)}, u32[]{:S(2)}, u32[]{:S(2)}) %collective-permute-start.8) | collective-permute-done | bytes 262176 | tf_op jit(solution)/shard_map/ppermute | solution.py:298
  52.1 0.0 collective-permute-done.9.refs_3_
  52.1 0.1 shard_map.62.t_b
  52.2 0.0 collective-permute-done.refs_2_
  52.2 0.5 shard_map.57
  52.7 1.6 %collective-permute-start.1 = (bf16[64,2176]{1,0:T(8,128)(2,1)S(1)}, bf16[64,2176]{1,0:T(8,128)(2,1)S(1)}, u32[]{:S(2)}, u32[]{:S(2)}) collective-permute-start(bf16[64,2176]{1,0:T(8,128)(2,1)S(1)} %get-tuple-element.72.refs_5_), channel_id=1, source_target_pairs={{0,16},{4,20},{8,24},{12,28},{16,0},{20,4},{24,8},{28,12},{1,17},{... | collective-permute-start | bytes 835592 | tf_op jit(solution)/shard_map/ppermute | solution.py:298
  54.3 1.5 %collective-permute-start.2 = (bf16[64,2176]{1,0:T(8,128)(2,1)S(1)}, bf16[64,2176]{1,0:T(8,128)(2,1)S(1)}, u32[]{:S(2)}, u32[]{:S(2)}) collective-permute-start(bf16[64,2176]{1,0:T(8,128)(2,1)S(1)} %get-tuple-element.73.refs_6_), channel_id=1, source_target_pairs={{0,8},{4,12},{8,0},{12,4},{16,24},{20,28},{24,16},{28,20},{1,9},{5... | collective-permute-start | bytes 835592 | tf_op jit(solution)/shard_map/ppermute | solution.py:298
  55.7 0.5 collective-permute-start.3
  56.2 4.5 %shard_map.61.t_m = bf16[256,2048]{1,0:T(8,128)(2,1)S(1)} custom-call(bf16[512,4096]{1,0:T(8,128)(2,1)S(1)} %get-tuple-element.81.refs_0_, bf16[512,4096]{1,0:T(8,128)(2,1)S(1)} %get-tuple-element.82.refs_1_, bf16[512,4096]{1,0:T(8,128)(2,1)S(1)} %get-tuple-element.83.refs_2_, bf16[512,4096]{1,0:T(8,128)(2,1)S(1)} %get-tuple-element.84.refs_3_, ...), custom_call_target="tpu_custom_call" | custom-call | flops 4294967296 | bytes 1048576 | tf_op jit(solution)/shard_map/pallas_call | solution.py:358
  60.7 2.1 %shard_map.63 = (f32[128,1152]{1,0:T(8,128)S(1)}, f32[32,1152]{1,0:T(8,128)S(1)}, bf16[160,1152]{1,0:T(8,128)(2,1)S(1)}, bf16[2176,2048]{1,0:T(8,128)(2,1)S(1)},...) custom-call(s32[1]{0:T(128)} %bitcast.place, ...), custom_call_target="tpu_custom_call", output_to_operand_aliasing={{3}: (1, {}), {4}: (2, {}), {5}: (3, {})} | custom-call | flops 1509949440 | bytes 1048576 | tf_op jit(solution)/shard_map/pallas_call | solution.py:358
  62.8 0.0 copy-start.1
  62.8 1.7 %shard_map.65 = (f32[128,1024]{1,0:T(8,128)S(1)}, f32[32,1024]{1,0:T(8,128)S(1)}, bf16[160,1024]{1,0:T(8,128)(2,1)S(1)}) custom-call(s32[1]{0:T(128)} %bitcast.place, bf16[2176,2048]{1,0:T(8,128)(2,1)S(1)} %get-tuple-element.92.density, bf16[256,2048]{1,0:T(8,128)(2,1)S(1)} %get-tuple-element.93.t_m, bf16[64,2048]{1,0:T(8,128)(2,1)S(1)} %get-tuple-element.94.t_b), custom_call_target="tpu_custom_call" | custom-call | flops 1342177280 | bytes 1048576 | tf_op jit(solution)/shard_map/pallas_call | solution.py:358
  64.5 0.1 collective-permute-start.11
  64.6 0.0 collective-permute-done.1.refs_2_
  64.6 0.0 collective-permute-done.2.refs_3_
  64.6 2.5 %collective-permute-done.3.refs_4_ = bf16[64,2176]{1,0:T(8,128)(2,1)S(1)} collective-permute-done((bf16[64,2176]{1,0:T(8,128)(2,1)S(1)}, bf16[64,2176]{1,0:T(8,128)(2,1)S(1)}, u32[]{:S(2)}, u32[]{:S(2)}) %collective-permute-start.3) | collective-permute-done | bytes 278560 | tf_op jit(solution)/shard_map/ppermute | solution.py:298
  67.0 0.2 shard_map.58
  67.2 6.1 %collective-permute-start.4 = (bf16[16,2176]{1,0:T(8,128)(2,1)S(1)}, bf16[16,2176]{1,0:T(8,128)(2,1)S(1)}, u32[]{:S(2)}, u32[]{:S(2)}) collective-permute-start(bf16[16,2176]{1,0:T(8,128)(2,1)S(1)} %get-tuple-element.77), channel_id=1, source_target_pairs={{0,1},{1,0},{2,3},{3,2},{4,5},{5,4},{6,7},{7,6},{8,9},{9,8},{10,11... | collective-permute-start | bytes 208904 | tf_op jit(solution)/shard_map/ppermute | solution.py:298
  73.3 1.1 collective-permute-start.5
  74.4 1.4 %collective-permute-start.6 = (bf16[16,2176]{1,0:T(8,128)(2,1)S(1)}, bf16[16,2176]{1,0:T(8,128)(2,1)S(1)}, u32[]{:S(2)}, u32[]{:S(2)}) collective-permute-start(bf16[16,2176]{1,0:T(8,128)(2,1)S(1)} %get-tuple-element.79), channel_id=1, source_target_pairs={{0,3},{1,2},{2,1},{3,0},{4,7},{5,6},{6,5},{7,4},{8,11},{9,10},{10,... | collective-permute-start | bytes 208904 | tf_op jit(solution)/shard_map/ppermute | solution.py:298
  75.8 0.4 hot.1.pick
  76.3 0.0 collective-permute-done.11.refs_2_
  76.3 0.1 shard_map.66
  76.4 1.6 %collective-permute-start.13 = (bf16[40,1024]{1,0:T(8,128)(2,1)S(1)}, bf16[40,1024]{1,0:T(8,128)(2,1)S(1)}, u32[]{:S(2)}, u32[]{:S(2)}) collective-permute-start(bf16[40,1024]{1,0:T(8,128)(2,1)S(1)} %get-tuple-element.100), channel_id=1, source_target_pairs={{0,16},{4,20},{8,24},{12,28},{16,0},{20,4},{24,8},{28,12},{1,17},{... | collective-permute-start | bytes 245768 | tf_op jit(solution)/shard_map/ppermute | solution.py:298
  78.0 0.0 collective-permute-done.4.refs_2_
  78.0 1.5 %collective-permute-start.15 = (bf16[40,1024]{1,0:T(8,128)(2,1)S(1)}, bf16[40,1024]{1,0:T(8,128)(2,1)S(1)}, u32[]{:S(2)}, u32[]{:S(2)}) collective-permute-start(bf16[40,1024]{1,0:T(8,128)(2,1)S(1)} %get-tuple-element.102), channel_id=1, source_target_pairs={{0,8},{4,12},{8,0},{12,4},{16,24},{20,28},{24,16},{28,20},{1,9},{5... | collective-permute-start | bytes 245768 | tf_op jit(solution)/shard_map/ppermute | solution.py:298
  79.5 0.0 collective-permute-done.5.refs_3_
  79.5 2.3 %collective-permute-start.17 = (bf16[40,1024]{1,0:T(8,128)(2,1)S(1)}, bf16[40,1024]{1,0:T(8,128)(2,1)S(1)}, u32[]{:S(2)}, u32[]{:S(2)}) collective-permute-start(bf16[40,1024]{1,0:T(8,128)(2,1)S(1)} %get-tuple-element.104), channel_id=1, source_target_pairs={{0,24},{4,28},{8,16},{12,20},{16,8},{20,12},{24,0},{28,4},{1,25},{... | collective-permute-start | bytes 245768 | tf_op jit(solution)/shard_map/ppermute | solution.py:298
  81.8 0.0 collective-permute-done.6.refs_4_
  81.8 0.0 collective-permute-done.10.refs_2_
  81.8 0.2 shard_map.64
  82.0 0.6 collective-permute-start.12
  82.6 1.4 %collective-permute-start.14 = (bf16[40,1152]{1,0:T(8,128)(2,1)S(1)}, bf16[40,1152]{1,0:T(8,128)(2,1)S(1)}, u32[]{:S(2)}, u32[]{:S(2)}) collective-permute-start(bf16[40,1152]{1,0:T(8,128)(2,1)S(1)} %get-tuple-element.101), channel_id=1, source_target_pairs={{0,8},{4,12},{8,0},{12,4},{16,24},{20,28},{24,16},{28,20},{1,9},{5... | collective-permute-start | bytes 276488 | tf_op jit(solution)/shard_map/ppermute | solution.py:298
  84.0 2.6 %collective-permute-done.12 = bf16[40,1152]{1,0:T(8,128)(2,1)S(1)} collective-permute-done((bf16[40,1152]{1,0:T(8,128)(2,1)S(1)}, bf16[40,1152]{1,0:T(8,128)(2,1)S(1)}, u32[]{:S(2)}, u32[]{:S(2)}) %collective-permute-start.12) | collective-permute-done | bytes 92192 | tf_op jit(solution)/shard_map/ppermute | solution.py:298
  86.7 1.8 %collective-permute-start.16 = (bf16[40,1152]{1,0:T(8,128)(2,1)S(1)}, bf16[40,1152]{1,0:T(8,128)(2,1)S(1)}, u32[]{:S(2)}, u32[]{:S(2)}) collective-permute-start(bf16[40,1152]{1,0:T(8,128)(2,1)S(1)} %get-tuple-element.103), channel_id=1, source_target_pairs={{0,24},{4,28},{8,16},{12,20},{16,8},{20,12},{24,0},{28,4},{1,25},{... | collective-permute-start | bytes 276488 | tf_op jit(solution)/shard_map/ppermute | solution.py:298
  88.5 3.6 %collective-permute-done.16 = bf16[40,1152]{1,0:T(8,128)(2,1)S(1)} collective-permute-done((bf16[40,1152]{1,0:T(8,128)(2,1)S(1)}, bf16[40,1152]{1,0:T(8,128)(2,1)S(1)}, u32[]{:S(2)}, u32[]{:S(2)}) %collective-permute-start.16) | collective-permute-done | bytes 92192 | tf_op jit(solution)/shard_map/ppermute | solution.py:298
  92.2 1.9 %collective-permute-start.20 = (bf16[24,2176]{1,0:T(8,128)(2,1)S(1)}, bf16[24,2176]{1,0:T(8,128)(2,1)S(1)}, u32[]{:S(2)}, u32[]{:S(2)}) collective-permute-start(bf16[24,2176]{1,0:T(8,128)(2,1)S(1)} %pad_maximum_fusion.2), channel_id=1, source_target_pairs={{0,24},{4,28},{8,16},{12,20},{16,8},{20,12},{24,0},{28,4},{1,25},{... | collective-permute-start | bytes 313352 | tf_op jit(solution)/shard_map/ppermute | solution.py:298
  94.1 0.6 collective-permute-start.19
  94.7 0.1 shard_map.68
  94.8 1.0 collective-permute-start.22
  95.8 2.6 %collective-permute-start.23 = (bf16[8,2176]{1,0:T(8,128)(2,1)S(1)}, bf16[8,2176]{1,0:T(8,128)(2,1)S(1)}, u32[]{:S(2)}, u32[]{:S(2)}) collective-permute-start(bf16[8,2176]{1,0:T(8,128)(2,1)S(1)} %get-tuple-element.109), channel_id=1, source_target_pairs={{0,2},{1,3},{2,0},{3,1},{4,6},{5,7},{6,4},{7,5},{8,10},{9,11},{10,... | collective-permute-start | bytes 104456 | tf_op jit(solution)/shard_map/ppermute | solution.py:298
  98.3 0.9 collective-permute-start.24
  99.3 1.3 %collective-permute-done.23.refs_2_ = bf16[8,2176]{1,0:T(8,128)(2,1)S(1)} collective-permute-done((bf16[8,2176]{1,0:T(8,128)(2,1)S(1)}, bf16[8,2176]{1,0:T(8,128)(2,1)S(1)}, u32[]{:S(2)}, u32[]{:S(2)}) %collective-permute-start.23) | collective-permute-done | bytes 34848 | tf_op jit(solution)/shard_map/ppermute | solution.py:298
  100.6 3.5 %collective-permute-done.24.refs_3_ = bf16[8,2176]{1,0:T(8,128)(2,1)S(1)} collective-permute-done((bf16[8,2176]{1,0:T(8,128)(2,1)S(1)}, bf16[8,2176]{1,0:T(8,128)(2,1)S(1)}, u32[]{:S(2)}, u32[]{:S(2)}) %collective-permute-start.24) | collective-permute-done | bytes 34848 | tf_op jit(solution)/shard_map/ppermute | solution.py:298
  104.1 1.5 %collective-permute-start.27 = (bf16[8,2176]{1,0:T(8,128)(2,1)S(1)}, bf16[8,2176]{1,0:T(8,128)(2,1)S(1)}, u32[]{:S(2)}, u32[]{:S(2)}) collective-permute-start(bf16[8,2176]{1,0:T(8,128)(2,1)S(1)} %shard_map.69), channel_id=1, source_target_pairs={{0,24},{4,28},{8,16},{12,20},{16,8},{20,12},{24,0},{28,4},{1,25},{... | collective-permute-start | bytes 104456 | tf_op jit(solution)/shard_map/ppermute | solution.py:298
  105.7 1.1 collective-permute-start.26
  106.7 0.9 collective-permute-start.25
  107.7 1.3 %collective-permute-done.27 = bf16[8,2176]{1,0:T(8,128)(2,1)S(1)} collective-permute-done((bf16[8,2176]{1,0:T(8,128)(2,1)S(1)}, bf16[8,2176]{1,0:T(8,128)(2,1)S(1)}, u32[]{:S(2)}, u32[]{:S(2)}) %collective-permute-start.27) | collective-permute-done | bytes 34848 | tf_op jit(solution)/shard_map/ppermute | solution.py:298
  109.0 1.1 collective-permute-start.18
  110.1 0.6 collective-permute-done.25
  110.7 0.1 collective-permute-start.28
  110.8 2.9 %collective-permute-done.18 = bf16[24,2176]{1,0:T(8,128)(2,1)S(1)} collective-permute-done((bf16[24,2176]{1,0:T(8,128)(2,1)S(1)}, bf16[24,2176]{1,0:T(8,128)(2,1)S(1)}, u32[]{:S(2)}, u32[]{:S(2)}) %collective-permute-start.18) | collective-permute-done | bytes 104480 | tf_op jit(solution)/shard_map/ppermute | solution.py:298
  113.8 0.1 collective-permute-start.21
  113.9 1.7 %collective-permute-done.21 = bf16[96,2176]{1,0:T(8,128)(2,1)S(1)} collective-permute-done((bf16[96,2176]{1,0:T(8,128)(2,1)S(1)}, bf16[96,2176]{1,0:T(8,128)(2,1)S(1)}, u32[]{:S(2)}, u32[]{:S(2)}) %collective-permute-start.21) | collective-permute-done | bytes 417824 | tf_op jit(solution)/shard_map/ppermute | solution.py:298
  115.6 1.7 %pick.1 = f32[512,256]{1,0:T(8,128)} custom-call(s32[1]{0:T(128)} %bitcast.place, bf16[2176,512]{1,0:T(8,128)(2,1)S(1)} %hot.1.pick, bf16[192,2176]{1,0:T(8,128)(2,1)S(1)} %constant_dynamic-update-slice_fusion.11.refs_0_, bf16[64,2176]{1,0:T(8,128)(2,1)S(1)} %constant_dynamic-update-slice_fusion.17.refs_1_), custom_call_target="tpu_custom_call" | custom-call | tf_op jit(solution)/shard_map/pick/pallas_call | solution.py:533
  (36 shorter events, 0.4 us)
Async XLA Ops:
  11.8 21.5 %copy-start = (bf16[45,4096]{1,0:T(8,128)(2,1)S(1)}, bf16[45,4096]{1,0:T(8,128)(2,1)}, u32[]{:S(2)}) copy-start(bf16[45,4096]{1,0:T(8,128)(2,1)} %val.3) | copy-start | bytes 1105924
  27.5 24.7 %collective-permute-start = (bf16[256,2176]{1,0:T(8,128)(2,1)S(1)}, bf16[256,2176]{1,0:T(8,128)(2,1)S(1)}, u32[]{:S(2)}, u32[]{:S(2)}) collective-permute-start(bf16[256,2176]{1,0:T(8,128)(2,1)S(1)} %get-tuple-element.67.refs_0_), channel_id=1, source_target_pairs={{0,4},{4,0},{8,12},{12,8},{16,20},{20,16},{24,28},{28,24},{1,5},{5... | collective-permute-start | bytes 3342344 | tf_op jit(solution)/shard_map/ppermute | solution.py:298
  28.1 14.7 %collective-permute-start.7 = (bf16[64,2048]{1,0:T(8,128)(2,1)S(1)}, bf16[64,2048]{1,0:T(8,128)(2,1)S(1)}, u32[]{:S(2)}, u32[]{:S(2)}) collective-permute-start(bf16[64,2048]{1,0:T(8,128)(2,1)S(1)} %get-tuple-element.64.refs_6_), channel_id=1, source_target_pairs={{0,1},{1,0},{2,3},{3,2},{4,5},{5,4},{6,7},{7,6},{8,9},{9,8},{10,11... | collective-permute-start | bytes 786440 | tf_op jit(solution)/shard_map/ppermute | solution.py:298
  30.7 21.4 %collective-permute-start.8 = (bf16[64,2048]{1,0:T(8,128)(2,1)S(1)}, bf16[64,2048]{1,0:T(8,128)(2,1)S(1)}, u32[]{:S(2)}, u32[]{:S(2)}) collective-permute-start(bf16[64,2048]{1,0:T(8,128)(2,1)S(1)} %get-tuple-element.65.refs_7_), channel_id=1, source_target_pairs={{0,2},{1,3},{2,0},{3,1},{4,6},{5,7},{6,4},{7,5},{8,10},{9,11},{10,... | collective-permute-start | bytes 786440 | tf_op jit(solution)/shard_map/ppermute | solution.py:298
  33.3 18.8 %collective-permute-start.9 = (bf16[64,2048]{1,0:T(8,128)(2,1)S(1)}, bf16[64,2048]{1,0:T(8,128)(2,1)S(1)}, u32[]{:S(2)}, u32[]{:S(2)}) collective-permute-start(bf16[64,2048]{1,0:T(8,128)(2,1)S(1)} %get-tuple-element.66.refs_8_), channel_id=1, source_target_pairs={{0,3},{1,2},{2,1},{3,0},{4,7},{5,6},{6,5},{7,4},{8,11},{9,10},{10,... | collective-permute-start | bytes 786440 | tf_op jit(solution)/shard_map/ppermute | solution.py:298
  52.7 11.9 %collective-permute-start.1 = (bf16[64,2176]{1,0:T(8,128)(2,1)S(1)}, bf16[64,2176]{1,0:T(8,128)(2,1)S(1)}, u32[]{:S(2)}, u32[]{:S(2)}) collective-permute-start(bf16[64,2176]{1,0:T(8,128)(2,1)S(1)} %get-tuple-element.72.refs_5_), channel_id=1, source_target_pairs={{0,16},{4,20},{8,24},{12,28},{16,0},{20,4},{24,8},{28,12},{1,17},{... | collective-permute-start | bytes 835592 | tf_op jit(solution)/shard_map/ppermute | solution.py:298
  54.3 10.3 %collective-permute-start.2 = (bf16[64,2176]{1,0:T(8,128)(2,1)S(1)}, bf16[64,2176]{1,0:T(8,128)(2,1)S(1)}, u32[]{:S(2)}, u32[]{:S(2)}) collective-permute-start(bf16[64,2176]{1,0:T(8,128)(2,1)S(1)} %get-tuple-element.73.refs_6_), channel_id=1, source_target_pairs={{0,8},{4,12},{8,0},{12,4},{16,24},{20,28},{24,16},{28,20},{1,9},{5... | collective-permute-start | bytes 835592 | tf_op jit(solution)/shard_map/ppermute | solution.py:298
  55.7 11.3 %collective-permute-start.3 = (bf16[64,2176]{1,0:T(8,128)(2,1)S(1)}, bf16[64,2176]{1,0:T(8,128)(2,1)S(1)}, u32[]{:S(2)}, u32[]{:S(2)}) collective-permute-start(bf16[64,2176]{1,0:T(8,128)(2,1)S(1)} %get-tuple-element.74.refs_7_), channel_id=1, source_target_pairs={{0,24},{4,28},{8,16},{12,20},{16,8},{20,12},{24,0},{28,4},{1,25},{... | collective-permute-start | bytes 835592 | tf_op jit(solution)/shard_map/ppermute | solution.py:298
  62.8 13.1 %copy-start.1 = (s32[4096,2]{0,1:T(2,128)S(1)}, s32[4096,2]{0,1:T(2,128)}, u32[]{:S(2)}) copy-start(s32[4096,2]{0,1:T(2,128)} %param.9) | copy-start | bytes 98308
  64.5 11.8 %collective-permute-start.11 = (bf16[160,1024]{1,0:T(8,128)(2,1)S(1)}, bf16[160,1024]{1,0:T(8,128)(2,1)S(1)}, u32[]{:S(2)}, u32[]{:S(2)}) collective-permute-start(bf16[160,1024]{1,0:T(8,128)(2,1)S(1)} %get-tuple-element.97), channel_id=1, source_target_pairs={{0,4},{4,0},{8,12},{12,8},{16,20},{20,16},{24,28},{28,24},{1,5},{5... | collective-permute-start | bytes 983048 | tf_op jit(solution)/shard_map/ppermute | solution.py:298
  67.2 10.8 %collective-permute-start.4 = (bf16[16,2176]{1,0:T(8,128)(2,1)S(1)}, bf16[16,2176]{1,0:T(8,128)(2,1)S(1)}, u32[]{:S(2)}, u32[]{:S(2)}) collective-permute-start(bf16[16,2176]{1,0:T(8,128)(2,1)S(1)} %get-tuple-element.77), channel_id=1, source_target_pairs={{0,1},{1,0},{2,3},{3,2},{4,5},{5,4},{6,7},{7,6},{8,9},{9,8},{10,11... | collective-permute-start | bytes 208904 | tf_op jit(solution)/shard_map/ppermute | solution.py:298
  73.3 6.1 %collective-permute-start.5 = (bf16[16,2176]{1,0:T(8,128)(2,1)S(1)}, bf16[16,2176]{1,0:T(8,128)(2,1)S(1)}, u32[]{:S(2)}, u32[]{:S(2)}) collective-permute-start(bf16[16,2176]{1,0:T(8,128)(2,1)S(1)} %get-tuple-element.78), channel_id=1, source_target_pairs={{0,2},{1,3},{2,0},{3,1},{4,6},{5,7},{6,4},{7,5},{8,10},{9,11},{10,... | collective-permute-start | bytes 208904 | tf_op jit(solution)/shard_map/ppermute | solution.py:298
  74.4 7.3 %collective-permute-start.6 = (bf16[16,2176]{1,0:T(8,128)(2,1)S(1)}, bf16[16,2176]{1,0:T(8,128)(2,1)S(1)}, u32[]{:S(2)}, u32[]{:S(2)}) collective-permute-start(bf16[16,2176]{1,0:T(8,128)(2,1)S(1)} %get-tuple-element.79), channel_id=1, source_target_pairs={{0,3},{1,2},{2,1},{3,0},{4,7},{5,6},{6,5},{7,4},{8,11},{9,10},{10,... | collective-permute-start | bytes 208904 | tf_op jit(solution)/shard_map/ppermute | solution.py:298
  75.8 6.0 %collective-permute-start.10 = (bf16[160,1152]{1,0:T(8,128)(2,1)S(1)}, bf16[160,1152]{1,0:T(8,128)(2,1)S(1)}, u32[]{:S(2)}, u32[]{:S(2)}) collective-permute-start(bf16[160,1152]{1,0:T(8,128)(2,1)S(1)} %get-tuple-element.90), channel_id=1, source_target_pairs={{0,4},{4,0},{8,12},{12,8},{16,20},{20,16},{24,28},{28,24},{1,5},{5... | collective-permute-start | bytes 1105928 | tf_op jit(solution)/shard_map/ppermute | solution.py:298
  76.4 15.7 %collective-permute-start.13 = (bf16[40,1024]{1,0:T(8,128)(2,1)S(1)}, bf16[40,1024]{1,0:T(8,128)(2,1)S(1)}, u32[]{:S(2)}, u32[]{:S(2)}) collective-permute-start(bf16[40,1024]{1,0:T(8,128)(2,1)S(1)} %get-tuple-element.100), channel_id=1, source_target_pairs={{0,16},{4,20},{8,24},{12,28},{16,0},{20,4},{24,8},{28,12},{1,17},{... | collective-permute-start | bytes 245768 | tf_op jit(solution)/shard_map/ppermute | solution.py:298
  78.0 14.2 %collective-permute-start.15 = (bf16[40,1024]{1,0:T(8,128)(2,1)S(1)}, bf16[40,1024]{1,0:T(8,128)(2,1)S(1)}, u32[]{:S(2)}, u32[]{:S(2)}) collective-permute-start(bf16[40,1024]{1,0:T(8,128)(2,1)S(1)} %get-tuple-element.102), channel_id=1, source_target_pairs={{0,8},{4,12},{8,0},{12,4},{16,24},{20,28},{24,16},{28,20},{1,9},{5... | collective-permute-start | bytes 245768 | tf_op jit(solution)/shard_map/ppermute | solution.py:298
  79.5 12.7 %collective-permute-start.17 = (bf16[40,1024]{1,0:T(8,128)(2,1)S(1)}, bf16[40,1024]{1,0:T(8,128)(2,1)S(1)}, u32[]{:S(2)}, u32[]{:S(2)}) collective-permute-start(bf16[40,1024]{1,0:T(8,128)(2,1)S(1)} %get-tuple-element.104), channel_id=1, source_target_pairs={{0,24},{4,28},{8,16},{12,20},{16,8},{20,12},{24,0},{28,4},{1,25},{... | collective-permute-start | bytes 245768 | tf_op jit(solution)/shard_map/ppermute | solution.py:298
  82.0 4.7 %collective-permute-start.12 = (bf16[40,1152]{1,0:T(8,128)(2,1)S(1)}, bf16[40,1152]{1,0:T(8,128)(2,1)S(1)}, u32[]{:S(2)}, u32[]{:S(2)}) collective-permute-start(bf16[40,1152]{1,0:T(8,128)(2,1)S(1)} %get-tuple-element.99), channel_id=1, source_target_pairs={{0,16},{4,20},{8,24},{12,28},{16,0},{20,4},{24,8},{28,12},{1,17},{... | collective-permute-start | bytes 276488 | tf_op jit(solution)/shard_map/ppermute | solution.py:298
  82.6 5.9 %collective-permute-start.14 = (bf16[40,1152]{1,0:T(8,128)(2,1)S(1)}, bf16[40,1152]{1,0:T(8,128)(2,1)S(1)}, u32[]{:S(2)}, u32[]{:S(2)}) collective-permute-start(bf16[40,1152]{1,0:T(8,128)(2,1)S(1)} %get-tuple-element.101), channel_id=1, source_target_pairs={{0,8},{4,12},{8,0},{12,4},{16,24},{20,28},{24,16},{28,20},{1,9},{5... | collective-permute-start | bytes 276488 | tf_op jit(solution)/shard_map/ppermute | solution.py:298
  86.7 5.5 %collective-permute-start.16 = (bf16[40,1152]{1,0:T(8,128)(2,1)S(1)}, bf16[40,1152]{1,0:T(8,128)(2,1)S(1)}, u32[]{:S(2)}, u32[]{:S(2)}) collective-permute-start(bf16[40,1152]{1,0:T(8,128)(2,1)S(1)} %get-tuple-element.103), channel_id=1, source_target_pairs={{0,24},{4,28},{8,16},{12,20},{16,8},{20,12},{24,0},{28,4},{1,25},{... | collective-permute-start | bytes 276488 | tf_op jit(solution)/shard_map/ppermute | solution.py:298
  92.2 21.5 %collective-permute-start.20 = (bf16[24,2176]{1,0:T(8,128)(2,1)S(1)}, bf16[24,2176]{1,0:T(8,128)(2,1)S(1)}, u32[]{:S(2)}, u32[]{:S(2)}) collective-permute-start(bf16[24,2176]{1,0:T(8,128)(2,1)S(1)} %pad_maximum_fusion.2), channel_id=1, source_target_pairs={{0,24},{4,28},{8,16},{12,20},{16,8},{20,12},{24,0},{28,4},{1,25},{... | collective-permute-start | bytes 313352 | tf_op jit(solution)/shard_map/ppermute | solution.py:298
  94.1 19.6 %collective-permute-start.19 = (bf16[24,2176]{1,0:T(8,128)(2,1)S(1)}, bf16[24,2176]{1,0:T(8,128)(2,1)S(1)}, u32[]{:S(2)}, u32[]{:S(2)}) collective-permute-start(bf16[24,2176]{1,0:T(8,128)(2,1)S(1)} %pad_maximum_fusion.2), channel_id=1, source_target_pairs={{0,16},{4,20},{8,24},{12,28},{16,0},{20,4},{24,8},{28,12},{1,17},{... | collective-permute-start | bytes 313352 | tf_op jit(solution)/shard_map/ppermute | solution.py:298
  94.8 4.5 %collective-permute-start.22 = (bf16[8,2176]{1,0:T(8,128)(2,1)S(1)}, bf16[8,2176]{1,0:T(8,128)(2,1)S(1)}, u32[]{:S(2)}, u32[]{:S(2)}) collective-permute-start(bf16[8,2176]{1,0:T(8,128)(2,1)S(1)} %get-tuple-element.108), channel_id=1, source_target_pairs={{0,1},{1,0},{2,3},{3,2},{4,5},{5,4},{6,7},{7,6},{8,9},{9,8},{10,11... | collective-permute-start | bytes 104456 | tf_op jit(solution)/shard_map/ppermute | solution.py:298
  95.8 4.8 %collective-permute-start.23 = (bf16[8,2176]{1,0:T(8,128)(2,1)S(1)}, bf16[8,2176]{1,0:T(8,128)(2,1)S(1)}, u32[]{:S(2)}, u32[]{:S(2)}) collective-permute-start(bf16[8,2176]{1,0:T(8,128)(2,1)S(1)} %get-tuple-element.109), channel_id=1, source_target_pairs={{0,2},{1,3},{2,0},{3,1},{4,6},{5,7},{6,4},{7,5},{8,10},{9,11},{10,... | collective-permute-start | bytes 104456 | tf_op jit(solution)/shard_map/ppermute | solution.py:298
  98.3 5.7 %collective-permute-start.24 = (bf16[8,2176]{1,0:T(8,128)(2,1)S(1)}, bf16[8,2176]{1,0:T(8,128)(2,1)S(1)}, u32[]{:S(2)}, u32[]{:S(2)}) collective-permute-start(bf16[8,2176]{1,0:T(8,128)(2,1)S(1)} %get-tuple-element.110), channel_id=1, source_target_pairs={{0,3},{1,2},{2,1},{3,0},{4,7},{5,6},{6,5},{7,4},{8,11},{9,10},{10,... | collective-permute-start | bytes 104456 | tf_op jit(solution)/shard_map/ppermute | solution.py:298
  104.1 4.9 %collective-permute-start.27 = (bf16[8,2176]{1,0:T(8,128)(2,1)S(1)}, bf16[8,2176]{1,0:T(8,128)(2,1)S(1)}, u32[]{:S(2)}, u32[]{:S(2)}) collective-permute-start(bf16[8,2176]{1,0:T(8,128)(2,1)S(1)} %shard_map.69), channel_id=1, source_target_pairs={{0,24},{4,28},{8,16},{12,20},{16,8},{20,12},{24,0},{28,4},{1,25},{... | collective-permute-start | bytes 104456 | tf_op jit(solution)/shard_map/ppermute | solution.py:298
  105.7 4.5 %collective-permute-start.26 = (bf16[8,2176]{1,0:T(8,128)(2,1)S(1)}, bf16[8,2176]{1,0:T(8,128)(2,1)S(1)}, u32[]{:S(2)}, u32[]{:S(2)}) collective-permute-start(bf16[8,2176]{1,0:T(8,128)(2,1)S(1)} %shard_map.69), channel_id=1, source_target_pairs={{0,16},{4,20},{8,24},{12,28},{16,0},{20,4},{24,8},{28,12},{1,17},{... | collective-permute-start | bytes 104456 | tf_op jit(solution)/shard_map/ppermute | solution.py:298
  106.7 3.9 %collective-permute-start.25 = (bf16[8,2176]{1,0:T(8,128)(2,1)S(1)}, bf16[8,2176]{1,0:T(8,128)(2,1)S(1)}, u32[]{:S(2)}, u32[]{:S(2)}) collective-permute-start(bf16[8,2176]{1,0:T(8,128)(2,1)S(1)} %shard_map.69), channel_id=1, source_target_pairs={{0,8},{4,12},{8,0},{12,4},{16,24},{20,28},{24,16},{28,20},{1,9},{5... | collective-permute-start | bytes 104456 | tf_op jit(solution)/shard_map/ppermute | solution.py:298
  109.0 4.7 %collective-permute-start.18 = (bf16[24,2176]{1,0:T(8,128)(2,1)S(1)}, bf16[24,2176]{1,0:T(8,128)(2,1)S(1)}, u32[]{:S(2)}, u32[]{:S(2)}) collective-permute-start(bf16[24,2176]{1,0:T(8,128)(2,1)S(1)} %pad_maximum_fusion.2), channel_id=1, source_target_pairs={{0,8},{4,12},{8,0},{12,4},{16,24},{20,28},{24,16},{28,20},{1,9},{5... | collective-permute-start | bytes 313352 | tf_op jit(solution)/shard_map/ppermute | solution.py:298
  110.7 3.2 %collective-permute-start.28 = (bf16[32,2176]{1,0:T(8,128)(2,1)S(1)}, bf16[32,2176]{1,0:T(8,128)(2,1)S(1)}, u32[]{:S(2)}, u32[]{:S(2)}) collective-permute-start(bf16[32,2176]{1,0:T(8,128)(2,1)S(1)} %pad_maximum_fusion.1), channel_id=1, source_target_pairs={{0,4},{4,0},{8,12},{12,8},{16,20},{20,16},{24,28},{28,24},{1,5},{5... | collective-permute-start | bytes 417800 | tf_op jit(solution)/shard_map/ppermute | solution.py:298
  113.8 1.8 %collective-permute-start.21 = (bf16[96,2176]{1,0:T(8,128)(2,1)S(1)}, bf16[96,2176]{1,0:T(8,128)(2,1)S(1)}, u32[]{:S(2)}, u32[]{:S(2)}) collective-permute-start(bf16[96,2176]{1,0:T(8,128)(2,1)S(1)} %get-tuple-element.111), channel_id=1, source_target_pairs={{0,4},{4,0},{8,12},{12,8},{16,20},{20,16},{24,28},{28,24},{1,5},{5... | collective-permute-start | bytes 1253384 | tf_op jit(solution)/shard_map/ppermute | solution.py:298
